TPU v7x, 32 devices: a whole 2x2x4 slice. The times are simulated.
32 devices in a mesh: groups: 2 (over y), dp: 4 (over z), replica: 2 (over x), chan: 2 (over core).
Axes of the slice: x: 2, y: 2, z: 4, core: 2. Of those that a mesh axis runs over, the one named last changes fastest.
Arguments:
- activations: bfloat16 [8192, 768], P(('groups', 'dp', 'replica'), 'chan'), parts along dimension 0, may hold values from -6 to 6
- cotangent: bfloat16 [8192, 768], P(('groups', 'dp', 'replica'), 'chan'), parts along dimension 0, may hold values from -0.1875 to 0.1875
- conv_weights: bfloat16 [3, 3, 768, 768], P(None, None, None, 'chan'), may hold values from -0.125 to 0.125
- snake_alpha: float32 [3, 768], P(None, 'chan'), may hold values from 0.4 to 2.5
- seg_lengths: int32 [32], P('groups'), parts along dimension 0, may hold values from 32 to 248, as said below
- seg_owner: int32 [32], P('groups'), parts along dimension 0, may hold values from 0 to 7, as said below
- seg_start: int32 [32], P('groups'), parts along dimension 0, may hold values from 5 to 261, as said below
Outputs:
- residual_out: bfloat16 [8192, 768], P(('groups', 'dp', 'replica'), 'chan'), parts along dimension 0
- weight_grads: float32 [6, 3, 768, 768], P('groups', None, 'dp', 'chan'), parts along dimension 0
- alpha_grads: float32 [6, 768], P('groups', 'chan'), parts along dimension 0
There are 2 independent parts, one for each index of `groups`. A program takes and returns all parts, laid end to end along the dimension named above; an argument that names none is the same for every part. Nothing has to cross between parts.
Inputs may be any that keep to these rules, and one draw needn't show every extreme that they name: `seg_lengths`: every clip has 32 to 248 positions; some clip has exactly 248. `seg_owner`: every data device (numbered in the order dp, then replica) holds exactly 2 clips. `seg_start`: A device's clips lie one after another in its buffer; the first starts at position 5, and 5 to 8 unused positions stand before every later one; all end within the buffer; some clip starts at exactly 261.
All inputs are finite; a program needn't handle non-finite values.
Results may differ from a plain program's by a relative error of at most 0.014.
The roundings to bfloat16 on the way count: a program that leaves them out, or rounds other values in their place, can miss the bound.
Values may be sent and summed in bfloat16 or wider, within the bound.
No kernel may reach another device: no remote copies, remote signals or barrier semaphores. Data moves between devices by JAX's collectives and lax.ppermute only.
A program may use at most 64 MiB of HBM per device.

v0:
```python
import jax
import jax.numpy as jnp
from jax import lax
from jax.sharding import PartitionSpec as P

dilations = (1, 3, 5)


def from_partner(x, axis, apart):
    return lax.ppermute(x, axis, [(i, i ^ 1 << apart) for i in range(lax.axis_size(axis))])


def shift_rows(values, offset):
    if offset == 0:
        return values
    if offset > 0:
        return jnp.pad(values[offset:], ((0, offset), (0, 0)))
    return jnp.pad(values[:offset], ((-offset, 0), (0, 0)))


def live_mask(seg_lengths, seg_owner, seg_start, device, row_count):
    position = jnp.arange(row_count, dtype=jnp.int32)[None, :]
    inside = (
        (seg_owner[:, None] == device)
        & (position >= seg_start[:, None])
        & (position < seg_start[:, None] + seg_lengths[:, None])
    )
    return jnp.any(inside, axis=0).astype(jnp.float32)[:, None]


def reduce_rows(partials):
    summed = lax.psum_scatter(partials.astype(jnp.bfloat16), "dp", scatter_dimension=2, tiled=True)
    return lax.psum(summed, "replica").astype(jnp.float32)


def on_device(activations, cotangent, conv_weights, snake_alpha, seg_lengths, seg_owner, seg_start):
    row_count = activations.shape[0]
    layer_count = conv_weights.shape[0]
    tap_count = conv_weights.shape[1]
    half_width = conv_weights.shape[3]
    device = lax.axis_index(("dp", "replica"))
    chan_index = lax.axis_index("chan")
    live_rows = live_mask(seg_lengths, seg_owner, seg_start, device, row_count)
    stream = activations.astype(jnp.float32) * live_rows
    saved_streams = []
    saved_snaked = []
    for layer_idx in range(layer_count):
        dilation = dilations[layer_idx]
        alpha_row = snake_alpha[layer_idx][None, :]
        snaked = (stream + jnp.sin(alpha_row * stream) ** 2 / alpha_row).astype(jnp.bfloat16)
        full_snaked = lax.all_gather(snaked, "chan", axis=1, tiled=True)
        conv_out = jnp.zeros(stream.shape, jnp.float32)
        for tap_index in range(tap_count):
            conv_out = conv_out + jnp.dot(
                shift_rows(full_snaked, (tap_index - 1) * dilation),
                conv_weights[layer_idx, tap_index],
                preferred_element_type=jnp.float32,
            )
        saved_streams.append(stream)
        saved_snaked.append(full_snaked)
        stream = (stream + conv_out) * live_rows
    residual_out = stream.astype(jnp.bfloat16)
    grad_flow = cotangent.astype(jnp.float32) * live_rows
    layer_parts = [None] * layer_count
    alpha_parts = [None] * layer_count
    for layer_idx in reversed(range(layer_count)):
        dilation = dilations[layer_idx]
        alpha_row = snake_alpha[layer_idx][None, :]
        grad_bf = grad_flow.astype(jnp.bfloat16)
        full_snaked = saved_snaked[layer_idx]
        weight_part = jnp.stack(
            [
                lax.dot_general(
                    shift_rows(full_snaked, (tap_index - 1) * dilation),
                    grad_bf,
                    (((0,), (0,)), ((), ())),
                    preferred_element_type=jnp.float32,
                )
                for tap_index in range(tap_count)
            ]
        )
        back_full = jnp.zeros((row_count, conv_weights.shape[2]), jnp.float32)
        for tap_index in range(tap_count):
            back_full = back_full + lax.dot_general(
                shift_rows(grad_bf, -(tap_index - 1) * dilation),
                conv_weights[layer_idx, tap_index],
                (((1,), (1,)), ((), ())),
                preferred_element_type=jnp.float32,
            )
        own_part = lax.dynamic_slice_in_dim(back_full, chan_index * half_width, half_width, 1)
        partner_part = lax.dynamic_slice_in_dim(
            back_full, jnp.bitwise_xor(chan_index, 1) * half_width, half_width, 1
        )
        snake_back = own_part + from_partner(partner_part.astype(jnp.bfloat16), "chan", 0).astype(
            partner_part.dtype
        )
        previous = saved_streams[layer_idx]
        alpha_parts[layer_idx] = jnp.sum(
            snake_back
            * (
                previous * jnp.sin(2.0 * alpha_row * previous) / alpha_row
                - jnp.sin(alpha_row * previous) ** 2 / alpha_row**2
            ),
            axis=0,
        )
        if layer_idx > 0:
            grad_flow = (
                grad_flow + snake_back * (1.0 + jnp.sin(2.0 * alpha_row * previous))
            ) * live_rows
        layer_parts[layer_idx] = weight_part
    weight_grads = reduce_rows(jnp.stack(layer_parts))
    alpha_grads = lax.psum(jnp.stack(alpha_parts), ("dp", "replica"))
    return (residual_out, weight_grads, alpha_grads)


def solution(mesh):
    return jax.shard_map(
        on_device,
        mesh=mesh,
        in_specs=(
            P(("groups", "dp", "replica"), "chan"),
            P(("groups", "dp", "replica"), "chan"),
            P(None, None, None, "chan"),
            P(None, "chan"),
            P("groups"),
            P("groups"),
            P("groups"),
        ),
        out_specs=(
            P(("groups", "dp", "replica"), "chan"),
            P("groups", None, "dp", "chan"),
            P("groups", "chan"),
        ),
        check_vma=False,
    )
```

profile of v0, /device:TPU:0, one launch (start us, length us, event | category | flops | bytes accessed | tf_op | source)
XLA Modules:
  0.0 233.2 jit_solution(4009976965716789816)
XLA Ops:
  7.2 1.4 multiply_reduce_fusion.6
  10.7 4.7 %fusion.16 = (bf16[512,384]{1,0:T(8,128)(2,1)S(1)}, bf16[512,384]{1,0:T(8,128)(2,1)}) fusion(bf16[512,384]{1,0:T(8,128)(2,1)} %param.8, f32[512]{0:T(512)S(1)} %convert_element_type.87, f32[384]{0:T(512)S(1)} %get-tuple-element.9, bf16[512,384]{1,0:T(8,128)(2,1)} %param.7), kind=kLoop, calls=%fused_computation.51 | loop fusion | flops 1966080 | bytes 1576448 | tf_op jit(solution)/shard_map/convert_element_type | solution.py:69
  16.3 1.7 fusion.34
  17.9 1.7 fusion.37
  19.6 1.8 add_add_fusion.2
  21.5 0.9 dynamic-slice_convert_fusion.2
  22.8 2.4 %all_gather.9 = bf16[512,768]{1,0:T(8,128)(2,1)S(1)} all-gather(bf16[512,384]{1,0:T(8,128)(2,1)S(1)} %copy-done.11), channel_id=1, replica_groups=mesh['groups'=2,'dp'=4,'replica'=2,'chan'=2] {'chan'}, dimensions={1}, use_global_device_ids=true | all-gather | bytes 1179648 | tf_op jit(solution)/shard_map/all_gather | solution.py:51
  25.4 1.9 fusion.30
  27.4 1.7 convolution_add_fusion.5
  29.1 5.1 %add_convert_fusion.1 = (bf16[512,384]{1,0:T(8,128)(2,1)S(1)}, f32[512,384]{1,0:T(8,128)}) fusion(f32[384]{0:T(512)S(1)} %copy-done.20, f32[512,384]{1,0:T(8,128)S(1)} %convolution_add_fusion.5, bf16[3,3,768,384]{3,2,1,0:T(8,128)(2,1)} %param.9, bf16[511,768]{1,0:T(8,128)(2,1)S(1)} %get-tuple-element.22, f32[512]{0:T(512)S(1)} %convert_element_type.87, ...), kind=kOutput, calls=%fused_computation.54 | convolution fusion | flops 303955968 | bytes 3737600 | tf_op jit(solution)/shard_map/dot_general | solution.py:54
  34.2 2.5 %all_gather.10 = bf16[512,768]{1,0:T(8,128)(2,1)S(1)} all-gather(bf16[512,384]{1,0:T(8,128)(2,1)S(1)} %get-tuple-element.32), channel_id=1, replica_groups=mesh['groups'=2,'dp'=4,'replica'=2,'chan'=2] {'chan'}, dimensions={1}, use_global_device_ids=true | all-gather | bytes 1179648 | tf_op jit(solution)/shard_map/all_gather | solution.py:51
  36.8 1.1 fusion.103
  38.8 1.6 fusion.25
  40.5 1.8 convolution_add_fusion.3
  42.3 8.8 %fusion.101 = (bf16[512,384]{1,0:T(8,128)(2,1)S(1)}, f32[512,384]{1,0:T(8,128)S(1)}, f32[384]{0:T(512)}, bf16[512,384]{1,0:T(8,128)(2,1)S(1)}, f32[512,384]{1,0:T(8,128)}) fusion(f32[384]{0:T(512)} %get-tuple-element.7, bf16[512,384]{1,0:T(8,128)(2,1)} %collective-permute-done, f32[512,768]{1,0:T(8,128)S(1)} %copy-done.8, s32[]{:T(128)S(6)} %select_n.4, ...), kind=kOutput, calls=%fused_computation.156 | convolution fusion | flops 306708096 | bytes 6891012 | tf_op jit(solution)/shard_map/dot_general | solution.py:54
  51.1 2.4 %all_gather.11 = bf16[512,768]{1,0:T(8,128)(2,1)S(1)} all-gather(bf16[512,384]{1,0:T(8,128)(2,1)S(1)} %get-tuple-element.17), channel_id=1, replica_groups=mesh['groups'=2,'dp'=4,'replica'=2,'chan'=2] {'chan'}, dimensions={1}, use_global_device_ids=true | all-gather | bytes 1179648 | tf_op jit(solution)/shard_map/all_gather | solution.py:51
  56.3 1.7 fusion.42
  59.2 1.7 fusion.45
  60.8 1.7 add_add_fusion.1
  64.4 6.3 %multiply_reduce_fusion.1 = (f32[384]{0:T(512)}, bf16[512,384]{1,0:T(8,128)(2,1)S(1)}) fusion(f32[512,384]{1,0:T(8,128)S(1)} %copy-done.15, bf16[512,384]{1,0:T(8,128)(2,1)S(1)} %collective-permute-done.1, f32[512,768]{1,0:T(8,128)S(1)} %add_add_fusion.1, s32[]{:T(128)S(6)} %select_n.4, f32[384]{0:T(512)S(1)} %copy-done.19, f32[384]{0:T(512)S(1)} %copy-done.18, ...), kind=kLoop, calls=%fused_computation.39 | loop fusion | flops 3145344 | bytes 3153924 | tf_op jit(solution)/shard_map/reduce_sum | solution.py:98
  72.8 3.0 %pad_maximum_fusion = bf16[3,3,768,384]{3,2,1,0:T(8,128)(2,1)} fusion(bf16[1,3,768,384]{3,2,1,0:T(8,128)(2,1)S(1)} %maximum_bitcast_fusion.2, bf16[1,3,768,384]{3,2,1,0:T(8,128)(2,1)S(1)} %maximum_bitcast_fusion.1, bf16[1,3,768,384]{3,2,1,0:T(8,128)(2,1)S(1)} %maximum_bitcast_fusion), kind=kLoop, calls=%fused_computation | loop fusion | flops 5308416 | bytes 10616832 | tf_op jit(solution)/shard_map/stack | solution.py:111
  76.9 2.6 %fusion.20 = f32[512,384]{1,0:T(8,128)} fusion(bf16[507,768]{1,0:T(8,128)(2,1)S(1)} %copy-done.1, bf16[3,3,768,384]{3,2,1,0:T(8,128)(2,1)} %param.9), kind=kOutput, calls=%fused_computation.62 | convolution fusion | flops 301989888 | bytes 2155008 | tf_op jit(solution)/shard_map/dot_general | solution.py:54
  80.3 1.7 fusion.53
  82.0 2.8 %fusion.50 = f32[512,768]{1,0:T(8,128)} fusion(bf16[512,384]{1,0:T(8,128)(2,1)S(1)} %get-tuple-element.15, bf16[3,3,768,384]{3,2,1,0:T(8,128)(2,1)} %param.9), kind=kOutput, calls=%fused_computation.92 | convolution fusion | flops 301989888 | bytes 2555904 | tf_op jit(solution)/shard_map/dot_general | solution.py:84
  84.8 88.5 %reduce-scatter.2.cloned.1.call-done = bf16[3,3,192,384]{3,2,1,0:T(8,128)(2,1)} async-done(((bf16[3,3,768,384]{3,2,1,0:T(8,128)(2,1)}), bf16[3,3,192,384]{3,2,1,0:T(8,128)(2,1)}) %reduce-scatter.2.cloned.1.call-update) | async-done | bytes 1327120 | tf_op jit(solution)/shard_map/reduce_scatter | solution.py:32
  173.3 2.4 %add_add_fusion = f32[512,768]{1,0:T(8,128)S(1)} fusion(f32[512,768]{1,0:T(8,128)S(1)} %fusion.53, f32[512,768]{1,0:T(8,128)} %fusion.50, bf16[3,3,768,384]{3,2,1,0:T(8,128)(2,1)} %param.9, bf16[511,384]{1,0:T(8,128)(2,1)} %get-tuple-element.24), kind=kOutput, calls=%fused_computation.4 | convolution fusion | flops 302776320 | bytes 5701632 | tf_op jit(solution)/shard_map/dot_general | solution.py:84
  175.9 1.7 convolution_add_fusion.1
  177.7 2.5 %fusion.6 = bf16[512,384]{1,0:T(8,128)(2,1)} fusion(f32[512,384]{1,0:T(8,128)S(1)} %copy-done.12, f32[512,384]{1,0:T(8,128)S(1)} %convolution_add_fusion.1, bf16[507,768]{1,0:T(8,128)(2,1)S(1)} %copy-done.6, bf16[3,3,768,384]{3,2,1,0:T(8,128)(2,1)} %param.9, f32[512]{0:T(512)S(1)} %convert_element_type.87), kind=kOutput, calls=%fused_computation.28 | convolution fusion | flops 302776320 | bytes 3336704 | tf_op jit(solution)/shard_map/dot_general | solution.py:54
  180.2 5.7 %multiply_reduce_fusion.2 = f32[384]{0:T(512)S(1)} fusion(bf16[512,384]{1,0:T(8,128)(2,1)S(1)} %collective-permute-done.2, f32[512,768]{1,0:T(8,128)S(1)} %add_add_fusion, s32[]{:T(128)S(6)} %select_n.4, bf16[512,384]{1,0:T(8,128)(2,1)S(1)} %copy-done.10, f32[384]{0:T(512)S(1)} %get-tuple-element.4, f32[384]{0:T(512)S(1)} %get-tuple-element.3, ...), kind=kLoop, calls=%fused_computation.40 | loop fusion | flops 2555520 | bytes 1581060 | tf_op jit(solution)/shard_map/reduce_sum | solution.py:98
  185.9 21.6 %psum.15 = f32[3,384]{1,0:T(4,128)} all-reduce(f32[3,384]{1,0:T(4,128)S(1)} %pad_maximum_fusion.1), channel_id=1, replica_groups=mesh['groups'=2,'dp'=4,'replica'=2,'chan'=2] {'dp','replica'}, use_global_device_ids=true, to_apply=%region_6.7 | all-reduce | flops 1152 | bytes 9216 | tf_op jit(solution)/shard_map/psum | solution.py:112
  207.6 15.7 %all-reduce.14.cloned.1.call-done = bf16[3,3,192,384]{3,2,1,0:T(8,128)(2,1)} async-done(((bf16[3,3,192,384]{3,2,1,0:T(8,128)(2,1)}), bf16[3,3,192,384]{3,2,1,0:T(8,128)(2,1)}) %all-reduce.14.cloned.1.call-update) | async-done | bytes 1327120 | tf_op jit(solution)/shard_map/psum | solution.py:33
  223.3 3.0 %convert_element_type.100 = f32[3,3,192,384]{3,2,1,0:T(8,128)} convert(bf16[3,3,192,384]{3,2,1,0:T(8,128)(2,1)} %all-reduce.14.cloned.1.call-done) | non-fusion elementwise | flops 663552 | bytes 3981312 | tf_op jit(solution)/shard_map/convert_element_type | solution.py:33
  (85 shorter events, 14.6 us)
Async XLA Ops:
  7.2 166.1 %reduce-scatter.2.cloned.1.call-start = ((), (), s32[]{:S(2)}) async-start(), calls=%async_computation.1 | async-start | bytes 6635520 | tf_op jit(solution)/shard_map/reduce_scatter | solution.py:32
  19.6 3.2 %copy-start.11 = (bf16[512,384]{1,0:T(8,128)(2,1)S(1)}, bf16[512,384]{1,0:T(8,128)(2,1)}, u32[]{:S(2)}) copy-start(bf16[512,384]{1,0:T(8,128)(2,1)} %get-tuple-element.31) | copy-start | bytes 1179652
  21.5 4.0 %copy-start.7 = (f32[512,768]{1,0:T(8,128)}, f32[512,768]{1,0:T(8,128)S(1)}, u32[]{:S(2)}) copy-start(f32[512,768]{1,0:T(8,128)S(1)} %add_add_fusion.2) | copy-start | bytes 4718596
  22.4 19.9 %collective-permute-start = (bf16[512,384]{1,0:T(8,128)(2,1)}, bf16[512,384]{1,0:T(8,128)(2,1)}, u32[]{:S(2)}, u32[]{:S(2)}) collective-permute-start(bf16[512,384]{1,0:T(8,128)(2,1)} %dynamic-slice_convert_fusion.2), channel_id=1, source_target_pairs={{0,1},{1,0},{2,3},{3,2},{4,5},{5,4},{6,7},{7,6},{8,9},{9,8},{10,11... | collective-permute-start | bytes 1179656 | tf_op jit(solution)/shard_map/ppermute | solution.py:10
  25.4 3.7 %copy-start.13 = (bf16[511,768]{1,0:T(8,128)(2,1)}, bf16[511,768]{1,0:T(8,128)(2,1)S(1)}, u32[]{:S(2)}) copy-start(bf16[511,768]{1,0:T(8,128)(2,1)S(1)} %get-tuple-element.22) | copy-start | bytes 2354692
  27.4 1.7 copy-start.9
  27.4 1.7 copy-start.20
  37.9 0.9 copy-start.2
  40.4 1.8 copy-start.8
  40.4 1.8 copy-start.15
  40.4 1.9 copy-start.17
  53.5 1.1 copy-start.16
  53.7 4.2 %copy-start.5 = (bf16[507,768]{1,0:T(8,128)(2,1)}, bf16[507,768]{1,0:T(8,128)(2,1)S(1)}, u32[]{:S(2)}) copy-start(bf16[507,768]{1,0:T(8,128)(2,1)S(1)} %get-tuple-element.18) | copy-start | bytes 2336260
  53.7 4.8 %copy-start = (bf16[507,768]{1,0:T(8,128)(2,1)}, bf16[507,768]{1,0:T(8,128)(2,1)S(1)}, u32[]{:S(2)}) copy-start(bf16[507,768]{1,0:T(8,128)(2,1)S(1)} %get-tuple-element.19) | copy-start | bytes 2336260
  53.7 1.8 copy-start.3
  62.6 1.8 collective-permute-start.1
  63.7 0.7 copy-start.18
  63.7 0.7 copy-start.19
  63.7 0.7 copy-start.21
  63.9 6.8 %copy-start.14 = (bf16[511,768]{1,0:T(8,128)(2,1)S(1)}, bf16[511,768]{1,0:T(8,128)(2,1)}, u32[]{:S(2)}) copy-start(bf16[511,768]{1,0:T(8,128)(2,1)} %copy-done.13) | copy-start | bytes 2354692
  75.7 1.1 copy-start.1
  75.8 147.6 %all-reduce.14.cloned.1.call-start = ((), (), s32[]{:S(2)}) async-start(), calls=%async_computation.2 | async-start | bytes 2654208 | tf_op jit(solution)/shard_map/psum | solution.py:33
  173.3 2.6 %copy-start.4 = (f32[512,384]{1,0:T(8,128)S(1)}, f32[512,384]{1,0:T(8,128)}, u32[]{:S(2)}) copy-start(f32[512,384]{1,0:T(8,128)} %fusion.20) | copy-start | bytes 2359300
  175.7 1.9 copy-start.23
  175.7 2.0 copy-start.6
  175.7 2.0 copy-start.12
  175.8 4.3 %collective-permute-start.2 = (bf16[512,384]{1,0:T(8,128)(2,1)S(1)}, bf16[512,384]{1,0:T(8,128)(2,1)S(1)}, u32[]{:S(2)}, u32[]{:S(2)}) collective-permute-start(bf16[512,384]{1,0:T(8,128)(2,1)S(1)} %dynamic-slice_convert_fusion), channel_id=1, source_target_pairs={{0,1},{1,0},{2,3},{3,2},{4,5},{5,4},{6,7},{7,6},{8,9},{9,8},{10,11... | collective-permute-start | bytes 1179656 | tf_op jit(solution)/shard_map/ppermute | solution.py:10
  177.6 2.5 %copy-start.22 = (f32[384]{0:T(512)S(1)}, f32[384]{0:T(512)}, u32[]{:S(2)}) copy-start(f32[384]{0:T(512)} %get-tuple-element.14) | copy-start | bytes 4612
  177.7 2.5 %copy-start.10 = (bf16[512,384]{1,0:T(8,128)(2,1)S(1)}, bf16[512,384]{1,0:T(8,128)(2,1)}, u32[]{:S(2)}) copy-start(bf16[512,384]{1,0:T(8,128)(2,1)} %param.7) | copy-start | bytes 1179652
Sparse Core Ops, SparseCore 0:
  75.9 97.3 reduce-scatter.1
  175.7 47.5 all-reduce.13
where the time goes:
time: 234 us; the launch traced here: 233 us
  waiting for transfers between devices  105 us (45%)
  matrix products  50.2 us (21%)
  blocking collectives  28.9 us (12%)
  other arithmetic  27 us (12%)
  between operations  14.6 us (6%)
  local copies, waits for them, and re-layouts  6.84 us (3%)
    reduce_scatter x1, waiting for transfers between devices, reduce_rows(): lax.psum_scatter(partials.astype(jnp.bfloat16), 'dp', scatter_dimension=2...  88.5 us
    dot_general x9, matrix products, on_device(): jnp.dot(shift_rows(full_snaked, (tap_index - 1) * dilation), conv_weights...  27.8 us
    psum x1, blocking collectives, on_device(): alpha_grads = lax.psum(jnp.stack(alpha_parts), ('dp', 'replica'))  21.6 us
    dot_general x9, matrix products, on_device(): lax.dot_general(shift_rows(grad_bf, -(tap_index - 1) * dilation), conv_we...  17 us
    psum x1, waiting for transfers between devices, reduce_rows(): return lax.psum(summed, 'replica').astype(jnp.float32)  15.7 us
    reduce_sum x2, other arithmetic, on_device(): jnp.sum(snake_back * (previous * jnp.sin(2.0 * alpha_row * previous) / al...  12 us
    all_gather x3, blocking collectives, on_device(): full_snaked = lax.all_gather(snaked, 'chan', axis=1, tiled=True)  7.25 us
    dot_general x9, matrix products, on_device(): lax.dot_general(shift_rows(full_snaked, (tap_index - 1) * dilation), grad...  5.44 us
  transfers between devices with their start and end apart: 5, of which 3 were waited for; matrix products, arithmetic and copies ran while one was open for 15% of the time, Pallas kernels for 0%

commit v1 on v0

v1 whole, which is shorter than its diff:
```python
import functools

import jax
import jax.numpy as jnp
from jax import lax
from jax.experimental import pallas as pl
from jax.experimental.pallas import tpu as pltpu
from jax.sharding import PartitionSpec as P

dilations = (1, 3, 5)
F32, BF16 = jnp.float32, jnp.bfloat16
PI_PARTS = (3.140625, 9.67502593994140625e-4, 1.509957990978376432e-7)
SIN_TERMS = (-1.0 / 39916800, 1.0 / 362880, -1.0 / 5040, 1.0 / 120, -1.0 / 6)
COS_TERMS = (1.0 / 479001600, -1.0 / 3628800, 1.0 / 40320, -1.0 / 720, 1.0 / 24, -0.5)
RANGE = 8192.0
CHUNK = 64


def horner(terms, x):
    total = jnp.full_like(x, terms[0])
    for term in terms[1:]:
        total = total * x + term
    return total


def reduced(angle):
    turns = jnp.round(angle * (1.0 / 3.14159265358979))
    for part in PI_PARTS:
        angle = angle - turns * part
    return angle


def sine(angle, exact_range):
    if not exact_range:
        return jnp.sin(angle)
    rest = reduced(angle)
    square = rest * rest
    return rest + rest * (square * horner(SIN_TERMS, square))


def sine_cosine(angle, exact_range):
    if not exact_range:
        return jnp.sin(angle), jnp.cos(angle)
    rest = reduced(angle)
    square = rest * rest
    return (
        rest + rest * (square * horner(SIN_TERMS, square)),
        1.0 + square * horner(COS_TERMS, square),
    )


def by_range(bound, body):
    @pl.when(bound < RANGE)
    def _():
        body(True)

    @pl.when(bound >= RANGE)
    def _():
        body(False)


def wide(live_ref, rows, width):
    return jnp.tile(live_ref[rows, :], (1, width // 128))


def write_snake(stream_ref, alpha_ref, out_ref):
    alpha = alpha_ref[0]
    inverse = 1.0 / alpha
    bound = jnp.max(jnp.abs(stream_ref[...])) * jnp.max(alpha)

    def body(exact_range):
        @pl.loop(0, stream_ref.shape[0] // CHUNK)
        def _(step):
            rows = pl.ds(pl.multiple_of(step * CHUNK, CHUNK), CHUNK)
            stream = stream_ref[rows, :]
            wave = sine(alpha * stream, exact_range)
            out_ref[rows, :] = (stream + wave * wave * inverse).astype(BF16)

    by_range(bound, body)


def moved(values, offset):
    if offset == 0:
        return values
    rows = values.shape[0]
    place = lax.broadcasted_iota(jnp.int32, values.shape, 0)
    turned = pltpu.roll(values, (-offset) % rows, 0)
    inside = place < rows - offset if offset > 0 else place >= -offset
    return jnp.where(inside, turned, 0.0)


def prep_kernel(len_ref, own_ref, start_ref, act_ref, cot_ref, alpha_ref, stream_ref, snake_ref, grad_ref, live_ref):
    replicas = lax.axis_size("replica")
    device = lax.axis_index("dp") * replicas + lax.axis_index("replica")
    rows = act_ref.shape[0]
    place = lax.broadcasted_iota(jnp.int32, (rows, 128), 0)
    live_ref[...] = jnp.zeros((rows, 128), F32)

    @pl.loop(0, len_ref.shape[0])
    def _(clip):
        @pl.when(own_ref[clip] == device)
        def _():
            first = start_ref[clip]
            inside = (place >= first) & (place < first + len_ref[clip])
            live_ref[...] = jnp.where(inside, 1.0, live_ref[...])

    width = act_ref.shape[1]
    live = jnp.tile(live_ref[...], (1, width // 128))
    stream_ref[...] = act_ref[...].astype(F32) * live
    grad_ref[...] = cot_ref[...].astype(F32) * live
    write_snake(stream_ref, alpha_ref, snake_ref)


def forward_own_kernel(dilation, snake_ref, weight_ref, out_ref):
    half = snake_ref.shape[1]
    begin = pl.multiple_of(lax.axis_index("chan") * half, 128)
    part = jnp.dot(snake_ref[...], weight_ref[0, 0, pl.ds(begin, half), :], preferred_element_type=F32)
    step = pl.program_id(0)

    @pl.when(step == 0)
    def _():
        out_ref[...] = moved(part, -dilation)

    @pl.when(step == 1)
    def _():
        out_ref[...] += part

    @pl.when(step == 2)
    def _():
        out_ref[...] += moved(part, dilation)


def forward_partner_kernel(dilation, last, snake_ref, weight_ref, own_ref, old_ref, live_ref, *rest):
    if last:
        result_ref, total_ref = rest
    else:
        alpha_ref, stream_ref, next_ref, total_ref = rest
    half = snake_ref.shape[1]
    begin = pl.multiple_of((1 - lax.axis_index("chan")) * half, 128)
    part = jnp.dot(snake_ref[...], weight_ref[0, 0, pl.ds(begin, half), :], preferred_element_type=F32)
    step = pl.program_id(0)

    @pl.when(step == 0)
    def _():
        total_ref[...] = own_ref[...] + moved(part, -dilation)

    @pl.when(step == 1)
    def _():
        total_ref[...] += part

    @pl.when(step == 2)
    def _():
        live = jnp.tile(live_ref[...], (1, half // 128))
        new = (old_ref[...] + (total_ref[...] + moved(part, dilation))) * live
        if last:
            result_ref[...] = new.astype(BF16)
        else:
            stream_ref[...] = new
            write_snake(stream_ref, alpha_ref, next_ref)


def back_partner_kernel(dilation, grad_ref, weight_ref, shifted_ref, out_ref, total_ref):
    half = grad_ref.shape[1]
    begin = pl.multiple_of((1 - lax.axis_index("chan")) * half, 128)
    step = pl.program_id(0)
    for tap in range(3):

        @pl.when(step == tap)
        def _():
            rounded = grad_ref[...].astype(BF16).astype(F32)
            shifted_ref[...] = moved(rounded, (1 - tap) * dilation).astype(BF16)

    part = lax.dot_general(
        shifted_ref[...], weight_ref[0, 0, pl.ds(begin, half), :], (((1,), (1,)), ((), ())), preferred_element_type=F32
    )

    @pl.when(step == 0)
    def _():
        total_ref[...] = part

    @pl.when(step == 1)
    def _():
        total_ref[...] += part

    @pl.when(step == 2)
    def _():
        out_ref[...] = (total_ref[...] + part).astype(BF16)


def back_own_kernel(shifted_ref, weight_ref, out_ref):
    half = shifted_ref.shape[1]
    begin = pl.multiple_of(lax.axis_index("chan") * half, 128)
    part = lax.dot_general(
        shifted_ref[...], weight_ref[0, 0, pl.ds(begin, half), :], (((1,), (1,)), ((), ())), preferred_element_type=F32
    )
    step = pl.program_id(0)

    @pl.when(step == 0)
    def _():
        out_ref[...] = part

    @pl.when(step > 0)
    def _():
        out_ref[...] += part


def combine_kernel(first, own_ref, partner_ref, stream_ref, alpha_ref, *rest):
    if first:
        (alpha_grad_ref,) = rest
    else:
        old_ref, live_ref, alpha_grad_ref, grad_ref = rest
    alpha = alpha_ref[0]
    inverse = 1.0 / alpha
    bound = jnp.max(jnp.abs(stream_ref[...])) * jnp.max(alpha)
    width = stream_ref.shape[1]

    def body(exact_range):
        def step_body(step, total):
            rows = pl.ds(pl.multiple_of(step * CHUNK, CHUNK), CHUNK)
            stream = stream_ref[rows, :]
            back = own_ref[rows, :] + partner_ref[rows, :].astype(F32)
            sin, cos = sine_cosine(alpha * stream, exact_range)
            double = 2.0 * sin * cos
            ratio = sin * inverse
            term = back * (stream * double * inverse - ratio * ratio)
            if not first:
                live = wide(live_ref, rows, width)
                grad_ref[rows, :] = (old_ref[rows, :] + back * (1.0 + double)) * live
            return total + jnp.sum(term.reshape(CHUNK // 8, 8, width), axis=0)

        total = lax.fori_loop(0, stream_ref.shape[0] // CHUNK, step_body, jnp.zeros((8, width), F32))
        alpha_grad_ref[...] = jnp.sum(total, axis=0, keepdims=True)

    by_range(bound, body)


def block_place(fast, slice_index, part):
    if not fast:
        return slice_index * 2 + part
    apart = jnp.bitwise_xor(slice_index, lax.axis_index("dp"))
    order = (4, 0, 1, 5) if part == 0 else (6, 7, 3, 2)
    return jnp.where(
        apart == 0, order[0], jnp.where(apart == 1, order[1], jnp.where(apart == 2, order[2], order[3]))
    )


def weight_kernel(fast, own_ref, partner_ref, shifted_ref, *rest):
    outs, turned_ref = rest[:-1], rest[-1]
    half = own_ref.shape[1]
    rows = half // 4

    @pl.when(pl.program_id(0) == 0)
    def _():
        chan = lax.axis_index("chan")
        for ref, side in ((own_ref, chan), (partner_ref, 1 - chan)):
            turned = ref[...].T
            for local in range(2):
                for part in range(2):
                    place = block_place(fast, side * 2 + local, part)
                    begin = pl.multiple_of(place * rows, rows)
                    low = (local * 2 + part) * rows
                    turned_ref[pl.ds(begin, rows), :] = turned[low : low + rows, :]

    product = jnp.dot(turned_ref[...], shifted_ref[...], preferred_element_type=F32).astype(BF16)
    size = product.shape[0] // len(outs)
    for index, ref in enumerate(outs):
        ref[...] = product[index * size : (index + 1) * size, :]


def finish_kernel(aliased, *refs):
    mine_ref, other_ref, out_ref = refs[1:] if aliased else refs
    out_ref[0, 0] = mine_ref[...].astype(F32) + other_ref[...].astype(F32)


def full(shape):
    return pl.BlockSpec(shape, lambda *_: (0,) * len(shape))


def struct(shape, dtype):
    return jax.ShapeDtypeStruct(shape, dtype)


def cost(flops, size):
    return pl.CostEstimate(flops=int(flops), bytes_accessed=int(size), transcendentals=0)


PARAMS = pltpu.CompilerParams(vmem_limit_bytes=40 * 1024 * 1024)


def swap(x, axis, other):
    return lax.ppermute(x, axis, [(i, other(i)) for i in range(lax.axis_size(axis))])


def reduce_weights(parts, fast):
    if not fast:
        (whole,) = parts
        summed = lax.psum(lax.psum_scatter(whole, "dp", scatter_dimension=0, tiled=True), "replica")
        return summed, jnp.zeros_like(summed)
    send_a, send_b, keep_a, keep_b = parts
    rows = keep_a.shape[0] // 2
    got_a = swap(send_a, "dp", lambda i: i ^ 1)
    got_b = swap(send_b, "dp", lambda i: i ^ 3)
    late_a = swap(keep_a[rows:] + got_a[rows:], "dp", lambda i: i ^ 3)
    late_b = swap(keep_b[rows:] + got_b[rows:], "dp", lambda i: i ^ 1)

    def total(keep, got, late):
        return (keep[:rows].astype(F32) + got[:rows].astype(F32) + late.astype(F32)).astype(BF16)

    mine = jnp.concatenate([total(keep_a, got_a, late_a), total(keep_b, got_b, late_b)])
    return mine, swap(mine, "replica", lambda i: i ^ 1)


def sum_over(values, axis):
    size = lax.axis_size(axis)
    if size & (size - 1):
        return lax.psum(values, axis)
    apart = 1
    while apart < size:
        values = values + swap(values, axis, lambda i, apart=apart: i ^ apart)
        apart *= 2
    return values


def on_device(activations, cotangent, conv_weights, snake_alpha, seg_lengths, seg_owner, seg_start):
    rows, half = activations.shape
    layers, taps, channels, _ = conv_weights.shape
    fast = lax.axis_size("dp") == 4 and lax.axis_size("replica") == 2
    tile = (rows, half)
    alpha_rows = snake_alpha.reshape(layers, 1, half)
    flops = 2 * rows * half * half * taps
    smem = pl.BlockSpec(memory_space=pltpu.SMEM)

    def weight_spec(layer):
        return pl.BlockSpec((1, 1, channels, half), lambda tap: (layer, tap, 0, 0))

    def alpha_spec(layer):
        return pl.BlockSpec((1, 1, half), lambda *_: (layer, 0, 0))

    stream, snaked, grad, live = pl.pallas_call(
        prep_kernel,
        grid=(1,),
        in_specs=[smem, smem, smem, full(tile), full(tile), alpha_spec(0)],
        out_specs=[full(tile), full(tile), full(tile), full((rows, 128))],
        out_shape=[struct(tile, F32), struct(tile, BF16), struct(tile, F32), struct((rows, 128), F32)],
        compiler_params=PARAMS,
        cost_estimate=cost(40 * rows * half, 14 * rows * half),
        name="prep",
    )(seg_lengths, seg_owner, seg_start, activations, cotangent, alpha_rows)

    streams, mine, partners = [], [], []
    for layer in range(layers):
        dilation = dilations[layer]
        last = layer == layers - 1
        other = swap(snaked, "chan", lambda i: i ^ 1)
        streams.append(stream)
        mine.append(snaked)
        partners.append(other)
        own = pl.pallas_call(
            functools.partial(forward_own_kernel, dilation),
            grid=(taps,),
            in_specs=[full(tile), weight_spec(layer)],
            out_specs=full(tile),
            out_shape=struct(tile, F32),
            compiler_params=PARAMS,
            cost_estimate=cost(flops, 2 * taps * channels * half + 6 * rows * half),
            name="forward_own",
        )(snaked, conv_weights)
        ins = [full(tile), weight_spec(layer), full(tile), full(tile), full((rows, 128))]
        args = [other, conv_weights, own, stream, live]
        if last:
            outs, shapes = full(tile), struct(tile, BF16)
        else:
            ins.append(alpha_spec(layer + 1))
            args.append(alpha_rows)
            outs, shapes = [full(tile)] * 2, [struct(tile, F32), struct(tile, BF16)]
        result = pl.pallas_call(
            functools.partial(forward_partner_kernel, dilation, last),
            grid=(taps,),
            in_specs=ins,
            out_specs=outs,
            out_shape=shapes,
            scratch_shapes=[pltpu.VMEM(tile, F32)],
            compiler_params=PARAMS,
            cost_estimate=cost(flops, 2 * taps * channels * half + 16 * rows * half),
            name="forward_partner",
        )(*args)
        if last:
            residual_out = result
        else:
            stream, snaked = result

    alpha_parts = [None] * layers
    reduced_parts = [None] * layers
    for layer in reversed(range(layers)):
        dilation = dilations[layer]
        first = layer == 0
        shifted, partner_part = pl.pallas_call(
            functools.partial(back_partner_kernel, dilation),
            grid=(taps,),
            in_specs=[full(tile), weight_spec(layer)],
            out_specs=[pl.BlockSpec(tile, lambda tap: (0, tap)), full(tile)],
            out_shape=[struct((rows, taps * half), BF16), struct(tile, BF16)],
            scratch_shapes=[pltpu.VMEM(tile, F32)],
            compiler_params=PARAMS,
            cost_estimate=cost(flops, 2 * taps * channels * half + 12 * rows * half),
            name="back_partner",
        )(grad, conv_weights)
        arrived = swap(partner_part, "chan", lambda i: i ^ 1)
        own_part = pl.pallas_call(
            back_own_kernel,
            grid=(taps,),
            in_specs=[pl.BlockSpec(tile, lambda tap: (0, tap)), weight_spec(layer)],
            out_specs=full(tile),
            out_shape=struct(tile, F32),
            compiler_params=PARAMS,
            cost_estimate=cost(flops, 2 * taps * channels * half + 10 * rows * half),
            name="back_own",
        )(shifted, conv_weights)
        pieces = 4 if fast else 1
        piece = (channels // pieces, taps * half)
        parts = pl.pallas_call(
            functools.partial(weight_kernel, fast),
            grid=(taps,),
            in_specs=[full(tile), full(tile), pl.BlockSpec(tile, lambda tap: (0, tap))],
            out_specs=[pl.BlockSpec((piece[0], half), lambda tap: (0, tap))] * pieces,
            out_shape=[struct(piece, BF16)] * pieces,
            scratch_shapes=[pltpu.VMEM((channels, rows), BF16)],
            compiler_params=PARAMS,
            cost_estimate=cost(2 * flops, 10 * rows * half + 2 * taps * channels * half),
            name="weight_part",
        )(mine[layer], partners[layer], shifted)
        reduced_parts[layer] = reduce_weights(parts, fast)
        ins = [full(tile), full(tile), full(tile), alpha_spec(layer)]
        args = [own_part, arrived, streams[layer], alpha_rows]
        outs, shapes = [full((1, half))], [struct((1, half), F32)]
        if not first:
            ins += [full(tile), full((rows, 128))]
            args += [grad, live]
            outs.append(full(tile))
            shapes.append(struct(tile, F32))
        result = pl.pallas_call(
            functools.partial(combine_kernel, first),
            grid=(1,),
            in_specs=ins,
            out_specs=outs,
            out_shape=shapes,
            compiler_params=PARAMS,
            cost_estimate=cost(60 * rows * half, 18 * rows * half),
            name="combine",
        )(*args)
        alpha_parts[layer] = result[0]
        if not first:
            grad = result[1]

    alpha_grads = sum_over(sum_over(jnp.concatenate(alpha_parts), "replica"), "dp")
    weight_grads = None
    for layer in reversed(range(layers)):
        summed, other = reduced_parts[layer]
        depth = summed.shape[0]
        block = pl.BlockSpec((depth, half), lambda tap: (0, tap))
        aliased = weight_grads is not None
        weight_grads = pl.pallas_call(
            functools.partial(finish_kernel, aliased),
            grid=(taps,),
            in_specs=([pl.BlockSpec(memory_space=pl.ANY)] if aliased else []) + [block, block],
            out_specs=pl.BlockSpec((1, 1, depth, half), lambda tap, layer=layer: (layer, tap, 0, 0)),
            out_shape=struct((layers, taps, depth, half), F32),
            input_output_aliases={0: 0} if aliased else {},
            compiler_params=PARAMS,
            cost_estimate=cost(taps * depth * half, 8 * taps * depth * half),
            name="finish",
        )(*(([weight_grads] if aliased else []) + [summed, other]))
    return (residual_out, weight_grads, alpha_grads)


def solution(mesh):
    return jax.shard_map(
        on_device,
        mesh=mesh,
        in_specs=(
            P(("groups", "dp", "replica"), "chan"),
            P(("groups", "dp", "replica"), "chan"),
            P(None, None, None, "chan"),
            P(None, "chan"),
            P("groups"),
            P("groups"),
            P("groups"),
        ),
        out_specs=(
            P(("groups", "dp", "replica"), "chan"),
            P("groups", None, "dp", "chan"),
            P("groups", "chan"),
        ),
        check_vma=False,
    )
```

time: 234 us -> 152 us (0.65)
  matrix products: 50.2 us -> 0 us
  waiting for transfers between devices: 105 us -> 57.5 us
  starting transfers between devices: 1.02 us -> 43.2 us
  Pallas kernels: 0 us -> 40.1 us
  blocking collectives: 28.9 us -> 0 us
  other arithmetic: 27 us -> 1.42 us
  between operations: 14.6 us -> 0.98 us
    reduce_scatter x1 -> x0, waiting for transfers between devices: 88.5 us -> none  [reduce_rows(): lax.psum_scatter(partials.astype(jnp.bfloat16), 'dp', scatter_dimension=2...]
    ppermute x3 -> x24, waiting for transfers between devices: 0.45 us -> 57.5 us  [swap(): lax.ppermute(x, axis, [(i, other(i)) for i in range(lax.axis_size(axis))])]
    dot_general x27 -> x0, matrix products: 50.2 us -> none  [the longest x9 27.8 us: on_device(): jnp.dot(shift_rows(full_snaked, (tap_index - 1) * dilation), conv_weights...]
    ppermute x3 -> x24, starting transfers between devices: 0.72 us -> 43.2 us  [swap(): lax.ppermute(x, axis, [(i, other(i)) for i in range(lax.axis_size(axis))])]
    pallas_call x0 -> x22, Pallas kernels: none -> 40.1 us  [the longest x3 7.27 us: on_device(): pl.pallas_call(functools.partial(forward_partner_kernel, dilation, last),...]
    psum x1 -> x0, blocking collectives: 21.6 us -> none  [on_device(): alpha_grads = lax.psum(jnp.stack(alpha_parts), ('dp', 'replica'))]
    psum x1 -> x0, waiting for transfers between devices: 15.7 us -> none  [reduce_rows(): return lax.psum(summed, 'replica').astype(jnp.float32)]
    reduce_sum x2 -> x0, other arithmetic: 12 us -> none  [on_device(): jnp.sum(snake_back * (previous * jnp.sin(2.0 * alpha_row * previous) / al...]
  transfers between devices with their start and end apart: 5 -> 24, of which waited for: 3 -> 9; matrix products, arithmetic and copies ran while one was open for 15% -> 1% of each run, Pallas kernels for 0% -> 23%
where the time goes in v1:
time: 152 us; the launch traced here: 151 us
  waiting for transfers between devices  57.5 us (38%)
  starting transfers between devices  43.2 us (28%)
  Pallas kernels  40.1 us (26%)
  local copies, waits for them, and re-layouts  8.19 us (5%)
    ppermute x24, waiting for transfers between devices, swap(): lax.ppermute(x, axis, [(i, other(i)) for i in range(lax.axis_size(axis))])  57.5 us
    ppermute x24, starting transfers between devices, swap(): lax.ppermute(x, axis, [(i, other(i)) for i in range(lax.axis_size(axis))])  43.2 us
    unnamed x14, local copies, waits for them, and re-layouts  7.5 us
    pallas_call x3, Pallas kernels, on_device(): pl.pallas_call(functools.partial(forward_partner_kernel, dilation, last),...  7.27 us
    pallas_call x3, Pallas kernels, on_device(): pl.pallas_call(functools.partial(weight_kernel, fast), grid=(taps,), in_s...  6.98 us
    pallas_call x3, Pallas kernels, on_device(): pl.pallas_call(functools.partial(back_partner_kernel, dilation), grid=(ta...  5.41 us
    pallas_call x3, Pallas kernels, on_device(): pl.pallas_call(back_own_kernel, grid=(taps,), in_specs=[pl.BlockSpec(tile...  4.86 us
    pallas_call x3, Pallas kernels, on_device(): pl.pallas_call(functools.partial(finish_kernel, aliased), grid=(taps,), i...  4.72 us
  transfers between devices with their start and end apart: 24, of which 9 were waited for; matrix products, arithmetic and copies ran while one was open for 1% of the time, Pallas kernels for 23%

profile of v1, /device:TPU:0, one launch (start us, length us, event | category | flops | bytes accessed | tf_op | source)
XLA Modules:
  0.0 151.5 jit_solution(4019584970202907970)
XLA Ops:
  5.3 1.9 %prep.1 = (f32[512,384]{1,0:T(8,128)S(1)}, bf16[512,384]{1,0:T(8,128)(2,1)S(1)}, f32[512,384]{1,0:T(8,128)S(1)}, f32[512,128]{1,0:T(8,128)S(1)}) custom-call(s32[16]{0:T(128)S(1)} %copy-done.4, s32[16]{0:T(128)S(1)} %copy-done.5, s32[16]{0:T(128)S(1)} %copy-done.6, bf16[512,384]{1,0:T(8,128)(2,1)S(1)} %copy-done.2, bf16[512,384]{1,0:T(8,128)(2,1)S(1)} %copy-done.3, ...), custom_call_target="tpu_custom_call" | custom-call | flops 7864320 | bytes 2752512 | tf_op jit(solution)/shard_map/prep/pallas_call | solution.py:339
  7.7 2.5 %copy-done = bf16[3,3,768,384]{3,2,1,0:T(8,128)(2,1)S(1)} copy-done((bf16[3,3,768,384]{3,2,1,0:T(8,128)(2,1)S(1)}, bf16[3,3,768,384]{3,2,1,0:T(8,128)(2,1)}, u32[]{:S(2)}) %copy-start) | copy-done | bytes 5308440
  12.7 2.4 %forward_partner.3 = (f32[512,384]{1,0:T(8,128)S(1)}, bf16[512,384]{1,0:T(8,128)(2,1)S(1)}) custom-call(bf16[512,384]{1,0:T(8,128)(2,1)S(1)} %collective-permute-done.snake_ref.partner_ref, bf16[3,3,768,384]{3,2,1,0:T(8,128)(2,1)S(1)} %copy-done.1, f32[512,384]{1,0:T(8,128)S(1)} %forward_own.3.own_ref, f32[512,384]{1,0:T(8,128)S(1)} %get-tuple-element.34.old_ref.stream_ref, ...), custom_call_target="tpu_custom_call" | custom-call | flops 452984832 | bytes 4915200 | tf_op jit(solution)/shard_map/forward_partner/pallas_call | solution.py:376
  15.3 1.8 %back_partner.3 = (bf16[512,1152]{1,0:T(8,128)(2,1)S(1)}, bf16[512,384]{1,0:T(8,128)(2,1)S(1)}) custom-call(f32[512,384]{1,0:T(8,128)S(1)} %get-tuple-element.40.grad_ref.rest_0_, bf16[3,3,768,384]{3,2,1,0:T(8,128)(2,1)S(1)} %copy-done.1), custom_call_target="tpu_custom_call" | custom-call | flops 452984832 | bytes 4128768 | tf_op jit(solution)/shard_map/back_partner/pallas_call | solution.py:397
  19.1 2.5 %forward_partner.4 = (f32[512,384]{1,0:T(8,128)S(1)}, bf16[512,384]{1,0:T(8,128)(2,1)S(1)}) custom-call(bf16[512,384]{1,0:T(8,128)(2,1)S(1)} %collective-permute-done.1.snake_ref.partner_ref, bf16[3,3,768,384]{3,2,1,0:T(8,128)(2,1)S(1)} %copy-done.1, f32[512,384]{1,0:T(8,128)S(1)} %forward_own.4.own_ref, ...), custom_call_target="tpu_custom_call" | custom-call | flops 452984832 | bytes 4915200 | tf_op jit(solution)/shard_map/forward_partner/pallas_call | solution.py:376
  21.7 1.6 %back_own.3.own_ref = f32[512,384]{1,0:T(8,128)S(1)} custom-call(bf16[512,1152]{1,0:T(8,128)(2,1)S(1)} %get-tuple-element.41.shifted_ref, bf16[3,3,768,384]{3,2,1,0:T(8,128)(2,1)S(1)} %copy-done.1), custom_call_target="tpu_custom_call" | custom-call | flops 452984832 | bytes 3735552 | tf_op jit(solution)/shard_map/back_own/pallas_call | solution.py:409
  24.9 1.8 %back_partner.4 = (bf16[512,1152]{1,0:T(8,128)(2,1)S(1)}, bf16[512,384]{1,0:T(8,128)(2,1)S(1)}) custom-call(f32[512,384]{1,0:T(8,128)S(1)} %get-tuple-element.47.grad_ref.rest_0_, bf16[3,3,768,384]{3,2,1,0:T(8,128)(2,1)S(1)} %copy-done.1), custom_call_target="tpu_custom_call" | custom-call | flops 452984832 | bytes 4128768 | tf_op jit(solution)/shard_map/back_partner/pallas_call | solution.py:397
  27.3 2.3 %weight_part.4 = (bf16[192,1152]{1,0:T(8,128)(2,1)S(1)}, bf16[192,1152]{1,0:T(8,128)(2,1)S(1)}, bf16[192,1152]{1,0:T(8,128)(2,1)S(1)}, bf16[192,1152]{1,0:T(8,128)(2,1)S(1)}) custom-call(bf16[512,384]{1,0:T(8,128)(2,1)S(1)} %get-tuple-element.36.snake_ref.own_ref, bf16[512,384]{1,0:T(8,128)(2,1)S(1)} %collective-permute-done.1.snake_ref.partner_ref, ...), custom_call_target="tpu_custom_call" | custom-call | flops 905969664 | bytes 3735552 | tf_op jit(solution)/shard_map/weight_part/pallas_call | solution.py:421
  29.6 2.7 %collective-permute-start.9 = (bf16[192,1152]{1,0:T(8,128)(2,1)S(1)}, bf16[192,1152]{1,0:T(8,128)(2,1)S(1)}, u32[]{:S(2)}, u32[]{:S(2)}) collective-permute-start(bf16[192,1152]{1,0:T(8,128)(2,1)S(1)} %get-tuple-element.50), channel_id=1, source_target_pairs={{0,4},{4,0},{8,12},{12,8},{1,5},{5,1},{9,13},{13,9},{2,6},{6,2},{1... | collective-permute-start | bytes 1327112 | tf_op jit(solution)/shard_map/ppermute | solution.py:291
  32.2 2.5 %collective-permute-start.11 = (bf16[192,1152]{1,0:T(8,128)(2,1)S(1)}, bf16[192,1152]{1,0:T(8,128)(2,1)S(1)}, u32[]{:S(2)}, u32[]{:S(2)}) collective-permute-start(bf16[192,1152]{1,0:T(8,128)(2,1)S(1)} %get-tuple-element.52), channel_id=1, source_target_pairs={{0,12},{4,8},{8,4},{12,0},{1,13},{5,9},{9,5},{13,1},{2,14},{6,10},... | collective-permute-start | bytes 1327112 | tf_op jit(solution)/shard_map/ppermute | solution.py:291
  34.7 1.6 %back_own.4.own_ref = f32[512,384]{1,0:T(8,128)S(1)} custom-call(bf16[512,1152]{1,0:T(8,128)(2,1)S(1)} %get-tuple-element.48.shifted_ref, bf16[3,3,768,384]{3,2,1,0:T(8,128)(2,1)S(1)} %copy-done.1), custom_call_target="tpu_custom_call" | custom-call | flops 452984832 | bytes 3735552 | tf_op jit(solution)/shard_map/back_own/pallas_call | solution.py:409
  36.3 2.3 %weight_part.3 = (bf16[192,1152]{1,0:T(8,128)(2,1)S(1)}, bf16[192,1152]{1,0:T(8,128)(2,1)S(1)}, bf16[192,1152]{1,0:T(8,128)(2,1)S(1)}, bf16[192,1152]{1,0:T(8,128)(2,1)S(1)}) custom-call(bf16[512,384]{1,0:T(8,128)(2,1)S(1)} %get-tuple-element.38.snake_ref.own_ref, bf16[512,384]{1,0:T(8,128)(2,1)S(1)} %collective-permute-done.2.snake_ref.partner_ref, ...), custom_call_target="tpu_custom_call" | custom-call | flops 905969664 | bytes 3735552 | tf_op jit(solution)/shard_map/weight_part/pallas_call | solution.py:421
  40.3 1.7 %combine.4 = (f32[1,384]{1,0:T(1,128)S(1)}, f32[512,384]{1,0:T(8,128)S(1)}) custom-call(f32[512,384]{1,0:T(8,128)S(1)} %back_own.4.own_ref, bf16[512,384]{1,0:T(8,128)(2,1)S(1)} %collective-permute-done.14.partner_ref, f32[512,384]{1,0:T(8,128)S(1)} %get-tuple-element.37.old_ref.stream_ref, f32[3,1,384]{2,1,0:T(1,128)S(1)} %reshape.9.alpha_ref.rest_0_, ...), custom_call_target="tpu_custom_call" | custom-call | flops 11796480 | bytes 3538944 | tf_op jit(solution)/shard_map/combine/pallas_call | solution.py:441
  42.1 1.8 %back_partner.5 = (bf16[512,1152]{1,0:T(8,128)(2,1)S(1)}, bf16[512,384]{1,0:T(8,128)(2,1)S(1)}) custom-call(f32[512,384]{1,0:T(8,128)S(1)} %get-tuple-element.54.grad_ref, bf16[3,3,768,384]{3,2,1,0:T(8,128)(2,1)S(1)} %copy-done.1), custom_call_target="tpu_custom_call" | custom-call | flops 452984832 | bytes 4128768 | tf_op jit(solution)/shard_map/back_partner/pallas_call | solution.py:397
  44.0 1.6 %back_own.5.own_ref = f32[512,384]{1,0:T(8,128)S(1)} custom-call(bf16[512,1152]{1,0:T(8,128)(2,1)S(1)} %get-tuple-element.55.shifted_ref, bf16[3,3,768,384]{3,2,1,0:T(8,128)(2,1)S(1)} %copy-done.1), custom_call_target="tpu_custom_call" | custom-call | flops 452984832 | bytes 3735552 | tf_op jit(solution)/shard_map/back_own/pallas_call | solution.py:409
  45.6 2.3 %weight_part.5 = (bf16[192,1152]{1,0:T(8,128)(2,1)S(1)}, bf16[192,1152]{1,0:T(8,128)(2,1)S(1)}, bf16[192,1152]{1,0:T(8,128)(2,1)S(1)}, bf16[192,1152]{1,0:T(8,128)(2,1)S(1)}) custom-call(bf16[512,384]{1,0:T(8,128)(2,1)S(1)} %get-tuple-element.33.snake_ref.own_ref, bf16[512,384]{1,0:T(8,128)(2,1)S(1)} %collective-permute-done.snake_ref.partner_ref, ...), custom_call_target="tpu_custom_call" | custom-call | flops 905969664 | bytes 3735552 | tf_op jit(solution)/shard_map/weight_part/pallas_call | solution.py:421
  48.9 6.3 %collective-permute-done.11 = bf16[192,1152]{1,0:T(8,128)(2,1)S(1)} collective-permute-done((bf16[192,1152]{1,0:T(8,128)(2,1)S(1)}, bf16[192,1152]{1,0:T(8,128)(2,1)S(1)}, u32[]{:S(2)}, u32[]{:S(2)}) %collective-permute-start.11) | collective-permute-done | bytes 442400 | tf_op jit(solution)/shard_map/ppermute | solution.py:291
  55.2 1.6 %collective-permute-start.10 = (bf16[96,1152]{1,0:T(8,128)(2,1)S(1)}, bf16[96,1152]{1,0:T(8,128)(2,1)S(1)}, u32[]{:S(2)}, u32[]{:S(2)}) collective-permute-start(bf16[96,1152]{1,0:T(8,128)(2,1)S(1)} %slice_add_fusion.3), channel_id=1, source_target_pairs={{0,12},{4,8},{8,4},{12,0},{1,13},{5,9},{9,5},{13,1},{2,14},{6,10},... | collective-permute-start | bytes 663560 | tf_op jit(solution)/shard_map/ppermute | solution.py:291
  56.9 31.1 %collective-permute-done.10 = bf16[96,1152]{1,0:T(8,128)(2,1)S(1)} collective-permute-done((bf16[96,1152]{1,0:T(8,128)(2,1)S(1)}, bf16[96,1152]{1,0:T(8,128)(2,1)S(1)}, u32[]{:S(2)}, u32[]{:S(2)}) %collective-permute-start.10) | collective-permute-done | bytes 221216 | tf_op jit(solution)/shard_map/ppermute | solution.py:291
  88.1 6.9 %collective-permute-done.12 = bf16[96,1152]{1,0:T(8,128)(2,1)S(1)} collective-permute-done((bf16[96,1152]{1,0:T(8,128)(2,1)S(1)}, bf16[96,1152]{1,0:T(8,128)(2,1)S(1)}, u32[]{:S(2)}, u32[]{:S(2)}) %collective-permute-start.12) | collective-permute-done | bytes 221216 | tf_op jit(solution)/shard_map/ppermute | solution.py:291
  100.2 2.5 %collective-permute-start.4 = (bf16[96,1152]{1,0:T(8,128)(2,1)S(1)}, bf16[96,1152]{1,0:T(8,128)(2,1)S(1)}, u32[]{:S(2)}, u32[]{:S(2)}) collective-permute-start(bf16[96,1152]{1,0:T(8,128)(2,1)S(1)} %slice_add_fusion.5), channel_id=1, source_target_pairs={{0,12},{4,8},{8,4},{12,0},{1,13},{5,9},{9,5},{13,1},{2,14},{6,10},... | collective-permute-start | bytes 663560 | tf_op jit(solution)/shard_map/ppermute | solution.py:291
  102.8 7.2 %collective-permute-done.17 = bf16[192,1152]{1,0:T(8,128)(2,1)S(1)} collective-permute-done((bf16[192,1152]{1,0:T(8,128)(2,1)S(1)}, bf16[192,1152]{1,0:T(8,128)(2,1)S(1)}, u32[]{:S(2)}, u32[]{:S(2)}) %collective-permute-start.17) | collective-permute-done | bytes 442400 | tf_op jit(solution)/shard_map/ppermute | solution.py:291
  111.5 3.2 %collective-permute-done.4 = bf16[96,1152]{1,0:T(8,128)(2,1)S(1)} collective-permute-done((bf16[96,1152]{1,0:T(8,128)(2,1)S(1)}, bf16[96,1152]{1,0:T(8,128)(2,1)S(1)}, u32[]{:S(2)}, u32[]{:S(2)}) %collective-permute-start.4) | collective-permute-done | bytes 221216 | tf_op jit(solution)/shard_map/ppermute | solution.py:291
  114.7 17.4 %collective-permute-start.18 = (bf16[96,1152]{1,0:T(8,128)(2,1)S(1)}, bf16[96,1152]{1,0:T(8,128)(2,1)S(1)}, u32[]{:S(2)}, u32[]{:S(2)}) collective-permute-start(bf16[96,1152]{1,0:T(8,128)(2,1)S(1)} %slice_add_fusion), channel_id=1, source_target_pairs={{0,4},{4,0},{8,12},{12,8},{1,5},{5,1},{9,13},{13,9},{2,6},{6,2},{1... | collective-permute-start | bytes 663560 | tf_op jit(solution)/shard_map/ppermute | solution.py:291
  132.3 1.6 %collective-permute-start.7 = (bf16[192,1152]{1,0:T(8,128)(2,1)S(1)}, bf16[192,1152]{1,0:T(8,128)(2,1)S(1)}, u32[]{:S(2)}, u32[]{:S(2)}) collective-permute-start(bf16[192,1152]{1,0:T(8,128)(2,1)S(1)} %pad_maximum_fusion.refs_0_), channel_id=1, source_target_pairs={{0,2},{2,0},{1,3},{3,1},{4,6},{6,4},{5,7},{7,5},{8,10},{10,8},{9,1... | collective-permute-start | bytes 1327112 | tf_op jit(solution)/shard_map/ppermute | solution.py:291
  134.0 2.1 %collective-permute-done.18 = bf16[96,1152]{1,0:T(8,128)(2,1)S(1)} collective-permute-done((bf16[96,1152]{1,0:T(8,128)(2,1)S(1)}, bf16[96,1152]{1,0:T(8,128)(2,1)S(1)}, u32[]{:S(2)}, u32[]{:S(2)}) %collective-permute-start.18) | collective-permute-done | bytes 221216 | tf_op jit(solution)/shard_map/ppermute | solution.py:291
  137.8 2.1 %collective-permute-start.22 = (f32[3,384]{1,0:T(4,128)S(1)}, f32[3,384]{1,0:T(4,128)S(1)}, u32[]{:S(2)}, u32[]{:S(2)}) collective-permute-start(f32[3,384]{1,0:T(4,128)S(1)} %fusion), channel_id=1, source_target_pairs={{0,4},{4,0},{8,12},{12,8},{1,5},{5,1},{9,13},{13,9},{2,6},{6,2},{1... | collective-permute-start | bytes 13832 | tf_op jit(solution)/shard_map/ppermute | solution.py:291
  141.5 1.8 %collective-permute-start.23 = (f32[3,384]{1,0:T(4,128)S(1)}, f32[3,384]{1,0:T(4,128)S(1)}, u32[]{:S(2)}, u32[]{:S(2)}) collective-permute-start(f32[3,384]{1,0:T(4,128)S(1)} %fusion.1), channel_id=1, source_target_pairs={{0,8},{4,12},{8,0},{12,4},{1,9},{5,13},{9,1},{13,5},{2,10},{6,14},... | collective-permute-start | bytes 13832 | tf_op jit(solution)/shard_map/ppermute | solution.py:291
  143.3 2.3 %forward_partner.5 = bf16[512,384]{1,0:T(8,128)(2,1)} custom-call(bf16[512,384]{1,0:T(8,128)(2,1)S(1)} %collective-permute-done.2.snake_ref.partner_ref, bf16[3,3,768,384]{3,2,1,0:T(8,128)(2,1)S(1)} %copy-done.1, f32[512,384]{1,0:T(8,128)S(1)} %forward_own.5.own_ref, f32[512,384]{1,0:T(8,128)S(1)} %get-tuple-element.39.old_ref.stream_ref, ...), custom_call_target="tpu_custom_call" | custom-call | flops 452984832 | bytes 4915200 | tf_op jit(solution)/shard_map/forward_partner/pallas_call | solution.py:376
  146.7 1.6 %finish.3.refs_0_ = f32[3,3,192,384]{3,2,1,0:T(8,128)} custom-call(bf16[192,1152]{1,0:T(8,128)(2,1)S(1)} %pad_maximum_fusion.refs_0_, bf16[192,1152]{1,0:T(8,128)(2,1)S(1)} %collective-permute-done.7.refs_1_), custom_call_target="tpu_custom_call" | custom-call | flops 221184 | bytes 1769472 | tf_op jit(solution)/shard_map/finish/pallas_call | solution.py:462
  148.2 1.6 %finish.4.refs_0_ = f32[3,3,192,384]{3,2,1,0:T(8,128)} custom-call(f32[3,3,192,384]{3,2,1,0:T(8,128)} %finish.3.refs_0_, bf16[192,1152]{1,0:T(8,128)(2,1)S(1)} %pad_maximum_fusion.1.refs_1_, bf16[192,1152]{1,0:T(8,128)(2,1)S(1)} %collective-permute-done.13.refs_2_), custom_call_target="tpu_custom_call", output_to_operand_aliasing={{}: (0, {})} | custom-call | flops 221184 | bytes 1769472 | tf_op jit(solution)/shard_map/finish/pallas_call | solution.py:462
  149.9 1.6 %finish.5 = f32[3,3,192,384]{3,2,1,0:T(8,128)} custom-call(f32[3,3,192,384]{3,2,1,0:T(8,128)} %finish.4.refs_0_, bf16[192,1152]{1,0:T(8,128)(2,1)S(1)} %pad_maximum_fusion.2.refs_1_, bf16[192,1152]{1,0:T(8,128)(2,1)S(1)} %collective-permute-done.19.refs_2_), custom_call_target="tpu_custom_call", output_to_operand_aliasing={{}: (0, {})} | custom-call | flops 221184 | bytes 1769472 | tf_op jit(solution)/shard_map/finish/pallas_call | solution.py:462
  (72 shorter events, 26.2 us)
Async XLA Ops:
  1.3 1.0 copy-start.2
  2.3 1.0 copy-start.3
  3.3 0.7 copy-start.4
  4.0 0.7 copy-start.5
  4.6 0.7 copy-start.6
  7.2 4.5 %collective-permute-start = (bf16[512,384]{1,0:T(8,128)(2,1)S(1)}, bf16[512,384]{1,0:T(8,128)(2,1)S(1)}, u32[]{:S(2)}, u32[]{:S(2)}) collective-permute-start(bf16[512,384]{1,0:T(8,128)(2,1)S(1)} %get-tuple-element.33.snake_ref.own_ref), channel_id=1, source_target_pairs={{0,1},{1,0},{2,3},{3,2},{4,5},{5,4},{6,7},{7,6},{8,9},{9,8},{10,11... | collective-permute-start | bytes 1179656 | tf_op jit(solution)/shard_map/ppermute | solution.py:291
  7.7 2.5 %copy-start = (bf16[3,3,768,384]{3,2,1,0:T(8,128)(2,1)S(1)}, bf16[3,3,768,384]{3,2,1,0:T(8,128)(2,1)}, u32[]{:S(2)}) copy-start(bf16[3,3,768,384]{3,2,1,0:T(8,128)(2,1)} %weight_ref.23) | copy-start | bytes 15925252
  10.2 2.5 %copy-start.1 = (bf16[3,3,768,384]{3,2,1,0:T(8,128)(2,1)S(1)}, bf16[3,3,768,384]{3,2,1,0:T(8,128)(2,1)}, u32[]{:S(2)}) copy-start(bf16[3,3,768,384]{3,2,1,0:T(8,128)(2,1)} %weight_ref.23) | copy-start | bytes 15925252
  15.1 3.9 %collective-permute-start.1 = (bf16[512,384]{1,0:T(8,128)(2,1)S(1)}, bf16[512,384]{1,0:T(8,128)(2,1)S(1)}, u32[]{:S(2)}, u32[]{:S(2)}) collective-permute-start(bf16[512,384]{1,0:T(8,128)(2,1)S(1)} %get-tuple-element.36.snake_ref.own_ref), channel_id=1, source_target_pairs={{0,1},{1,0},{2,3},{3,2},{4,5},{5,4},{6,7},{7,6},{8,9},{9,8},{10,11... | collective-permute-start | bytes 1179656 | tf_op jit(solution)/shard_map/ppermute | solution.py:291
  17.1 6.3 %collective-permute-start.8 = (bf16[512,384]{1,0:T(8,128)(2,1)S(1)}, bf16[512,384]{1,0:T(8,128)(2,1)S(1)}, u32[]{:S(2)}, u32[]{:S(2)}) collective-permute-start(bf16[512,384]{1,0:T(8,128)(2,1)S(1)} %get-tuple-element.46), channel_id=1, source_target_pairs={{0,1},{1,0},{2,3},{3,2},{4,5},{5,4},{6,7},{7,6},{8,9},{9,8},{10,11... | collective-permute-start | bytes 1179656 | tf_op jit(solution)/shard_map/ppermute | solution.py:291
  21.6 14.8 %collective-permute-start.2 = (bf16[512,384]{1,0:T(8,128)(2,1)S(1)}, bf16[512,384]{1,0:T(8,128)(2,1)S(1)}, u32[]{:S(2)}, u32[]{:S(2)}) collective-permute-start(bf16[512,384]{1,0:T(8,128)(2,1)S(1)} %get-tuple-element.38.snake_ref.own_ref), channel_id=1, source_target_pairs={{0,1},{1,0},{2,3},{3,2},{4,5},{5,4},{6,7},{7,6},{8,9},{9,8},{10,11... | collective-permute-start | bytes 1179656 | tf_op jit(solution)/shard_map/ppermute | solution.py:291
  26.7 13.6 %collective-permute-start.14 = (bf16[512,384]{1,0:T(8,128)(2,1)S(1)}, bf16[512,384]{1,0:T(8,128)(2,1)S(1)}, u32[]{:S(2)}, u32[]{:S(2)}) collective-permute-start(bf16[512,384]{1,0:T(8,128)(2,1)S(1)} %get-tuple-element.53), channel_id=1, source_target_pairs={{0,1},{1,0},{2,3},{3,2},{4,5},{5,4},{6,7},{7,6},{8,9},{9,8},{10,11... | collective-permute-start | bytes 1179656 | tf_op jit(solution)/shard_map/ppermute | solution.py:291
  29.6 18.4 %collective-permute-start.9 = (bf16[192,1152]{1,0:T(8,128)(2,1)S(1)}, bf16[192,1152]{1,0:T(8,128)(2,1)S(1)}, u32[]{:S(2)}, u32[]{:S(2)}) collective-permute-start(bf16[192,1152]{1,0:T(8,128)(2,1)S(1)} %get-tuple-element.50), channel_id=1, source_target_pairs={{0,4},{4,0},{8,12},{12,8},{1,5},{5,1},{9,13},{13,9},{2,6},{6,2},{1... | collective-permute-start | bytes 1327112 | tf_op jit(solution)/shard_map/ppermute | solution.py:291
  32.2 23.0 %collective-permute-start.11 = (bf16[192,1152]{1,0:T(8,128)(2,1)S(1)}, bf16[192,1152]{1,0:T(8,128)(2,1)S(1)}, u32[]{:S(2)}, u32[]{:S(2)}) collective-permute-start(bf16[192,1152]{1,0:T(8,128)(2,1)S(1)} %get-tuple-element.52), channel_id=1, source_target_pairs={{0,12},{4,8},{8,4},{12,0},{1,13},{5,9},{9,5},{13,1},{2,14},{6,10},... | collective-permute-start | bytes 1327112 | tf_op jit(solution)/shard_map/ppermute | solution.py:291
  38.7 60.8 %collective-permute-start.3 = (bf16[192,1152]{1,0:T(8,128)(2,1)S(1)}, bf16[192,1152]{1,0:T(8,128)(2,1)S(1)}, u32[]{:S(2)}, u32[]{:S(2)}) collective-permute-start(bf16[192,1152]{1,0:T(8,128)(2,1)S(1)} %get-tuple-element.43), channel_id=1, source_target_pairs={{0,4},{4,0},{8,12},{12,8},{1,5},{5,1},{9,13},{13,9},{2,6},{6,2},{1... | collective-permute-start | bytes 1327112 | tf_op jit(solution)/shard_map/ppermute | solution.py:291
  39.4 60.7 %collective-permute-start.5 = (bf16[192,1152]{1,0:T(8,128)(2,1)S(1)}, bf16[192,1152]{1,0:T(8,128)(2,1)S(1)}, u32[]{:S(2)}, u32[]{:S(2)}) collective-permute-start(bf16[192,1152]{1,0:T(8,128)(2,1)S(1)} %get-tuple-element.45), channel_id=1, source_target_pairs={{0,12},{4,8},{8,4},{12,0},{1,13},{5,9},{9,5},{13,1},{2,14},{6,10},... | collective-permute-start | bytes 1327112 | tf_op jit(solution)/shard_map/ppermute | solution.py:291
  43.9 52.6 %collective-permute-start.20 = (bf16[512,384]{1,0:T(8,128)(2,1)S(1)}, bf16[512,384]{1,0:T(8,128)(2,1)S(1)}, u32[]{:S(2)}, u32[]{:S(2)}) collective-permute-start(bf16[512,384]{1,0:T(8,128)(2,1)S(1)} %get-tuple-element.60), channel_id=1, source_target_pairs={{0,1},{1,0},{2,3},{3,2},{4,5},{5,4},{6,7},{7,6},{8,9},{9,8},{10,11... | collective-permute-start | bytes 1179656 | tf_op jit(solution)/shard_map/ppermute | solution.py:291
  47.9 54.8 %collective-permute-start.15 = (bf16[192,1152]{1,0:T(8,128)(2,1)S(1)}, bf16[192,1152]{1,0:T(8,128)(2,1)S(1)}, u32[]{:S(2)}, u32[]{:S(2)}) collective-permute-start(bf16[192,1152]{1,0:T(8,128)(2,1)S(1)} %get-tuple-element.57), channel_id=1, source_target_pairs={{0,4},{4,0},{8,12},{12,8},{1,5},{5,1},{9,13},{13,9},{2,6},{6,2},{1... | collective-permute-start | bytes 1327112 | tf_op jit(solution)/shard_map/ppermute | solution.py:291
  55.2 32.8 %collective-permute-start.10 = (bf16[96,1152]{1,0:T(8,128)(2,1)S(1)}, bf16[96,1152]{1,0:T(8,128)(2,1)S(1)}, u32[]{:S(2)}, u32[]{:S(2)}) collective-permute-start(bf16[96,1152]{1,0:T(8,128)(2,1)S(1)} %slice_add_fusion.3), channel_id=1, source_target_pairs={{0,12},{4,8},{8,4},{12,0},{1,13},{5,9},{9,5},{13,1},{2,14},{6,10},... | collective-permute-start | bytes 663560 | tf_op jit(solution)/shard_map/ppermute | solution.py:291
  88.0 7.0 %collective-permute-start.12 = (bf16[96,1152]{1,0:T(8,128)(2,1)S(1)}, bf16[96,1152]{1,0:T(8,128)(2,1)S(1)}, u32[]{:S(2)}, u32[]{:S(2)}) collective-permute-start(bf16[96,1152]{1,0:T(8,128)(2,1)S(1)} %slice_add_fusion.2), channel_id=1, source_target_pairs={{0,4},{4,0},{8,12},{12,8},{1,5},{5,1},{9,13},{13,9},{2,6},{6,2},{1... | collective-permute-start | bytes 663560 | tf_op jit(solution)/shard_map/ppermute | solution.py:291
  95.0 15.1 %collective-permute-start.17 = (bf16[192,1152]{1,0:T(8,128)(2,1)S(1)}, bf16[192,1152]{1,0:T(8,128)(2,1)S(1)}, u32[]{:S(2)}, u32[]{:S(2)}) collective-permute-start(bf16[192,1152]{1,0:T(8,128)(2,1)S(1)} %get-tuple-element.59), channel_id=1, source_target_pairs={{0,12},{4,8},{8,4},{12,0},{1,13},{5,9},{9,5},{13,1},{2,14},{6,10},... | collective-permute-start | bytes 1327112 | tf_op jit(solution)/shard_map/ppermute | solution.py:291
  96.5 51.7 %collective-permute-start.13 = (bf16[192,1152]{1,0:T(8,128)(2,1)S(1)}, bf16[192,1152]{1,0:T(8,128)(2,1)S(1)}, u32[]{:S(2)}, u32[]{:S(2)}) collective-permute-start(bf16[192,1152]{1,0:T(8,128)(2,1)S(1)} %pad_maximum_fusion.1.refs_1_), channel_id=1, source_target_pairs={{0,2},{2,0},{1,3},{3,1},{4,6},{6,4},{5,7},{7,5},{8,10},{10,8},{9,1... | collective-permute-start | bytes 1327112 | tf_op jit(solution)/shard_map/ppermute | solution.py:291
  99.5 38.2 %collective-permute-start.21 = (f32[3,384]{1,0:T(4,128)S(1)}, f32[3,384]{1,0:T(4,128)S(1)}, u32[]{:S(2)}, u32[]{:S(2)}) collective-permute-start(f32[3,384]{1,0:T(4,128)S(1)} %pad_maximum_fusion.3), channel_id=1, source_target_pairs={{0,2},{2,0},{1,3},{3,1},{4,6},{6,4},{5,7},{7,5},{8,10},{10,8},{9,1... | collective-permute-start | bytes 13832 | tf_op jit(solution)/shard_map/ppermute | solution.py:291
  100.2 14.5 %collective-permute-start.4 = (bf16[96,1152]{1,0:T(8,128)(2,1)S(1)}, bf16[96,1152]{1,0:T(8,128)(2,1)S(1)}, u32[]{:S(2)}, u32[]{:S(2)}) collective-permute-start(bf16[96,1152]{1,0:T(8,128)(2,1)S(1)} %slice_add_fusion.5), channel_id=1, source_target_pairs={{0,12},{4,8},{8,4},{12,0},{1,13},{5,9},{9,5},{13,1},{2,14},{6,10},... | collective-permute-start | bytes 663560 | tf_op jit(solution)/shard_map/ppermute | solution.py:291
  102.7 29.4 %collective-permute-start.6 = (bf16[96,1152]{1,0:T(8,128)(2,1)S(1)}, bf16[96,1152]{1,0:T(8,128)(2,1)S(1)}, u32[]{:S(2)}, u32[]{:S(2)}) collective-permute-start(bf16[96,1152]{1,0:T(8,128)(2,1)S(1)} %slice_add_fusion.4), channel_id=1, source_target_pairs={{0,4},{4,0},{8,12},{12,8},{1,5},{5,1},{9,13},{13,9},{2,6},{6,2},{1... | collective-permute-start | bytes 663560 | tf_op jit(solution)/shard_map/ppermute | solution.py:291
  110.1 23.8 %collective-permute-start.16 = (bf16[96,1152]{1,0:T(8,128)(2,1)S(1)}, bf16[96,1152]{1,0:T(8,128)(2,1)S(1)}, u32[]{:S(2)}, u32[]{:S(2)}) collective-permute-start(bf16[96,1152]{1,0:T(8,128)(2,1)S(1)} %slice_add_fusion.1), channel_id=1, source_target_pairs={{0,12},{4,8},{8,4},{12,0},{1,13},{5,9},{9,5},{13,1},{2,14},{6,10},... | collective-permute-start | bytes 663560 | tf_op jit(solution)/shard_map/ppermute | solution.py:291
  114.7 21.4 %collective-permute-start.18 = (bf16[96,1152]{1,0:T(8,128)(2,1)S(1)}, bf16[96,1152]{1,0:T(8,128)(2,1)S(1)}, u32[]{:S(2)}, u32[]{:S(2)}) collective-permute-start(bf16[96,1152]{1,0:T(8,128)(2,1)S(1)} %slice_add_fusion), channel_id=1, source_target_pairs={{0,4},{4,0},{8,12},{12,8},{1,5},{5,1},{9,13},{13,9},{2,6},{6,2},{1... | collective-permute-start | bytes 663560 | tf_op jit(solution)/shard_map/ppermute | solution.py:291
  132.3 14.4 %collective-permute-start.7 = (bf16[192,1152]{1,0:T(8,128)(2,1)S(1)}, bf16[192,1152]{1,0:T(8,128)(2,1)S(1)}, u32[]{:S(2)}, u32[]{:S(2)}) collective-permute-start(bf16[192,1152]{1,0:T(8,128)(2,1)S(1)} %pad_maximum_fusion.refs_0_), channel_id=1, source_target_pairs={{0,2},{2,0},{1,3},{3,1},{4,6},{6,4},{5,7},{7,5},{8,10},{10,8},{9,1... | collective-permute-start | bytes 1327112 | tf_op jit(solution)/shard_map/ppermute | solution.py:291
  136.2 13.7 %collective-permute-start.19 = (bf16[192,1152]{1,0:T(8,128)(2,1)S(1)}, bf16[192,1152]{1,0:T(8,128)(2,1)S(1)}, u32[]{:S(2)}, u32[]{:S(2)}) collective-permute-start(bf16[192,1152]{1,0:T(8,128)(2,1)S(1)} %pad_maximum_fusion.2.refs_1_), channel_id=1, source_target_pairs={{0,2},{2,0},{1,3},{3,1},{4,6},{6,4},{5,7},{7,5},{8,10},{10,8},{9,1... | collective-permute-start | bytes 1327112 | tf_op jit(solution)/shard_map/ppermute | solution.py:291
  137.8 3.7 %collective-permute-start.22 = (f32[3,384]{1,0:T(4,128)S(1)}, f32[3,384]{1,0:T(4,128)S(1)}, u32[]{:S(2)}, u32[]{:S(2)}) collective-permute-start(f32[3,384]{1,0:T(4,128)S(1)} %fusion), channel_id=1, source_target_pairs={{0,4},{4,0},{8,12},{12,8},{1,5},{5,1},{9,13},{13,9},{2,6},{6,2},{1... | collective-permute-start | bytes 13832 | tf_op jit(solution)/shard_map/ppermute | solution.py:291
  141.5 4.6 %collective-permute-start.23 = (f32[3,384]{1,0:T(4,128)S(1)}, f32[3,384]{1,0:T(4,128)S(1)}, u32[]{:S(2)}, u32[]{:S(2)}) collective-permute-start(f32[3,384]{1,0:T(4,128)S(1)} %fusion.1), channel_id=1, source_target_pairs={{0,8},{4,12},{8,0},{12,4},{1,9},{5,13},{9,1},{13,5},{2,10},{6,14},... | collective-permute-start | bytes 13832 | tf_op jit(solution)/shard_map/ppermute | solution.py:291

commit v2 on v0

v2 whole, which is shorter than its diff:
```python
import functools
import math

import jax
import jax.numpy as jnp
from jax import lax
from jax.experimental import pallas as pl
from jax.experimental.pallas import tpu as pltpu
from jax.sharding import PartitionSpec as P

dilations = (1, 3, 5)
F32, BF16 = jnp.float32, jnp.bfloat16
ANY_HBM = pl.BlockSpec(memory_space=pltpu.HBM)
IN_VMEM = pl.BlockSpec(memory_space=pltpu.VMEM)
DMA = pltpu.SemaphoreType.DMA
PI_PARTS = (3.140625, 9.67502593994140625e-4, 1.509957990978376432e-7)
SIN_TERMS = (-1.0 / 39916800, 1.0 / 362880, -1.0 / 5040, 1.0 / 120, -1.0 / 6)
COS_TERMS = (1.0 / 479001600, -1.0 / 3628800, 1.0 / 40320, -1.0 / 720, 1.0 / 24, -0.5)
RANGE = 8192.0
CHUNK = 64


def horner(terms, x):
    total = jnp.full_like(x, terms[0])
    for term in terms[1:]:
        total = total * x + term
    return total


def reduced(angle):
    turns = jnp.round(angle * (1.0 / 3.14159265358979))
    for part in PI_PARTS:
        angle = angle - turns * part
    return angle


def sine(angle, exact_range):
    if not exact_range:
        return jnp.sin(angle)
    rest = reduced(angle)
    square = rest * rest
    return rest + rest * (square * horner(SIN_TERMS, square))


def sine_cosine(angle, exact_range):
    if not exact_range:
        return jnp.sin(angle), jnp.cos(angle)
    rest = reduced(angle)
    square = rest * rest
    return (
        rest + rest * (square * horner(SIN_TERMS, square)),
        1.0 + square * horner(COS_TERMS, square),
    )


def by_range(bound, body):
    @pl.when(bound < RANGE)
    def _():
        body(True)

    @pl.when(bound >= RANGE)
    def _():
        body(False)


def write_snake(stream_ref, alpha, out_ref):
    inverse = 1.0 / alpha
    bound = jnp.max(jnp.abs(stream_ref[...])) * jnp.max(alpha)

    def body(exact_range):
        @pl.loop(0, stream_ref.shape[0] // CHUNK)
        def _(step):
            rows = pl.ds(pl.multiple_of(step * CHUNK, CHUNK), CHUNK)
            stream = stream_ref[rows, :]
            wave = sine(alpha * stream, exact_range)
            out_ref[rows, :] = (stream + wave * wave * inverse).astype(BF16)

    by_range(bound, body)


def moved(values, offset):
    if offset == 0:
        return values
    rows = values.shape[0]
    place = lax.broadcasted_iota(jnp.int32, values.shape, 0)
    turned = pltpu.roll(values, (-offset) % rows, 0)
    inside = place < rows - offset if offset > 0 else place >= -offset
    return jnp.where(inside, turned, 0.0)


def write_shifts(values_ref, out_ref, dilation):
    width = values_ref.shape[1]
    values = values_ref[...].astype(F32)
    for tap in range(3):
        out_ref[:, tap * width : (tap + 1) * width] = moved(values, (tap - 1) * dilation).astype(BF16)


def chan_begin(side, half):
    chan = lax.axis_index("chan")
    return pl.multiple_of((chan if side == 0 else 1 - chan) * half, half)


def prep_kernel(
    len_hbm, own_hbm, start_hbm, act_hbm, cot_hbm, alpha_hbm,
    stream_ref, snake_ref, grad_ref, live_ref, alpha_ref,
    len_ref, own_ref, start_ref, act_ref, cot_ref, sems,
):
    pairs = (
        (len_hbm, len_ref), (own_hbm, own_ref), (start_hbm, start_ref),
        (alpha_hbm, alpha_ref), (act_hbm, act_ref), (cot_hbm, cot_ref),
    )
    copies = [pltpu.make_async_copy(a, b, sems.at[i]) for i, (a, b) in enumerate(pairs)]
    for copy in copies:
        copy.start()
    replicas = lax.axis_size("replica")
    device = lax.axis_index("dp") * replicas + lax.axis_index("replica")
    rows, width = act_ref.shape
    place = lax.broadcasted_iota(jnp.int32, (rows, 128), 0)
    live_ref[...] = jnp.zeros((rows, 128), F32)
    for copy in copies[:3]:
        copy.wait()

    @pl.loop(0, len_ref.shape[0])
    def _(clip):
        @pl.when(own_ref[clip] == device)
        def _():
            first = start_ref[clip]
            inside = (place >= first) & (place < first + len_ref[clip])
            live_ref[...] = jnp.where(inside, 1.0, live_ref[...])

    live = jnp.tile(live_ref[...], (1, width // 128))
    for copy in copies[3:5]:
        copy.wait()
    stream_ref[...] = act_ref[...].astype(F32) * live
    write_snake(stream_ref, alpha_ref[0:1, :], snake_ref)
    copies[5].wait()
    grad_ref[...] = (cot_ref[...].astype(F32) * live).astype(BF16)


def fetch(layer, side, weight_hbm, held, sems, beside):
    half = weight_hbm.shape[3]
    begin = chan_begin(side, half)
    copies = []
    for tap in range(3):
        span = pl.ds(tap * half, half)
        target = held.at[:, span] if beside else held.at[span, :]
        copies.append(
            pltpu.make_async_copy(weight_hbm.at[layer, tap, pl.ds(begin, half), :], target, sems.at[tap])
        )
    for copy in copies:
        copy.start()
    return copies


def forward_own_kernel(layer, snake_ref, weight_hbm, out_ref, shifts_ref, held, sems):
    copies = fetch(layer, 0, weight_hbm, held, sems, False)
    write_shifts(snake_ref, shifts_ref, dilations[layer])
    for copy in copies:
        copy.wait()
    out_ref[...] = jnp.dot(shifts_ref[...], held[...], preferred_element_type=F32)


def forward_partner_kernel(layer, last, snake_ref, weight_hbm, own_ref, old_ref, live_ref, *rest):
    if last:
        result_ref, shifts_ref, held, sems = rest
    else:
        alpha_ref, result_ref, next_ref, shifts_ref, held, sems = rest
    copies = fetch(layer, 1, weight_hbm, held, sems, False)
    write_shifts(snake_ref, shifts_ref, dilations[layer])
    for copy in copies:
        copy.wait()
    part = jnp.dot(shifts_ref[...], held[...], preferred_element_type=F32)
    live = jnp.tile(live_ref[...], (1, old_ref.shape[1] // 128))
    new = (old_ref[...] + (own_ref[...] + part)) * live
    result_ref[...] = new.astype(result_ref.dtype)
    if not last:
        write_snake(result_ref, alpha_ref[layer + 1 : layer + 2, :], next_ref)


def back_partner_kernel(layer, grad_ref, weight_hbm, shifted_ref, out_ref, held, sems):
    copies = fetch(layer, 1, weight_hbm, held, sems, True)
    write_shifts(grad_ref, shifted_ref, -dilations[layer])
    for copy in copies:
        copy.wait()
    out_ref[...] = lax.dot_general(
        shifted_ref[...], held[...], (((1,), (1,)), ((), ())), preferred_element_type=F32
    ).astype(BF16)


def back_own_kernel(layer, shifted_ref, weight_hbm, out_ref, held, sems):
    for copy in fetch(layer, 0, weight_hbm, held, sems, True):
        copy.wait()
    out_ref[...] = lax.dot_general(
        shifted_ref[...], held[...], (((1,), (1,)), ((), ())), preferred_element_type=F32
    )


def combine_kernel(layer, own_ref, partner_ref, stream_ref, alphas_ref, *rest):
    if layer == 0:
        (alpha_grad_ref,) = rest
    elif len(rest) == 5:
        old_ref, live_ref, alpha_grad_ref, grad_ref, rounded_ref = rest
    else:
        old_ref, live_ref, alpha_grad_ref, rounded_ref = rest
        grad_ref = None
    alpha = alphas_ref[layer : layer + 1, :]
    inverse = 1.0 / alpha
    bound = jnp.max(jnp.abs(stream_ref[...])) * jnp.max(alpha)
    width = stream_ref.shape[1]

    def body(exact_range):
        def step_body(step, total):
            rows = pl.ds(pl.multiple_of(step * CHUNK, CHUNK), CHUNK)
            stream = stream_ref[rows, :]
            back = own_ref[rows, :] + partner_ref[rows, :].astype(F32)
            sin, cos = sine_cosine(alpha * stream, exact_range)
            double = 2.0 * sin * cos
            ratio = sin * inverse
            term = back * (stream * double * inverse - ratio * ratio)
            if layer > 0:
                live = jnp.tile(live_ref[rows, :], (1, width // 128))
                grad = (old_ref[rows, :].astype(F32) + back * (1.0 + double)) * live
                if grad_ref is not None:
                    grad_ref[rows, :] = grad
                rounded_ref[rows, :] = grad.astype(BF16)
            return total + jnp.sum(term.reshape(CHUNK // 8, 8, width), axis=0)

        total = lax.fori_loop(0, stream_ref.shape[0] // CHUNK, step_body, jnp.zeros((8, width), F32))
        alpha_grad_ref[...] = jnp.sum(total, axis=0, keepdims=True)

    by_range(bound, body)


def block_place(fast, slice_index, part):
    if not fast:
        return slice_index * 2 + part
    apart = jnp.bitwise_xor(slice_index, lax.axis_index("dp"))
    order = (4, 0, 1, 5) if part == 0 else (6, 7, 3, 2)
    return jnp.where(
        apart == 0, order[0], jnp.where(apart == 1, order[1], jnp.where(apart == 2, order[2], order[3]))
    )


def place_rows(fast, turned, side, size, target_ref, columns):
    for local in range(2):
        for part in range(2):
            begin = pl.multiple_of(block_place(fast, side * 2 + local, part) * size, size)
            low = (local * 2 + part) * size
            target_ref[pl.ds(begin, size), columns] = turned[low : low + size, :]


def weight_kernel(fast, own_ref, partner_ref, shifted_ref, *rest):
    outs, turned_ref = rest[:-1], rest[-1]
    rows, half = own_ref.shape
    chan = lax.axis_index("chan")
    for ref, side in ((own_ref, chan), (partner_ref, 1 - chan)):
        place_rows(fast, ref[...].T, side, half // 4, turned_ref, slice(0, rows))
    for tap in range(3):
        span = slice(tap * half, (tap + 1) * half)
        product = jnp.dot(turned_ref[...], shifted_ref[:, span], preferred_element_type=F32).astype(BF16)
        size = product.shape[0] // len(outs)
        for index, ref in enumerate(outs):
            ref[:, span] = product[index * size : (index + 1) * size, :]


def pick_parts(turned_ref, part, size):
    begin = pl.multiple_of(part * size, size)
    return [turned_ref[pl.ds(local * 2 * size + begin, size), :] for local in range(2)]


def turn_kernel(*refs):
    ins, out_ref, turned_ref = refs[:-2], refs[-2], refs[-1]
    size = ins[0].shape[1] // 4
    for index, ref in enumerate(ins):
        turned_ref[...] = ref[...].T
        low = index * 2 * size
        for local, piece in enumerate(pick_parts(turned_ref, 1 - lax.axis_index("replica"), size)):
            out_ref[low + local * size : low + (local + 1) * size, :] = piece


def paired_weight_kernel(
    layer, index, own_ref, partner_ref, shifted_ref, across_ref, across_other_ref, grad_ref, *rest
):
    outs, (turned_ref, half_ref, far_ref) = rest[:-3], rest[-3:]
    rows, half = own_ref.shape
    size = half // 4
    chan = lax.axis_index("chan")
    mine = lax.axis_index("replica")
    low = index * 2 * size
    for ref, side in ((own_ref, chan), (partner_ref, 1 - chan)):
        half_ref[...] = ref[...].T
        both = jnp.concatenate(pick_parts(half_ref, mine, size), 0)
        place_rows(True, both, side, size // 2, turned_ref, slice(0, rows))
    for ref, side in ((across_ref, chan), (across_other_ref, 1 - chan)):
        place_rows(True, ref[low : low + 2 * size, :], side, size // 2, turned_ref, slice(rows, 2 * rows))
    write_shifts(grad_ref, far_ref, -dilations[layer])
    for tap in range(3):
        span = slice(tap * half, (tap + 1) * half)
        product = jnp.dot(turned_ref[:, 0:rows], shifted_ref[:, span], preferred_element_type=F32)
        product += jnp.dot(turned_ref[:, rows:], far_ref[:, span], preferred_element_type=F32)
        product = product.astype(BF16)
        size_out = product.shape[0] // len(outs)
        for place, ref in enumerate(outs):
            ref[:, span] = product[place * size_out : (place + 1) * size_out, :]


def finish_kernel(modes, *refs):
    out_ref = refs[-1]
    half = out_ref.shape[3]
    for layer, paired in enumerate(modes):
        mine_ref, other_ref = refs[2 * layer], refs[2 * layer + 1]
        for tap in range(3):
            span = slice(tap * half, (tap + 1) * half)
            mine, other = mine_ref[:, span].astype(F32), other_ref[:, span].astype(F32)
            if paired:
                size = mine.shape[0]
                begin = lax.axis_index("replica") * size
                out_ref[layer, tap, pl.ds(pl.multiple_of(begin, size), size), :] = mine
                out_ref[layer, tap, pl.ds(pl.multiple_of(size - begin, size), size), :] = other
            else:
                out_ref[layer, tap] = mine + other


def struct(shape, dtype):
    return jax.ShapeDtypeStruct(shape, dtype)


def call(kernel, name, ins, outs, scratch, flops, *args):
    single = not isinstance(outs, list)
    size = sum(a.size * a.dtype.itemsize for a in args if a.size < 2000000)
    size += sum(math.prod(o.shape) * o.dtype.itemsize for o in ([outs] if single else outs))
    return pl.pallas_call(
        kernel,
        in_specs=[ANY_HBM if i else IN_VMEM for i in ins],
        out_specs=IN_VMEM if single else [IN_VMEM] * len(outs),
        out_shape=outs,
        scratch_shapes=scratch,
        compiler_params=pltpu.CompilerParams(vmem_limit_bytes=24 * 1024 * 1024),
        cost_estimate=pl.CostEstimate(flops=int(flops), bytes_accessed=int(size), transcendentals=0),
        name=name,
    )(*args)


def swap(x, axis, other):
    return lax.ppermute(x, axis, [(i, other(i)) for i in range(lax.axis_size(axis))])


def after(value, *others):
    return lax.optimization_barrier((value,) + others)[0]


def reduce_weights(parts, fast):
    if not fast:
        return lax.psum(lax.psum_scatter(parts[0], "dp", scatter_dimension=0, tiled=True), "replica")
    send_a, send_b, keep_a, keep_b = parts
    rows = keep_a.shape[0] // 2
    got_a = swap(send_a, "dp", lambda i: i ^ 1)
    got_b = swap(send_b, "dp", lambda i: i ^ 3)
    late_a = swap(keep_a[rows:] + got_a[rows:], "dp", lambda i: i ^ 3)
    late_b = swap(keep_b[rows:] + got_b[rows:], "dp", lambda i: i ^ 1)

    def total(keep, got, late):
        return (keep[:rows].astype(F32) + got[:rows].astype(F32) + late.astype(F32)).astype(BF16)

    return jnp.concatenate([total(keep_a, got_a, late_a), total(keep_b, got_b, late_b)])


def sum_over(values, axis):
    size = lax.axis_size(axis)
    if size & (size - 1):
        return lax.psum(values, axis)
    apart = 1
    while apart < size:
        values = values + swap(values, axis, lambda i, apart=apart: i ^ apart)
        apart *= 2
    return values


def on_device(activations, cotangent, conv_weights, snake_alpha, seg_lengths, seg_owner, seg_start):
    rows, half = activations.shape
    layers, taps, channels, _ = conv_weights.shape
    fast = lax.axis_size("dp") == 4 and lax.axis_size("replica") == 2
    paired = [fast and layer < layers - 1 for layer in range(layers)]
    tile, triple = (rows, half), (rows, taps * half)
    flops = 2 * rows * half * half * taps
    clips = seg_lengths.shape
    by_rows = [pltpu.VMEM((taps * half, half), BF16), DMA((3,))]
    by_columns = [pltpu.VMEM((half, taps * half), BF16), DMA((3,))]

    stream, snaked, grad, live, alphas = call(
        prep_kernel, "prep", [1] * 6,
        [struct(tile, F32), struct(tile, BF16), struct(tile, BF16), struct((rows, 128), F32), struct(snake_alpha.shape, F32)],
        [pltpu.SMEM(clips, jnp.int32)] * 3 + [pltpu.VMEM(tile, BF16)] * 2 + [DMA((6,))],
        40 * rows * half,
        seg_lengths, seg_owner, seg_start, activations, cotangent, snake_alpha,
    )

    streams, mine, partners = [], [], []
    for layer in range(layers):
        last = layer == layers - 1
        other = swap(snaked, "chan", lambda i: i ^ 1)
        streams.append(stream)
        mine.append(snaked)
        partners.append(other)
        own = call(
            functools.partial(forward_own_kernel, layer), "forward_own", [0, 1], struct(tile, F32),
            [pltpu.VMEM(triple, BF16)] + by_rows, flops, snaked, conv_weights,
        )
        outs = struct(tile, BF16) if last else [struct(tile, F32), struct(tile, BF16)]
        result = call(
            functools.partial(forward_partner_kernel, layer, last), "forward_partner",
            [0, 1, 0, 0, 0] + ([] if last else [0]), outs,
            [pltpu.VMEM(triple, BF16)] + by_rows, flops,
            other, conv_weights, own, stream, live, *([] if last else [alphas]),
        )
        if last:
            residual_out = result
        else:
            stream, snaked = result

    if any(paired):
        sources = [layer for layer in range(layers) if paired[layer]]
        turned = call(
            turn_kernel, "turn", [0] * len(sources), struct((len(sources) * half // 2, rows), BF16),
            [pltpu.VMEM((half, rows), BF16)], 10 * rows * half, *[mine[layer] for layer in sources],
        )
        across = swap(turned, "replica", lambda i: i ^ 1)
        across_other = swap(across, "chan", lambda i: i ^ 1)

    alpha_parts = [None] * layers
    summed = [None] * layers
    rounded = grad
    for layer in reversed(range(layers)):
        shifted, partner_part = call(
            functools.partial(back_partner_kernel, layer), "back_partner", [0, 1],
            [struct(triple, BF16), struct(tile, BF16)], by_columns, flops, rounded, conv_weights,
        )
        arrived = swap(partner_part, "chan", lambda i: i ^ 1)
        own_part = call(
            functools.partial(back_own_kernel, layer), "back_own", [0, 1], struct(tile, F32),
            by_columns, flops, shifted, conv_weights,
        )
        pieces = 4 if fast else 1
        if paired[layer]:
            far = swap(rounded, "replica", lambda i: i ^ 1)
            piece = struct((channels // 2 // pieces, taps * half), BF16)
            parts = call(
                functools.partial(paired_weight_kernel, layer, sources.index(layer)), "paired_weight", [0] * 6,
                [piece] * pieces,
                [pltpu.VMEM((half, 2 * rows), BF16), pltpu.VMEM((half, rows), BF16), pltpu.VMEM(triple, BF16)],
                2 * flops, mine[layer], partners[layer], shifted, across, across_other, far,
            )
        else:
            piece = struct((channels // pieces, taps * half), BF16)
            parts = call(
                functools.partial(weight_kernel, fast), "weight", [0] * 3, [piece] * pieces,
                [pltpu.VMEM((channels, rows), BF16)], 2 * flops, mine[layer], partners[layer], shifted,
            )
        summed[layer] = reduce_weights(parts, fast)
        args = [own_part, arrived, streams[layer], alphas]
        outs = [struct((1, half), F32)]
        if layer > 0:
            args += [grad, live]
            outs += [struct(tile, F32)] * (layer > 1) + [struct(tile, BF16)]
        result = call(
            functools.partial(combine_kernel, layer), "combine", [0] * len(args), outs, [], 60 * rows * half, *args
        )
        alpha_parts[layer] = result[0]
        if layer > 0:
            grad, rounded = result[1], result[-1]

    alpha_grads = sum_over(sum_over(jnp.concatenate(alpha_parts), "replica"), "dp")
    pairs = []
    for values in summed:
        pairs += [values, swap(values, "replica", lambda i: i ^ 1) if fast else jnp.zeros_like(values)]
    depth = channels // lax.axis_size("dp")
    weight_grads = call(
        functools.partial(finish_kernel, tuple(paired)), "finish", [0] * len(pairs),
        struct((layers, taps, depth, half), F32), [], layers * taps * depth * half, *pairs,
    )
    return (residual_out, weight_grads, alpha_grads)


def solution(mesh):
    return jax.shard_map(
        on_device,
        mesh=mesh,
        in_specs=(
            P(("groups", "dp", "replica"), "chan"),
            P(("groups", "dp", "replica"), "chan"),
            P(None, None, None, "chan"),
            P(None, "chan"),
            P("groups"),
            P("groups"),
            P("groups"),
        ),
        out_specs=(
            P(("groups", "dp", "replica"), "chan"),
            P("groups", None, "dp", "chan"),
            P("groups", "chan"),
        ),
        check_vma=False,
    )
```

time: 234 us -> 135 us (0.58)
  matrix products: 50.2 us -> 0 us
  waiting for transfers between devices: 105 us -> 57 us
  starting transfers between devices: 1.02 us -> 36.8 us
  Pallas kernels: 0 us -> 29.8 us
  blocking collectives: 28.9 us -> 0 us
  other arithmetic: 27 us -> 1.22 us
  between operations: 14.6 us -> 0.99 us
    reduce_scatter x1 -> x0, waiting for transfers between devices: 88.5 us -> none  [reduce_rows(): lax.psum_scatter(partials.astype(jnp.bfloat16), 'dp', scatter_dimension=2...]
    ppermute x3 -> x28, waiting for transfers between devices: 0.45 us -> 57 us  [swap(): lax.ppermute(x, axis, [(i, other(i)) for i in range(lax.axis_size(axis))])]
    dot_general x27 -> x0, matrix products: 50.2 us -> none  [the longest x9 27.8 us: on_device(): jnp.dot(shift_rows(full_snaked, (tap_index - 1) * dilation), conv_weights...]
    ppermute x3 -> x28, starting transfers between devices: 0.72 us -> 36.8 us  [swap(): lax.ppermute(x, axis, [(i, other(i)) for i in range(lax.axis_size(axis))])]
    pallas_call x0 -> x21, Pallas kernels: none -> 29.8 us  [call(): pl.pallas_call(kernel, in_specs=[ANY_HBM if i else IN_VMEM for i in ins],...]
    psum x1 -> x0, blocking collectives: 21.6 us -> none  [on_device(): alpha_grads = lax.psum(jnp.stack(alpha_parts), ('dp', 'replica'))]
    psum x1 -> x0, waiting for transfers between devices: 15.7 us -> none  [reduce_rows(): return lax.psum(summed, 'replica').astype(jnp.float32)]
    reduce_sum x2 -> x0, other arithmetic: 12 us -> none  [on_device(): jnp.sum(snake_back * (previous * jnp.sin(2.0 * alpha_row * previous) / al...]
  transfers between devices with their start and end apart: 5 -> 28, of which waited for: 3 -> 10; matrix products, arithmetic and copies ran while one was open for 15% -> 1% of each run, Pallas kernels for 0% -> 18%
where the time goes in v2:
time: 135 us; the launch traced here: 134 us
  waiting for transfers between devices  57 us (42%)
  starting transfers between devices  36.8 us (27%)
  Pallas kernels  29.8 us (22%)
  local copies, waits for them, and re-layouts  8.41 us (6%)
    ppermute x28, waiting for transfers between devices, swap(): lax.ppermute(x, axis, [(i, other(i)) for i in range(lax.axis_size(axis))])  57 us
    ppermute x28, starting transfers between devices, swap(): lax.ppermute(x, axis, [(i, other(i)) for i in range(lax.axis_size(axis))])  36.8 us
    pallas_call x21, Pallas kernels, call(): pl.pallas_call(kernel, in_specs=[ANY_HBM if i else IN_VMEM for i in ins],...  29.8 us
    unnamed x16, local copies, waits for them, and re-layouts  8.41 us
  transfers between devices with their start and end apart: 28, of which 10 were waited for; matrix products, arithmetic and copies ran while one was open for 1% of the time, Pallas kernels for 18%

profile of v2, /device:TPU:0, one launch (start us, length us, event | category | flops | bytes accessed | tf_op | source)
XLA Modules:
  0.0 134.2 jit_solution(3673630730818305025)
XLA Ops:
  5.3 1.9 %prep.1 = (f32[512,384]{1,0:T(8,128)S(1)}, bf16[512,384]{1,0:T(8,128)(2,1)S(1)}, bf16[512,384]{1,0:T(8,128)(2,1)S(1)}, f32[512,128]{1,0:T(8,128)S(1)}, f32[3,384]{1,0:T(4,128)S(1)}) custom-call(s32[16]{0:T(128)S(1)} %copy-done.5, s32[16]{0:T(128)S(1)} %copy-done.6, s32[16]{0:T(128)S(1)} %copy-done.7, bf16[512,384]{1,0:T(8,128)(2,1)S(1)} %copy-done.2, ...), custom_call_target="tpu_custom_call" | custom-call | flops 7864320 | bytes 2630848 | tf_op jit(solution)/shard_map/prep/pallas_call | solution.py:332
  7.7 2.5 %copy-done = bf16[3,3,768,384]{3,2,1,0:T(8,128)(2,1)S(1)} copy-done((bf16[3,3,768,384]{3,2,1,0:T(8,128)(2,1)S(1)}, bf16[3,3,768,384]{3,2,1,0:T(8,128)(2,1)}, u32[]{:S(2)}) %copy-start) | copy-done | bytes 5308440
  12.8 2.2 %forward_partner.3 = (f32[512,384]{1,0:T(8,128)S(1)}, bf16[512,384]{1,0:T(8,128)(2,1)S(1)}) custom-call(bf16[512,384]{1,0:T(8,128)(2,1)S(1)} %collective-permute-done.snake_ref.partner_ref, bf16[3,3,768,384]{3,2,1,0:T(8,128)(2,1)S(1)} %copy-done.1, f32[512,384]{1,0:T(8,128)S(1)} %forward_own.3.own_ref, f32[512,384]{1,0:T(8,128)S(1)} %get-tuple-element.36.old_ref.stream_ref, ...), custom_call_target="tpu_custom_call" | custom-call | flops 452984832 | bytes 3412480 | tf_op jit(solution)/shard_map/forward_partner/pallas_call | solution.py:332
  17.0 2.6 %collective-permute-start.5 = (bf16[384,512]{1,0:T(8,128)(2,1)S(1)}, bf16[384,512]{1,0:T(8,128)(2,1)S(1)}, u32[]{:S(2)}, u32[]{:S(2)}) collective-permute-start(bf16[384,512]{1,0:T(8,128)(2,1)S(1)} %turn.1), channel_id=1, source_target_pairs={{0,2},{2,0},{1,3},{3,1},{4,6},{6,4},{5,7},{7,5},{8,10},{10,8},{9,1... | collective-permute-start | bytes 1179656 | tf_op jit(solution)/shard_map/ppermute | solution.py:345
  21.8 2.2 %forward_partner.4 = (f32[512,384]{1,0:T(8,128)S(1)}, bf16[512,384]{1,0:T(8,128)(2,1)S(1)}) custom-call(bf16[512,384]{1,0:T(8,128)(2,1)S(1)} %collective-permute-done.1.snake_ref.partner_ref, bf16[3,3,768,384]{3,2,1,0:T(8,128)(2,1)S(1)} %copy-done.1, f32[512,384]{1,0:T(8,128)S(1)} %forward_own.4.own_ref, ...), custom_call_target="tpu_custom_call" | custom-call | flops 452984832 | bytes 3412480 | tf_op jit(solution)/shard_map/forward_partner/pallas_call | solution.py:332
  24.0 1.8 %combine.3 = (f32[1,384]{1,0:T(1,128)S(1)}, f32[512,384]{1,0:T(8,128)S(1)}, bf16[512,384]{1,0:T(8,128)(2,1)S(1)}) custom-call(f32[512,384]{1,0:T(8,128)S(1)} %back_own.3.own_ref, bf16[512,384]{1,0:T(8,128)(2,1)S(1)} %collective-permute-done.3.partner_ref, f32[512,384]{1,0:T(8,128)S(1)} %get-tuple-element.42.old_ref.stream_ref, ...), custom_call_target="tpu_custom_call" | custom-call | flops 11796480 | bytes 3807232 | tf_op jit(solution)/shard_map/combine/pallas_call | solution.py:332
  25.8 3.7 %collective-permute-done.5.across_ref = bf16[384,512]{1,0:T(8,128)(2,1)S(1)} collective-permute-done((bf16[384,512]{1,0:T(8,128)(2,1)S(1)}, bf16[384,512]{1,0:T(8,128)(2,1)S(1)}, u32[]{:S(2)}, u32[]{:S(2)}) %collective-permute-start.5) | collective-permute-done | bytes 393248 | tf_op jit(solution)/shard_map/ppermute | solution.py:345
  31.4 6.4 %collective-permute-done.13.grad_ref = bf16[512,384]{1,0:T(8,128)(2,1)S(1)} collective-permute-done((bf16[512,384]{1,0:T(8,128)(2,1)S(1)}, bf16[512,384]{1,0:T(8,128)(2,1)S(1)}, u32[]{:S(2)}, u32[]{:S(2)}) %collective-permute-start.13) | collective-permute-done | bytes 393248 | tf_op jit(solution)/shard_map/ppermute | solution.py:345
  37.8 1.5 %paired_weight.3 = (bf16[96,1152]{1,0:T(8,128)(2,1)S(1)}, bf16[96,1152]{1,0:T(8,128)(2,1)S(1)}, bf16[96,1152]{1,0:T(8,128)(2,1)S(1)}, bf16[96,1152]{1,0:T(8,128)(2,1)S(1)}) custom-call(bf16[512,384]{1,0:T(8,128)(2,1)S(1)} %get-tuple-element.39.snake_ref.refs_1_.own_ref, bf16[512,384]{1,0:T(8,128)(2,1)S(1)} %collective-permute-done.1.snake_ref.partner_ref, ...), custom_call_target="tpu_custom_call" | custom-call | flops 905969664 | bytes 4030464 | tf_op jit(solution)/shard_map/paired_weight/pallas_call | solution.py:332
  39.3 1.9 %collective-permute-start.14 = (bf16[96,1152]{1,0:T(8,128)(2,1)S(1)}, bf16[96,1152]{1,0:T(8,128)(2,1)S(1)}, u32[]{:S(2)}, u32[]{:S(2)}) collective-permute-start(bf16[96,1152]{1,0:T(8,128)(2,1)S(1)} %get-tuple-element.57), channel_id=1, source_target_pairs={{0,4},{4,0},{8,12},{12,8},{1,5},{5,1},{9,13},{13,9},{2,6},{6,2},{1... | collective-permute-start | bytes 663560 | tf_op jit(solution)/shard_map/ppermute | solution.py:345
  43.4 1.5 %combine.4 = (f32[1,384]{1,0:T(1,128)S(1)}, bf16[512,384]{1,0:T(8,128)(2,1)S(1)}) custom-call(f32[512,384]{1,0:T(8,128)S(1)} %back_own.4.own_ref, bf16[512,384]{1,0:T(8,128)(2,1)S(1)} %collective-permute-done.4.partner_ref, f32[512,384]{1,0:T(8,128)S(1)} %get-tuple-element.40.old_ref.stream_ref, f32[3,384]{1,0:T(4,128)S(1)} %get-tuple-element.38.rest_0_.alphas_ref, ...), custom_call_target="tpu_custom_call" | custom-call | flops 11796480 | bytes 3414016 | tf_op jit(solution)/shard_map/combine/pallas_call | solution.py:332
  45.0 1.6 %collective-permute-start.7 = (bf16[512,384]{1,0:T(8,128)(2,1)S(1)}, bf16[512,384]{1,0:T(8,128)(2,1)S(1)}, u32[]{:S(2)}, u32[]{:S(2)}) collective-permute-start(bf16[512,384]{1,0:T(8,128)(2,1)S(1)} %get-tuple-element.50.grad_ref), channel_id=1, source_target_pairs={{0,2},{2,0},{1,3},{3,1},{4,6},{6,4},{5,7},{7,5},{8,10},{10,8},{9,1... | collective-permute-start | bytes 1179656 | tf_op jit(solution)/shard_map/ppermute | solution.py:345
  49.8 3.6 %collective-permute-start.21 = (bf16[192,1152]{1,0:T(8,128)(2,1)S(1)}, bf16[192,1152]{1,0:T(8,128)(2,1)S(1)}, u32[]{:S(2)}, u32[]{:S(2)}) collective-permute-start(bf16[192,1152]{1,0:T(8,128)(2,1)S(1)} %get-tuple-element.63), channel_id=1, source_target_pairs={{0,12},{4,8},{8,4},{12,0},{1,13},{5,9},{9,5},{13,1},{2,14},{6,10},... | collective-permute-start | bytes 1327112 | tf_op jit(solution)/shard_map/ppermute | solution.py:345
  54.7 23.6 %collective-permute-done.16 = bf16[96,1152]{1,0:T(8,128)(2,1)S(1)} collective-permute-done((bf16[96,1152]{1,0:T(8,128)(2,1)S(1)}, bf16[96,1152]{1,0:T(8,128)(2,1)S(1)}, u32[]{:S(2)}, u32[]{:S(2)}) %collective-permute-start.16) | collective-permute-done | bytes 221216 | tf_op jit(solution)/shard_map/ppermute | solution.py:345
  78.6 6.2 %collective-permute-done.15 = bf16[48,1152]{1,0:T(8,128)(2,1)S(1)} collective-permute-done((bf16[48,1152]{1,0:T(8,128)(2,1)S(1)}, bf16[48,1152]{1,0:T(8,128)(2,1)S(1)}, u32[]{:S(2)}, u32[]{:S(2)}) %collective-permute-start.15) | collective-permute-done | bytes 110624 | tf_op jit(solution)/shard_map/ppermute | solution.py:345
  84.8 4.5 %collective-permute-start.17 = (bf16[48,1152]{1,0:T(8,128)(2,1)S(1)}, bf16[48,1152]{1,0:T(8,128)(2,1)S(1)}, u32[]{:S(2)}, u32[]{:S(2)}) collective-permute-start(bf16[48,1152]{1,0:T(8,128)(2,1)S(1)} %slice_add_fusion.2), channel_id=1, source_target_pairs={{0,4},{4,0},{8,12},{12,8},{1,5},{5,1},{9,13},{13,9},{2,6},{6,2},{1... | collective-permute-start | bytes 331784 | tf_op jit(solution)/shard_map/ppermute | solution.py:345
  89.3 2.7 %collective-permute-done.17 = bf16[48,1152]{1,0:T(8,128)(2,1)S(1)} collective-permute-done((bf16[48,1152]{1,0:T(8,128)(2,1)S(1)}, bf16[48,1152]{1,0:T(8,128)(2,1)S(1)}, u32[]{:S(2)}, u32[]{:S(2)}) %collective-permute-start.17) | collective-permute-done | bytes 110624 | tf_op jit(solution)/shard_map/ppermute | solution.py:345
  92.7 1.6 %combine.5 = f32[1,384]{1,0:T(1,128)S(1)} custom-call(f32[512,384]{1,0:T(8,128)S(1)} %back_own.5.own_ref, bf16[512,384]{1,0:T(8,128)(2,1)S(1)} %collective-permute-done.24.partner_ref, f32[512,384]{1,0:T(8,128)S(1)} %get-tuple-element.36.old_ref.stream_ref, f32[3,384]{1,0:T(4,128)S(1)} %get-tuple-element.38.rest_0_.alphas_ref), custom_call_target="tpu_custom_call" | custom-call | flops 11796480 | bytes 1972224 | tf_op jit(solution)/shard_map/combine/pallas_call | solution.py:332
  94.4 1.6 %collective-permute-start.25 = (f32[3,384]{1,0:T(4,128)S(1)}, f32[3,384]{1,0:T(4,128)S(1)}, u32[]{:S(2)}, u32[]{:S(2)}) collective-permute-start(f32[3,384]{1,0:T(4,128)S(1)} %pad_maximum_fusion.3), channel_id=1, source_target_pairs={{0,2},{2,0},{1,3},{3,1},{4,6},{6,4},{5,7},{7,5},{8,10},{10,8},{9,1... | collective-permute-start | bytes 13832 | tf_op jit(solution)/shard_map/ppermute | solution.py:345
  95.9 1.5 %paired_weight.2 = (bf16[96,1152]{1,0:T(8,128)(2,1)S(1)}, bf16[96,1152]{1,0:T(8,128)(2,1)S(1)}, bf16[96,1152]{1,0:T(8,128)(2,1)S(1)}, bf16[96,1152]{1,0:T(8,128)(2,1)S(1)}) custom-call(bf16[512,384]{1,0:T(8,128)(2,1)S(1)} %get-tuple-element.35.snake_ref.refs_0_.own_ref, bf16[512,384]{1,0:T(8,128)(2,1)S(1)} %collective-permute-done.snake_ref.partner_ref, ...), custom_call_target="tpu_custom_call" | custom-call | flops 905969664 | bytes 4030464 | tf_op jit(solution)/shard_map/paired_weight/pallas_call | solution.py:332
  97.5 2.1 %collective-permute-start.8 = (bf16[96,1152]{1,0:T(8,128)(2,1)S(1)}, bf16[96,1152]{1,0:T(8,128)(2,1)S(1)}, u32[]{:S(2)}, u32[]{:S(2)}) collective-permute-start(bf16[96,1152]{1,0:T(8,128)(2,1)S(1)} %get-tuple-element.53), channel_id=1, source_target_pairs={{0,4},{4,0},{8,12},{12,8},{1,5},{5,1},{9,13},{13,9},{2,6},{6,2},{1... | collective-permute-start | bytes 663560 | tf_op jit(solution)/shard_map/ppermute | solution.py:345
  99.6 2.9 %collective-permute-start.10 = (bf16[96,1152]{1,0:T(8,128)(2,1)S(1)}, bf16[96,1152]{1,0:T(8,128)(2,1)S(1)}, u32[]{:S(2)}, u32[]{:S(2)}) collective-permute-start(bf16[96,1152]{1,0:T(8,128)(2,1)S(1)} %get-tuple-element.55), channel_id=1, source_target_pairs={{0,12},{4,8},{8,4},{12,0},{1,13},{5,9},{9,5},{13,1},{2,14},{6,10},... | collective-permute-start | bytes 663560 | tf_op jit(solution)/shard_map/ppermute | solution.py:345
  103.7 7.0 %collective-permute-done.8 = bf16[96,1152]{1,0:T(8,128)(2,1)S(1)} collective-permute-done((bf16[96,1152]{1,0:T(8,128)(2,1)S(1)}, bf16[96,1152]{1,0:T(8,128)(2,1)S(1)}, u32[]{:S(2)}, u32[]{:S(2)}) %collective-permute-start.8) | collective-permute-done | bytes 221216 | tf_op jit(solution)/shard_map/ppermute | solution.py:345
  110.7 2.9 %collective-permute-done.10 = bf16[96,1152]{1,0:T(8,128)(2,1)S(1)} collective-permute-done((bf16[96,1152]{1,0:T(8,128)(2,1)S(1)}, bf16[96,1152]{1,0:T(8,128)(2,1)S(1)}, u32[]{:S(2)}, u32[]{:S(2)}) %collective-permute-start.10) | collective-permute-done | bytes 221216 | tf_op jit(solution)/shard_map/ppermute | solution.py:345
  113.6 1.9 %collective-permute-start.9 = (bf16[48,1152]{1,0:T(8,128)(2,1)S(1)}, bf16[48,1152]{1,0:T(8,128)(2,1)S(1)}, u32[]{:S(2)}, u32[]{:S(2)}) collective-permute-start(bf16[48,1152]{1,0:T(8,128)(2,1)S(1)} %slice_add_fusion.5), channel_id=1, source_target_pairs={{0,12},{4,8},{8,4},{12,0},{1,13},{5,9},{9,5},{13,1},{2,14},{6,10},... | collective-permute-start | bytes 331784 | tf_op jit(solution)/shard_map/ppermute | solution.py:345
  115.5 2.7 %collective-permute-done.20 = bf16[96,1152]{1,0:T(8,128)(2,1)S(1)} collective-permute-done((bf16[96,1152]{1,0:T(8,128)(2,1)S(1)}, bf16[96,1152]{1,0:T(8,128)(2,1)S(1)}, u32[]{:S(2)}, u32[]{:S(2)}) %collective-permute-start.20) | collective-permute-done | bytes 221216 | tf_op jit(solution)/shard_map/ppermute | solution.py:345
  118.2 3.3 %collective-permute-start.11 = (bf16[48,1152]{1,0:T(8,128)(2,1)S(1)}, bf16[48,1152]{1,0:T(8,128)(2,1)S(1)}, u32[]{:S(2)}, u32[]{:S(2)}) collective-permute-start(bf16[48,1152]{1,0:T(8,128)(2,1)S(1)} %slice_add_fusion.4), channel_id=1, source_target_pairs={{0,4},{4,0},{8,12},{12,8},{1,5},{5,1},{9,13},{13,9},{2,6},{6,2},{1... | collective-permute-start | bytes 331784 | tf_op jit(solution)/shard_map/ppermute | solution.py:345
  121.7 1.8 %collective-permute-start.23 = (bf16[192,1152]{1,0:T(8,128)(2,1)S(1)}, bf16[192,1152]{1,0:T(8,128)(2,1)S(1)}, u32[]{:S(2)}, u32[]{:S(2)}) collective-permute-start(bf16[192,1152]{1,0:T(8,128)(2,1)S(1)} %pad_maximum_fusion.refs_4_), channel_id=1, source_target_pairs={{0,2},{2,0},{1,3},{3,1},{4,6},{6,4},{5,7},{7,5},{8,10},{10,8},{9,1... | collective-permute-start | bytes 1327112 | tf_op jit(solution)/shard_map/ppermute | solution.py:345
  124.3 1.9 %collective-permute-start.12 = (bf16[96,1152]{1,0:T(8,128)(2,1)S(1)}, bf16[96,1152]{1,0:T(8,128)(2,1)S(1)}, u32[]{:S(2)}, u32[]{:S(2)}) collective-permute-start(bf16[96,1152]{1,0:T(8,128)(2,1)S(1)} %pad_maximum_fusion.1.refs_0_), channel_id=1, source_target_pairs={{0,2},{2,0},{1,3},{3,1},{4,6},{6,4},{5,7},{7,5},{8,10},{10,8},{9,1... | collective-permute-start | bytes 663560 | tf_op jit(solution)/shard_map/ppermute | solution.py:345
  126.2 2.6 %collective-permute-start.27 = (f32[3,384]{1,0:T(4,128)S(1)}, f32[3,384]{1,0:T(4,128)S(1)}, u32[]{:S(2)}, u32[]{:S(2)}) collective-permute-start(f32[3,384]{1,0:T(4,128)S(1)} %fusion.1), channel_id=1, source_target_pairs={{0,8},{4,12},{8,0},{12,4},{1,9},{5,13},{9,1},{13,5},{2,10},{6,14},... | collective-permute-start | bytes 13832 | tf_op jit(solution)/shard_map/ppermute | solution.py:345
  128.8 2.0 %forward_partner.5 = bf16[512,384]{1,0:T(8,128)(2,1)} custom-call(bf16[512,384]{1,0:T(8,128)(2,1)S(1)} %collective-permute-done.2.snake_ref.partner_ref, bf16[3,3,768,384]{3,2,1,0:T(8,128)(2,1)S(1)} %copy-done.1, f32[512,384]{1,0:T(8,128)S(1)} %forward_own.5.own_ref, f32[512,384]{1,0:T(8,128)S(1)} %get-tuple-element.42.old_ref.stream_ref, ...), custom_call_target="tpu_custom_call" | custom-call | flops 452984832 | bytes 2621440 | tf_op jit(solution)/shard_map/forward_partner/pallas_call | solution.py:332
  132.4 1.7 %finish.1 = f32[3,3,192,384]{3,2,1,0:T(8,128)} custom-call(bf16[96,1152]{1,0:T(8,128)(2,1)S(1)} %pad_maximum_fusion.1.refs_0_, bf16[96,1152]{1,0:T(8,128)(2,1)S(1)} %collective-permute-done.12.refs_1_, bf16[96,1152]{1,0:T(8,128)(2,1)S(1)} %pad_maximum_fusion.2.refs_2_, bf16[96,1152]{1,0:T(8,128)(2,1)S(1)} %collective-permute-done.18.refs_3_, ...), custom_call_target="tpu_custom_call" | custom-call | flops 663552 | bytes 4423680 | tf_op jit(solution)/shard_map/finish/pallas_call | solution.py:332
  (80 shorter events, 25.3 us)
Async XLA Ops:
  0.6 1.0 copy-start.2
  1.6 1.0 copy-start.3
  7.2 4.3 %collective-permute-start = (bf16[512,384]{1,0:T(8,128)(2,1)S(1)}, bf16[512,384]{1,0:T(8,128)(2,1)S(1)}, u32[]{:S(2)}, u32[]{:S(2)}) collective-permute-start(bf16[512,384]{1,0:T(8,128)(2,1)S(1)} %get-tuple-element.35.snake_ref.refs_0_.own_ref), channel_id=1, source_target_pairs={{0,1},{1,0},{2,3},{3,2},{4,5},{5,4},{6,7},{7,6},{8,9},{9,8},{10,11... | collective-permute-start | bytes 1179656 | tf_op jit(solution)/shard_map/ppermute | solution.py:345
  7.7 2.5 %copy-start = (bf16[3,3,768,384]{3,2,1,0:T(8,128)(2,1)S(1)}, bf16[3,3,768,384]{3,2,1,0:T(8,128)(2,1)}, u32[]{:S(2)}) copy-start(bf16[3,3,768,384]{3,2,1,0:T(8,128)(2,1)} %weight_hbm.23) | copy-start | bytes 15925252
  10.3 2.5 %copy-start.1 = (bf16[3,3,768,384]{3,2,1,0:T(8,128)(2,1)S(1)}, bf16[3,3,768,384]{3,2,1,0:T(8,128)(2,1)}, u32[]{:S(2)}) copy-start(bf16[3,3,768,384]{3,2,1,0:T(8,128)(2,1)} %weight_hbm.23) | copy-start | bytes 15925252
  14.9 6.9 %collective-permute-start.1 = (bf16[512,384]{1,0:T(8,128)(2,1)S(1)}, bf16[512,384]{1,0:T(8,128)(2,1)S(1)}, u32[]{:S(2)}, u32[]{:S(2)}) collective-permute-start(bf16[512,384]{1,0:T(8,128)(2,1)S(1)} %get-tuple-element.39.snake_ref.refs_1_.own_ref), channel_id=1, source_target_pairs={{0,1},{1,0},{2,3},{3,2},{4,5},{5,4},{6,7},{7,6},{8,9},{9,8},{10,11... | collective-permute-start | bytes 1179656 | tf_op jit(solution)/shard_map/ppermute | solution.py:345
  16.2 7.8 %collective-permute-start.3 = (bf16[512,384]{1,0:T(8,128)(2,1)S(1)}, bf16[512,384]{1,0:T(8,128)(2,1)S(1)}, u32[]{:S(2)}, u32[]{:S(2)}) collective-permute-start(bf16[512,384]{1,0:T(8,128)(2,1)S(1)} %get-tuple-element.45), channel_id=1, source_target_pairs={{0,1},{1,0},{2,3},{3,2},{4,5},{5,4},{6,7},{7,6},{8,9},{9,8},{10,11... | collective-permute-start | bytes 1179656 | tf_op jit(solution)/shard_map/ppermute | solution.py:345
  17.0 12.5 %collective-permute-start.5 = (bf16[384,512]{1,0:T(8,128)(2,1)S(1)}, bf16[384,512]{1,0:T(8,128)(2,1)S(1)}, u32[]{:S(2)}, u32[]{:S(2)}) collective-permute-start(bf16[384,512]{1,0:T(8,128)(2,1)S(1)} %turn.1), channel_id=1, source_target_pairs={{0,2},{2,0},{1,3},{3,1},{4,6},{6,4},{5,7},{7,5},{8,10},{10,8},{9,1... | collective-permute-start | bytes 1179656 | tf_op jit(solution)/shard_map/ppermute | solution.py:345
  25.7 12.0 %collective-permute-start.13 = (bf16[512,384]{1,0:T(8,128)(2,1)S(1)}, bf16[512,384]{1,0:T(8,128)(2,1)S(1)}, u32[]{:S(2)}, u32[]{:S(2)}) collective-permute-start(bf16[512,384]{1,0:T(8,128)(2,1)S(1)} %get-tuple-element.46.grad_ref), channel_id=1, source_target_pairs={{0,2},{2,0},{1,3},{3,1},{4,6},{6,4},{5,7},{7,5},{8,10},{10,8},{9,1... | collective-permute-start | bytes 1179656 | tf_op jit(solution)/shard_map/ppermute | solution.py:345
  29.5 8.2 %collective-permute-start.6 = (bf16[384,512]{1,0:T(8,128)(2,1)S(1)}, bf16[384,512]{1,0:T(8,128)(2,1)S(1)}, u32[]{:S(2)}, u32[]{:S(2)}) collective-permute-start(bf16[384,512]{1,0:T(8,128)(2,1)S(1)} %collective-permute-done.5.across_ref), channel_id=1, source_target_pairs={{0,1},{1,0},{2,3},{3,2},{4,5},{5,4},{6,7},{7,6},{8,9},{9,8},{10,11... | collective-permute-start | bytes 1179656 | tf_op jit(solution)/shard_map/ppermute | solution.py:345
  30.7 12.7 %collective-permute-start.4 = (bf16[512,384]{1,0:T(8,128)(2,1)S(1)}, bf16[512,384]{1,0:T(8,128)(2,1)S(1)}, u32[]{:S(2)}, u32[]{:S(2)}) collective-permute-start(bf16[512,384]{1,0:T(8,128)(2,1)S(1)} %get-tuple-element.48), channel_id=1, source_target_pairs={{0,1},{1,0},{2,3},{3,2},{4,5},{5,4},{6,7},{7,6},{8,9},{9,8},{10,11... | collective-permute-start | bytes 1179656 | tf_op jit(solution)/shard_map/ppermute | solution.py:345
  31.3 16.5 %collective-permute-start.2 = (bf16[512,384]{1,0:T(8,128)(2,1)S(1)}, bf16[512,384]{1,0:T(8,128)(2,1)S(1)}, u32[]{:S(2)}, u32[]{:S(2)}) collective-permute-start(bf16[512,384]{1,0:T(8,128)(2,1)S(1)} %get-tuple-element.41.snake_ref.own_ref), channel_id=1, source_target_pairs={{0,1},{1,0},{2,3},{3,2},{4,5},{5,4},{6,7},{7,6},{8,9},{9,8},{10,11... | collective-permute-start | bytes 1179656 | tf_op jit(solution)/shard_map/ppermute | solution.py:345
  39.3 15.0 %collective-permute-start.14 = (bf16[96,1152]{1,0:T(8,128)(2,1)S(1)}, bf16[96,1152]{1,0:T(8,128)(2,1)S(1)}, u32[]{:S(2)}, u32[]{:S(2)}) collective-permute-start(bf16[96,1152]{1,0:T(8,128)(2,1)S(1)} %get-tuple-element.57), channel_id=1, source_target_pairs={{0,4},{4,0},{8,12},{12,8},{1,5},{5,1},{9,13},{13,9},{2,6},{6,2},{1... | collective-permute-start | bytes 663560 | tf_op jit(solution)/shard_map/ppermute | solution.py:345
  45.0 51.0 %collective-permute-start.7 = (bf16[512,384]{1,0:T(8,128)(2,1)S(1)}, bf16[512,384]{1,0:T(8,128)(2,1)S(1)}, u32[]{:S(2)}, u32[]{:S(2)}) collective-permute-start(bf16[512,384]{1,0:T(8,128)(2,1)S(1)} %get-tuple-element.50.grad_ref), channel_id=1, source_target_pairs={{0,2},{2,0},{1,3},{3,1},{4,6},{6,4},{5,7},{7,5},{8,10},{10,8},{9,1... | collective-permute-start | bytes 1179656 | tf_op jit(solution)/shard_map/ppermute | solution.py:345
  47.7 45.0 %collective-permute-start.24 = (bf16[512,384]{1,0:T(8,128)(2,1)S(1)}, bf16[512,384]{1,0:T(8,128)(2,1)S(1)}, u32[]{:S(2)}, u32[]{:S(2)}) collective-permute-start(bf16[512,384]{1,0:T(8,128)(2,1)S(1)} %get-tuple-element.64), channel_id=1, source_target_pairs={{0,1},{1,0},{2,3},{3,2},{4,5},{5,4},{6,7},{7,6},{8,9},{9,8},{10,11... | collective-permute-start | bytes 1179656 | tf_op jit(solution)/shard_map/ppermute | solution.py:345
  49.3 53.2 %collective-permute-start.19 = (bf16[192,1152]{1,0:T(8,128)(2,1)S(1)}, bf16[192,1152]{1,0:T(8,128)(2,1)S(1)}, u32[]{:S(2)}, u32[]{:S(2)}) collective-permute-start(bf16[192,1152]{1,0:T(8,128)(2,1)S(1)} %get-tuple-element.61), channel_id=1, source_target_pairs={{0,4},{4,0},{8,12},{12,8},{1,5},{5,1},{9,13},{13,9},{2,6},{6,2},{1... | collective-permute-start | bytes 1327112 | tf_op jit(solution)/shard_map/ppermute | solution.py:345
  49.8 52.8 %collective-permute-start.21 = (bf16[192,1152]{1,0:T(8,128)(2,1)S(1)}, bf16[192,1152]{1,0:T(8,128)(2,1)S(1)}, u32[]{:S(2)}, u32[]{:S(2)}) collective-permute-start(bf16[192,1152]{1,0:T(8,128)(2,1)S(1)} %get-tuple-element.63), channel_id=1, source_target_pairs={{0,12},{4,8},{8,4},{12,0},{1,13},{5,9},{9,5},{13,1},{2,14},{6,10},... | collective-permute-start | bytes 1327112 | tf_op jit(solution)/shard_map/ppermute | solution.py:345
  54.4 23.9 %collective-permute-start.16 = (bf16[96,1152]{1,0:T(8,128)(2,1)S(1)}, bf16[96,1152]{1,0:T(8,128)(2,1)S(1)}, u32[]{:S(2)}, u32[]{:S(2)}) collective-permute-start(bf16[96,1152]{1,0:T(8,128)(2,1)S(1)} %get-tuple-element.59), channel_id=1, source_target_pairs={{0,12},{4,8},{8,4},{12,0},{1,13},{5,9},{9,5},{13,1},{2,14},{6,10},... | collective-permute-start | bytes 663560 | tf_op jit(solution)/shard_map/ppermute | solution.py:345
  78.3 6.5 %collective-permute-start.15 = (bf16[48,1152]{1,0:T(8,128)(2,1)S(1)}, bf16[48,1152]{1,0:T(8,128)(2,1)S(1)}, u32[]{:S(2)}, u32[]{:S(2)}) collective-permute-start(bf16[48,1152]{1,0:T(8,128)(2,1)S(1)} %slice_add_fusion.3), channel_id=1, source_target_pairs={{0,12},{4,8},{8,4},{12,0},{1,13},{5,9},{9,5},{13,1},{2,14},{6,10},... | collective-permute-start | bytes 331784 | tf_op jit(solution)/shard_map/ppermute | solution.py:345
  84.8 7.2 %collective-permute-start.17 = (bf16[48,1152]{1,0:T(8,128)(2,1)S(1)}, bf16[48,1152]{1,0:T(8,128)(2,1)S(1)}, u32[]{:S(2)}, u32[]{:S(2)}) collective-permute-start(bf16[48,1152]{1,0:T(8,128)(2,1)S(1)} %slice_add_fusion.2), channel_id=1, source_target_pairs={{0,4},{4,0},{8,12},{12,8},{1,5},{5,1},{9,13},{13,9},{2,6},{6,2},{1... | collective-permute-start | bytes 331784 | tf_op jit(solution)/shard_map/ppermute | solution.py:345
  92.1 39.3 %collective-permute-start.18 = (bf16[96,1152]{1,0:T(8,128)(2,1)S(1)}, bf16[96,1152]{1,0:T(8,128)(2,1)S(1)}, u32[]{:S(2)}, u32[]{:S(2)}) collective-permute-start(bf16[96,1152]{1,0:T(8,128)(2,1)S(1)} %pad_maximum_fusion.2.refs_2_), channel_id=1, source_target_pairs={{0,2},{2,0},{1,3},{3,1},{4,6},{6,4},{5,7},{7,5},{8,10},{10,8},{9,1... | collective-permute-start | bytes 663560 | tf_op jit(solution)/shard_map/ppermute | solution.py:345
  94.4 5.2 %collective-permute-start.25 = (f32[3,384]{1,0:T(4,128)S(1)}, f32[3,384]{1,0:T(4,128)S(1)}, u32[]{:S(2)}, u32[]{:S(2)}) collective-permute-start(f32[3,384]{1,0:T(4,128)S(1)} %pad_maximum_fusion.3), channel_id=1, source_target_pairs={{0,2},{2,0},{1,3},{3,1},{4,6},{6,4},{5,7},{7,5},{8,10},{10,8},{9,1... | collective-permute-start | bytes 13832 | tf_op jit(solution)/shard_map/ppermute | solution.py:345
  97.5 13.2 %collective-permute-start.8 = (bf16[96,1152]{1,0:T(8,128)(2,1)S(1)}, bf16[96,1152]{1,0:T(8,128)(2,1)S(1)}, u32[]{:S(2)}, u32[]{:S(2)}) collective-permute-start(bf16[96,1152]{1,0:T(8,128)(2,1)S(1)} %get-tuple-element.53), channel_id=1, source_target_pairs={{0,4},{4,0},{8,12},{12,8},{1,5},{5,1},{9,13},{13,9},{2,6},{6,2},{1... | collective-permute-start | bytes 663560 | tf_op jit(solution)/shard_map/ppermute | solution.py:345
  99.6 14.0 %collective-permute-start.10 = (bf16[96,1152]{1,0:T(8,128)(2,1)S(1)}, bf16[96,1152]{1,0:T(8,128)(2,1)S(1)}, u32[]{:S(2)}, u32[]{:S(2)}) collective-permute-start(bf16[96,1152]{1,0:T(8,128)(2,1)S(1)} %get-tuple-element.55), channel_id=1, source_target_pairs={{0,12},{4,8},{8,4},{12,0},{1,13},{5,9},{9,5},{13,1},{2,14},{6,10},... | collective-permute-start | bytes 663560 | tf_op jit(solution)/shard_map/ppermute | solution.py:345
  102.5 23.6 %collective-permute-start.26 = (f32[3,384]{1,0:T(4,128)S(1)}, f32[3,384]{1,0:T(4,128)S(1)}, u32[]{:S(2)}, u32[]{:S(2)}) collective-permute-start(f32[3,384]{1,0:T(4,128)S(1)} %fusion), channel_id=1, source_target_pairs={{0,4},{4,0},{8,12},{12,8},{1,5},{5,1},{9,13},{13,9},{2,6},{6,2},{1... | collective-permute-start | bytes 13832 | tf_op jit(solution)/shard_map/ppermute | solution.py:345
  102.6 15.5 %collective-permute-start.20 = (bf16[96,1152]{1,0:T(8,128)(2,1)S(1)}, bf16[96,1152]{1,0:T(8,128)(2,1)S(1)}, u32[]{:S(2)}, u32[]{:S(2)}) collective-permute-start(bf16[96,1152]{1,0:T(8,128)(2,1)S(1)} %slice_add_fusion.1), channel_id=1, source_target_pairs={{0,12},{4,8},{8,4},{12,0},{1,13},{5,9},{9,5},{13,1},{2,14},{6,10},... | collective-permute-start | bytes 663560 | tf_op jit(solution)/shard_map/ppermute | solution.py:345
  110.7 10.9 %collective-permute-start.22 = (bf16[96,1152]{1,0:T(8,128)(2,1)S(1)}, bf16[96,1152]{1,0:T(8,128)(2,1)S(1)}, u32[]{:S(2)}, u32[]{:S(2)}) collective-permute-start(bf16[96,1152]{1,0:T(8,128)(2,1)S(1)} %slice_add_fusion), channel_id=1, source_target_pairs={{0,4},{4,0},{8,12},{12,8},{1,5},{5,1},{9,13},{13,9},{2,6},{6,2},{1... | collective-permute-start | bytes 663560 | tf_op jit(solution)/shard_map/ppermute | solution.py:345
  113.6 9.9 %collective-permute-start.9 = (bf16[48,1152]{1,0:T(8,128)(2,1)S(1)}, bf16[48,1152]{1,0:T(8,128)(2,1)S(1)}, u32[]{:S(2)}, u32[]{:S(2)}) collective-permute-start(bf16[48,1152]{1,0:T(8,128)(2,1)S(1)} %slice_add_fusion.5), channel_id=1, source_target_pairs={{0,12},{4,8},{8,4},{12,0},{1,13},{5,9},{9,5},{13,1},{2,14},{6,10},... | collective-permute-start | bytes 331784 | tf_op jit(solution)/shard_map/ppermute | solution.py:345
  118.2 6.0 %collective-permute-start.11 = (bf16[48,1152]{1,0:T(8,128)(2,1)S(1)}, bf16[48,1152]{1,0:T(8,128)(2,1)S(1)}, u32[]{:S(2)}, u32[]{:S(2)}) collective-permute-start(bf16[48,1152]{1,0:T(8,128)(2,1)S(1)} %slice_add_fusion.4), channel_id=1, source_target_pairs={{0,4},{4,0},{8,12},{12,8},{1,5},{5,1},{9,13},{13,9},{2,6},{6,2},{1... | collective-permute-start | bytes 331784 | tf_op jit(solution)/shard_map/ppermute | solution.py:345
  121.7 10.7 %collective-permute-start.23 = (bf16[192,1152]{1,0:T(8,128)(2,1)S(1)}, bf16[192,1152]{1,0:T(8,128)(2,1)S(1)}, u32[]{:S(2)}, u32[]{:S(2)}) collective-permute-start(bf16[192,1152]{1,0:T(8,128)(2,1)S(1)} %pad_maximum_fusion.refs_4_), channel_id=1, source_target_pairs={{0,2},{2,0},{1,3},{3,1},{4,6},{6,4},{5,7},{7,5},{8,10},{10,8},{9,1... | collective-permute-start | bytes 1327112 | tf_op jit(solution)/shard_map/ppermute | solution.py:345
  124.3 8.2 %collective-permute-start.12 = (bf16[96,1152]{1,0:T(8,128)(2,1)S(1)}, bf16[96,1152]{1,0:T(8,128)(2,1)S(1)}, u32[]{:S(2)}, u32[]{:S(2)}) collective-permute-start(bf16[96,1152]{1,0:T(8,128)(2,1)S(1)} %pad_maximum_fusion.1.refs_0_), channel_id=1, source_target_pairs={{0,2},{2,0},{1,3},{3,1},{4,6},{6,4},{5,7},{7,5},{8,10},{10,8},{9,1... | collective-permute-start | bytes 663560 | tf_op jit(solution)/shard_map/ppermute | solution.py:345
  126.2 4.6 %collective-permute-start.27 = (f32[3,384]{1,0:T(4,128)S(1)}, f32[3,384]{1,0:T(4,128)S(1)}, u32[]{:S(2)}, u32[]{:S(2)}) collective-permute-start(f32[3,384]{1,0:T(4,128)S(1)} %fusion.1), channel_id=1, source_target_pairs={{0,8},{4,12},{8,0},{12,4},{1,9},{5,13},{9,1},{13,5},{2,10},{6,14},... | collective-permute-start | bytes 13832 | tf_op jit(solution)/shard_map/ppermute | solution.py:345
  (4 other events, 2.7 us)

commit v3 on v2

--- a/solution.py
+++ b/solution.py
@@ -321,57 +321,75 @@
                 out_ref[layer, tap] = mine + other
 
 
+def fold_kernel(keep_a, got_a, keep_b, got_b, send_a, send_b):
+    rows = send_a.shape[0]
+    for keep, got, send in ((keep_a, got_a, send_a), (keep_b, got_b, send_b)):
+        send[...] = (keep[rows:, :].astype(F32) + got[rows:, :].astype(F32)).astype(BF16)
+
+
+def total_kernel(keep_a, got_a, late_a, keep_b, got_b, late_b, out_ref):
+    rows = late_a.shape[0]
+    for index, (keep, got, late) in enumerate(((keep_a, got_a, late_a), (keep_b, got_b, late_b))):
+        total = keep[0:rows, :].astype(F32) + got[0:rows, :].astype(F32) + late[...].astype(F32)
+        out_ref[index * rows : (index + 1) * rows, :] = total.astype(BF16)
+
+
 def struct(shape, dtype):
     return jax.ShapeDtypeStruct(shape, dtype)
 
 
-def call(kernel, name, ins, outs, scratch, flops, *args):
-    single = not isinstance(outs, list)
-    size = sum(a.size * a.dtype.itemsize for a in args if a.size < 2000000)
-    size += sum(math.prod(o.shape) * o.dtype.itemsize for o in ([outs] if single else outs))
-    return pl.pallas_call(
-        kernel,
-        in_specs=[ANY_HBM if i else IN_VMEM for i in ins],
-        out_specs=IN_VMEM if single else [IN_VMEM] * len(outs),
-        out_shape=outs,
-        scratch_shapes=scratch,
-        compiler_params=pltpu.CompilerParams(vmem_limit_bytes=24 * 1024 * 1024),
-        cost_estimate=pl.CostEstimate(flops=int(flops), bytes_accessed=int(size), transcendentals=0),
-        name=name,
-    )(*args)
+def after(value, other):
+    return value if other is None else lax.optimization_barrier((value, other))[0]
+
+
+class Sequence:
+    def __init__(self):
+        self.latest = None
+
+    def hold(self, value):
+        return after(value, self.latest)
+
+    def call(self, kernel, name, ins, outs, scratch, flops, *args):
+        single = not isinstance(outs, list)
+        size = sum(a.size * a.dtype.itemsize for a in args if a.size < 2000000)
+        size += sum(math.prod(o.shape) * o.dtype.itemsize for o in ([outs] if single else outs))
+        args = [pltpu.with_memory_space_constraint(a, pltpu.HBM) if i else a for i, a in zip(ins, args)]
+        if self.latest is not None:
+            held = ins.index(0)
+            args[held] = self.hold(args[held])
+        result = pl.pallas_call(
+            kernel,
+            in_specs=[ANY_HBM if i else IN_VMEM for i in ins],
+            out_specs=IN_VMEM if single else [IN_VMEM] * len(outs),
+            out_shape=outs,
+            scratch_shapes=scratch,
+            compiler_params=pltpu.CompilerParams(vmem_limit_bytes=24 * 1024 * 1024),
+            cost_estimate=pl.CostEstimate(flops=int(flops) * 10, bytes_accessed=int(size) * 10, transcendentals=0),
+            name=name,
+        )(*args)
+        self.latest = result if single else result[0]
+        return result
 
 
 def swap(x, axis, other):
     return lax.ppermute(x, axis, [(i, other(i)) for i in range(lax.axis_size(axis))])
 
 
-def after(value, *others):
-    return lax.optimization_barrier((value,) + others)[0]
-
-
-def reduce_weights(parts, fast):
-    if not fast:
-        return lax.psum(lax.psum_scatter(parts[0], "dp", scatter_dimension=0, tiled=True), "replica")
-    send_a, send_b, keep_a, keep_b = parts
-    rows = keep_a.shape[0] // 2
-    got_a = swap(send_a, "dp", lambda i: i ^ 1)
-    got_b = swap(send_b, "dp", lambda i: i ^ 3)
-    late_a = swap(keep_a[rows:] + got_a[rows:], "dp", lambda i: i ^ 3)
-    late_b = swap(keep_b[rows:] + got_b[rows:], "dp", lambda i: i ^ 1)
-
-    def total(keep, got, late):
-        return (keep[:rows].astype(F32) + got[:rows].astype(F32) + late.astype(F32)).astype(BF16)
-
-    return jnp.concatenate([total(keep_a, got_a, late_a), total(keep_b, got_b, late_b)])
-
-
-def sum_over(values, axis):
+def across_chan(x):
+    return swap(x, "chan", lambda i: i ^ 1)
+
+
+def across_replica(x):
+    return swap(x, "replica", lambda i: i ^ 1)
+
+
+def sum_rounds(values, axis, sequence):
     size = lax.axis_size(axis)
     if size & (size - 1):
         return lax.psum(values, axis)
     apart = 1
     while apart < size:
-        values = values + swap(values, axis, lambda i, apart=apart: i ^ apart)
+        values = values + swap(sequence.hold(values), axis, lambda i, apart=apart: i ^ apart)
         apart *= 2
     return values
 
@@ -379,102 +397,165 @@
 def on_device(activations, cotangent, conv_weights, snake_alpha, seg_lengths, seg_owner, seg_start):
     rows, half = activations.shape
     layers, taps, channels, _ = conv_weights.shape
+    top = layers - 1
     fast = lax.axis_size("dp") == 4 and lax.axis_size("replica") == 2
-    paired = [fast and layer < layers - 1 for layer in range(layers)]
+    paired = [fast and layer < top for layer in range(layers)]
+    sources = [layer for layer in range(layers) if paired[layer]]
     tile, triple = (rows, half), (rows, taps * half)
     flops = 2 * rows * half * half * taps
-    clips = seg_lengths.shape
     by_rows = [pltpu.VMEM((taps * half, half), BF16), DMA((3,))]
     by_columns = [pltpu.VMEM((half, taps * half), BF16), DMA((3,))]
-
-    stream, snaked, grad, live, alphas = call(
-        prep_kernel, "prep", [1] * 6,
-        [struct(tile, F32), struct(tile, BF16), struct(tile, BF16), struct((rows, 128), F32), struct(snake_alpha.shape, F32)],
-        [pltpu.SMEM(clips, jnp.int32)] * 3 + [pltpu.VMEM(tile, BF16)] * 2 + [DMA((6,))],
-        40 * rows * half,
-        seg_lengths, seg_owner, seg_start, activations, cotangent, snake_alpha,
-    )
-
-    streams, mine, partners = [], [], []
-    for layer in range(layers):
-        last = layer == layers - 1
-        other = swap(snaked, "chan", lambda i: i ^ 1)
-        streams.append(stream)
-        mine.append(snaked)
-        partners.append(other)
-        own = call(
+    sequence = Sequence()
+    streams, mine, partners, owns = [], [], {}, {}
+    rounded, shifted, arrived, back_owns, far = {}, {}, {}, {}, {}
+    alpha_parts = [None] * layers
+    parts, got, late, summed, crossed = {}, {}, {}, {}, {}
+
+    def forward_own(layer):
+        owns[layer] = sequence.call(
             functools.partial(forward_own_kernel, layer), "forward_own", [0, 1], struct(tile, F32),
-            [pltpu.VMEM(triple, BF16)] + by_rows, flops, snaked, conv_weights,
-        )
-        outs = struct(tile, BF16) if last else [struct(tile, F32), struct(tile, BF16)]
-        result = call(
+            [pltpu.VMEM(triple, BF16)] + by_rows, flops, mine[layer], conv_weights,
+        )
+
+    def forward_partner(layer):
+        last = layer == top
+        result = sequence.call(
             functools.partial(forward_partner_kernel, layer, last), "forward_partner",
-            [0, 1, 0, 0, 0] + ([] if last else [0]), outs,
+            [0, 1, 0, 0, 0] + ([] if last else [0]),
+            struct(tile, BF16) if last else [struct(tile, F32), struct(tile, BF16)],
             [pltpu.VMEM(triple, BF16)] + by_rows, flops,
-            other, conv_weights, own, stream, live, *([] if last else [alphas]),
+            partners[layer], conv_weights, owns[layer], streams[layer], live, *([] if last else [alphas]),
         )
         if last:
-            residual_out = result
-        else:
-            stream, snaked = result
-
-    if any(paired):
-        sources = [layer for layer in range(layers) if paired[layer]]
-        turned = call(
-            turn_kernel, "turn", [0] * len(sources), struct((len(sources) * half // 2, rows), BF16),
-            [pltpu.VMEM((half, rows), BF16)], 10 * rows * half, *[mine[layer] for layer in sources],
-        )
-        across = swap(turned, "replica", lambda i: i ^ 1)
-        across_other = swap(across, "chan", lambda i: i ^ 1)
-
-    alpha_parts = [None] * layers
-    summed = [None] * layers
-    rounded = grad
-    for layer in reversed(range(layers)):
-        shifted, partner_part = call(
+            return result
+        streams.append(result[0])
+        mine.append(result[1])
+        partners[layer + 1] = across_chan(result[1])
+
+    def back_partner(layer):
+        shifted[layer], part = sequence.call(
             functools.partial(back_partner_kernel, layer), "back_partner", [0, 1],
-            [struct(triple, BF16), struct(tile, BF16)], by_columns, flops, rounded, conv_weights,
-        )
-        arrived = swap(partner_part, "chan", lambda i: i ^ 1)
-        own_part = call(
+            [struct(triple, BF16), struct(tile, BF16)], by_columns, flops, rounded[layer + 1], conv_weights,
+        )
+        arrived[layer] = across_chan(part)
+
+    def back_own(layer):
+        back_owns[layer] = sequence.call(
             functools.partial(back_own_kernel, layer), "back_own", [0, 1], struct(tile, F32),
-            by_columns, flops, shifted, conv_weights,
-        )
-        pieces = 4 if fast else 1
-        if paired[layer]:
-            far = swap(rounded, "replica", lambda i: i ^ 1)
-            piece = struct((channels // 2 // pieces, taps * half), BF16)
-            parts = call(
-                functools.partial(paired_weight_kernel, layer, sources.index(layer)), "paired_weight", [0] * 6,
-                [piece] * pieces,
-                [pltpu.VMEM((half, 2 * rows), BF16), pltpu.VMEM((half, rows), BF16), pltpu.VMEM(triple, BF16)],
-                2 * flops, mine[layer], partners[layer], shifted, across, across_other, far,
-            )
-        else:
-            piece = struct((channels // pieces, taps * half), BF16)
-            parts = call(
-                functools.partial(weight_kernel, fast), "weight", [0] * 3, [piece] * pieces,
-                [pltpu.VMEM((channels, rows), BF16)], 2 * flops, mine[layer], partners[layer], shifted,
-            )
-        summed[layer] = reduce_weights(parts, fast)
-        args = [own_part, arrived, streams[layer], alphas]
+            by_columns, flops, shifted[layer], conv_weights,
+        )
+
+    def combine(layer, grad):
+        args = [back_owns[layer], arrived[layer], streams[layer], alphas]
         outs = [struct((1, half), F32)]
         if layer > 0:
             args += [grad, live]
             outs += [struct(tile, F32)] * (layer > 1) + [struct(tile, BF16)]
-        result = call(
+        result = sequence.call(
             functools.partial(combine_kernel, layer), "combine", [0] * len(args), outs, [], 60 * rows * half, *args
         )
         alpha_parts[layer] = result[0]
         if layer > 0:
-            grad, rounded = result[1], result[-1]
-
-    alpha_grads = sum_over(sum_over(jnp.concatenate(alpha_parts), "replica"), "dp")
+            rounded[layer] = result[-1]
+            if paired[layer - 1]:
+                far[layer - 1] = across_replica(result[-1])
+            return result[1]
+
+    def weights(layer):
+        pieces = 4 if fast else 1
+        if paired[layer]:
+            piece = struct((channels // 2 // pieces, taps * half), BF16)
+            out = sequence.call(
+                functools.partial(paired_weight_kernel, layer, sources.index(layer)), "paired_weight", [0] * 6,
+                [piece] * pieces,
+                [pltpu.VMEM((half, 2 * rows), BF16), pltpu.VMEM((half, rows), BF16), pltpu.VMEM(triple, BF16)],
+                2 * flops, mine[layer], partners[layer], shifted[layer], across, across_other, far[layer],
+            )
+        else:
+            piece = struct((channels // pieces, taps * half), BF16)
+            out = sequence.call(
+                functools.partial(weight_kernel, fast), "weight", [0] * 3, [piece] * pieces,
+                [pltpu.VMEM((channels, rows), BF16)], 2 * flops, mine[layer], partners[layer], shifted[layer],
+            )
+        if not fast:
+            part = lax.psum_scatter(out[0], "dp", scatter_dimension=0, tiled=True)
+            summed[layer] = lax.psum(part, "replica")
+            crossed[layer] = jnp.zeros_like(part)
+            return
+        send_a, send_b, keep_a, keep_b = out
+        parts[layer] = (keep_a, keep_b)
+        got[layer] = (swap(send_a, "dp", lambda i: i ^ 1), swap(send_b, "dp", lambda i: i ^ 3))
+
+    def fold(layer):
+        if not fast:
+            return
+        (keep_a, keep_b), (got_a, got_b) = parts[layer], got[layer]
+        piece = struct((keep_a.shape[0] // 2, keep_a.shape[1]), BF16)
+        send_a, send_b = sequence.call(
+            fold_kernel, "fold", [0] * 4, [piece, piece], [], keep_a.size, keep_a, got_a, keep_b, got_b
+        )
+        late[layer] = (swap(send_a, "dp", lambda i: i ^ 3), swap(send_b, "dp", lambda i: i ^ 1))
+
+    def total(layer):
+        if not fast:
+            return
+        (keep_a, keep_b), (got_a, got_b), (late_a, late_b) = parts[layer], got[layer], late[layer]
+        summed[layer] = sequence.call(
+            total_kernel, "total", [0] * 6, struct(keep_a.shape, BF16), [], keep_a.size,
+            keep_a, got_a, late_a, keep_b, got_b, late_b,
+        )
+        crossed[layer] = across_replica(summed[layer])
+
+    stream, snaked, grad, live, alphas = sequence.call(
+        prep_kernel, "prep", [1] * 6,
+        [struct(tile, F32), struct(tile, BF16), struct(tile, BF16), struct((rows, 128), F32), struct(snake_alpha.shape, F32)],
+        [pltpu.SMEM(seg_lengths.shape, jnp.int32)] * 3 + [pltpu.VMEM(tile, BF16)] * 2 + [DMA((6,))],
+        40 * rows * half,
+        seg_lengths, seg_owner, seg_start, activations, cotangent, snake_alpha,
+    )
+    streams.append(stream)
+    mine.append(snaked)
+    partners[0] = across_chan(snaked)
+    rounded[layers] = grad
+    back_partner(2)
+    forward_own(0)
+    forward_partner(0)
+    if sources:
+        turned = sequence.call(
+            turn_kernel, "turn", [0] * len(sources), struct((len(sources) * half // 2, rows), BF16),
+            [pltpu.VMEM((half, rows), BF16)], 10 * rows * half, *[mine[layer] for layer in sources],
+        )
+        across = across_replica(turned)
+    back_own(2)
+    forward_own(1)
+    forward_partner(1)
+    grad = combine(2, grad)
+    back_partner(1)
+    weights(2)
+    back_own(1)
+    combine(1, grad)
+    back_partner(0)
+    forward_own(2)
+    if sources:
+        across_other = across_chan(sequence.hold(across))
+    back_own(0)
+    combine(0, None)
+    alpha_grads = sum_rounds(jnp.concatenate(alpha_parts), "replica", sequence)
+    residual_out = forward_partner(2)
+    weights(1)
+    fold(2)
+    weights(0)
+    total(2)
+    alpha_grads = sum_rounds(alpha_grads, "dp", sequence)
+    fold(1)
+    fold(0)
+    total(1)
+    total(0)
     pairs = []
-    for values in summed:
-        pairs += [values, swap(values, "replica", lambda i: i ^ 1) if fast else jnp.zeros_like(values)]
+    for layer in range(layers):
+        pairs += [summed[layer], crossed[layer]]
     depth = channels // lax.axis_size("dp")
-    weight_grads = call(
+    weight_grads = sequence.call(
         functools.partial(finish_kernel, tuple(paired)), "finish", [0] * len(pairs),
         struct((layers, taps, depth, half), F32), [], layers * taps * depth * half, *pairs,
     )

time: 135 us -> 100 us (0.74)
  waiting for transfers between devices: 57 us -> 26.6 us
  Pallas kernels: 29.8 us -> 40.3 us
  local copies, waits for them, and re-layouts: 8.41 us -> 0 us
  starting transfers between devices: 36.8 us -> 31.4 us
    ppermute x28, waiting for transfers between devices: 57 us -> 26.6 us  [swap(): lax.ppermute(x, axis, [(i, other(i)) for i in range(lax.axis_size(axis))])]
    pallas_call x21 -> x27, Pallas kernels: 29.8 us -> 40.3 us  [call(): pl.pallas_call(kernel, in_specs=[ANY_HBM if i else IN_VMEM for i in ins],...]
    unnamed x16 -> x0, local copies, waits for them, and re-layouts: 8.41 us -> none
    ppermute x28, starting transfers between devices: 36.8 us -> 31.4 us  [swap(): lax.ppermute(x, axis, [(i, other(i)) for i in range(lax.axis_size(axis))])]
  transfers between devices with their start and end apart: 28 -> 28, of which waited for: 10 -> 6; matrix products, arithmetic and copies ran while one was open for 1% -> 1% of each run, Pallas kernels for 18% -> 37%
where the time goes in v3:
time: 100 us; the launch traced here: 99.8 us
  Pallas kernels  40.3 us (40%)
  starting transfers between devices  31.4 us (31%)
  waiting for transfers between devices  26.6 us (27%)
    pallas_call x27, Pallas kernels, call(): pl.pallas_call(kernel, in_specs=[ANY_HBM if i else IN_VMEM for i in ins],...  40.3 us
    ppermute x28, starting transfers between devices, swap(): lax.ppermute(x, axis, [(i, other(i)) for i in range(lax.axis_size(axis))])  31.4 us
    ppermute x28, waiting for transfers between devices, swap(): lax.ppermute(x, axis, [(i, other(i)) for i in range(lax.axis_size(axis))])  26.6 us
  transfers between devices with their start and end apart: 28, of which 6 were waited for; matrix products, arithmetic and copies ran while one was open for 1% of the time, Pallas kernels for 37%

profile of v3, /device:TPU:0, one launch (start us, length us, event | category | flops | bytes accessed | tf_op | source)
XLA Modules:
  0.0 99.8 jit_solution(674048731466318230)
XLA Ops:
  0.6 2.1 %prep.1 = (f32[512,384]{1,0:T(8,128)S(1)}, bf16[512,384]{1,0:T(8,128)(2,1)S(1)}, bf16[512,384]{1,0:T(8,128)(2,1)S(1)}, f32[512,128]{1,0:T(8,128)S(1)}, f32[3,384]{1,0:T(4,128)S(1)}) custom-call(s32[16]{0:T(128)} %len_hbm.1, s32[16]{0:T(128)} %own_hbm.1, s32[16]{0:T(128)} %start_hbm.1, bf16[512,384]{1,0:T(8,128)(2,1)} %act_hbm.1, bf16[512,384]{1,0:T(8,128)(2,1)} %cot_hbm.1, ...), custom_call_target="tpu_custom_call" | custom-call | flops 78643200 | bytes 26308480 | tf_op jit(solution)/shard_map/prep/pallas_call | solution.py:360
  3.2 2.0 %back_partner.3 = (bf16[512,1152]{1,0:T(8,128)(2,1)S(1)}, bf16[512,384]{1,0:T(8,128)(2,1)S(1)}) custom-call(bf16[512,384]{1,0:T(8,128)(2,1)S(1)} %get-tuple-element.72.grad_ref.rest_0_, bf16[3,3,768,384]{3,2,1,0:T(8,128)(2,1)} %weight_hbm.23), custom_call_target="tpu_custom_call" | custom-call | flops 4529848320 | bytes 19660800 | tf_op jit(solution)/shard_map/back_partner/pallas_call | solution.py:360
  5.4 2.0 %forward_own.3.own_ref = f32[512,384]{1,0:T(8,128)S(1)} custom-call(bf16[512,384]{1,0:T(8,128)(2,1)S(1)} %get-tuple-element.113.snake_ref.refs_0_.own_ref, bf16[3,3,768,384]{3,2,1,0:T(8,128)(2,1)} %weight_hbm.23), custom_call_target="tpu_custom_call" | custom-call | flops 4529848320 | bytes 11796480 | tf_op jit(solution)/shard_map/forward_own/pallas_call | solution.py:360
  7.3 2.9 %forward_partner.3 = (f32[512,384]{1,0:T(8,128)S(1)}, bf16[512,384]{1,0:T(8,128)(2,1)S(1)}) custom-call(bf16[512,384]{1,0:T(8,128)(2,1)S(1)} %collective-permute-done.snake_ref.partner_ref, bf16[3,3,768,384]{3,2,1,0:T(8,128)(2,1)} %weight_hbm.23, f32[512,384]{1,0:T(8,128)S(1)} %forward_own.3.own_ref, f32[512,384]{1,0:T(8,128)S(1)} %get-tuple-element.71.old_ref.stream_ref, ...), custom_call_target="tpu_custom_call" | custom-call | flops 4529848320 | bytes 34124800 | tf_op jit(solution)/shard_map/forward_partner/pallas_call | solution.py:360
  10.5 3.0 %collective-permute-start.6 = (bf16[384,512]{1,0:T(8,128)(2,1)S(1)}, bf16[384,512]{1,0:T(8,128)(2,1)S(1)}, u32[]{:S(2)}, u32[]{:S(2)}) collective-permute-start(bf16[384,512]{1,0:T(8,128)(2,1)S(1)} %turn.1), channel_id=1, source_target_pairs={{0,2},{2,0},{1,3},{3,1},{4,6},{6,4},{5,7},{7,5},{8,10},{10,8},{9,1... | collective-permute-start | bytes 1179656 | tf_op jit(solution)/shard_map/ppermute | solution.py:375
  13.5 2.0 %back_own.3.own_ref = f32[512,384]{1,0:T(8,128)S(1)} custom-call(bf16[512,1152]{1,0:T(8,128)(2,1)S(1)} %get-tuple-element.81.shifted_ref, bf16[3,3,768,384]{3,2,1,0:T(8,128)(2,1)} %weight_hbm.23), custom_call_target="tpu_custom_call" | custom-call | flops 4529848320 | bytes 19660800 | tf_op jit(solution)/shard_map/back_own/pallas_call | solution.py:360
  15.5 2.0 %forward_own.4.own_ref = f32[512,384]{1,0:T(8,128)S(1)} custom-call(bf16[512,384]{1,0:T(8,128)(2,1)S(1)} %get-tuple-element.106.refs_1_.snake_ref.own_ref, bf16[3,3,768,384]{3,2,1,0:T(8,128)(2,1)} %weight_hbm.23), custom_call_target="tpu_custom_call" | custom-call | flops 4529848320 | bytes 11796480 | tf_op jit(solution)/shard_map/forward_own/pallas_call | solution.py:360
  17.5 2.9 %forward_partner.4 = (f32[512,384]{1,0:T(8,128)S(1)}, bf16[512,384]{1,0:T(8,128)(2,1)S(1)}) custom-call(bf16[512,384]{1,0:T(8,128)(2,1)S(1)} %collective-permute-done.1.snake_ref.partner_ref, bf16[3,3,768,384]{3,2,1,0:T(8,128)(2,1)} %weight_hbm.23, f32[512,384]{1,0:T(8,128)S(1)} %forward_own.4.own_ref, f32[512,384]{1,0:T(8,128)S(1)} %get-tuple-element.79.old_ref.stream_ref, ...), custom_call_target="tpu_custom_call" | custom-call | flops 4529848320 | bytes 34124800 | tf_op jit(solution)/shard_map/forward_partner/pallas_call | solution.py:360
  20.4 1.6 %combine.3 = (f32[1,384]{1,0:T(1,128)S(1)}, f32[512,384]{1,0:T(8,128)S(1)}, bf16[512,384]{1,0:T(8,128)(2,1)S(1)}) custom-call(f32[512,384]{1,0:T(8,128)S(1)} %back_own.3.own_ref, bf16[512,384]{1,0:T(8,128)(2,1)S(1)} %collective-permute-done.3.partner_ref, f32[512,384]{1,0:T(8,128)S(1)} %get-tuple-element.85.stream_ref.old_ref, ...), custom_call_target="tpu_custom_call" | custom-call | flops 117964800 | bytes 38072320 | tf_op jit(solution)/shard_map/combine/pallas_call | solution.py:360
  22.6 2.0 %back_partner.4 = (bf16[512,1152]{1,0:T(8,128)(2,1)S(1)}, bf16[512,384]{1,0:T(8,128)(2,1)S(1)}) custom-call(bf16[512,384]{1,0:T(8,128)(2,1)S(1)} %get-tuple-element.90.grad_ref, bf16[3,3,768,384]{3,2,1,0:T(8,128)(2,1)} %weight_hbm.23), custom_call_target="tpu_custom_call" | custom-call | flops 4529848320 | bytes 19660800 | tf_op jit(solution)/shard_map/back_partner/pallas_call | solution.py:360
  24.7 1.5 %weight.1 = (bf16[192,1152]{1,0:T(8,128)(2,1)S(1)}, bf16[192,1152]{1,0:T(8,128)(2,1)S(1)}, bf16[192,1152]{1,0:T(8,128)(2,1)S(1)}, bf16[192,1152]{1,0:T(8,128)(2,1)S(1)}) custom-call(bf16[512,384]{1,0:T(8,128)(2,1)S(1)} %get-tuple-element.101.own_ref.snake_ref, bf16[512,384]{1,0:T(8,128)(2,1)S(1)} %collective-permute-done.2.partner_ref.snake_ref, ...), custom_call_target="tpu_custom_call" | custom-call | flops 9059696640 | bytes 37355520 | tf_op jit(solution)/shard_map/weight/pallas_call | solution.py:360
  26.2 2.1 %collective-permute-start.9 = (bf16[192,1152]{1,0:T(8,128)(2,1)S(1)}, bf16[192,1152]{1,0:T(8,128)(2,1)S(1)}, u32[]{:S(2)}, u32[]{:S(2)}) collective-permute-start(bf16[192,1152]{1,0:T(8,128)(2,1)S(1)} %get-tuple-element.93), channel_id=1, source_target_pairs={{0,4},{4,0},{8,12},{12,8},{1,5},{5,1},{9,13},{13,9},{2,6},{6,2},{1... | collective-permute-start | bytes 1327112 | tf_op jit(solution)/shard_map/ppermute | solution.py:375
  28.3 2.5 %collective-permute-start.10 = (bf16[192,1152]{1,0:T(8,128)(2,1)S(1)}, bf16[192,1152]{1,0:T(8,128)(2,1)S(1)}, u32[]{:S(2)}, u32[]{:S(2)}) collective-permute-start(bf16[192,1152]{1,0:T(8,128)(2,1)S(1)} %get-tuple-element.111), channel_id=1, source_target_pairs={{0,12},{4,8},{8,4},{12,0},{1,13},{5,9},{9,5},{13,1},{2,14},{6,10},... | collective-permute-start | bytes 1327112 | tf_op jit(solution)/shard_map/ppermute | solution.py:375
  30.8 2.0 %back_own.4.own_ref = f32[512,384]{1,0:T(8,128)S(1)} custom-call(bf16[512,1152]{1,0:T(8,128)(2,1)S(1)} %get-tuple-element.94.shifted_ref, bf16[3,3,768,384]{3,2,1,0:T(8,128)(2,1)} %weight_hbm.23), custom_call_target="tpu_custom_call" | custom-call | flops 4529848320 | bytes 19660800 | tf_op jit(solution)/shard_map/back_own/pallas_call | solution.py:360
  32.8 1.7 %combine.4 = (f32[1,384]{1,0:T(1,128)S(1)}, bf16[512,384]{1,0:T(8,128)(2,1)S(1)}) custom-call(f32[512,384]{1,0:T(8,128)S(1)} %back_own.4.own_ref, bf16[512,384]{1,0:T(8,128)(2,1)S(1)} %collective-permute-done.4.partner_ref, f32[512,384]{1,0:T(8,128)S(1)} %get-tuple-element.79.old_ref.stream_ref, f32[3,384]{1,0:T(4,128)S(1)} %get-tuple-element.77.rest_0_.alphas_ref, ...), custom_call_target="tpu_custom_call" | custom-call | flops 117964800 | bytes 34140160 | tf_op jit(solution)/shard_map/combine/pallas_call | solution.py:360
  34.5 1.6 %collective-permute-start.11 = (bf16[512,384]{1,0:T(8,128)(2,1)S(1)}, bf16[512,384]{1,0:T(8,128)(2,1)S(1)}, u32[]{:S(2)}, u32[]{:S(2)}) collective-permute-start(bf16[512,384]{1,0:T(8,128)(2,1)S(1)} %get-tuple-element.99.grad_ref), channel_id=1, source_target_pairs={{0,2},{2,0},{1,3},{3,1},{4,6},{6,4},{5,7},{7,5},{8,10},{10,8},{9,1... | collective-permute-start | bytes 1179656 | tf_op jit(solution)/shard_map/ppermute | solution.py:375
  36.0 2.0 %back_partner.5 = (bf16[512,1152]{1,0:T(8,128)(2,1)S(1)}, bf16[512,384]{1,0:T(8,128)(2,1)S(1)}) custom-call(bf16[512,384]{1,0:T(8,128)(2,1)S(1)} %get-tuple-element.99.grad_ref, bf16[3,3,768,384]{3,2,1,0:T(8,128)(2,1)} %weight_hbm.23), custom_call_target="tpu_custom_call" | custom-call | flops 4529848320 | bytes 19660800 | tf_op jit(solution)/shard_map/back_partner/pallas_call | solution.py:360
  38.0 2.0 %forward_own.5.own_ref = f32[512,384]{1,0:T(8,128)S(1)} custom-call(bf16[512,384]{1,0:T(8,128)(2,1)S(1)} %get-tuple-element.101.own_ref.snake_ref, bf16[3,3,768,384]{3,2,1,0:T(8,128)(2,1)} %weight_hbm.23), custom_call_target="tpu_custom_call" | custom-call | flops 4529848320 | bytes 11796480 | tf_op jit(solution)/shard_map/forward_own/pallas_call | solution.py:360
  40.1 2.0 %back_own.5.own_ref = f32[512,384]{1,0:T(8,128)S(1)} custom-call(bf16[512,1152]{1,0:T(8,128)(2,1)S(1)} %get-tuple-element.102.shifted_ref, bf16[3,3,768,384]{3,2,1,0:T(8,128)(2,1)} %weight_hbm.23), custom_call_target="tpu_custom_call" | custom-call | flops 4529848320 | bytes 19660800 | tf_op jit(solution)/shard_map/back_own/pallas_call | solution.py:360
  42.7 1.4 %combine.5 = f32[1,384]{1,0:T(1,128)S(1)} custom-call(f32[512,384]{1,0:T(8,128)S(1)} %back_own.5.own_ref, bf16[512,384]{1,0:T(8,128)(2,1)S(1)} %collective-permute-done.5.partner_ref, f32[512,384]{1,0:T(8,128)S(1)} %get-tuple-element.71.old_ref.stream_ref, f32[3,384]{1,0:T(4,128)S(1)} %get-tuple-element.77.rest_0_.alphas_ref), custom_call_target="tpu_custom_call" | custom-call | flops 117964800 | bytes 19722240 | tf_op jit(solution)/shard_map/combine/pallas_call | solution.py:360
  44.1 2.8 %forward_partner.5 = bf16[512,384]{1,0:T(8,128)(2,1)} custom-call(bf16[512,384]{1,0:T(8,128)(2,1)S(1)} %collective-permute-done.2.partner_ref.snake_ref, bf16[3,3,768,384]{3,2,1,0:T(8,128)(2,1)} %weight_hbm.23, f32[512,384]{1,0:T(8,128)S(1)} %forward_own.5.own_ref, f32[512,384]{1,0:T(8,128)S(1)} %get-tuple-element.85.stream_ref.old_ref, ...), custom_call_target="tpu_custom_call" | custom-call | flops 4529848320 | bytes 26214400 | tf_op jit(solution)/shard_map/forward_partner/pallas_call | solution.py:360
  46.9 1.6 %paired_weight.2 = (bf16[96,1152]{1,0:T(8,128)(2,1)S(1)}, bf16[96,1152]{1,0:T(8,128)(2,1)S(1)}, bf16[96,1152]{1,0:T(8,128)(2,1)S(1)}, bf16[96,1152]{1,0:T(8,128)(2,1)S(1)}) custom-call(bf16[512,384]{1,0:T(8,128)(2,1)S(1)} %get-tuple-element.106.refs_1_.snake_ref.own_ref, bf16[512,384]{1,0:T(8,128)(2,1)S(1)} %collective-permute-done.1.snake_ref.partner_ref, ...), custom_call_target="tpu_custom_call" | custom-call | flops 9059696640 | bytes 40304640 | tf_op jit(solution)/shard_map/paired_weight/pallas_call | solution.py:360
  50.7 2.5 %collective-permute-start.12 = (bf16[96,1152]{1,0:T(8,128)(2,1)S(1)}, bf16[96,1152]{1,0:T(8,128)(2,1)S(1)}, u32[]{:S(2)}, u32[]{:S(2)}) collective-permute-start(bf16[96,1152]{1,0:T(8,128)(2,1)S(1)} %get-tuple-element.112), channel_id=1, source_target_pairs={{0,12},{4,8},{8,4},{12,0},{1,13},{5,9},{9,5},{13,1},{2,14},{6,10},... | collective-permute-start | bytes 663560 | tf_op jit(solution)/shard_map/ppermute | solution.py:375
  53.2 1.5 %paired_weight.3 = (bf16[96,1152]{1,0:T(8,128)(2,1)S(1)}, bf16[96,1152]{1,0:T(8,128)(2,1)S(1)}, bf16[96,1152]{1,0:T(8,128)(2,1)S(1)}, bf16[96,1152]{1,0:T(8,128)(2,1)S(1)}) custom-call(bf16[512,384]{1,0:T(8,128)(2,1)S(1)} %get-tuple-element.113.snake_ref.refs_0_.own_ref, bf16[512,384]{1,0:T(8,128)(2,1)S(1)} %collective-permute-done.snake_ref.partner_ref, ...), custom_call_target="tpu_custom_call" | custom-call | flops 9059696640 | bytes 40304640 | tf_op jit(solution)/shard_map/paired_weight/pallas_call | solution.py:360
  54.8 1.5 %collective-permute-start.17 = (bf16[96,1152]{1,0:T(8,128)(2,1)S(1)}, bf16[96,1152]{1,0:T(8,128)(2,1)S(1)}, u32[]{:S(2)}, u32[]{:S(2)}) collective-permute-start(bf16[96,1152]{1,0:T(8,128)(2,1)S(1)} %get-tuple-element.125), channel_id=1, source_target_pairs={{0,12},{4,8},{8,4},{12,0},{1,13},{5,9},{9,5},{13,1},{2,14},{6,10},... | collective-permute-start | bytes 663560 | tf_op jit(solution)/shard_map/ppermute | solution.py:375
  56.3 18.3 %collective-permute-done.13.late_b = bf16[96,1152]{1,0:T(8,128)(2,1)S(1)} collective-permute-done((bf16[96,1152]{1,0:T(8,128)(2,1)S(1)}, bf16[96,1152]{1,0:T(8,128)(2,1)S(1)}, u32[]{:S(2)}, u32[]{:S(2)}) %collective-permute-start.13) | collective-permute-done | bytes 221216 | tf_op jit(solution)/shard_map/ppermute | solution.py:375
  74.8 2.1 %collective-permute-start.24 = (bf16[192,1152]{1,0:T(8,128)(2,1)S(1)}, bf16[192,1152]{1,0:T(8,128)(2,1)S(1)}, u32[]{:S(2)}, u32[]{:S(2)}) collective-permute-start(bf16[192,1152]{1,0:T(8,128)(2,1)S(1)} %total.3.refs_4_), channel_id=1, source_target_pairs={{0,2},{2,0},{1,3},{3,1},{4,6},{6,4},{5,7},{7,5},{8,10},{10,8},{9,1... | collective-permute-start | bytes 1327112 | tf_op jit(solution)/shard_map/ppermute | solution.py:375
  77.0 7.9 %collective-permute-start.19 = (bf16[48,1152]{1,0:T(8,128)(2,1)S(1)}, bf16[48,1152]{1,0:T(8,128)(2,1)S(1)}, u32[]{:S(2)}, u32[]{:S(2)}) collective-permute-start(bf16[48,1152]{1,0:T(8,128)(2,1)S(1)} %get-tuple-element.128), channel_id=1, source_target_pairs={{0,4},{4,0},{8,12},{12,8},{1,5},{5,1},{9,13},{13,9},{2,6},{6,2},{1... | collective-permute-start | bytes 331784 | tf_op jit(solution)/shard_map/ppermute | solution.py:375
  86.5 2.0 %collective-permute-done.19.late_b = bf16[48,1152]{1,0:T(8,128)(2,1)S(1)} collective-permute-done((bf16[48,1152]{1,0:T(8,128)(2,1)S(1)}, bf16[48,1152]{1,0:T(8,128)(2,1)S(1)}, u32[]{:S(2)}, u32[]{:S(2)}) %collective-permute-start.19) | collective-permute-done | bytes 110624 | tf_op jit(solution)/shard_map/ppermute | solution.py:375
  90.3 1.4 %collective-permute-done.20.late_a = bf16[48,1152]{1,0:T(8,128)(2,1)S(1)} collective-permute-done((bf16[48,1152]{1,0:T(8,128)(2,1)S(1)}, bf16[48,1152]{1,0:T(8,128)(2,1)S(1)}, u32[]{:S(2)}, u32[]{:S(2)}) %collective-permute-start.20) | collective-permute-done | bytes 110624 | tf_op jit(solution)/shard_map/ppermute | solution.py:375
  93.2 3.8 %collective-permute-done.27 = f32[3,384]{1,0:T(4,128)S(1)} collective-permute-done((f32[3,384]{1,0:T(4,128)S(1)}, f32[3,384]{1,0:T(4,128)S(1)}, u32[]{:S(2)}, u32[]{:S(2)}) %collective-permute-start.27) | collective-permute-done | bytes 4640 | tf_op jit(solution)/shard_map/ppermute | solution.py:375
  98.1 1.7 %finish.1 = f32[3,3,192,384]{3,2,1,0:T(8,128)} custom-call(bf16[96,1152]{1,0:T(8,128)(2,1)S(1)} %total.5.refs_0_, bf16[96,1152]{1,0:T(8,128)(2,1)S(1)} %collective-permute-done.22.refs_1_, bf16[96,1152]{1,0:T(8,128)(2,1)S(1)} %total.4.refs_2_, bf16[96,1152]{1,0:T(8,128)(2,1)S(1)} %collective-permute-done.23.refs_3_, bf16[192,1152]{1,0:T(8,128)(2,1)S(1)} %total.3.refs_4_, ...), custom_call_target="tpu_custom_call" | custom-call | flops 6635520 | bytes 44236800 | tf_op jit(solution)/shard_map/finish/pallas_call | solution.py:360
  (55 shorter events, 10.9 us)
Async XLA Ops:
  2.7 4.6 %collective-permute-start = (bf16[512,384]{1,0:T(8,128)(2,1)S(1)}, bf16[512,384]{1,0:T(8,128)(2,1)S(1)}, u32[]{:S(2)}, u32[]{:S(2)}) collective-permute-start(bf16[512,384]{1,0:T(8,128)(2,1)S(1)} %get-tuple-element.113.snake_ref.refs_0_.own_ref), channel_id=1, source_target_pairs={{0,1},{1,0},{2,3},{3,2},{4,5},{5,4},{6,7},{7,6},{8,9},{9,8},{10,11... | collective-permute-start | bytes 1179656 | tf_op jit(solution)/shard_map/ppermute | solution.py:375
  5.2 15.1 %collective-permute-start.3 = (bf16[512,384]{1,0:T(8,128)(2,1)S(1)}, bf16[512,384]{1,0:T(8,128)(2,1)S(1)}, u32[]{:S(2)}, u32[]{:S(2)}) collective-permute-start(bf16[512,384]{1,0:T(8,128)(2,1)S(1)} %get-tuple-element.87), channel_id=1, source_target_pairs={{0,1},{1,0},{2,3},{3,2},{4,5},{5,4},{6,7},{7,6},{8,9},{9,8},{10,11... | collective-permute-start | bytes 1179656 | tf_op jit(solution)/shard_map/ppermute | solution.py:375
  10.5 29.5 %collective-permute-start.6 = (bf16[384,512]{1,0:T(8,128)(2,1)S(1)}, bf16[384,512]{1,0:T(8,128)(2,1)S(1)}, u32[]{:S(2)}, u32[]{:S(2)}) collective-permute-start(bf16[384,512]{1,0:T(8,128)(2,1)S(1)} %turn.1), channel_id=1, source_target_pairs={{0,2},{2,0},{1,3},{3,1},{4,6},{6,4},{5,7},{7,5},{8,10},{10,8},{9,1... | collective-permute-start | bytes 1179656 | tf_op jit(solution)/shard_map/ppermute | solution.py:375
  13.5 4.0 %collective-permute-start.1 = (bf16[512,384]{1,0:T(8,128)(2,1)S(1)}, bf16[512,384]{1,0:T(8,128)(2,1)S(1)}, u32[]{:S(2)}, u32[]{:S(2)}) collective-permute-start(bf16[512,384]{1,0:T(8,128)(2,1)S(1)} %get-tuple-element.106.refs_1_.snake_ref.own_ref), channel_id=1, source_target_pairs={{0,1},{1,0},{2,3},{3,2},{4,5},{5,4},{6,7},{7,6},{8,9},{9,8},{10,11... | collective-permute-start | bytes 1179656 | tf_op jit(solution)/shard_map/ppermute | solution.py:375
  22.0 24.9 %collective-permute-start.8 = (bf16[512,384]{1,0:T(8,128)(2,1)S(1)}, bf16[512,384]{1,0:T(8,128)(2,1)S(1)}, u32[]{:S(2)}, u32[]{:S(2)}) collective-permute-start(bf16[512,384]{1,0:T(8,128)(2,1)S(1)} %get-tuple-element.90.grad_ref), channel_id=1, source_target_pairs={{0,2},{2,0},{1,3},{3,1},{4,6},{6,4},{5,7},{7,5},{8,10},{10,8},{9,1... | collective-permute-start | bytes 1179656 | tf_op jit(solution)/shard_map/ppermute | solution.py:375
  22.1 2.6 %collective-permute-start.2 = (bf16[512,384]{1,0:T(8,128)(2,1)S(1)}, bf16[512,384]{1,0:T(8,128)(2,1)S(1)}, u32[]{:S(2)}, u32[]{:S(2)}) collective-permute-start(bf16[512,384]{1,0:T(8,128)(2,1)S(1)} %get-tuple-element.101.own_ref.snake_ref), channel_id=1, source_target_pairs={{0,1},{1,0},{2,3},{3,2},{4,5},{5,4},{6,7},{7,6},{8,9},{9,8},{10,11... | collective-permute-start | bytes 1179656 | tf_op jit(solution)/shard_map/ppermute | solution.py:375
  24.6 8.1 %collective-permute-start.4 = (bf16[512,384]{1,0:T(8,128)(2,1)S(1)}, bf16[512,384]{1,0:T(8,128)(2,1)S(1)}, u32[]{:S(2)}, u32[]{:S(2)}) collective-permute-start(bf16[512,384]{1,0:T(8,128)(2,1)S(1)} %get-tuple-element.95), channel_id=1, source_target_pairs={{0,1},{1,0},{2,3},{3,2},{4,5},{5,4},{6,7},{7,6},{8,9},{9,8},{10,11... | collective-permute-start | bytes 1179656 | tf_op jit(solution)/shard_map/ppermute | solution.py:375
  26.2 24.4 %collective-permute-start.9 = (bf16[192,1152]{1,0:T(8,128)(2,1)S(1)}, bf16[192,1152]{1,0:T(8,128)(2,1)S(1)}, u32[]{:S(2)}, u32[]{:S(2)}) collective-permute-start(bf16[192,1152]{1,0:T(8,128)(2,1)S(1)} %get-tuple-element.93), channel_id=1, source_target_pairs={{0,4},{4,0},{8,12},{12,8},{1,5},{5,1},{9,13},{13,9},{2,6},{6,2},{1... | collective-permute-start | bytes 1327112 | tf_op jit(solution)/shard_map/ppermute | solution.py:375
  28.3 22.3 %collective-permute-start.10 = (bf16[192,1152]{1,0:T(8,128)(2,1)S(1)}, bf16[192,1152]{1,0:T(8,128)(2,1)S(1)}, u32[]{:S(2)}, u32[]{:S(2)}) collective-permute-start(bf16[192,1152]{1,0:T(8,128)(2,1)S(1)} %get-tuple-element.111), channel_id=1, source_target_pairs={{0,12},{4,8},{8,4},{12,0},{1,13},{5,9},{9,5},{13,1},{2,14},{6,10},... | collective-permute-start | bytes 1327112 | tf_op jit(solution)/shard_map/ppermute | solution.py:375
  34.5 18.7 %collective-permute-start.11 = (bf16[512,384]{1,0:T(8,128)(2,1)S(1)}, bf16[512,384]{1,0:T(8,128)(2,1)S(1)}, u32[]{:S(2)}, u32[]{:S(2)}) collective-permute-start(bf16[512,384]{1,0:T(8,128)(2,1)S(1)} %get-tuple-element.99.grad_ref), channel_id=1, source_target_pairs={{0,2},{2,0},{1,3},{3,1},{4,6},{6,4},{5,7},{7,5},{8,10},{10,8},{9,1... | collective-permute-start | bytes 1179656 | tf_op jit(solution)/shard_map/ppermute | solution.py:375
  40.0 2.1 %collective-permute-start.5 = (bf16[512,384]{1,0:T(8,128)(2,1)S(1)}, bf16[512,384]{1,0:T(8,128)(2,1)S(1)}, u32[]{:S(2)}, u32[]{:S(2)}) collective-permute-start(bf16[512,384]{1,0:T(8,128)(2,1)S(1)} %get-tuple-element.103), channel_id=1, source_target_pairs={{0,1},{1,0},{2,3},{3,2},{4,5},{5,4},{6,7},{7,6},{8,9},{9,8},{10,11... | collective-permute-start | bytes 1179656 | tf_op jit(solution)/shard_map/ppermute | solution.py:375
  42.1 4.8 %collective-permute-start.7 = (bf16[384,512]{1,0:T(8,128)(2,1)S(1)}, bf16[384,512]{1,0:T(8,128)(2,1)S(1)}, u32[]{:S(2)}, u32[]{:S(2)}) collective-permute-start(bf16[384,512]{1,0:T(8,128)(2,1)S(1)} %collective-permute-done.6.across_ref), channel_id=1, source_target_pairs={{0,1},{1,0},{2,3},{3,2},{4,5},{5,4},{6,7},{7,6},{8,9},{9,8},{10,11... | collective-permute-start | bytes 1179656 | tf_op jit(solution)/shard_map/ppermute | solution.py:375
  48.5 28.4 %collective-permute-start.14 = (bf16[96,1152]{1,0:T(8,128)(2,1)S(1)}, bf16[96,1152]{1,0:T(8,128)(2,1)S(1)}, u32[]{:S(2)}, u32[]{:S(2)}) collective-permute-start(bf16[96,1152]{1,0:T(8,128)(2,1)S(1)} %get-tuple-element.108), channel_id=1, source_target_pairs={{0,4},{4,0},{8,12},{12,8},{1,5},{5,1},{9,13},{13,9},{2,6},{6,2},{1... | collective-permute-start | bytes 663560 | tf_op jit(solution)/shard_map/ppermute | solution.py:375
  49.2 25.6 %collective-permute-start.15 = (bf16[96,1152]{1,0:T(8,128)(2,1)S(1)}, bf16[96,1152]{1,0:T(8,128)(2,1)S(1)}, u32[]{:S(2)}, u32[]{:S(2)}) collective-permute-start(bf16[96,1152]{1,0:T(8,128)(2,1)S(1)} %get-tuple-element.121), channel_id=1, source_target_pairs={{0,12},{4,8},{8,4},{12,0},{1,13},{5,9},{9,5},{13,1},{2,14},{6,10},... | collective-permute-start | bytes 663560 | tf_op jit(solution)/shard_map/ppermute | solution.py:375
  50.7 23.8 %collective-permute-start.12 = (bf16[96,1152]{1,0:T(8,128)(2,1)S(1)}, bf16[96,1152]{1,0:T(8,128)(2,1)S(1)}, u32[]{:S(2)}, u32[]{:S(2)}) collective-permute-start(bf16[96,1152]{1,0:T(8,128)(2,1)S(1)} %get-tuple-element.112), channel_id=1, source_target_pairs={{0,12},{4,8},{8,4},{12,0},{1,13},{5,9},{9,5},{13,1},{2,14},{6,10},... | collective-permute-start | bytes 663560 | tf_op jit(solution)/shard_map/ppermute | solution.py:375
  53.2 21.3 %collective-permute-start.13 = (bf16[96,1152]{1,0:T(8,128)(2,1)S(1)}, bf16[96,1152]{1,0:T(8,128)(2,1)S(1)}, u32[]{:S(2)}, u32[]{:S(2)}) collective-permute-start(bf16[96,1152]{1,0:T(8,128)(2,1)S(1)} %get-tuple-element.118), channel_id=1, source_target_pairs={{0,4},{4,0},{8,12},{12,8},{1,5},{5,1},{9,13},{13,9},{2,6},{6,2},{1... | collective-permute-start | bytes 663560 | tf_op jit(solution)/shard_map/ppermute | solution.py:375
  54.8 22.3 %collective-permute-start.17 = (bf16[96,1152]{1,0:T(8,128)(2,1)S(1)}, bf16[96,1152]{1,0:T(8,128)(2,1)S(1)}, u32[]{:S(2)}, u32[]{:S(2)}) collective-permute-start(bf16[96,1152]{1,0:T(8,128)(2,1)S(1)} %get-tuple-element.125), channel_id=1, source_target_pairs={{0,12},{4,8},{8,4},{12,0},{1,13},{5,9},{9,5},{13,1},{2,14},{6,10},... | collective-permute-start | bytes 663560 | tf_op jit(solution)/shard_map/ppermute | solution.py:375
  74.5 10.4 %collective-permute-start.16 = (bf16[96,1152]{1,0:T(8,128)(2,1)S(1)}, bf16[96,1152]{1,0:T(8,128)(2,1)S(1)}, u32[]{:S(2)}, u32[]{:S(2)}) collective-permute-start(bf16[96,1152]{1,0:T(8,128)(2,1)S(1)} %get-tuple-element.116), channel_id=1, source_target_pairs={{0,4},{4,0},{8,12},{12,8},{1,5},{5,1},{9,13},{13,9},{2,6},{6,2},{1... | collective-permute-start | bytes 663560 | tf_op jit(solution)/shard_map/ppermute | solution.py:375
  74.6 10.5 %collective-permute-start.25 = (f32[3,384]{1,0:T(4,128)S(1)}, f32[3,384]{1,0:T(4,128)S(1)}, u32[]{:S(2)}, u32[]{:S(2)}) collective-permute-start(f32[3,384]{1,0:T(4,128)S(1)} %pad_maximum_fusion), channel_id=1, source_target_pairs={{0,2},{2,0},{1,3},{3,1},{4,6},{6,4},{5,7},{7,5},{8,10},{10,8},{9,1... | collective-permute-start | bytes 13832 | tf_op jit(solution)/shard_map/ppermute | solution.py:375
  74.8 23.3 %collective-permute-start.24 = (bf16[192,1152]{1,0:T(8,128)(2,1)S(1)}, bf16[192,1152]{1,0:T(8,128)(2,1)S(1)}, u32[]{:S(2)}, u32[]{:S(2)}) collective-permute-start(bf16[192,1152]{1,0:T(8,128)(2,1)S(1)} %total.3.refs_4_), channel_id=1, source_target_pairs={{0,2},{2,0},{1,3},{3,1},{4,6},{6,4},{5,7},{7,5},{8,10},{10,8},{9,1... | collective-permute-start | bytes 1327112 | tf_op jit(solution)/shard_map/ppermute | solution.py:375
  77.0 12.7 %collective-permute-start.18 = (bf16[48,1152]{1,0:T(8,128)(2,1)S(1)}, bf16[48,1152]{1,0:T(8,128)(2,1)S(1)}, u32[]{:S(2)}, u32[]{:S(2)}) collective-permute-start(bf16[48,1152]{1,0:T(8,128)(2,1)S(1)} %get-tuple-element.122), channel_id=1, source_target_pairs={{0,12},{4,8},{8,4},{12,0},{1,13},{5,9},{9,5},{13,1},{2,14},{6,10},... | collective-permute-start | bytes 331784 | tf_op jit(solution)/shard_map/ppermute | solution.py:375
  77.0 11.4 %collective-permute-start.19 = (bf16[48,1152]{1,0:T(8,128)(2,1)S(1)}, bf16[48,1152]{1,0:T(8,128)(2,1)S(1)}, u32[]{:S(2)}, u32[]{:S(2)}) collective-permute-start(bf16[48,1152]{1,0:T(8,128)(2,1)S(1)} %get-tuple-element.128), channel_id=1, source_target_pairs={{0,4},{4,0},{8,12},{12,8},{1,5},{5,1},{9,13},{13,9},{2,6},{6,2},{1... | collective-permute-start | bytes 331784 | tf_op jit(solution)/shard_map/ppermute | solution.py:375
  85.0 5.4 %collective-permute-start.21 = (bf16[48,1152]{1,0:T(8,128)(2,1)S(1)}, bf16[48,1152]{1,0:T(8,128)(2,1)S(1)}, u32[]{:S(2)}, u32[]{:S(2)}) collective-permute-start(bf16[48,1152]{1,0:T(8,128)(2,1)S(1)} %get-tuple-element.130), channel_id=1, source_target_pairs={{0,4},{4,0},{8,12},{12,8},{1,5},{5,1},{9,13},{13,9},{2,6},{6,2},{1... | collective-permute-start | bytes 331784 | tf_op jit(solution)/shard_map/ppermute | solution.py:375
  85.1 6.7 %collective-permute-start.20 = (bf16[48,1152]{1,0:T(8,128)(2,1)S(1)}, bf16[48,1152]{1,0:T(8,128)(2,1)S(1)}, u32[]{:S(2)}, u32[]{:S(2)}) collective-permute-start(bf16[48,1152]{1,0:T(8,128)(2,1)S(1)} %get-tuple-element.126), channel_id=1, source_target_pairs={{0,12},{4,8},{8,4},{12,0},{1,13},{5,9},{9,5},{13,1},{2,14},{6,10},... | collective-permute-start | bytes 331784 | tf_op jit(solution)/shard_map/ppermute | solution.py:375
  88.5 4.0 %collective-permute-start.26 = (f32[3,384]{1,0:T(4,128)S(1)}, f32[3,384]{1,0:T(4,128)S(1)}, u32[]{:S(2)}, u32[]{:S(2)}) collective-permute-start(f32[3,384]{1,0:T(4,128)S(1)} %fusion), channel_id=1, source_target_pairs={{0,4},{4,0},{8,12},{12,8},{1,5},{5,1},{9,13},{13,9},{2,6},{6,2},{1... | collective-permute-start | bytes 13832 | tf_op jit(solution)/shard_map/ppermute | solution.py:375
  89.7 8.4 %collective-permute-start.23 = (bf16[96,1152]{1,0:T(8,128)(2,1)S(1)}, bf16[96,1152]{1,0:T(8,128)(2,1)S(1)}, u32[]{:S(2)}, u32[]{:S(2)}) collective-permute-start(bf16[96,1152]{1,0:T(8,128)(2,1)S(1)} %total.4.refs_2_), channel_id=1, source_target_pairs={{0,2},{2,0},{1,3},{3,1},{4,6},{6,4},{5,7},{7,5},{8,10},{10,8},{9,1... | collective-permute-start | bytes 663560 | tf_op jit(solution)/shard_map/ppermute | solution.py:375
  91.9 6.3 %collective-permute-start.22 = (bf16[96,1152]{1,0:T(8,128)(2,1)S(1)}, bf16[96,1152]{1,0:T(8,128)(2,1)S(1)}, u32[]{:S(2)}, u32[]{:S(2)}) collective-permute-start(bf16[96,1152]{1,0:T(8,128)(2,1)S(1)} %total.5.refs_0_), channel_id=1, source_target_pairs={{0,2},{2,0},{1,3},{3,1},{4,6},{6,4},{5,7},{7,5},{8,10},{10,8},{9,1... | collective-permute-start | bytes 663560 | tf_op jit(solution)/shard_map/ppermute | solution.py:375
  92.5 4.6 %collective-permute-start.27 = (f32[3,384]{1,0:T(4,128)S(1)}, f32[3,384]{1,0:T(4,128)S(1)}, u32[]{:S(2)}, u32[]{:S(2)}) collective-permute-start(f32[3,384]{1,0:T(4,128)S(1)} %fusion.1), channel_id=1, source_target_pairs={{0,8},{4,12},{8,0},{12,4},{1,9},{5,13},{9,1},{13,5},{2,10},{6,14},... | collective-permute-start | bytes 13832 | tf_op jit(solution)/shard_map/ppermute | solution.py:375

commit v4 on v3

v4 whole, which is shorter than its diff:
```python
import functools
import math

import jax
import jax.numpy as jnp
from jax import lax
from jax.experimental import pallas as pl
from jax.experimental.pallas import tpu as pltpu
from jax.sharding import PartitionSpec as P

dilations = (1, 3, 5)
F32, BF16 = jnp.float32, jnp.bfloat16
ANY_HBM = pl.BlockSpec(memory_space=pltpu.HBM)
IN_VMEM = pl.BlockSpec(memory_space=pltpu.VMEM)
DMA = pltpu.SemaphoreType.DMA
PI_PARTS = (3.140625, 9.67502593994140625e-4, 1.509957990978376432e-7)
SIN_TERMS = (-1.0 / 39916800, 1.0 / 362880, -1.0 / 5040, 1.0 / 120, -1.0 / 6)
COS_TERMS = (1.0 / 479001600, -1.0 / 3628800, 1.0 / 40320, -1.0 / 720, 1.0 / 24, -0.5)
RANGE = 8192.0
CHUNK = 64


def horner(terms, x):
    total = jnp.full_like(x, terms[0])
    for term in terms[1:]:
        total = total * x + term
    return total


def reduced(angle):
    turns = jnp.round(angle * (1.0 / 3.14159265358979))
    for part in PI_PARTS:
        angle = angle - turns * part
    return angle


def sine(angle, exact_range):
    if not exact_range:
        return jnp.sin(angle)
    rest = reduced(angle)
    square = rest * rest
    return rest + rest * (square * horner(SIN_TERMS, square))


def sine_cosine(angle, exact_range):
    if not exact_range:
        return jnp.sin(angle), jnp.cos(angle)
    rest = reduced(angle)
    square = rest * rest
    return (
        rest + rest * (square * horner(SIN_TERMS, square)),
        1.0 + square * horner(COS_TERMS, square),
    )


def by_range(bound, body):
    @pl.when(bound < RANGE)
    def _():
        body(True)

    @pl.when(bound >= RANGE)
    def _():
        body(False)


def write_snake(stream_ref, alpha, out_ref):
    inverse = 1.0 / alpha
    bound = jnp.max(jnp.abs(stream_ref[...])) * jnp.max(alpha)

    def body(exact_range):
        @pl.loop(0, stream_ref.shape[0] // CHUNK)
        def _(step):
            rows = pl.ds(pl.multiple_of(step * CHUNK, CHUNK), CHUNK)
            stream = stream_ref[rows, :]
            wave = sine(alpha * stream, exact_range)
            out_ref[rows, :] = (stream + wave * wave * inverse).astype(BF16)

    by_range(bound, body)


def moved(values, offset):
    if offset == 0:
        return values
    rows = values.shape[0]
    place = lax.broadcasted_iota(jnp.int32, values.shape, 0)
    turned = pltpu.roll(values, (-offset) % rows, 0)
    inside = place < rows - offset if offset > 0 else place >= -offset
    return jnp.where(inside, turned, 0.0)


def write_shifts(values_ref, out_ref, dilation):
    width = values_ref.shape[1]
    values = values_ref[...].astype(F32)
    for tap in range(3):
        out_ref[:, tap * width : (tap + 1) * width] = moved(values, (tap - 1) * dilation).astype(BF16)


def chan_begin(side, half):
    chan = lax.axis_index("chan")
    return pl.multiple_of((chan if side == 0 else 1 - chan) * half, half)


def prep_kernel(
    len_hbm, own_hbm, start_hbm, act_hbm, cot_hbm, alpha_hbm, weight_hbm,
    stream_ref, snake_ref, grad_ref, live_ref, alpha_ref, weight_ref,
    len_ref, own_ref, start_ref, act_ref, cot_ref, sems, weight_sems,
):
    pairs = (
        (len_hbm, len_ref), (own_hbm, own_ref), (start_hbm, start_ref),
        (alpha_hbm, alpha_ref), (act_hbm, act_ref), (cot_hbm, cot_ref),
    )
    copies = [pltpu.make_async_copy(a, b, sems.at[i]) for i, (a, b) in enumerate(pairs)]
    layers, taps, _, half = weight_hbm.shape
    loads = []
    for layer in range(layers):
        for side in range(2):
            for tap in range(taps):
                source = weight_hbm.at[layer, tap, pl.ds(chan_begin(side, half), half), :]
                target = weight_ref.at[layer, side, pl.ds(tap * half, half), :]
                loads.append(pltpu.make_async_copy(source, target, weight_sems.at[len(loads)]))
    for copy in copies + loads:
        copy.start()
    replicas = lax.axis_size("replica")
    device = lax.axis_index("dp") * replicas + lax.axis_index("replica")
    rows, width = act_ref.shape
    place = lax.broadcasted_iota(jnp.int32, (rows, 128), 0)
    live_ref[...] = jnp.zeros((rows, 128), F32)
    for copy in copies[:3]:
        copy.wait()

    @pl.loop(0, len_ref.shape[0])
    def _(clip):
        @pl.when(own_ref[clip] == device)
        def _():
            first = start_ref[clip]
            inside = (place >= first) & (place < first + len_ref[clip])
            live_ref[...] = jnp.where(inside, 1.0, live_ref[...])

    live = jnp.tile(live_ref[...], (1, width // 128))
    for copy in copies[3:5]:
        copy.wait()
    stream_ref[...] = act_ref[...].astype(F32) * live
    write_snake(stream_ref, alpha_ref[0:1, :], snake_ref)
    copies[5].wait()
    grad_ref[...] = (cot_ref[...].astype(F32) * live).astype(BF16)
    for copy in loads:
        copy.wait()


def forward_own_kernel(layer, snake_ref, weight_ref, out_ref, shifts_ref):
    write_shifts(snake_ref, shifts_ref, dilations[layer])
    out_ref[...] = jnp.dot(shifts_ref[...], weight_ref[layer, 0], preferred_element_type=F32)


def forward_partner_kernel(layer, last, snake_ref, weight_ref, own_ref, old_ref, live_ref, *rest):
    if last:
        result_ref, shifts_ref = rest
    else:
        alpha_ref, result_ref, next_ref, shifts_ref = rest
    write_shifts(snake_ref, shifts_ref, dilations[layer])
    part = jnp.dot(shifts_ref[...], weight_ref[layer, 1], preferred_element_type=F32)
    live = jnp.tile(live_ref[...], (1, old_ref.shape[1] // 128))
    new = (old_ref[...] + (own_ref[...] + part)) * live
    result_ref[...] = new.astype(result_ref.dtype)
    if not last:
        write_snake(result_ref, alpha_ref[layer + 1 : layer + 2, :], next_ref)


def back_product(shifted_ref, weight_ref, layer, side):
    half = weight_ref.shape[3]
    total = None
    for tap in range(3):
        span = slice(tap * half, (tap + 1) * half)
        part = lax.dot_general(
            shifted_ref[:, span], weight_ref[layer, side, span, :], (((1,), (1,)), ((), ())),
            preferred_element_type=F32,
        )
        total = part if total is None else total + part
    return total


def back_partner_kernel(layer, grad_ref, weight_ref, shifted_ref, out_ref):
    write_shifts(grad_ref, shifted_ref, -dilations[layer])
    out_ref[...] = back_product(shifted_ref, weight_ref, layer, 1).astype(BF16)


def back_own_kernel(layer, shifted_ref, weight_ref, out_ref):
    out_ref[...] = back_product(shifted_ref, weight_ref, layer, 0)


def combine_kernel(layer, own_ref, partner_ref, stream_ref, alphas_ref, *rest):
    if layer == 0:
        (alpha_grad_ref,) = rest
    elif len(rest) == 5:
        old_ref, live_ref, alpha_grad_ref, grad_ref, rounded_ref = rest
    else:
        old_ref, live_ref, alpha_grad_ref, rounded_ref = rest
        grad_ref = None
    alpha = alphas_ref[layer : layer + 1, :]
    inverse = 1.0 / alpha
    bound = jnp.max(jnp.abs(stream_ref[...])) * jnp.max(alpha)
    width = stream_ref.shape[1]

    def body(exact_range):
        def step_body(step, total):
            rows = pl.ds(pl.multiple_of(step * CHUNK, CHUNK), CHUNK)
            stream = stream_ref[rows, :]
            back = own_ref[rows, :] + partner_ref[rows, :].astype(F32)
            sin, cos = sine_cosine(alpha * stream, exact_range)
            double = 2.0 * sin * cos
            ratio = sin * inverse
            term = back * (stream * double * inverse - ratio * ratio)
            if layer > 0:
                live = jnp.tile(live_ref[rows, :], (1, width // 128))
                grad = (old_ref[rows, :].astype(F32) + back * (1.0 + double)) * live
                if grad_ref is not None:
                    grad_ref[rows, :] = grad
                rounded_ref[rows, :] = grad.astype(BF16)
            return total + jnp.sum(term.reshape(CHUNK // 8, 8, width), axis=0)

        total = lax.fori_loop(0, stream_ref.shape[0] // CHUNK, step_body, jnp.zeros((8, width), F32))
        alpha_grad_ref[...] = jnp.sum(total, axis=0, keepdims=True)

    by_range(bound, body)


def block_place(pieces, slice_index, part):
    apart = jnp.bitwise_xor(slice_index, lax.axis_index("dp"))
    order = (2 * pieces, 0, 1, 2 * pieces + 1)
    return 2 * part + jnp.where(
        apart == 0, order[0], jnp.where(apart == 1, order[1], jnp.where(apart == 2, order[2], order[3]))
    )


def weight_kernel(own_ref, partner_ref, shifted_ref, out_ref, turned_ref):
    half = own_ref.shape[1]
    chan = lax.axis_index("chan")
    for ref, side in ((own_ref, chan), (partner_ref, 1 - chan)):
        turned_ref[pl.ds(pl.multiple_of(side * half, half), half), :] = ref[...].T
    for tap in range(3):
        span = slice(tap * half, (tap + 1) * half)
        out_ref[:, span] = jnp.dot(turned_ref[...], shifted_ref[:, span], preferred_element_type=F32).astype(BF16)


def place_rows(pieces, rows_of, side, target_ref, columns):
    size = rows_of.shape[0] // (2 * pieces)
    for local in range(2):
        for part in range(pieces):
            begin = pl.multiple_of(block_place(pieces, side * 2 + local, part) * size, size)
            low = (local * pieces + part) * size
            target_ref[pl.ds(begin, size), columns] = rows_of[low : low + size, :]


def pick_parts(turned_ref, part, size):
    begin = pl.multiple_of(part * size, size)
    return [turned_ref[pl.ds(local * 2 * size + begin, size), :] for local in range(2)]


def turn_kernel(snake_ref, out_ref, turned_ref):
    size = snake_ref.shape[1] // 4
    turned_ref[...] = snake_ref[...].T
    for local, piece in enumerate(pick_parts(turned_ref, 1 - lax.axis_index("replica"), size)):
        out_ref[local * size : (local + 1) * size, :] = piece


def paired_weight_kernel(
    layer, pieces, own_ref, partner_ref, shifted_ref, across_ref, across_other_ref, grad_ref, *rest
):
    outs, (turned_ref, half_ref, far_ref) = rest[:-3], rest[-3:]
    rows, half = own_ref.shape
    chan = lax.axis_index("chan")
    mine = lax.axis_index("replica")
    for ref, side in ((own_ref, chan), (partner_ref, 1 - chan)):
        half_ref[...] = ref[...].T
        both = jnp.concatenate(pick_parts(half_ref, mine, half // 4), 0)
        place_rows(pieces, both, side, turned_ref, slice(0, rows))
    for ref, side in ((across_ref, chan), (across_other_ref, 1 - chan)):
        place_rows(pieces, ref[...], side, turned_ref, slice(rows, 2 * rows))
    write_shifts(grad_ref, far_ref, -dilations[layer])
    for tap in range(3):
        span = slice(tap * half, (tap + 1) * half)
        product = jnp.dot(turned_ref[:, 0:rows], shifted_ref[:, span], preferred_element_type=F32)
        product += jnp.dot(turned_ref[:, rows:], far_ref[:, span], preferred_element_type=F32)
        product = product.astype(BF16)
        size = product.shape[0] // len(outs)
        for place, ref in enumerate(outs):
            ref[:, span] = product[place * size : (place + 1) * size, :]


def finish_kernel(paired, counts, *refs):
    out_ref, refs = refs[-1], list(refs[:-1])
    half = out_ref.shape[3]
    for layer, pieces in enumerate(counts):
        for part in range(pieces):
            mine_ref, other_ref = refs.pop(0), refs.pop(0)
            size = mine_ref.shape[0]
            for tap in range(3):
                span = slice(tap * half, (tap + 1) * half)
                mine, other = mine_ref[:, span].astype(F32), other_ref[:, span].astype(F32)
                if paired:
                    begin = lax.axis_index("replica") * (size * pieces)
                    for values, start in ((mine, begin), (other, size * pieces - begin)):
                        place = pl.multiple_of(start + part * size, size)
                        out_ref[layer, tap, pl.ds(place, size), :] = values
                else:
                    out_ref[layer, tap] = mine + other


def fold_kernel(keep, got, send):
    rows = send.shape[0]
    send[...] = (keep[rows:, :].astype(F32) + got[rows:, :].astype(F32)).astype(BF16)


def total_kernel(keep, got, late, out_ref):
    rows = late.shape[0]
    total = keep[0:rows, :].astype(F32) + got[0:rows, :].astype(F32) + late[...].astype(F32)
    out_ref[...] = total.astype(BF16)


def struct(shape, dtype):
    return jax.ShapeDtypeStruct(shape, dtype)


def after(value, other):
    return value if other is None else lax.optimization_barrier((value, other))[0]


class Sequence:
    def __init__(self):
        self.latest = None

    def hold(self, value):
        return after(value, self.latest)

    def call(self, kernel, name, ins, outs, scratch, flops, *args):
        single = not isinstance(outs, list)
        size = sum(a.size * a.dtype.itemsize for a in args if a.size < 2000000)
        size += sum(math.prod(o.shape) * o.dtype.itemsize for o in ([outs] if single else outs))
        args = [pltpu.with_memory_space_constraint(a, pltpu.HBM) if i else a for i, a in zip(ins, args)]
        if self.latest is not None:
            args[0] = self.hold(args[0])
        result = pl.pallas_call(
            kernel,
            in_specs=[ANY_HBM if i else IN_VMEM for i in ins],
            out_specs=IN_VMEM if single else [IN_VMEM] * len(outs),
            out_shape=outs,
            scratch_shapes=scratch,
            compiler_params=pltpu.CompilerParams(vmem_limit_bytes=24 * 1024 * 1024),
            cost_estimate=pl.CostEstimate(flops=int(flops) * 10, bytes_accessed=int(size) * 10, transcendentals=0),
            name=name,
        )(*args)
        self.latest = result if single else result[0]
        return result


def swap(x, axis, other):
    return lax.ppermute(x, axis, [(i, other(i)) for i in range(lax.axis_size(axis))])


def across_chan(x):
    return swap(x, "chan", lambda i: i ^ 1)


def across_replica(x):
    return swap(x, "replica", lambda i: i ^ 1)


def sum_rounds(values, axis, sequence):
    size = lax.axis_size(axis)
    if size & (size - 1):
        return lax.psum(values, axis)
    apart = 1
    while apart < size:
        values = values + swap(sequence.hold(values), axis, lambda i, apart=apart: i ^ apart)
        apart *= 2
    return values


def on_device(activations, cotangent, conv_weights, snake_alpha, seg_lengths, seg_owner, seg_start):
    rows, half = activations.shape
    layers, taps, channels, _ = conv_weights.shape
    top = layers - 1
    fast = lax.axis_size("dp") == 4 and lax.axis_size("replica") == 2
    counts = [2, 1, 1] if fast else [1, 1, 1]
    tile, triple = (rows, half), (rows, taps * half)
    flops = 2 * rows * half * half * taps
    sequence = Sequence()
    streams, mine, partners, owns = [], [], {}, {}
    rounded, shifted, arrived, back_owns, far = {}, {}, {}, {}, {}
    across, across_other = {}, {}
    alpha_parts = [None] * layers
    kept, got, late, summed, crossed = {}, {}, {}, {}, {}

    def forward_own(layer):
        owns[layer] = sequence.call(
            functools.partial(forward_own_kernel, layer), "forward_own", [0, 0], struct(tile, F32),
            [pltpu.VMEM(triple, BF16)], flops, mine[layer], weight,
        )

    def forward_partner(layer):
        last = layer == top
        result = sequence.call(
            functools.partial(forward_partner_kernel, layer, last), "forward_partner",
            [0, 0, 0, 0, 0] + ([] if last else [0]),
            struct(tile, BF16) if last else [struct(tile, F32), struct(tile, BF16)],
            [pltpu.VMEM(triple, BF16)], flops,
            partners[layer], weight, owns[layer], streams[layer], live, *([] if last else [alphas]),
        )
        if last:
            return result
        streams.append(result[0])
        mine.append(result[1])
        partners[layer + 1] = across_chan(result[1])

    def back_partner(layer):
        shifted[layer], part = sequence.call(
            functools.partial(back_partner_kernel, layer), "back_partner", [0, 0],
            [struct(triple, BF16), struct(tile, BF16)], [], flops, rounded[layer + 1], weight,
        )
        arrived[layer] = across_chan(part)

    def back_own(layer):
        back_owns[layer] = sequence.call(
            functools.partial(back_own_kernel, layer), "back_own", [0, 0], struct(tile, F32),
            [], flops, shifted[layer], weight,
        )

    def send_gradient(layer):
        if fast:
            far[layer] = across_replica(sequence.hold(rounded[layer + 1]))

    def combine(layer, grad):
        args = [back_owns[layer], arrived[layer], streams[layer], alphas]
        outs = [struct((1, half), F32)]
        if layer > 0:
            args += [grad, live]
            outs += [struct(tile, F32)] * (layer > 1) + [struct(tile, BF16)]
        result = sequence.call(
            functools.partial(combine_kernel, layer), "combine", [0] * len(args), outs, [], 60 * rows * half, *args
        )
        alpha_parts[layer] = result[0]
        if layer > 0:
            rounded[layer] = result[-1]
            return result[1]

    def turn(layer):
        if fast:
            across[layer] = across_replica(sequence.call(
                turn_kernel, "turn", [0], struct((half // 2, rows), BF16),
                [pltpu.VMEM((half, rows), BF16)], 10 * rows * half, mine[layer],
            ))

    def share(layer):
        if fast:
            across_other[layer] = across_chan(sequence.hold(across[layer]))

    def weights(layer):
        if not fast:
            out = sequence.call(
                weight_kernel, "weight", [0] * 3, struct((channels, taps * half), BF16),
                [pltpu.VMEM((channels, rows), BF16)], 2 * flops, mine[layer], partners[layer], shifted[layer],
            )
            part = lax.psum_scatter(out, "dp", scatter_dimension=0, tiled=True)
            summed[layer, 0] = lax.psum(part, "replica")
            crossed[layer, 0] = jnp.zeros_like(part)
            return
        pieces = counts[layer]
        piece = struct((channels // 4 // pieces, taps * half), BF16)
        out = sequence.call(
            functools.partial(paired_weight_kernel, layer, pieces), "paired_weight", [0] * 6,
            [piece] * (2 * pieces),
            [pltpu.VMEM((half, 2 * rows), BF16), pltpu.VMEM((half, rows), BF16), pltpu.VMEM(triple, BF16)],
            2 * flops, mine[layer], partners[layer], shifted[layer], across[layer], across_other[layer], far[layer],
        )
        for part in range(pieces):
            got[layer, part] = swap(out[part], "dp", lambda i: i ^ 1)
            kept[layer, part] = out[pieces + part]

    def fold(layer, part=0):
        if not fast:
            return
        keep, came = kept[layer, part], got[layer, part]
        send = sequence.call(
            fold_kernel, "fold", [0] * 2, struct((keep.shape[0] // 2, keep.shape[1]), BF16), [], keep.size, keep, came
        )
        late[layer, part] = swap(send, "dp", lambda i: i ^ 3)

    def total(layer, part=0):
        if not fast:
            return
        keep, came, last = kept[layer, part], got[layer, part], late[layer, part]
        summed[layer, part] = sequence.call(
            total_kernel, "total", [0] * 3, struct(last.shape, BF16), [], keep.size, keep, came, last
        )
        crossed[layer, part] = across_replica(summed[layer, part])

    stream, snaked, grad, live, alphas, weight = sequence.call(
        prep_kernel, "prep", [1] * 7,
        [struct(tile, F32), struct(tile, BF16), struct(tile, BF16), struct((rows, 128), F32),
         struct(snake_alpha.shape, F32), struct((layers, 2, taps * half, half), BF16)],
        [pltpu.SMEM(seg_lengths.shape, jnp.int32)] * 3 + [pltpu.VMEM(tile, BF16)] * 2 + [DMA((6,)), DMA((2 * layers * taps,))],
        40 * rows * half,
        seg_lengths, seg_owner, seg_start, activations, cotangent, snake_alpha, conv_weights,
    )
    streams.append(stream)
    mine.append(snaked)
    partners[0] = across_chan(snaked)
    rounded[layers] = grad
    send_gradient(2)
    back_partner(2)
    forward_own(0)
    forward_partner(0)
    back_own(2)
    forward_own(1)
    forward_partner(1)
    turn(2)
    grad = combine(2, grad)
    send_gradient(1)
    turn(1)
    back_partner(1)
    back_own(1)
    share(2)
    combine(1, grad)
    weights(2)
    back_partner(0)
    forward_own(2)
    back_own(0)
    share(1)
    combine(0, None)
    alpha_grads = sum_rounds(jnp.concatenate(alpha_parts), "replica", sequence)
    residual_out = forward_partner(2)
    weights(1)
    send_gradient(0)
    turn(0)
    fold(2)
    share(0)
    weights(0)
    total(2)
    alpha_grads = sum_rounds(alpha_grads, "dp", sequence)
    fold(1)
    for part in range(counts[0]):
        fold(0, part)
    total(1)
    for part in range(counts[0]):
        total(0, part)
    pairs = []
    for layer in range(layers):
        for part in range(counts[layer]):
            pairs += [summed[layer, part], crossed[layer, part]]
    depth = channels // lax.axis_size("dp")
    weight_grads = sequence.call(
        functools.partial(finish_kernel, fast, tuple(counts)), "finish", [0] * len(pairs),
        struct((layers, taps, depth, half), F32), [], layers * taps * depth * half, *pairs,
    )
    return (residual_out, weight_grads, alpha_grads)


def solution(mesh):
    return jax.shard_map(
        on_device,
        mesh=mesh,
        in_specs=(
            P(("groups", "dp", "replica"), "chan"),
            P(("groups", "dp", "replica"), "chan"),
            P(None, None, None, "chan"),
            P(None, "chan"),
            P("groups"),
            P("groups"),
            P("groups"),
        ),
        out_specs=(
            P(("groups", "dp", "replica"), "chan"),
            P("groups", None, "dp", "chan"),
            P("groups", "chan"),
        ),
        check_vma=False,
    )
```

time: 100 us -> 97.2 us (0.972)
  Pallas kernels: 40.3 us -> 28.6 us
  waiting for transfers between devices: 26.6 us -> 34 us
  starting transfers between devices: 31.4 us -> 32.9 us
    pallas_call x27 -> x31, Pallas kernels: 40.3 us -> 28.6 us  [call(): pl.pallas_call(kernel, in_specs=[ANY_HBM if i else IN_VMEM for i in ins],...]
    ppermute x28 -> x30, waiting for transfers between devices: 26.6 us -> 34 us  [swap(): lax.ppermute(x, axis, [(i, other(i)) for i in range(lax.axis_size(axis))])]
    ppermute x28 -> x30, starting transfers between devices: 31.4 us -> 32.9 us  [swap(): lax.ppermute(x, axis, [(i, other(i)) for i in range(lax.axis_size(axis))])]
  transfers between devices with their start and end apart: 28 -> 30, of which waited for: 6 -> 14; matrix products, arithmetic and copies ran while one was open for 1% -> 1% of each run, Pallas kernels for 37% -> 24%
where the time goes in v4:
time: 97.2 us; the launch traced here: 97.1 us
  waiting for transfers between devices  34 us (35%)
  starting transfers between devices  32.9 us (34%)
  Pallas kernels  28.6 us (29%)
    ppermute x30, waiting for transfers between devices, swap(): lax.ppermute(x, axis, [(i, other(i)) for i in range(lax.axis_size(axis))])  34 us
    ppermute x30, starting transfers between devices, swap(): lax.ppermute(x, axis, [(i, other(i)) for i in range(lax.axis_size(axis))])  32.9 us
    pallas_call x31, Pallas kernels, call(): pl.pallas_call(kernel, in_specs=[ANY_HBM if i else IN_VMEM for i in ins],...  28.6 us
  transfers between devices with their start and end apart: 30, of which 14 were waited for; matrix products, arithmetic and copies ran while one was open for 1% of the time, Pallas kernels for 24%

profile of v4, /device:TPU:0, one launch (start us, length us, event | category | flops | bytes accessed | tf_op | source)
XLA Modules:
  0.0 97.1 jit_solution(15363593359030428317)
XLA Ops:
  0.6 3.7 %prep.1 = (f32[512,384]{1,0:T(8,128)S(1)}, bf16[512,384]{1,0:T(8,128)(2,1)S(1)}, bf16[512,384]{1,0:T(8,128)(2,1)S(1)}, f32[512,128]{1,0:T(8,128)S(1)}, f32[3,384...) custom-call(s32[16]{0:T(128)} %len_hbm.1, s32[16]{0:T(128)} %own_hbm.1, s32[16]{0:T(128)} %start_hbm.1, ...), custom_call_target="tpu_custom_call" | custom-call | flops 78643200 | bytes 79392640 | tf_op jit(solution)/shard_map/prep/pallas_call | solution.py:342
  4.9 2.6 %collective-permute-start.7 = (bf16[512,384]{1,0:T(8,128)(2,1)S(1)}, bf16[512,384]{1,0:T(8,128)(2,1)S(1)}, u32[]{:S(2)}, u32[]{:S(2)}) collective-permute-start(bf16[512,384]{1,0:T(8,128)(2,1)S(1)} %get-tuple-element.73.grad_ref.rest_0_), channel_id=1, source_target_pairs={{0,2},{2,0},{1,3},{3,1},{4,6},{6,4},{5,7},{7,5},{8,10},{10,8},{9,1... | collective-permute-start | bytes 1179656 | tf_op jit(solution)/shard_map/ppermute | solution.py:357
  9.4 1.8 %forward_partner.3 = (f32[512,384]{1,0:T(8,128)S(1)}, bf16[512,384]{1,0:T(8,128)(2,1)S(1)}) custom-call(bf16[512,384]{1,0:T(8,128)(2,1)S(1)} %collective-permute-done.snake_ref.partner_ref, bf16[3,2,1152,384]{3,2,1,0:T(8,128)(2,1)S(1)} %get-tuple-element.74.weight_ref, f32[512,384]{1,0:T(8,128)S(1)} %forward_own.3.own_ref, ...), custom_call_target="tpu_custom_call" | custom-call | flops 4529848320 | bytes 34124800 | tf_op jit(solution)/shard_map/forward_partner/pallas_call | solution.py:342
  13.8 1.7 %forward_partner.4 = (f32[512,384]{1,0:T(8,128)S(1)}, bf16[512,384]{1,0:T(8,128)(2,1)S(1)}) custom-call(bf16[512,384]{1,0:T(8,128)(2,1)S(1)} %collective-permute-done.1.snake_ref.partner_ref, bf16[3,2,1152,384]{3,2,1,0:T(8,128)(2,1)S(1)} %get-tuple-element.74.weight_ref, f32[512,384]{1,0:T(8,128)S(1)} %forward_own.4.own_ref, ...), custom_call_target="tpu_custom_call" | custom-call | flops 4529848320 | bytes 34124800 | tf_op jit(solution)/shard_map/forward_partner/pallas_call | solution.py:342
  16.2 1.6 %combine.3 = (f32[1,384]{1,0:T(1,128)S(1)}, f32[512,384]{1,0:T(8,128)S(1)}, bf16[512,384]{1,0:T(8,128)(2,1)S(1)}) custom-call(f32[512,384]{1,0:T(8,128)S(1)} %back_own.3.own_ref, bf16[512,384]{1,0:T(8,128)(2,1)S(1)} %collective-permute-done.3.partner_ref, f32[512,384]{1,0:T(8,128)S(1)} %get-tuple-element.86.stream_ref.old_ref, ...), custom_call_target="tpu_custom_call" | custom-call | flops 117964800 | bytes 38072320 | tf_op jit(solution)/shard_map/combine/pallas_call | solution.py:342
  20.2 2.8 %collective-permute-done.5.across_ref = bf16[192,512]{1,0:T(8,128)(2,1)S(1)} collective-permute-done((bf16[192,512]{1,0:T(8,128)(2,1)S(1)}, bf16[192,512]{1,0:T(8,128)(2,1)S(1)}, u32[]{:S(2)}, u32[]{:S(2)}) %collective-permute-start.5) | collective-permute-done | bytes 196640 | tf_op jit(solution)/shard_map/ppermute | solution.py:357
  23.3 1.7 %collective-permute-start.11 = (bf16[512,384]{1,0:T(8,128)(2,1)S(1)}, bf16[512,384]{1,0:T(8,128)(2,1)S(1)}, u32[]{:S(2)}, u32[]{:S(2)}) collective-permute-start(bf16[512,384]{1,0:T(8,128)(2,1)S(1)} %get-tuple-element.114.grad_ref), channel_id=1, source_target_pairs={{0,2},{2,0},{1,3},{3,1},{4,6},{6,4},{5,7},{7,5},{8,10},{10,8},{9,1... | collective-permute-start | bytes 1179656 | tf_op jit(solution)/shard_map/ppermute | solution.py:357
  25.0 1.7 %combine.4 = (f32[1,384]{1,0:T(1,128)S(1)}, bf16[512,384]{1,0:T(8,128)(2,1)S(1)}) custom-call(f32[512,384]{1,0:T(8,128)S(1)} %back_own.4.own_ref, bf16[512,384]{1,0:T(8,128)(2,1)S(1)} %collective-permute-done.4.partner_ref, f32[512,384]{1,0:T(8,128)S(1)} %get-tuple-element.81.old_ref.stream_ref, f32[3,384]{1,0:T(4,128)S(1)} %get-tuple-element.79.rest_0_.alphas_ref, ...), custom_call_target="tpu_custom_call" | custom-call | flops 117964800 | bytes 34140160 | tf_op jit(solution)/shard_map/combine/pallas_call | solution.py:342
  26.7 1.6 %paired_weight.3 = (bf16[192,1152]{1,0:T(8,128)(2,1)S(1)}, bf16[192,1152]{1,0:T(8,128)(2,1)S(1)}) custom-call(bf16[512,384]{1,0:T(8,128)(2,1)S(1)} %get-tuple-element.106.snake_ref.own_ref, bf16[512,384]{1,0:T(8,128)(2,1)S(1)} %collective-permute-done.2.partner_ref.snake_ref, bf16[512,1152]{1,0:T(8,128)(2,1)S(1)} %get-tuple-element.82.shifted_ref, ...), custom_call_target="tpu_custom_call" | custom-call | flops 9059696640 | bytes 36372480 | tf_op jit(solution)/shard_map/paired_weight/pallas_call | solution.py:342
  28.4 1.6 %collective-permute-start.12 = (bf16[192,1152]{1,0:T(8,128)(2,1)S(1)}, bf16[192,1152]{1,0:T(8,128)(2,1)S(1)}, u32[]{:S(2)}, u32[]{:S(2)}) collective-permute-start(bf16[192,1152]{1,0:T(8,128)(2,1)S(1)} %get-tuple-element.103), channel_id=1, source_target_pairs={{0,4},{4,0},{8,12},{12,8},{1,5},{5,1},{9,13},{13,9},{2,6},{6,2},{1... | collective-permute-start | bytes 1327112 | tf_op jit(solution)/shard_map/ppermute | solution.py:357
  33.5 1.4 %combine.5 = f32[1,384]{1,0:T(1,128)S(1)} custom-call(f32[512,384]{1,0:T(8,128)S(1)} %back_own.5.own_ref, bf16[512,384]{1,0:T(8,128)(2,1)S(1)} %collective-permute-done.8.partner_ref, f32[512,384]{1,0:T(8,128)S(1)} %get-tuple-element.72.old_ref.stream_ref, f32[3,384]{1,0:T(4,128)S(1)} %get-tuple-element.79.rest_0_.alphas_ref), custom_call_target="tpu_custom_call" | custom-call | flops 117964800 | bytes 19722240 | tf_op jit(solution)/shard_map/combine/pallas_call | solution.py:342
  34.9 1.6 %forward_partner.5 = bf16[512,384]{1,0:T(8,128)(2,1)} custom-call(bf16[512,384]{1,0:T(8,128)(2,1)S(1)} %collective-permute-done.2.partner_ref.snake_ref, bf16[3,2,1152,384]{3,2,1,0:T(8,128)(2,1)S(1)} %get-tuple-element.74.weight_ref, f32[512,384]{1,0:T(8,128)S(1)} %forward_own.5.own_ref, f32[512,384]{1,0:T(8,128)S(1)} %get-tuple-element.86.stream_ref.old_ref, ...), custom_call_target="tpu_custom_call" | custom-call | flops 4529848320 | bytes 26214400 | tf_op jit(solution)/shard_map/forward_partner/pallas_call | solution.py:342
  36.5 2.2 %collective-permute-done.11.grad_ref = bf16[512,384]{1,0:T(8,128)(2,1)S(1)} collective-permute-done((bf16[512,384]{1,0:T(8,128)(2,1)S(1)}, bf16[512,384]{1,0:T(8,128)(2,1)S(1)}, u32[]{:S(2)}, u32[]{:S(2)}) %collective-permute-start.11) | collective-permute-done | bytes 393248 | tf_op jit(solution)/shard_map/ppermute | solution.py:357
  38.7 1.6 %paired_weight.4 = (bf16[192,1152]{1,0:T(8,128)(2,1)S(1)}, bf16[192,1152]{1,0:T(8,128)(2,1)S(1)}) custom-call(bf16[512,384]{1,0:T(8,128)(2,1)S(1)} %get-tuple-element.112.snake_ref.own_ref, bf16[512,384]{1,0:T(8,128)(2,1)S(1)} %collective-permute-done.1.snake_ref.partner_ref, bf16[512,1152]{1,0:T(8,128)(2,1)S(1)} %get-tuple-element.95.shifted_ref, ...), custom_call_target="tpu_custom_call" | custom-call | flops 9059696640 | bytes 36372480 | tf_op jit(solution)/shard_map/paired_weight/pallas_call | solution.py:342
  40.8 1.7 %collective-permute-start.15 = (bf16[512,384]{1,0:T(8,128)(2,1)S(1)}, bf16[512,384]{1,0:T(8,128)(2,1)S(1)}, u32[]{:S(2)}, u32[]{:S(2)}) collective-permute-start(bf16[512,384]{1,0:T(8,128)(2,1)S(1)} %get-tuple-element.120.grad_ref), channel_id=1, source_target_pairs={{0,2},{2,0},{1,3},{3,1},{4,6},{6,4},{5,7},{7,5},{8,10},{10,8},{9,1... | collective-permute-start | bytes 1179656 | tf_op jit(solution)/shard_map/ppermute | solution.py:357
  42.6 5.7 %collective-permute-done.13.across_ref = bf16[192,512]{1,0:T(8,128)(2,1)S(1)} collective-permute-done((bf16[192,512]{1,0:T(8,128)(2,1)S(1)}, bf16[192,512]{1,0:T(8,128)(2,1)S(1)}, u32[]{:S(2)}, u32[]{:S(2)}) %collective-permute-start.13) | collective-permute-done | bytes 196640 | tf_op jit(solution)/shard_map/ppermute | solution.py:357
  48.4 1.6 %collective-permute-start.17 = (bf16[192,1152]{1,0:T(8,128)(2,1)S(1)}, bf16[192,1152]{1,0:T(8,128)(2,1)S(1)}, u32[]{:S(2)}, u32[]{:S(2)}) collective-permute-start(bf16[192,1152]{1,0:T(8,128)(2,1)S(1)} %get-tuple-element.115), channel_id=1, source_target_pairs={{0,4},{4,0},{8,12},{12,8},{1,5},{5,1},{9,13},{13,9},{2,6},{6,2},{1... | collective-permute-start | bytes 1327112 | tf_op jit(solution)/shard_map/ppermute | solution.py:357
  49.9 2.5 %collective-permute-start.16 = (bf16[96,1152]{1,0:T(8,128)(2,1)S(1)}, bf16[96,1152]{1,0:T(8,128)(2,1)S(1)}, u32[]{:S(2)}, u32[]{:S(2)}) collective-permute-start(bf16[96,1152]{1,0:T(8,128)(2,1)S(1)} %fold.4), channel_id=1, source_target_pairs={{0,12},{4,8},{8,4},{12,0},{1,13},{5,9},{9,5},{13,1},{2,14},{6,10},... | collective-permute-start | bytes 663560 | tf_op jit(solution)/shard_map/ppermute | solution.py:357
  52.4 3.1 %collective-permute-done.15.grad_ref = bf16[512,384]{1,0:T(8,128)(2,1)S(1)} collective-permute-done((bf16[512,384]{1,0:T(8,128)(2,1)S(1)}, bf16[512,384]{1,0:T(8,128)(2,1)S(1)}, u32[]{:S(2)}, u32[]{:S(2)}) %collective-permute-start.15) | collective-permute-done | bytes 393248 | tf_op jit(solution)/shard_map/ppermute | solution.py:357
  55.5 1.6 %paired_weight.5 = (bf16[96,1152]{1,0:T(8,128)(2,1)S(1)}, bf16[96,1152]{1,0:T(8,128)(2,1)S(1)}, bf16[96,1152]{1,0:T(8,128)(2,1)S(1)}, bf16[96,1152]{1,0:T(8,128)(2,1)S(1)}) custom-call(bf16[512,384]{1,0:T(8,128)(2,1)S(1)} %get-tuple-element.118.snake_ref.own_ref, bf16[512,384]{1,0:T(8,128)(2,1)S(1)} %collective-permute-done.snake_ref.partner_ref, ...), custom_call_target="tpu_custom_call" | custom-call | flops 9059696640 | bytes 36372480 | tf_op jit(solution)/shard_map/paired_weight/pallas_call | solution.py:342
  57.1 1.6 %collective-permute-start.18 = (bf16[96,1152]{1,0:T(8,128)(2,1)S(1)}, bf16[96,1152]{1,0:T(8,128)(2,1)S(1)}, u32[]{:S(2)}, u32[]{:S(2)}) collective-permute-start(bf16[96,1152]{1,0:T(8,128)(2,1)S(1)} %get-tuple-element.124), channel_id=1, source_target_pairs={{0,4},{4,0},{8,12},{12,8},{1,5},{5,1},{9,13},{13,9},{2,6},{6,2},{1... | collective-permute-start | bytes 663560 | tf_op jit(solution)/shard_map/ppermute | solution.py:357
  59.6 8.6 %collective-permute-done.16.late = bf16[96,1152]{1,0:T(8,128)(2,1)S(1)} collective-permute-done((bf16[96,1152]{1,0:T(8,128)(2,1)S(1)}, bf16[96,1152]{1,0:T(8,128)(2,1)S(1)}, u32[]{:S(2)}, u32[]{:S(2)}) %collective-permute-start.16) | collective-permute-done | bytes 221216 | tf_op jit(solution)/shard_map/ppermute | solution.py:357
  68.3 1.4 %collective-permute-start.20 = (bf16[96,1152]{1,0:T(8,128)(2,1)S(1)}, bf16[96,1152]{1,0:T(8,128)(2,1)S(1)}, u32[]{:S(2)}, u32[]{:S(2)}) collective-permute-start(bf16[96,1152]{1,0:T(8,128)(2,1)S(1)} %fold.5), channel_id=1, source_target_pairs={{0,12},{4,8},{8,4},{12,0},{1,13},{5,9},{9,5},{13,1},{2,14},{6,10},... | collective-permute-start | bytes 663560 | tf_op jit(solution)/shard_map/ppermute | solution.py:357
  70.8 3.7 %collective-permute-start.21 = (bf16[48,1152]{1,0:T(8,128)(2,1)S(1)}, bf16[48,1152]{1,0:T(8,128)(2,1)S(1)}, u32[]{:S(2)}, u32[]{:S(2)}) collective-permute-start(bf16[48,1152]{1,0:T(8,128)(2,1)S(1)} %fold.6), channel_id=1, source_target_pairs={{0,12},{4,8},{8,4},{12,0},{1,13},{5,9},{9,5},{13,1},{2,14},{6,10},... | collective-permute-start | bytes 331784 | tf_op jit(solution)/shard_map/ppermute | solution.py:357
  75.2 4.3 %collective-permute-start.22 = (bf16[48,1152]{1,0:T(8,128)(2,1)S(1)}, bf16[48,1152]{1,0:T(8,128)(2,1)S(1)}, u32[]{:S(2)}, u32[]{:S(2)}) collective-permute-start(bf16[48,1152]{1,0:T(8,128)(2,1)S(1)} %fold.7), channel_id=1, source_target_pairs={{0,12},{4,8},{8,4},{12,0},{1,13},{5,9},{9,5},{13,1},{2,14},{6,10},... | collective-permute-start | bytes 331784 | tf_op jit(solution)/shard_map/ppermute | solution.py:357
  80.4 2.2 %collective-permute-done.20.late = bf16[96,1152]{1,0:T(8,128)(2,1)S(1)} collective-permute-done((bf16[96,1152]{1,0:T(8,128)(2,1)S(1)}, bf16[96,1152]{1,0:T(8,128)(2,1)S(1)}, u32[]{:S(2)}, u32[]{:S(2)}) %collective-permute-start.20) | collective-permute-done | bytes 221216 | tf_op jit(solution)/shard_map/ppermute | solution.py:357
  83.3 1.7 %collective-permute-done.21.late = bf16[48,1152]{1,0:T(8,128)(2,1)S(1)} collective-permute-done((bf16[48,1152]{1,0:T(8,128)(2,1)S(1)}, bf16[48,1152]{1,0:T(8,128)(2,1)S(1)}, u32[]{:S(2)}, u32[]{:S(2)}) %collective-permute-start.21) | collective-permute-done | bytes 110624 | tf_op jit(solution)/shard_map/ppermute | solution.py:357
  85.6 1.4 %collective-permute-done.22.late = bf16[48,1152]{1,0:T(8,128)(2,1)S(1)} collective-permute-done((bf16[48,1152]{1,0:T(8,128)(2,1)S(1)}, bf16[48,1152]{1,0:T(8,128)(2,1)S(1)}, u32[]{:S(2)}, u32[]{:S(2)}) %collective-permute-start.22) | collective-permute-done | bytes 110624 | tf_op jit(solution)/shard_map/ppermute | solution.py:357
  87.7 3.3 %collective-permute-start.29 = (f32[3,384]{1,0:T(4,128)S(1)}, f32[3,384]{1,0:T(4,128)S(1)}, u32[]{:S(2)}, u32[]{:S(2)}) collective-permute-start(f32[3,384]{1,0:T(4,128)S(1)} %fusion.1), channel_id=1, source_target_pairs={{0,8},{4,12},{8,0},{12,4},{1,9},{5,13},{9,1},{13,5},{2,10},{6,14},... | collective-permute-start | bytes 13832 | tf_op jit(solution)/shard_map/ppermute | solution.py:357
  90.9 1.6 %collective-permute-done.29 = f32[3,384]{1,0:T(4,128)S(1)} collective-permute-done((f32[3,384]{1,0:T(4,128)S(1)}, f32[3,384]{1,0:T(4,128)S(1)}, u32[]{:S(2)}, u32[]{:S(2)}) %collective-permute-start.29) | collective-permute-done | bytes 4640 | tf_op jit(solution)/shard_map/ppermute | solution.py:357
  93.1 2.3 %collective-permute-done.24.refs_3_ = bf16[48,1152]{1,0:T(8,128)(2,1)S(1)} collective-permute-done((bf16[48,1152]{1,0:T(8,128)(2,1)S(1)}, bf16[48,1152]{1,0:T(8,128)(2,1)S(1)}, u32[]{:S(2)}, u32[]{:S(2)}) %collective-permute-start.24) | collective-permute-done | bytes 110624 | tf_op jit(solution)/shard_map/ppermute | solution.py:357
  95.4 1.7 %finish.1 = f32[3,3,192,384]{3,2,1,0:T(8,128)} custom-call(bf16[48,1152]{1,0:T(8,128)(2,1)S(1)} %total.6.refs_0_, bf16[48,1152]{1,0:T(8,128)(2,1)S(1)} %collective-permute-done.23.refs_1_, bf16[48,1152]{1,0:T(8,128)(2,1)S(1)} %total.7.refs_2_, bf16[48,1152]{1,0:T(8,128)(2,1)S(1)} %collective-permute-done.24.refs_3_, bf16[96,1152]{1,0:T(8,128)(2,1)S(1)} %total.5.refs_4_, ...), custom_call_target="tpu_custom_call" | custom-call | flops 6635520 | bytes 39813120 | tf_op jit(solution)/shard_map/finish/pallas_call | solution.py:342
  (63 shorter events, 18.8 us)
Async XLA Ops:
  4.3 5.0 %collective-permute-start = (bf16[512,384]{1,0:T(8,128)(2,1)S(1)}, bf16[512,384]{1,0:T(8,128)(2,1)S(1)}, u32[]{:S(2)}, u32[]{:S(2)}) collective-permute-start(bf16[512,384]{1,0:T(8,128)(2,1)S(1)} %get-tuple-element.118.snake_ref.own_ref), channel_id=1, source_target_pairs={{0,1},{1,0},{2,3},{3,2},{4,5},{5,4},{6,7},{7,6},{8,9},{9,8},{10,11... | collective-permute-start | bytes 1179656 | tf_op jit(solution)/shard_map/ppermute | solution.py:357
  4.9 21.9 %collective-permute-start.7 = (bf16[512,384]{1,0:T(8,128)(2,1)S(1)}, bf16[512,384]{1,0:T(8,128)(2,1)S(1)}, u32[]{:S(2)}, u32[]{:S(2)}) collective-permute-start(bf16[512,384]{1,0:T(8,128)(2,1)S(1)} %get-tuple-element.73.grad_ref.rest_0_), channel_id=1, source_target_pairs={{0,2},{2,0},{1,3},{3,1},{4,6},{6,4},{5,7},{7,5},{8,10},{10,8},{9,1... | collective-permute-start | bytes 1179656 | tf_op jit(solution)/shard_map/ppermute | solution.py:357
  8.3 7.9 %collective-permute-start.3 = (bf16[512,384]{1,0:T(8,128)(2,1)S(1)}, bf16[512,384]{1,0:T(8,128)(2,1)S(1)}, u32[]{:S(2)}, u32[]{:S(2)}) collective-permute-start(bf16[512,384]{1,0:T(8,128)(2,1)S(1)} %get-tuple-element.89), channel_id=1, source_target_pairs={{0,1},{1,0},{2,3},{3,2},{4,5},{5,4},{6,7},{7,6},{8,9},{9,8},{10,11... | collective-permute-start | bytes 1179656 | tf_op jit(solution)/shard_map/ppermute | solution.py:357
  12.0 1.8 %collective-permute-start.1 = (bf16[512,384]{1,0:T(8,128)(2,1)S(1)}, bf16[512,384]{1,0:T(8,128)(2,1)S(1)}, u32[]{:S(2)}, u32[]{:S(2)}) collective-permute-start(bf16[512,384]{1,0:T(8,128)(2,1)S(1)} %get-tuple-element.112.snake_ref.own_ref), channel_id=1, source_target_pairs={{0,1},{1,0},{2,3},{3,2},{4,5},{5,4},{6,7},{7,6},{8,9},{9,8},{10,11... | collective-permute-start | bytes 1179656 | tf_op jit(solution)/shard_map/ppermute | solution.py:357
  15.7 7.2 %collective-permute-start.5 = (bf16[192,512]{1,0:T(8,128)(2,1)S(1)}, bf16[192,512]{1,0:T(8,128)(2,1)S(1)}, u32[]{:S(2)}, u32[]{:S(2)}) collective-permute-start(bf16[192,512]{1,0:T(8,128)(2,1)S(1)} %turn.3), channel_id=1, source_target_pairs={{0,2},{2,0},{1,3},{3,1},{4,6},{6,4},{5,7},{7,5},{8,10},{10,8},{9,1... | collective-permute-start | bytes 589832 | tf_op jit(solution)/shard_map/ppermute | solution.py:357
  16.1 10.7 %collective-permute-start.2 = (bf16[512,384]{1,0:T(8,128)(2,1)S(1)}, bf16[512,384]{1,0:T(8,128)(2,1)S(1)}, u32[]{:S(2)}, u32[]{:S(2)}) collective-permute-start(bf16[512,384]{1,0:T(8,128)(2,1)S(1)} %get-tuple-element.106.snake_ref.own_ref), channel_id=1, source_target_pairs={{0,1},{1,0},{2,3},{3,2},{4,5},{5,4},{6,7},{7,6},{8,9},{9,8},{10,11... | collective-permute-start | bytes 1179656 | tf_op jit(solution)/shard_map/ppermute | solution.py:357
  18.9 4.4 %collective-permute-start.4 = (bf16[512,384]{1,0:T(8,128)(2,1)S(1)}, bf16[512,384]{1,0:T(8,128)(2,1)S(1)}, u32[]{:S(2)}, u32[]{:S(2)}) collective-permute-start(bf16[512,384]{1,0:T(8,128)(2,1)S(1)} %get-tuple-element.97), channel_id=1, source_target_pairs={{0,1},{1,0},{2,3},{3,2},{4,5},{5,4},{6,7},{7,6},{8,9},{9,8},{10,11... | collective-permute-start | bytes 1179656 | tf_op jit(solution)/shard_map/ppermute | solution.py:357
  23.0 3.8 %collective-permute-start.6 = (bf16[192,512]{1,0:T(8,128)(2,1)S(1)}, bf16[192,512]{1,0:T(8,128)(2,1)S(1)}, u32[]{:S(2)}, u32[]{:S(2)}) collective-permute-start(bf16[192,512]{1,0:T(8,128)(2,1)S(1)} %collective-permute-done.5.across_ref), channel_id=1, source_target_pairs={{0,1},{1,0},{2,3},{3,2},{4,5},{5,4},{6,7},{7,6},{8,9},{9,8},{10,11... | collective-permute-start | bytes 589832 | tf_op jit(solution)/shard_map/ppermute | solution.py:357
  23.0 9.7 %collective-permute-start.9 = (bf16[192,512]{1,0:T(8,128)(2,1)S(1)}, bf16[192,512]{1,0:T(8,128)(2,1)S(1)}, u32[]{:S(2)}, u32[]{:S(2)}) collective-permute-start(bf16[192,512]{1,0:T(8,128)(2,1)S(1)} %turn.4), channel_id=1, source_target_pairs={{0,2},{2,0},{1,3},{3,1},{4,6},{6,4},{5,7},{7,5},{8,10},{10,8},{9,1... | collective-permute-start | bytes 589832 | tf_op jit(solution)/shard_map/ppermute | solution.py:357
  23.3 15.5 %collective-permute-start.11 = (bf16[512,384]{1,0:T(8,128)(2,1)S(1)}, bf16[512,384]{1,0:T(8,128)(2,1)S(1)}, u32[]{:S(2)}, u32[]{:S(2)}) collective-permute-start(bf16[512,384]{1,0:T(8,128)(2,1)S(1)} %get-tuple-element.114.grad_ref), channel_id=1, source_target_pairs={{0,2},{2,0},{1,3},{3,1},{4,6},{6,4},{5,7},{7,5},{8,10},{10,8},{9,1... | collective-permute-start | bytes 1179656 | tf_op jit(solution)/shard_map/ppermute | solution.py:357
  28.4 14.2 %collective-permute-start.12 = (bf16[192,1152]{1,0:T(8,128)(2,1)S(1)}, bf16[192,1152]{1,0:T(8,128)(2,1)S(1)}, u32[]{:S(2)}, u32[]{:S(2)}) collective-permute-start(bf16[192,1152]{1,0:T(8,128)(2,1)S(1)} %get-tuple-element.103), channel_id=1, source_target_pairs={{0,4},{4,0},{8,12},{12,8},{1,5},{5,1},{9,13},{13,9},{2,6},{6,2},{1... | collective-permute-start | bytes 1327112 | tf_op jit(solution)/shard_map/ppermute | solution.py:357
  31.7 1.8 %collective-permute-start.8 = (bf16[512,384]{1,0:T(8,128)(2,1)S(1)}, bf16[512,384]{1,0:T(8,128)(2,1)S(1)}, u32[]{:S(2)}, u32[]{:S(2)}) collective-permute-start(bf16[512,384]{1,0:T(8,128)(2,1)S(1)} %get-tuple-element.109), channel_id=1, source_target_pairs={{0,1},{1,0},{2,3},{3,2},{4,5},{5,4},{6,7},{7,6},{8,9},{9,8},{10,11... | collective-permute-start | bytes 1179656 | tf_op jit(solution)/shard_map/ppermute | solution.py:357
  32.7 6.0 %collective-permute-start.10 = (bf16[192,512]{1,0:T(8,128)(2,1)S(1)}, bf16[192,512]{1,0:T(8,128)(2,1)S(1)}, u32[]{:S(2)}, u32[]{:S(2)}) collective-permute-start(bf16[192,512]{1,0:T(8,128)(2,1)S(1)} %collective-permute-done.9.across_ref), channel_id=1, source_target_pairs={{0,1},{1,0},{2,3},{3,2},{4,5},{5,4},{6,7},{7,6},{8,9},{9,8},{10,11... | collective-permute-start | bytes 589832 | tf_op jit(solution)/shard_map/ppermute | solution.py:357
  40.5 7.9 %collective-permute-start.13 = (bf16[192,512]{1,0:T(8,128)(2,1)S(1)}, bf16[192,512]{1,0:T(8,128)(2,1)S(1)}, u32[]{:S(2)}, u32[]{:S(2)}) collective-permute-start(bf16[192,512]{1,0:T(8,128)(2,1)S(1)} %turn.5), channel_id=1, source_target_pairs={{0,2},{2,0},{1,3},{3,1},{4,6},{6,4},{5,7},{7,5},{8,10},{10,8},{9,1... | collective-permute-start | bytes 589832 | tf_op jit(solution)/shard_map/ppermute | solution.py:357
  40.8 14.7 %collective-permute-start.15 = (bf16[512,384]{1,0:T(8,128)(2,1)S(1)}, bf16[512,384]{1,0:T(8,128)(2,1)S(1)}, u32[]{:S(2)}, u32[]{:S(2)}) collective-permute-start(bf16[512,384]{1,0:T(8,128)(2,1)S(1)} %get-tuple-element.120.grad_ref), channel_id=1, source_target_pairs={{0,2},{2,0},{1,3},{3,1},{4,6},{6,4},{5,7},{7,5},{8,10},{10,8},{9,1... | collective-permute-start | bytes 1179656 | tf_op jit(solution)/shard_map/ppermute | solution.py:357
  48.4 7.2 %collective-permute-start.14 = (bf16[192,512]{1,0:T(8,128)(2,1)S(1)}, bf16[192,512]{1,0:T(8,128)(2,1)S(1)}, u32[]{:S(2)}, u32[]{:S(2)}) collective-permute-start(bf16[192,512]{1,0:T(8,128)(2,1)S(1)} %collective-permute-done.13.across_ref), channel_id=1, source_target_pairs={{0,1},{1,0},{2,3},{3,2},{4,5},{5,4},{6,7},{7,6},{8,9},{9,8},{10,11... | collective-permute-start | bytes 589832 | tf_op jit(solution)/shard_map/ppermute | solution.py:357
  48.4 19.9 %collective-permute-start.17 = (bf16[192,1152]{1,0:T(8,128)(2,1)S(1)}, bf16[192,1152]{1,0:T(8,128)(2,1)S(1)}, u32[]{:S(2)}, u32[]{:S(2)}) collective-permute-start(bf16[192,1152]{1,0:T(8,128)(2,1)S(1)} %get-tuple-element.115), channel_id=1, source_target_pairs={{0,4},{4,0},{8,12},{12,8},{1,5},{5,1},{9,13},{13,9},{2,6},{6,2},{1... | collective-permute-start | bytes 1327112 | tf_op jit(solution)/shard_map/ppermute | solution.py:357
  49.9 18.2 %collective-permute-start.16 = (bf16[96,1152]{1,0:T(8,128)(2,1)S(1)}, bf16[96,1152]{1,0:T(8,128)(2,1)S(1)}, u32[]{:S(2)}, u32[]{:S(2)}) collective-permute-start(bf16[96,1152]{1,0:T(8,128)(2,1)S(1)} %fold.4), channel_id=1, source_target_pairs={{0,12},{4,8},{8,4},{12,0},{1,13},{5,9},{9,5},{13,1},{2,14},{6,10},... | collective-permute-start | bytes 663560 | tf_op jit(solution)/shard_map/ppermute | solution.py:357
  57.1 13.7 %collective-permute-start.18 = (bf16[96,1152]{1,0:T(8,128)(2,1)S(1)}, bf16[96,1152]{1,0:T(8,128)(2,1)S(1)}, u32[]{:S(2)}, u32[]{:S(2)}) collective-permute-start(bf16[96,1152]{1,0:T(8,128)(2,1)S(1)} %get-tuple-element.124), channel_id=1, source_target_pairs={{0,4},{4,0},{8,12},{12,8},{1,5},{5,1},{9,13},{13,9},{2,6},{6,2},{1... | collective-permute-start | bytes 663560 | tf_op jit(solution)/shard_map/ppermute | solution.py:357
  58.7 16.4 %collective-permute-start.19 = (bf16[96,1152]{1,0:T(8,128)(2,1)S(1)}, bf16[96,1152]{1,0:T(8,128)(2,1)S(1)}, u32[]{:S(2)}, u32[]{:S(2)}) collective-permute-start(bf16[96,1152]{1,0:T(8,128)(2,1)S(1)} %get-tuple-element.129), channel_id=1, source_target_pairs={{0,4},{4,0},{8,12},{12,8},{1,5},{5,1},{9,13},{13,9},{2,6},{6,2},{1... | collective-permute-start | bytes 663560 | tf_op jit(solution)/shard_map/ppermute | solution.py:357
  59.2 20.3 %collective-permute-start.27 = (f32[3,384]{1,0:T(4,128)S(1)}, f32[3,384]{1,0:T(4,128)S(1)}, u32[]{:S(2)}, u32[]{:S(2)}) collective-permute-start(f32[3,384]{1,0:T(4,128)S(1)} %pad_maximum_fusion), channel_id=1, source_target_pairs={{0,2},{2,0},{1,3},{3,1},{4,6},{6,4},{5,7},{7,5},{8,10},{10,8},{9,1... | collective-permute-start | bytes 13832 | tf_op jit(solution)/shard_map/ppermute | solution.py:357
  68.3 14.2 %collective-permute-start.20 = (bf16[96,1152]{1,0:T(8,128)(2,1)S(1)}, bf16[96,1152]{1,0:T(8,128)(2,1)S(1)}, u32[]{:S(2)}, u32[]{:S(2)}) collective-permute-start(bf16[96,1152]{1,0:T(8,128)(2,1)S(1)} %fold.5), channel_id=1, source_target_pairs={{0,12},{4,8},{8,4},{12,0},{1,13},{5,9},{9,5},{13,1},{2,14},{6,10},... | collective-permute-start | bytes 663560 | tf_op jit(solution)/shard_map/ppermute | solution.py:357
  70.8 14.1 %collective-permute-start.21 = (bf16[48,1152]{1,0:T(8,128)(2,1)S(1)}, bf16[48,1152]{1,0:T(8,128)(2,1)S(1)}, u32[]{:S(2)}, u32[]{:S(2)}) collective-permute-start(bf16[48,1152]{1,0:T(8,128)(2,1)S(1)} %fold.6), channel_id=1, source_target_pairs={{0,12},{4,8},{8,4},{12,0},{1,13},{5,9},{9,5},{13,1},{2,14},{6,10},... | collective-permute-start | bytes 331784 | tf_op jit(solution)/shard_map/ppermute | solution.py:357
  75.2 11.8 %collective-permute-start.22 = (bf16[48,1152]{1,0:T(8,128)(2,1)S(1)}, bf16[48,1152]{1,0:T(8,128)(2,1)S(1)}, u32[]{:S(2)}, u32[]{:S(2)}) collective-permute-start(bf16[48,1152]{1,0:T(8,128)(2,1)S(1)} %fold.7), channel_id=1, source_target_pairs={{0,12},{4,8},{8,4},{12,0},{1,13},{5,9},{9,5},{13,1},{2,14},{6,10},... | collective-permute-start | bytes 331784 | tf_op jit(solution)/shard_map/ppermute | solution.py:357
  79.5 8.1 %collective-permute-start.28 = (f32[3,384]{1,0:T(4,128)S(1)}, f32[3,384]{1,0:T(4,128)S(1)}, u32[]{:S(2)}, u32[]{:S(2)}) collective-permute-start(f32[3,384]{1,0:T(4,128)S(1)} %fusion), channel_id=1, source_target_pairs={{0,4},{4,0},{8,12},{12,8},{1,5},{5,1},{9,13},{13,9},{2,6},{6,2},{1... | collective-permute-start | bytes 13832 | tf_op jit(solution)/shard_map/ppermute | solution.py:357
  79.6 13.5 %collective-permute-start.26 = (bf16[96,1152]{1,0:T(8,128)(2,1)S(1)}, bf16[96,1152]{1,0:T(8,128)(2,1)S(1)}, u32[]{:S(2)}, u32[]{:S(2)}) collective-permute-start(bf16[96,1152]{1,0:T(8,128)(2,1)S(1)} %total.4.refs_6_), channel_id=1, source_target_pairs={{0,2},{2,0},{1,3},{3,1},{4,6},{6,4},{5,7},{7,5},{8,10},{10,8},{9,1... | collective-permute-start | bytes 663560 | tf_op jit(solution)/shard_map/ppermute | solution.py:357
  82.6 12.8 %collective-permute-start.25 = (bf16[96,1152]{1,0:T(8,128)(2,1)S(1)}, bf16[96,1152]{1,0:T(8,128)(2,1)S(1)}, u32[]{:S(2)}, u32[]{:S(2)}) collective-permute-start(bf16[96,1152]{1,0:T(8,128)(2,1)S(1)} %total.5.refs_4_), channel_id=1, source_target_pairs={{0,2},{2,0},{1,3},{3,1},{4,6},{6,4},{5,7},{7,5},{8,10},{10,8},{9,1... | collective-permute-start | bytes 663560 | tf_op jit(solution)/shard_map/ppermute | solution.py:357
  85.0 10.4 %collective-permute-start.23 = (bf16[48,1152]{1,0:T(8,128)(2,1)S(1)}, bf16[48,1152]{1,0:T(8,128)(2,1)S(1)}, u32[]{:S(2)}, u32[]{:S(2)}) collective-permute-start(bf16[48,1152]{1,0:T(8,128)(2,1)S(1)} %total.6.refs_0_), channel_id=1, source_target_pairs={{0,2},{2,0},{1,3},{3,1},{4,6},{6,4},{5,7},{7,5},{8,10},{10,8},{9,1... | collective-permute-start | bytes 331784 | tf_op jit(solution)/shard_map/ppermute | solution.py:357
  87.0 8.4 %collective-permute-start.24 = (bf16[48,1152]{1,0:T(8,128)(2,1)S(1)}, bf16[48,1152]{1,0:T(8,128)(2,1)S(1)}, u32[]{:S(2)}, u32[]{:S(2)}) collective-permute-start(bf16[48,1152]{1,0:T(8,128)(2,1)S(1)} %total.7.refs_2_), channel_id=1, source_target_pairs={{0,2},{2,0},{1,3},{3,1},{4,6},{6,4},{5,7},{7,5},{8,10},{10,8},{9,1... | collective-permute-start | bytes 331784 | tf_op jit(solution)/shard_map/ppermute | solution.py:357
  87.7 4.9 %collective-permute-start.29 = (f32[3,384]{1,0:T(4,128)S(1)}, f32[3,384]{1,0:T(4,128)S(1)}, u32[]{:S(2)}, u32[]{:S(2)}) collective-permute-start(f32[3,384]{1,0:T(4,128)S(1)} %fusion.1), channel_id=1, source_target_pairs={{0,8},{4,12},{8,0},{12,4},{1,9},{5,13},{9,1},{13,5},{2,10},{6,14},... | collective-permute-start | bytes 13832 | tf_op jit(solution)/shard_map/ppermute | solution.py:357

commit v5 on v4

--- a/solution.py
+++ b/solution.py
@@ -256,41 +256,51 @@
     return [turned_ref[pl.ds(local * 2 * size + begin, size), :] for local in range(2)]
 
 
-def turn_kernel(snake_ref, out_ref, turned_ref):
-    size = snake_ref.shape[1] // 4
-    turned_ref[...] = snake_ref[...].T
-    for local, piece in enumerate(pick_parts(turned_ref, 1 - lax.axis_index("replica"), size)):
-        out_ref[local * size : (local + 1) * size, :] = piece
-
-
-def paired_weight_kernel(
-    layer, pieces, own_ref, partner_ref, shifted_ref, across_ref, across_other_ref, grad_ref, *rest
-):
-    outs, (turned_ref, half_ref, far_ref) = rest[:-3], rest[-3:]
-    rows, half = own_ref.shape
+def turn_kernel(*refs):
+    snakes, out_ref, turned_ref = refs[:-2], refs[-2], refs[-1]
+    size = snakes[0].shape[1] // 4
+    for index, ref in enumerate(snakes):
+        turned_ref[...] = ref[...].T
+        for local, piece in enumerate(pick_parts(turned_ref, 1 - lax.axis_index("replica"), size)):
+            low = (2 * index + local) * size
+            out_ref[low : low + size, :] = piece
+
+
+def own_rows_kernel(pieces, own_ref, partner_ref, out_ref, half_ref):
     chan = lax.axis_index("chan")
     mine = lax.axis_index("replica")
     for ref, side in ((own_ref, chan), (partner_ref, 1 - chan)):
         half_ref[...] = ref[...].T
-        both = jnp.concatenate(pick_parts(half_ref, mine, half // 4), 0)
-        place_rows(pieces, both, side, turned_ref, slice(0, rows))
+        both = jnp.concatenate(pick_parts(half_ref, mine, ref.shape[1] // 4), 0)
+        place_rows(pieces, both, side, out_ref, slice(None))
+
+
+def far_kernel(layer, grad_ref, out_ref):
+    write_shifts(grad_ref, out_ref, -dilations[layer])
+
+
+def paired_weight_kernel(pieces, low, own_ref, shifted_ref, across_ref, across_other_ref, far_ref, *rest):
+    outs, turned_ref = rest[:-1], rest[-1]
+    half = own_ref.shape[0]
+    chan = lax.axis_index("chan")
     for ref, side in ((across_ref, chan), (across_other_ref, 1 - chan)):
-        place_rows(pieces, ref[...], side, turned_ref, slice(rows, 2 * rows))
-    write_shifts(grad_ref, far_ref, -dilations[layer])
+        place_rows(pieces, ref[low : low + half // 2, :], side, turned_ref, slice(None))
     for tap in range(3):
         span = slice(tap * half, (tap + 1) * half)
-        product = jnp.dot(turned_ref[:, 0:rows], shifted_ref[:, span], preferred_element_type=F32)
-        product += jnp.dot(turned_ref[:, rows:], far_ref[:, span], preferred_element_type=F32)
+        product = jnp.dot(own_ref[...], shifted_ref[:, span], preferred_element_type=F32)
+        product += jnp.dot(turned_ref[...], far_ref[:, span], preferred_element_type=F32)
         product = product.astype(BF16)
         size = product.shape[0] // len(outs)
         for place, ref in enumerate(outs):
             ref[:, span] = product[place * size : (place + 1) * size, :]
 
 
-def finish_kernel(paired, counts, *refs):
-    out_ref, refs = refs[-1], list(refs[:-1])
-    half = out_ref.shape[3]
-    for layer, pieces in enumerate(counts):
+def finish_kernel(paired, held, counts, *refs):
+    out_ref, total_ref, sems = refs[-3:]
+    refs = list(refs[1:-3] if held else refs[:-3])
+    half = total_ref.shape[3]
+    copies = []
+    for index, (layer, pieces) in enumerate(counts):
         for part in range(pieces):
             mine_ref, other_ref = refs.pop(0), refs.pop(0)
             size = mine_ref.shape[0]
@@ -301,9 +311,13 @@
                     begin = lax.axis_index("replica") * (size * pieces)
                     for values, start in ((mine, begin), (other, size * pieces - begin)):
                         place = pl.multiple_of(start + part * size, size)
-                        out_ref[layer, tap, pl.ds(place, size), :] = values
+                        total_ref[index, tap, pl.ds(place, size), :] = values
                 else:
-                    out_ref[layer, tap] = mine + other
+                    total_ref[index, tap] = mine + other
+        copies.append(pltpu.make_async_copy(total_ref.at[index], out_ref.at[layer], sems.at[index]))
+        copies[-1].start()
+    for copy in copies:
+        copy.wait()
 
 
 def fold_kernel(keep, got, send):
@@ -317,6 +331,15 @@
     out_ref[...] = total.astype(BF16)
 
 
+def stack_kernel(*refs):
+    for index, ref in enumerate(refs[:-1]):
+        refs[-1][index : index + 1, :] = ref[...]
+
+
+def add_kernel(left, right, out_ref):
+    out_ref[...] = left[...] + right[...]
+
+
 def struct(shape, dtype):
     return jax.ShapeDtypeStruct(shape, dtype)
 
@@ -328,25 +351,28 @@
 class Sequence:
     def __init__(self):
         self.latest = None
+        self.weight = 10
 
     def hold(self, value):
         return after(value, self.latest)
 
-    def call(self, kernel, name, ins, outs, scratch, flops, *args):
+    def call(self, kernel, name, ins, outs, scratch, flops, *args, spec=IN_VMEM, aliases=None):
         single = not isinstance(outs, list)
         size = sum(a.size * a.dtype.itemsize for a in args if a.size < 2000000)
         size += sum(math.prod(o.shape) * o.dtype.itemsize for o in ([outs] if single else outs))
-        args = [pltpu.with_memory_space_constraint(a, pltpu.HBM) if i else a for i, a in zip(ins, args)]
+        args = [pltpu.with_memory_space_constraint(a, pltpu.HBM) if i == 1 else a for i, a in zip(ins, args)]
         if self.latest is not None:
-            args[0] = self.hold(args[0])
+            held = ins.index(0)
+            args[held] = self.hold(args[held])
         result = pl.pallas_call(
             kernel,
             in_specs=[ANY_HBM if i else IN_VMEM for i in ins],
-            out_specs=IN_VMEM if single else [IN_VMEM] * len(outs),
+            out_specs=spec if single else [IN_VMEM] * len(outs),
             out_shape=outs,
             scratch_shapes=scratch,
+            input_output_aliases=aliases or {},
             compiler_params=pltpu.CompilerParams(vmem_limit_bytes=24 * 1024 * 1024),
-            cost_estimate=pl.CostEstimate(flops=int(flops) * 10, bytes_accessed=int(size) * 10, transcendentals=0),
+            cost_estimate=pl.CostEstimate(flops=int(flops) * self.weight, bytes_accessed=int(size) * self.weight, transcendentals=0),
             name=name,
         )(*args)
         self.latest = result if single else result[0]
@@ -363,17 +389,6 @@
 
 def across_replica(x):
     return swap(x, "replica", lambda i: i ^ 1)
-
-
-def sum_rounds(values, axis, sequence):
-    size = lax.axis_size(axis)
-    if size & (size - 1):
-        return lax.psum(values, axis)
-    apart = 1
-    while apart < size:
-        values = values + swap(sequence.hold(values), axis, lambda i, apart=apart: i ^ apart)
-        apart *= 2
-    return values
 
 
 def on_device(activations, cotangent, conv_weights, snake_alpha, seg_lengths, seg_owner, seg_start):
@@ -381,7 +396,7 @@
     layers, taps, channels, _ = conv_weights.shape
     top = layers - 1
     fast = lax.axis_size("dp") == 4 and lax.axis_size("replica") == 2
-    counts = [2, 1, 1] if fast else [1, 1, 1]
+    counts = [1] * layers
     tile, triple = (rows, half), (rows, taps * half)
     flops = 2 * rows * half * half * taps
     sequence = Sequence()
@@ -443,16 +458,36 @@
             rounded[layer] = result[-1]
             return result[1]
 
-    def turn(layer):
+    def turn(*chosen):
         if fast:
-            across[layer] = across_replica(sequence.call(
-                turn_kernel, "turn", [0], struct((half // 2, rows), BF16),
-                [pltpu.VMEM((half, rows), BF16)], 10 * rows * half, mine[layer],
+            moved_rows = across_replica(sequence.call(
+                turn_kernel, "turn", [0] * len(chosen), struct((len(chosen) * half // 2, rows), BF16),
+                [pltpu.VMEM((half, rows), BF16)], 10 * rows * half, *[mine[layer] for layer in chosen],
             ))
-
-    def share(layer):
+            for index, layer in enumerate(chosen):
+                across[layer] = (moved_rows, index * half // 2)
+
+    def share(*chosen):
         if fast:
-            across_other[layer] = across_chan(sequence.hold(across[layer]))
+            shared = across_chan(sequence.hold(across[chosen[0]][0]))
+            for layer in chosen:
+                across_other[layer] = shared
+
+    own_turned, far_shifted = {}, {}
+
+    def own_rows(layer):
+        if fast:
+            own_turned[layer] = sequence.call(
+                functools.partial(own_rows_kernel, counts[layer]), "own_rows", [0, 0], struct((half, rows), BF16),
+                [pltpu.VMEM((half, rows), BF16)], 10 * rows * half, mine[layer], partners[layer],
+            )
+
+    def far_rows(layer):
+        if fast:
+            far_shifted[layer] = sequence.call(
+                functools.partial(far_kernel, layer), "far_rows", [0], struct(triple, BF16), [],
+                10 * rows * half, far[layer],
+            )
 
     def weights(layer):
         if not fast:
@@ -467,10 +502,9 @@
         pieces = counts[layer]
         piece = struct((channels // 4 // pieces, taps * half), BF16)
         out = sequence.call(
-            functools.partial(paired_weight_kernel, layer, pieces), "paired_weight", [0] * 6,
-            [piece] * (2 * pieces),
-            [pltpu.VMEM((half, 2 * rows), BF16), pltpu.VMEM((half, rows), BF16), pltpu.VMEM(triple, BF16)],
-            2 * flops, mine[layer], partners[layer], shifted[layer], across[layer], across_other[layer], far[layer],
+            functools.partial(paired_weight_kernel, pieces, across[layer][1]), "paired_weight", [0] * 5,
+            [piece] * (2 * pieces), [pltpu.VMEM((half, rows), BF16)], 2 * flops,
+            own_turned[layer], shifted[layer], across[layer][0], across_other[layer], far_shifted[layer],
         )
         for part in range(pieces):
             got[layer, part] = swap(out[part], "dp", lambda i: i ^ 1)
@@ -490,7 +524,7 @@
             return
         keep, came, last = kept[layer, part], got[layer, part], late[layer, part]
         summed[layer, part] = sequence.call(
-            total_kernel, "total", [0] * 3, struct(last.shape, BF16), [], keep.size, keep, came, last
+            total_kernel, "total", [0] * 3, struct(last.shape, BF16), [], 2 * flops, keep, came, last
         )
         crossed[layer, part] = across_replica(summed[layer, part])
 
@@ -506,6 +540,39 @@
     mine.append(snaked)
     partners[0] = across_chan(snaked)
     rounded[layers] = grad
+    depth = channels // lax.axis_size("dp")
+
+    def finish(chosen, before=None):
+        pairs = [] if before is None else [before]
+        for layer in chosen:
+            for part in range(counts[layer]):
+                pairs += [summed[layer, part], crossed[layer, part]]
+        return sequence.call(
+            functools.partial(finish_kernel, fast, before is not None, tuple((layer, counts[layer]) for layer in chosen)),
+            "finish", [2] * (before is not None) + [0] * (len(pairs) - (before is not None)),
+            struct((layers, taps, depth, half), F32),
+            [pltpu.VMEM((len(chosen), taps, depth, half), F32), DMA((len(chosen),))],
+            layers * taps * depth * half, *pairs, spec=ANY_HBM, aliases={0: 0} if before is not None else None,
+        )
+
+    rounds = [("replica", 1 << bit) for bit in range(8) if lax.axis_size("replica") >> (bit + 1)]
+    rounds += [("dp", 1 << bit) for bit in range(8) if lax.axis_size("dp") >> (bit + 1)]
+    arrivals = []
+
+    def alpha_round():
+        if arrivals:
+            value = sequence.call(
+                add_kernel, "add", [0, 0], struct((layers, half), F32), [], layers * half, *arrivals.pop()
+            )
+        else:
+            value = sequence.call(
+                stack_kernel, "stack", [0] * layers, struct((layers, half), F32), [], layers * half, *alpha_parts
+            )
+        if not rounds:
+            return value
+        axis, apart = rounds.pop(0)
+        arrivals.append((value, swap(value, axis, lambda place: place ^ apart)))
+
     send_gradient(2)
     back_partner(2)
     forward_own(0)
@@ -516,42 +583,40 @@
     turn(2)
     grad = combine(2, grad)
     send_gradient(1)
-    turn(1)
+    far_rows(2)
+    own_rows(2)
+    turn(1, 0)
     back_partner(1)
+    share(2)
     back_own(1)
-    share(2)
     combine(1, grad)
+    back_partner(0)
     weights(2)
-    back_partner(0)
+    own_rows(1)
+    back_own(0)
+    own_rows(0)
+    combine(0, None)
     forward_own(2)
-    back_own(0)
-    share(1)
-    combine(0, None)
-    alpha_grads = sum_rounds(jnp.concatenate(alpha_parts), "replica", sequence)
     residual_out = forward_partner(2)
+    far_rows(1)
+    share(1, 0)
+    send_gradient(0)
+    fold(2)
     weights(1)
-    send_gradient(0)
-    turn(0)
-    fold(2)
-    share(0)
+    total(2)
+    fold(1)
+    far_rows(0)
+    alpha_round()
     weights(0)
-    total(2)
-    alpha_grads = sum_rounds(alpha_grads, "dp", sequence)
-    fold(1)
-    for part in range(counts[0]):
-        fold(0, part)
     total(1)
-    for part in range(counts[0]):
-        total(0, part)
-    pairs = []
-    for layer in range(layers):
-        for part in range(counts[layer]):
-            pairs += [summed[layer, part], crossed[layer, part]]
-    depth = channels // lax.axis_size("dp")
-    weight_grads = sequence.call(
-        functools.partial(finish_kernel, fast, tuple(counts)), "finish", [0] * len(pairs),
-        struct((layers, taps, depth, half), F32), [], layers * taps * depth * half, *pairs,
-    )
+    alpha_round()
+    fold(0)
+    weight_grads = finish((2, 1))
+    alpha_grads = alpha_round()
+    total(0)
+    while alpha_grads is None:
+        alpha_grads = alpha_round()
+    weight_grads = finish((0,), weight_grads)
     return (residual_out, weight_grads, alpha_grads)
 
 

time: 97.2 us -> 96.2 us (0.990)
  starting transfers between devices: 32.9 us -> 29.4 us
  Pallas kernels: 28.6 us -> 30.7 us
    ppermute x30 -> x25, starting transfers between devices: 32.9 us -> 29.4 us  [swap(): lax.ppermute(x, axis, [(i, other(i)) for i in range(lax.axis_size(axis))])]
    pallas_call x31 -> x39, Pallas kernels: 28.6 us -> 30.7 us  [call(): pl.pallas_call(kernel, in_specs=[ANY_HBM if i else IN_VMEM for i in ins],...]
    ppermute x30 -> x25, waiting for transfers between devices: 34 us -> 34.9 us  [swap(): lax.ppermute(x, axis, [(i, other(i)) for i in range(lax.axis_size(axis))])]
  transfers between devices with their start and end apart: 30 -> 25, of which waited for: 14 -> 9; matrix products, arithmetic and copies ran while one was open for 1% -> 0% of each run, Pallas kernels for 24% -> 27%
where the time goes in v5:
time: 96.2 us; the launch traced here: 96.1 us
  waiting for transfers between devices  34.9 us (36%)
  Pallas kernels  30.7 us (32%)
  starting transfers between devices  29.4 us (31%)
  between operations  1.09 us (1%)
    ppermute x25, waiting for transfers between devices, swap(): lax.ppermute(x, axis, [(i, other(i)) for i in range(lax.axis_size(axis))])  34.9 us
    pallas_call x39, Pallas kernels, call(): pl.pallas_call(kernel, in_specs=[ANY_HBM if i else IN_VMEM for i in ins],...  30.7 us
    ppermute x25, starting transfers between devices, swap(): lax.ppermute(x, axis, [(i, other(i)) for i in range(lax.axis_size(axis))])  29.4 us
  transfers between devices with their start and end apart: 25, of which 9 were waited for; matrix products, arithmetic and copies ran while one was open for 0% of the time, Pallas kernels for 27%

profile of v5, /device:TPU:0, one launch (start us, length us, event | category | flops | bytes accessed | tf_op | source)
XLA Modules:
  0.0 96.1 jit_solution(8942402489887479273)
XLA Ops:
  0.6 3.7 %prep.1 = (f32[512,384]{1,0:T(8,128)S(1)}, bf16[512,384]{1,0:T(8,128)(2,1)S(1)}, bf16[512,384]{1,0:T(8,128)(2,1)S(1)}, f32[512,128]{1,0:T(8,128)S(1)}, f32[3,384...) custom-call(s32[16]{0:T(128)} %len_hbm.1, s32[16]{0:T(128)} %own_hbm.1, s32[16]{0:T(128)} %start_hbm.1, ...), custom_call_target="tpu_custom_call" | custom-call | flops 78643200 | bytes 79392640 | tf_op jit(solution)/shard_map/prep/pallas_call | solution.py:367
  4.9 2.6 %collective-permute-start.4 = (bf16[512,384]{1,0:T(8,128)(2,1)S(1)}, bf16[512,384]{1,0:T(8,128)(2,1)S(1)}, u32[]{:S(2)}, u32[]{:S(2)}) collective-permute-start(bf16[512,384]{1,0:T(8,128)(2,1)S(1)} %get-tuple-element.74.grad_ref.rest_0_), channel_id=1, source_target_pairs={{0,2},{2,0},{1,3},{3,1},{4,6},{6,4},{5,7},{7,5},{8,10},{10,8},{9,1... | collective-permute-start | bytes 1179656 | tf_op jit(solution)/shard_map/ppermute | solution.py:383
  9.4 1.7 %forward_partner.3 = (f32[512,384]{1,0:T(8,128)S(1)}, bf16[512,384]{1,0:T(8,128)(2,1)S(1)}) custom-call(bf16[512,384]{1,0:T(8,128)(2,1)S(1)} %collective-permute-done.snake_ref.partner_ref, bf16[3,2,1152,384]{3,2,1,0:T(8,128)(2,1)S(1)} %get-tuple-element.75.weight_ref, f32[512,384]{1,0:T(8,128)S(1)} %forward_own.3.own_ref, ...), custom_call_target="tpu_custom_call" | custom-call | flops 4529848320 | bytes 34124800 | tf_op jit(solution)/shard_map/forward_partner/pallas_call | solution.py:367
  13.3 1.8 %forward_partner.4 = (f32[512,384]{1,0:T(8,128)S(1)}, bf16[512,384]{1,0:T(8,128)(2,1)S(1)}) custom-call(bf16[512,384]{1,0:T(8,128)(2,1)S(1)} %collective-permute-done.1.snake_ref.partner_ref, bf16[3,2,1152,384]{3,2,1,0:T(8,128)(2,1)S(1)} %get-tuple-element.75.weight_ref, f32[512,384]{1,0:T(8,128)S(1)} %forward_own.4.own_ref, ...), custom_call_target="tpu_custom_call" | custom-call | flops 4529848320 | bytes 34124800 | tf_op jit(solution)/shard_map/forward_partner/pallas_call | solution.py:367
  15.8 1.6 %combine.3 = (f32[1,384]{1,0:T(1,128)S(1)}, f32[512,384]{1,0:T(8,128)S(1)}, bf16[512,384]{1,0:T(8,128)(2,1)S(1)}) custom-call(f32[512,384]{1,0:T(8,128)S(1)} %back_own.3.own_ref, bf16[512,384]{1,0:T(8,128)(2,1)S(1)} %collective-permute-done.3.partner_ref, f32[512,384]{1,0:T(8,128)S(1)} %get-tuple-element.87.stream_ref.old_ref, ...), custom_call_target="tpu_custom_call" | custom-call | flops 117964800 | bytes 38072320 | tf_op jit(solution)/shard_map/combine/pallas_call | solution.py:367
  17.6 1.8 %collective-permute-start.9 = (bf16[512,384]{1,0:T(8,128)(2,1)S(1)}, bf16[512,384]{1,0:T(8,128)(2,1)S(1)}, u32[]{:S(2)}, u32[]{:S(2)}) collective-permute-start(bf16[512,384]{1,0:T(8,128)(2,1)S(1)} %get-tuple-element.116.grad_ref), channel_id=1, source_target_pairs={{0,2},{2,0},{1,3},{3,1},{4,6},{6,4},{5,7},{7,5},{8,10},{10,8},{9,1... | collective-permute-start | bytes 1179656 | tf_op jit(solution)/shard_map/ppermute | solution.py:383
  20.3 0.9 back_partner.4
  22.2 1.0 %collective-permute-done.6.across_ref = bf16[192,512]{1,0:T(8,128)(2,1)S(1)} collective-permute-done((bf16[192,512]{1,0:T(8,128)(2,1)S(1)}, bf16[192,512]{1,0:T(8,128)(2,1)S(1)}, u32[]{:S(2)}, u32[]{:S(2)}) %collective-permute-start.6) | collective-permute-done | bytes 196640 | tf_op jit(solution)/shard_map/ppermute | solution.py:383
  23.2 1.7 %combine.4 = (f32[1,384]{1,0:T(1,128)S(1)}, bf16[512,384]{1,0:T(8,128)(2,1)S(1)}) custom-call(f32[512,384]{1,0:T(8,128)S(1)} %back_own.4.own_ref, bf16[512,384]{1,0:T(8,128)(2,1)S(1)} %collective-permute-done.5.partner_ref, f32[512,384]{1,0:T(8,128)S(1)} %get-tuple-element.82.old_ref.stream_ref, f32[3,384]{1,0:T(4,128)S(1)} %get-tuple-element.80.rest_0_.alphas_ref, ...), custom_call_target="tpu_custom_call" | custom-call | flops 117964800 | bytes 34140160 | tf_op jit(solution)/shard_map/combine/pallas_call | solution.py:367
  25.9 1.4 %paired_weight.3 = (bf16[192,1152]{1,0:T(8,128)(2,1)S(1)}, bf16[192,1152]{1,0:T(8,128)(2,1)S(1)}) custom-call(bf16[384,512]{1,0:T(8,128)(2,1)S(1)} %own_rows.3.own_ref, bf16[512,1152]{1,0:T(8,128)(2,1)S(1)} %get-tuple-element.83.shifted_ref, bf16[192,512]{1,0:T(8,128)(2,1)S(1)} %collective-permute-done.6.across_ref, ...), custom_call_target="tpu_custom_call" | custom-call | flops 9059696640 | bytes 40304640 | tf_op jit(solution)/shard_map/paired_weight/pallas_call | solution.py:367
  27.3 1.7 %collective-permute-start.10 = (bf16[192,1152]{1,0:T(8,128)(2,1)S(1)}, bf16[192,1152]{1,0:T(8,128)(2,1)S(1)}, u32[]{:S(2)}, u32[]{:S(2)}) collective-permute-start(bf16[192,1152]{1,0:T(8,128)(2,1)S(1)} %get-tuple-element.107), channel_id=1, source_target_pairs={{0,4},{4,0},{8,12},{12,8},{1,5},{5,1},{9,13},{13,9},{2,6},{6,2},{1... | collective-permute-start | bytes 1327112 | tf_op jit(solution)/shard_map/ppermute | solution.py:383
  31.0 1.4 %combine.5.refs_0_ = f32[1,384]{1,0:T(1,128)S(1)} custom-call(f32[512,384]{1,0:T(8,128)S(1)} %back_own.5.own_ref, bf16[512,384]{1,0:T(8,128)(2,1)S(1)} %collective-permute-done.8.partner_ref, f32[512,384]{1,0:T(8,128)S(1)} %get-tuple-element.73.old_ref.stream_ref, f32[3,384]{1,0:T(4,128)S(1)} %get-tuple-element.80.rest_0_.alphas_ref), custom_call_target="tpu_custom_call" | custom-call | flops 117964800 | bytes 19722240 | tf_op jit(solution)/shard_map/combine/pallas_call | solution.py:367
  33.3 1.6 %forward_partner.5 = bf16[512,384]{1,0:T(8,128)(2,1)} custom-call(bf16[512,384]{1,0:T(8,128)(2,1)S(1)} %collective-permute-done.2.partner_ref.snake_ref, bf16[3,2,1152,384]{3,2,1,0:T(8,128)(2,1)S(1)} %get-tuple-element.75.weight_ref, f32[512,384]{1,0:T(8,128)S(1)} %forward_own.5.own_ref, f32[512,384]{1,0:T(8,128)S(1)} %get-tuple-element.87.stream_ref.old_ref, ...), custom_call_target="tpu_custom_call" | custom-call | flops 4529848320 | bytes 26214400 | tf_op jit(solution)/shard_map/forward_partner/pallas_call | solution.py:367
  35.1 4.4 %collective-permute-done.11.across_ref = bf16[384,512]{1,0:T(8,128)(2,1)S(1)} collective-permute-done((bf16[384,512]{1,0:T(8,128)(2,1)S(1)}, bf16[384,512]{1,0:T(8,128)(2,1)S(1)}, u32[]{:S(2)}, u32[]{:S(2)}) %collective-permute-start.11) | collective-permute-done | bytes 393248 | tf_op jit(solution)/shard_map/ppermute | solution.py:383
  40.0 3.7 %collective-permute-start.13 = (bf16[96,1152]{1,0:T(8,128)(2,1)S(1)}, bf16[96,1152]{1,0:T(8,128)(2,1)S(1)}, u32[]{:S(2)}, u32[]{:S(2)}) collective-permute-start(bf16[96,1152]{1,0:T(8,128)(2,1)S(1)} %fold.3), channel_id=1, source_target_pairs={{0,12},{4,8},{8,4},{12,0},{1,13},{5,9},{9,5},{13,1},{2,14},{6,10},... | collective-permute-start | bytes 663560 | tf_op jit(solution)/shard_map/ppermute | solution.py:383
  43.8 1.4 %paired_weight.4 = (bf16[192,1152]{1,0:T(8,128)(2,1)S(1)}, bf16[192,1152]{1,0:T(8,128)(2,1)S(1)}) custom-call(bf16[384,512]{1,0:T(8,128)(2,1)S(1)} %own_rows.4.own_ref, bf16[512,1152]{1,0:T(8,128)(2,1)S(1)} %get-tuple-element.98.shifted_ref, bf16[384,512]{1,0:T(8,128)(2,1)S(1)} %collective-permute-done.11.across_ref, ...), custom_call_target="tpu_custom_call" | custom-call | flops 9059696640 | bytes 44236800 | tf_op jit(solution)/shard_map/paired_weight/pallas_call | solution.py:367
  45.2 4.9 %collective-permute-done.13.late = bf16[96,1152]{1,0:T(8,128)(2,1)S(1)} collective-permute-done((bf16[96,1152]{1,0:T(8,128)(2,1)S(1)}, bf16[96,1152]{1,0:T(8,128)(2,1)S(1)}, u32[]{:S(2)}, u32[]{:S(2)}) %collective-permute-start.13) | collective-permute-done | bytes 221216 | tf_op jit(solution)/shard_map/ppermute | solution.py:383
  50.3 1.6 %collective-permute-start.19 = (bf16[96,1152]{1,0:T(8,128)(2,1)S(1)}, bf16[96,1152]{1,0:T(8,128)(2,1)S(1)}, u32[]{:S(2)}, u32[]{:S(2)}) collective-permute-start(bf16[96,1152]{1,0:T(8,128)(2,1)S(1)} %total.3.refs_0_), channel_id=1, source_target_pairs={{0,2},{2,0},{1,3},{3,1},{4,6},{6,4},{5,7},{7,5},{8,10},{10,8},{9,1... | collective-permute-start | bytes 663560 | tf_op jit(solution)/shard_map/ppermute | solution.py:383
  51.9 7.3 %collective-permute-done.15.got = bf16[192,1152]{1,0:T(8,128)(2,1)S(1)} collective-permute-done((bf16[192,1152]{1,0:T(8,128)(2,1)S(1)}, bf16[192,1152]{1,0:T(8,128)(2,1)S(1)}, u32[]{:S(2)}, u32[]{:S(2)}) %collective-permute-start.15) | collective-permute-done | bytes 442400 | tf_op jit(solution)/shard_map/ppermute | solution.py:383
  59.2 3.6 %collective-permute-start.16 = (bf16[96,1152]{1,0:T(8,128)(2,1)S(1)}, bf16[96,1152]{1,0:T(8,128)(2,1)S(1)}, u32[]{:S(2)}, u32[]{:S(2)}) collective-permute-start(bf16[96,1152]{1,0:T(8,128)(2,1)S(1)} %fold.4), channel_id=1, source_target_pairs={{0,12},{4,8},{8,4},{12,0},{1,13},{5,9},{9,5},{13,1},{2,14},{6,10},... | collective-permute-start | bytes 663560 | tf_op jit(solution)/shard_map/ppermute | solution.py:383
  63.1 1.1 %collective-permute-start.17 = (f32[3,384]{1,0:T(4,128)S(1)}, f32[3,384]{1,0:T(4,128)S(1)}, u32[]{:S(2)}, u32[]{:S(2)}) collective-permute-start(f32[3,384]{1,0:T(4,128)S(1)} %stack.1.left), channel_id=1, source_target_pairs={{0,2},{2,0},{1,3},{3,1},{4,6},{6,4},{5,7},{7,5},{8,10},{10,8},{9,1... | collective-permute-start | bytes 13832 | tf_op jit(solution)/shard_map/ppermute | solution.py:383
  64.2 1.4 %paired_weight.5 = (bf16[192,1152]{1,0:T(8,128)(2,1)S(1)}, bf16[192,1152]{1,0:T(8,128)(2,1)S(1)}) custom-call(bf16[384,512]{1,0:T(8,128)(2,1)S(1)} %own_rows.5.own_ref, bf16[512,1152]{1,0:T(8,128)(2,1)S(1)} %get-tuple-element.109.shifted_ref, bf16[384,512]{1,0:T(8,128)(2,1)S(1)} %collective-permute-done.11.across_ref, ...), custom_call_target="tpu_custom_call" | custom-call | flops 9059696640 | bytes 44236800 | tf_op jit(solution)/shard_map/paired_weight/pallas_call | solution.py:367
  65.7 3.7 %collective-permute-done.16.late = bf16[96,1152]{1,0:T(8,128)(2,1)S(1)} collective-permute-done((bf16[96,1152]{1,0:T(8,128)(2,1)S(1)}, bf16[96,1152]{1,0:T(8,128)(2,1)S(1)}, u32[]{:S(2)}, u32[]{:S(2)}) %collective-permute-start.16) | collective-permute-done | bytes 221216 | tf_op jit(solution)/shard_map/ppermute | solution.py:383
  69.5 1.6 %collective-permute-start.20 = (bf16[96,1152]{1,0:T(8,128)(2,1)S(1)}, bf16[96,1152]{1,0:T(8,128)(2,1)S(1)}, u32[]{:S(2)}, u32[]{:S(2)}) collective-permute-start(bf16[96,1152]{1,0:T(8,128)(2,1)S(1)} %total.4.refs_2_), channel_id=1, source_target_pairs={{0,2},{2,0},{1,3},{3,1},{4,6},{6,4},{5,7},{7,5},{8,10},{10,8},{9,1... | collective-permute-start | bytes 663560 | tf_op jit(solution)/shard_map/ppermute | solution.py:383
  71.1 7.0 %collective-permute-done.18.got = bf16[192,1152]{1,0:T(8,128)(2,1)S(1)} collective-permute-done((bf16[192,1152]{1,0:T(8,128)(2,1)S(1)}, bf16[192,1152]{1,0:T(8,128)(2,1)S(1)}, u32[]{:S(2)}, u32[]{:S(2)}) %collective-permute-start.18) | collective-permute-done | bytes 442400 | tf_op jit(solution)/shard_map/ppermute | solution.py:383
  78.1 3.6 %collective-permute-start.22 = (bf16[96,1152]{1,0:T(8,128)(2,1)S(1)}, bf16[96,1152]{1,0:T(8,128)(2,1)S(1)}, u32[]{:S(2)}, u32[]{:S(2)}) collective-permute-start(bf16[96,1152]{1,0:T(8,128)(2,1)S(1)} %fold.5), channel_id=1, source_target_pairs={{0,12},{4,8},{8,4},{12,0},{1,13},{5,9},{9,5},{13,1},{2,14},{6,10},... | collective-permute-start | bytes 663560 | tf_op jit(solution)/shard_map/ppermute | solution.py:383
  81.7 1.3 %finish.2.refs_0_ = f32[3,3,192,384]{3,2,1,0:T(8,128)} custom-call(bf16[96,1152]{1,0:T(8,128)(2,1)S(1)} %total.3.refs_0_, bf16[96,1152]{1,0:T(8,128)(2,1)S(1)} %collective-permute-done.19.refs_1_, bf16[96,1152]{1,0:T(8,128)(2,1)S(1)} %total.4.refs_2_, bf16[96,1152]{1,0:T(8,128)(2,1)S(1)} %collective-permute-done.20.refs_3_), custom_call_target="tpu_custom_call" | custom-call | flops 6635520 | bytes 35389440 | tf_op jit(solution)/shard_map/finish/pallas_call | solution.py:367
  83.0 4.5 %collective-permute-done.21.right = f32[3,384]{1,0:T(4,128)S(1)} collective-permute-done((f32[3,384]{1,0:T(4,128)S(1)}, f32[3,384]{1,0:T(4,128)S(1)}, u32[]{:S(2)}, u32[]{:S(2)}) %collective-permute-start.21) | collective-permute-done | bytes 4640 | tf_op jit(solution)/shard_map/ppermute | solution.py:383
  87.6 1.0 %collective-permute-start.24 = (bf16[96,1152]{1,0:T(8,128)(2,1)S(1)}, bf16[96,1152]{1,0:T(8,128)(2,1)S(1)}, u32[]{:S(2)}, u32[]{:S(2)}) collective-permute-start(bf16[96,1152]{1,0:T(8,128)(2,1)S(1)} %total.5.refs_1_), channel_id=1, source_target_pairs={{0,2},{2,0},{1,3},{3,1},{4,6},{6,4},{5,7},{7,5},{8,10},{10,8},{9,1... | collective-permute-start | bytes 663560 | tf_op jit(solution)/shard_map/ppermute | solution.py:383
  88.7 4.0 %collective-permute-start.23 = (f32[3,384]{1,0:T(4,128)S(1)}, f32[3,384]{1,0:T(4,128)S(1)}, u32[]{:S(2)}, u32[]{:S(2)}) collective-permute-start(f32[3,384]{1,0:T(4,128)S(1)} %add.4.left), channel_id=1, source_target_pairs={{0,8},{4,12},{8,0},{12,4},{1,9},{5,13},{9,1},{13,5},{2,10},{6,14},... | collective-permute-start | bytes 13832 | tf_op jit(solution)/shard_map/ppermute | solution.py:383
  92.7 1.6 %collective-permute-done.23.right = f32[3,384]{1,0:T(4,128)S(1)} collective-permute-done((f32[3,384]{1,0:T(4,128)S(1)}, f32[3,384]{1,0:T(4,128)S(1)}, u32[]{:S(2)}, u32[]{:S(2)}) %collective-permute-start.23) | collective-permute-done | bytes 4640 | tf_op jit(solution)/shard_map/ppermute | solution.py:383
  94.9 1.0 %finish.3 = f32[3,3,192,384]{3,2,1,0:T(8,128)} custom-call(f32[3,3,192,384]{3,2,1,0:T(8,128)} %finish.2.refs_0_, bf16[96,1152]{1,0:T(8,128)(2,1)S(1)} %total.5.refs_1_, bf16[96,1152]{1,0:T(8,128)(2,1)S(1)} %collective-permute-done.24.refs_2_), custom_call_target="tpu_custom_call", output_to_operand_aliasing={{}: (0, {})} | custom-call | flops 6635520 | bytes 57507840 | tf_op jit(solution)/shard_map/finish/pallas_call | solution.py:367
  (57 shorter events, 13.3 us)
Async XLA Ops:
  4.3 5.0 %collective-permute-start = (bf16[512,384]{1,0:T(8,128)(2,1)S(1)}, bf16[512,384]{1,0:T(8,128)(2,1)S(1)}, u32[]{:S(2)}, u32[]{:S(2)}) collective-permute-start(bf16[512,384]{1,0:T(8,128)(2,1)S(1)} %get-tuple-element.110.snake_ref.refs_1_.own_ref), channel_id=1, source_target_pairs={{0,1},{1,0},{2,3},{3,2},{4,5},{5,4},{6,7},{7,6},{8,9},{9,8},{10,11... | collective-permute-start | bytes 1179656 | tf_op jit(solution)/shard_map/ppermute | solution.py:383
  4.9 12.5 %collective-permute-start.4 = (bf16[512,384]{1,0:T(8,128)(2,1)S(1)}, bf16[512,384]{1,0:T(8,128)(2,1)S(1)}, u32[]{:S(2)}, u32[]{:S(2)}) collective-permute-start(bf16[512,384]{1,0:T(8,128)(2,1)S(1)} %get-tuple-element.74.grad_ref.rest_0_), channel_id=1, source_target_pairs={{0,2},{2,0},{1,3},{3,1},{4,6},{6,4},{5,7},{7,5},{8,10},{10,8},{9,1... | collective-permute-start | bytes 1179656 | tf_op jit(solution)/shard_map/ppermute | solution.py:383
  8.3 7.4 %collective-permute-start.3 = (bf16[512,384]{1,0:T(8,128)(2,1)S(1)}, bf16[512,384]{1,0:T(8,128)(2,1)S(1)}, u32[]{:S(2)}, u32[]{:S(2)}) collective-permute-start(bf16[512,384]{1,0:T(8,128)(2,1)S(1)} %get-tuple-element.90), channel_id=1, source_target_pairs={{0,1},{1,0},{2,3},{3,2},{4,5},{5,4},{6,7},{7,6},{8,9},{9,8},{10,11... | collective-permute-start | bytes 1179656 | tf_op jit(solution)/shard_map/ppermute | solution.py:383
  11.1 2.1 %collective-permute-start.1 = (bf16[512,384]{1,0:T(8,128)(2,1)S(1)}, bf16[512,384]{1,0:T(8,128)(2,1)S(1)}, u32[]{:S(2)}, u32[]{:S(2)}) collective-permute-start(bf16[512,384]{1,0:T(8,128)(2,1)S(1)} %get-tuple-element.108.snake_ref.refs_0_.own_ref), channel_id=1, source_target_pairs={{0,1},{1,0},{2,3},{3,2},{4,5},{5,4},{6,7},{7,6},{8,9},{9,8},{10,11... | collective-permute-start | bytes 1179656 | tf_op jit(solution)/shard_map/ppermute | solution.py:383
  15.0 4.4 %collective-permute-start.2 = (bf16[512,384]{1,0:T(8,128)(2,1)S(1)}, bf16[512,384]{1,0:T(8,128)(2,1)S(1)}, u32[]{:S(2)}, u32[]{:S(2)}) collective-permute-start(bf16[512,384]{1,0:T(8,128)(2,1)S(1)} %get-tuple-element.113.refs_0_.own_ref.snake_ref), channel_id=1, source_target_pairs={{0,1},{1,0},{2,3},{3,2},{4,5},{5,4},{6,7},{7,6},{8,9},{9,8},{10,11... | collective-permute-start | bytes 1179656 | tf_op jit(solution)/shard_map/ppermute | solution.py:383
  15.4 7.8 %collective-permute-start.6 = (bf16[192,512]{1,0:T(8,128)(2,1)S(1)}, bf16[192,512]{1,0:T(8,128)(2,1)S(1)}, u32[]{:S(2)}, u32[]{:S(2)}) collective-permute-start(bf16[192,512]{1,0:T(8,128)(2,1)S(1)} %turn.2), channel_id=1, source_target_pairs={{0,2},{2,0},{1,3},{3,1},{4,6},{6,4},{5,7},{7,5},{8,10},{10,8},{9,1... | collective-permute-start | bytes 589832 | tf_op jit(solution)/shard_map/ppermute | solution.py:383
  17.6 17.3 %collective-permute-start.9 = (bf16[512,384]{1,0:T(8,128)(2,1)S(1)}, bf16[512,384]{1,0:T(8,128)(2,1)S(1)}, u32[]{:S(2)}, u32[]{:S(2)}) collective-permute-start(bf16[512,384]{1,0:T(8,128)(2,1)S(1)} %get-tuple-element.116.grad_ref), channel_id=1, source_target_pairs={{0,2},{2,0},{1,3},{3,1},{4,6},{6,4},{5,7},{7,5},{8,10},{10,8},{9,1... | collective-permute-start | bytes 1179656 | tf_op jit(solution)/shard_map/ppermute | solution.py:383
  20.0 19.5 %collective-permute-start.11 = (bf16[384,512]{1,0:T(8,128)(2,1)S(1)}, bf16[384,512]{1,0:T(8,128)(2,1)S(1)}, u32[]{:S(2)}, u32[]{:S(2)}) collective-permute-start(bf16[384,512]{1,0:T(8,128)(2,1)S(1)} %turn.3), channel_id=1, source_target_pairs={{0,2},{2,0},{1,3},{3,1},{4,6},{6,4},{5,7},{7,5},{8,10},{10,8},{9,1... | collective-permute-start | bytes 1179656 | tf_op jit(solution)/shard_map/ppermute | solution.py:383
  21.2 2.0 %collective-permute-start.5 = (bf16[512,384]{1,0:T(8,128)(2,1)S(1)}, bf16[512,384]{1,0:T(8,128)(2,1)S(1)}, u32[]{:S(2)}, u32[]{:S(2)}) collective-permute-start(bf16[512,384]{1,0:T(8,128)(2,1)S(1)} %get-tuple-element.99), channel_id=1, source_target_pairs={{0,1},{1,0},{2,3},{3,2},{4,5},{5,4},{6,7},{7,6},{8,9},{9,8},{10,11... | collective-permute-start | bytes 1179656 | tf_op jit(solution)/shard_map/ppermute | solution.py:383
  23.2 2.6 %collective-permute-start.7 = (bf16[192,512]{1,0:T(8,128)(2,1)S(1)}, bf16[192,512]{1,0:T(8,128)(2,1)S(1)}, u32[]{:S(2)}, u32[]{:S(2)}) collective-permute-start(bf16[192,512]{1,0:T(8,128)(2,1)S(1)} %collective-permute-done.6.across_ref), channel_id=1, source_target_pairs={{0,1},{1,0},{2,3},{3,2},{4,5},{5,4},{6,7},{7,6},{8,9},{9,8},{10,11... | collective-permute-start | bytes 589832 | tf_op jit(solution)/shard_map/ppermute | solution.py:383
  27.3 12.7 %collective-permute-start.10 = (bf16[192,1152]{1,0:T(8,128)(2,1)S(1)}, bf16[192,1152]{1,0:T(8,128)(2,1)S(1)}, u32[]{:S(2)}, u32[]{:S(2)}) collective-permute-start(bf16[192,1152]{1,0:T(8,128)(2,1)S(1)} %get-tuple-element.107), channel_id=1, source_target_pairs={{0,4},{4,0},{8,12},{12,8},{1,5},{5,1},{9,13},{13,9},{2,6},{6,2},{1... | collective-permute-start | bytes 1327112 | tf_op jit(solution)/shard_map/ppermute | solution.py:383
  29.2 1.8 %collective-permute-start.8 = (bf16[512,384]{1,0:T(8,128)(2,1)S(1)}, bf16[512,384]{1,0:T(8,128)(2,1)S(1)}, u32[]{:S(2)}, u32[]{:S(2)}) collective-permute-start(bf16[512,384]{1,0:T(8,128)(2,1)S(1)} %get-tuple-element.112), channel_id=1, source_target_pairs={{0,1},{1,0},{2,3},{3,2},{4,5},{5,4},{6,7},{7,6},{8,9},{9,8},{10,11... | collective-permute-start | bytes 1179656 | tf_op jit(solution)/shard_map/ppermute | solution.py:383
  39.5 4.3 %collective-permute-start.12 = (bf16[384,512]{1,0:T(8,128)(2,1)S(1)}, bf16[384,512]{1,0:T(8,128)(2,1)S(1)}, u32[]{:S(2)}, u32[]{:S(2)}) collective-permute-start(bf16[384,512]{1,0:T(8,128)(2,1)S(1)} %collective-permute-done.11.across_ref), channel_id=1, source_target_pairs={{0,1},{1,0},{2,3},{3,2},{4,5},{5,4},{6,7},{7,6},{8,9},{9,8},{10,11... | collective-permute-start | bytes 1179656 | tf_op jit(solution)/shard_map/ppermute | solution.py:383
  39.5 23.3 %collective-permute-start.14 = (bf16[512,384]{1,0:T(8,128)(2,1)S(1)}, bf16[512,384]{1,0:T(8,128)(2,1)S(1)}, u32[]{:S(2)}, u32[]{:S(2)}) collective-permute-start(bf16[512,384]{1,0:T(8,128)(2,1)S(1)} %get-tuple-element.123.grad_ref), channel_id=1, source_target_pairs={{0,2},{2,0},{1,3},{3,1},{4,6},{6,4},{5,7},{7,5},{8,10},{10,8},{9,1... | collective-permute-start | bytes 1179656 | tf_op jit(solution)/shard_map/ppermute | solution.py:383
  40.0 10.2 %collective-permute-start.13 = (bf16[96,1152]{1,0:T(8,128)(2,1)S(1)}, bf16[96,1152]{1,0:T(8,128)(2,1)S(1)}, u32[]{:S(2)}, u32[]{:S(2)}) collective-permute-start(bf16[96,1152]{1,0:T(8,128)(2,1)S(1)} %fold.3), channel_id=1, source_target_pairs={{0,12},{4,8},{8,4},{12,0},{1,13},{5,9},{9,5},{13,1},{2,14},{6,10},... | collective-permute-start | bytes 663560 | tf_op jit(solution)/shard_map/ppermute | solution.py:383
  45.2 14.0 %collective-permute-start.15 = (bf16[192,1152]{1,0:T(8,128)(2,1)S(1)}, bf16[192,1152]{1,0:T(8,128)(2,1)S(1)}, u32[]{:S(2)}, u32[]{:S(2)}) collective-permute-start(bf16[192,1152]{1,0:T(8,128)(2,1)S(1)} %get-tuple-element.121), channel_id=1, source_target_pairs={{0,4},{4,0},{8,12},{12,8},{1,5},{5,1},{9,13},{13,9},{2,6},{6,2},{1... | collective-permute-start | bytes 1327112 | tf_op jit(solution)/shard_map/ppermute | solution.py:383
  50.3 31.4 %collective-permute-start.19 = (bf16[96,1152]{1,0:T(8,128)(2,1)S(1)}, bf16[96,1152]{1,0:T(8,128)(2,1)S(1)}, u32[]{:S(2)}, u32[]{:S(2)}) collective-permute-start(bf16[96,1152]{1,0:T(8,128)(2,1)S(1)} %total.3.refs_0_), channel_id=1, source_target_pairs={{0,2},{2,0},{1,3},{3,1},{4,6},{6,4},{5,7},{7,5},{8,10},{10,8},{9,1... | collective-permute-start | bytes 663560 | tf_op jit(solution)/shard_map/ppermute | solution.py:383
  59.2 10.2 %collective-permute-start.16 = (bf16[96,1152]{1,0:T(8,128)(2,1)S(1)}, bf16[96,1152]{1,0:T(8,128)(2,1)S(1)}, u32[]{:S(2)}, u32[]{:S(2)}) collective-permute-start(bf16[96,1152]{1,0:T(8,128)(2,1)S(1)} %fold.4), channel_id=1, source_target_pairs={{0,12},{4,8},{8,4},{12,0},{1,13},{5,9},{9,5},{13,1},{2,14},{6,10},... | collective-permute-start | bytes 663560 | tf_op jit(solution)/shard_map/ppermute | solution.py:383
  63.1 8.0 %collective-permute-start.17 = (f32[3,384]{1,0:T(4,128)S(1)}, f32[3,384]{1,0:T(4,128)S(1)}, u32[]{:S(2)}, u32[]{:S(2)}) collective-permute-start(f32[3,384]{1,0:T(4,128)S(1)} %stack.1.left), channel_id=1, source_target_pairs={{0,2},{2,0},{1,3},{3,1},{4,6},{6,4},{5,7},{7,5},{8,10},{10,8},{9,1... | collective-permute-start | bytes 13832 | tf_op jit(solution)/shard_map/ppermute | solution.py:383
  65.6 12.4 %collective-permute-start.18 = (bf16[192,1152]{1,0:T(8,128)(2,1)S(1)}, bf16[192,1152]{1,0:T(8,128)(2,1)S(1)}, u32[]{:S(2)}, u32[]{:S(2)}) collective-permute-start(bf16[192,1152]{1,0:T(8,128)(2,1)S(1)} %get-tuple-element.130), channel_id=1, source_target_pairs={{0,4},{4,0},{8,12},{12,8},{1,5},{5,1},{9,13},{13,9},{2,6},{6,2},{1... | collective-permute-start | bytes 1327112 | tf_op jit(solution)/shard_map/ppermute | solution.py:383
  69.5 12.2 %collective-permute-start.20 = (bf16[96,1152]{1,0:T(8,128)(2,1)S(1)}, bf16[96,1152]{1,0:T(8,128)(2,1)S(1)}, u32[]{:S(2)}, u32[]{:S(2)}) collective-permute-start(bf16[96,1152]{1,0:T(8,128)(2,1)S(1)} %total.4.refs_2_), channel_id=1, source_target_pairs={{0,2},{2,0},{1,3},{3,1},{4,6},{6,4},{5,7},{7,5},{8,10},{10,8},{9,1... | collective-permute-start | bytes 663560 | tf_op jit(solution)/shard_map/ppermute | solution.py:383
  78.1 9.5 %collective-permute-start.22 = (bf16[96,1152]{1,0:T(8,128)(2,1)S(1)}, bf16[96,1152]{1,0:T(8,128)(2,1)S(1)}, u32[]{:S(2)}, u32[]{:S(2)}) collective-permute-start(bf16[96,1152]{1,0:T(8,128)(2,1)S(1)} %fold.5), channel_id=1, source_target_pairs={{0,12},{4,8},{8,4},{12,0},{1,13},{5,9},{9,5},{13,1},{2,14},{6,10},... | collective-permute-start | bytes 663560 | tf_op jit(solution)/shard_map/ppermute | solution.py:383
  81.7 5.8 %collective-permute-start.21 = (f32[3,384]{1,0:T(4,128)S(1)}, f32[3,384]{1,0:T(4,128)S(1)}, u32[]{:S(2)}, u32[]{:S(2)}) collective-permute-start(f32[3,384]{1,0:T(4,128)S(1)} %add.3.left), channel_id=1, source_target_pairs={{0,4},{4,0},{8,12},{12,8},{1,5},{5,1},{9,13},{13,9},{2,6},{6,2},{1... | collective-permute-start | bytes 13832 | tf_op jit(solution)/shard_map/ppermute | solution.py:383
  87.6 7.3 %collective-permute-start.24 = (bf16[96,1152]{1,0:T(8,128)(2,1)S(1)}, bf16[96,1152]{1,0:T(8,128)(2,1)S(1)}, u32[]{:S(2)}, u32[]{:S(2)}) collective-permute-start(bf16[96,1152]{1,0:T(8,128)(2,1)S(1)} %total.5.refs_1_), channel_id=1, source_target_pairs={{0,2},{2,0},{1,3},{3,1},{4,6},{6,4},{5,7},{7,5},{8,10},{10,8},{9,1... | collective-permute-start | bytes 663560 | tf_op jit(solution)/shard_map/ppermute | solution.py:383
  88.7 5.6 %collective-permute-start.23 = (f32[3,384]{1,0:T(4,128)S(1)}, f32[3,384]{1,0:T(4,128)S(1)}, u32[]{:S(2)}, u32[]{:S(2)}) collective-permute-start(f32[3,384]{1,0:T(4,128)S(1)} %add.4.left), channel_id=1, source_target_pairs={{0,8},{4,12},{8,0},{12,4},{1,9},{5,13},{9,1},{13,5},{2,10},{6,14},... | collective-permute-start | bytes 13832 | tf_op jit(solution)/shard_map/ppermute | solution.py:383

commit v6 on v5

--- a/solution.py
+++ b/solution.py
@@ -18,6 +18,7 @@
 COS_TERMS = (1.0 / 479001600, -1.0 / 3628800, 1.0 / 40320, -1.0 / 720, 1.0 / 24, -0.5)
 RANGE = 8192.0
 CHUNK = 64
+CARRIED = 16
 
 
 def horner(terms, x):
@@ -98,6 +99,19 @@
 def chan_begin(side, half):
     chan = lax.axis_index("chan")
     return pl.multiple_of((chan if side == 0 else 1 - chan) * half, half)
+
+
+def load_weights(layer, weight_hbm, weight_ref, sems):
+    half = weight_hbm.shape[3]
+    loads = []
+    for side in range(2):
+        for tap in range(3):
+            source = weight_hbm.at[layer, tap, pl.ds(chan_begin(side, half), half), :]
+            target = weight_ref.at[side, pl.ds(tap * half, half), :]
+            loads.append(pltpu.make_async_copy(source, target, sems.at[len(loads)]))
+    for copy in loads:
+        copy.start()
+    return loads
 
 
 def prep_kernel(
@@ -110,16 +124,9 @@
         (alpha_hbm, alpha_ref), (act_hbm, act_ref), (cot_hbm, cot_ref),
     )
     copies = [pltpu.make_async_copy(a, b, sems.at[i]) for i, (a, b) in enumerate(pairs)]
-    layers, taps, _, half = weight_hbm.shape
-    loads = []
-    for layer in range(layers):
-        for side in range(2):
-            for tap in range(taps):
-                source = weight_hbm.at[layer, tap, pl.ds(chan_begin(side, half), half), :]
-                target = weight_ref.at[layer, side, pl.ds(tap * half, half), :]
-                loads.append(pltpu.make_async_copy(source, target, weight_sems.at[len(loads)]))
-    for copy in copies + loads:
+    for copy in copies:
         copy.start()
+    loads = load_weights(0, weight_hbm, weight_ref, weight_sems)
     replicas = lax.axis_size("replica")
     device = lax.axis_index("dp") * replicas + lax.axis_index("replica")
     rows, width = act_ref.shape
@@ -147,32 +154,49 @@
         copy.wait()
 
 
-def forward_own_kernel(layer, snake_ref, weight_ref, out_ref, shifts_ref):
+def forward_own_kernel(layer, load, snake_ref, weight_ref, *rest):
+    if load is None:
+        out_ref, shifts_ref = rest
+        loads = []
+    else:
+        weight_hbm, out_ref, loaded_ref, shifts_ref, sems = rest
+        loads = load_weights(load, weight_hbm, loaded_ref, sems)
     write_shifts(snake_ref, shifts_ref, dilations[layer])
-    out_ref[...] = jnp.dot(shifts_ref[...], weight_ref[layer, 0], preferred_element_type=F32)
-
-
-def forward_partner_kernel(layer, last, snake_ref, weight_ref, own_ref, old_ref, live_ref, *rest):
-    if last:
-        result_ref, shifts_ref = rest
+    out_ref[...] = jnp.dot(shifts_ref[...], weight_ref[0], preferred_element_type=F32)
+    for copy in loads:
+        copy.wait()
+
+
+def forward_partner_kernel(layer, last, load, snake_ref, weight_ref, own_ref, old_ref, live_ref, *rest):
+    rest = list(rest)
+    alpha_ref = None if last else rest.pop(0)
+    weight_hbm = None if load is None else rest.pop(0)
+    result_ref = rest.pop(0)
+    next_ref = None if last else rest.pop(0)
+    loads = []
+    if load is not None:
+        loaded_ref, shifts_ref, sems = rest
+        loads = load_weights(load, weight_hbm, loaded_ref, sems)
     else:
-        alpha_ref, result_ref, next_ref, shifts_ref = rest
+        (shifts_ref,) = rest
     write_shifts(snake_ref, shifts_ref, dilations[layer])
-    part = jnp.dot(shifts_ref[...], weight_ref[layer, 1], preferred_element_type=F32)
+    part = jnp.dot(shifts_ref[...], weight_ref[1], preferred_element_type=F32)
     live = jnp.tile(live_ref[...], (1, old_ref.shape[1] // 128))
     new = (old_ref[...] + (own_ref[...] + part)) * live
     result_ref[...] = new.astype(result_ref.dtype)
     if not last:
         write_snake(result_ref, alpha_ref[layer + 1 : layer + 2, :], next_ref)
-
-
-def back_product(shifted_ref, weight_ref, layer, side):
-    half = weight_ref.shape[3]
+    for copy in loads:
+        copy.wait()
+
+
+def back_product(shifted_ref, weight_ref, side):
+    half = weight_ref.shape[2]
     total = None
     for tap in range(3):
         span = slice(tap * half, (tap + 1) * half)
         part = lax.dot_general(
-            shifted_ref[:, span], weight_ref[layer, side, span, :], (((1,), (1,)), ((), ())),
+            shifted_ref[:, span], weight_ref[side, span, :], (((1,), (1,)), ((), ())),
             preferred_element_type=F32,
         )
         total = part if total is None else total + part
@@ -181,11 +205,11 @@
 
 def back_partner_kernel(layer, grad_ref, weight_ref, shifted_ref, out_ref):
     write_shifts(grad_ref, shifted_ref, -dilations[layer])
-    out_ref[...] = back_product(shifted_ref, weight_ref, layer, 1).astype(BF16)
-
-
-def back_own_kernel(layer, shifted_ref, weight_ref, out_ref):
-    out_ref[...] = back_product(shifted_ref, weight_ref, layer, 0)
+    out_ref[...] = back_product(shifted_ref, weight_ref, 1).astype(BF16)
+
+
+def back_own_kernel(shifted_ref, weight_ref, out_ref):
+    out_ref[...] = back_product(shifted_ref, weight_ref, 0)
 
 
 def combine_kernel(layer, own_ref, partner_ref, stream_ref, alphas_ref, *rest):
@@ -279,7 +303,25 @@
     write_shifts(grad_ref, out_ref, -dilations[layer])
 
 
-def paired_weight_kernel(pieces, low, own_ref, shifted_ref, across_ref, across_other_ref, far_ref, *rest):
+def write_carried(values, out_ref, low):
+    first = values.astype(BF16).astype(F32)
+    second = (values - first).astype(BF16).astype(F32)
+    third = values - first - second
+    shape = (CARRIED, values.shape[1])
+    row = lax.broadcasted_iota(jnp.int32, shape, 0)
+    block = jnp.where(row == 0, first, jnp.where(row == 1, second, jnp.where(row == 2, third, 0.0)))
+    out_ref[low : low + CARRIED, :] = block.astype(BF16)
+
+
+def read_carried(ref, low):
+    block = ref[low : low + CARRIED, :].astype(F32)
+    return (block[0:1, :] + block[1:2, :]) + block[2:3, :]
+
+
+def paired_weight_kernel(pieces, low, carry, own_ref, shifted_ref, across_ref, across_other_ref, far_ref, *rest):
+    if carry:
+        write_carried(jnp.concatenate([ref[...] for ref in rest[:carry]], 1), rest[carry], own_ref.shape[0] // 2)
+        rest = rest[carry:]
     outs, turned_ref = rest[:-1], rest[-1]
     half = own_ref.shape[0]
     chan = lax.axis_index("chan")
@@ -292,21 +334,30 @@
         product = product.astype(BF16)
         size = product.shape[0] // len(outs)
         for place, ref in enumerate(outs):
-            ref[:, span] = product[place * size : (place + 1) * size, :]
-
-
-def finish_kernel(paired, held, counts, *refs):
-    out_ref, total_ref, sems = refs[-3:]
-    refs = list(refs[1:-3] if held else refs[:-3])
+            ref[0:size, span] = product[place * size : (place + 1) * size, :]
+
+
+def finish_kernel(paired, held, carry, counts, *refs):
+    total_ref, sems = refs[-2:]
+    refs = list(refs[1:-2] if held else refs[:-2])
+    if carry:
+        alpha_ref = refs.pop()
+        alpha_mine = refs.pop(0)
+    out_ref = refs.pop()
     half = total_ref.shape[3]
+    rows_of = total_ref.shape[2] // (2 if paired else 1)
     copies = []
     for index, (layer, pieces) in enumerate(counts):
         for part in range(pieces):
             mine_ref, other_ref = refs.pop(0), refs.pop(0)
-            size = mine_ref.shape[0]
+            size = rows_of
+            if carry and other_ref.shape[0] > size:
+                alpha = alpha_mine[...] + read_carried(other_ref, size)
+                for place in range(3):
+                    alpha_ref[place : place + 1, :] = alpha[:, place * half : (place + 1) * half]
             for tap in range(3):
                 span = slice(tap * half, (tap + 1) * half)
-                mine, other = mine_ref[:, span].astype(F32), other_ref[:, span].astype(F32)
+                mine, other = mine_ref[0:size, span].astype(F32), other_ref[0:size, span].astype(F32)
                 if paired:
                     begin = lax.axis_index("replica") * (size * pieces)
                     for values, start in ((mine, begin), (other, size * pieces - begin)):
@@ -320,15 +371,32 @@
         copy.wait()
 
 
-def fold_kernel(keep, got, send):
-    rows = send.shape[0]
-    send[...] = (keep[rows:, :].astype(F32) + got[rows:, :].astype(F32)).astype(BF16)
-
-
-def total_kernel(keep, got, late, out_ref):
-    rows = late.shape[0]
-    total = keep[0:rows, :].astype(F32) + got[0:rows, :].astype(F32) + late[...].astype(F32)
-    out_ref[...] = total.astype(BF16)
+def fold_kernel(carry, keep, got, *rest):
+    if carry:
+        mine, rest = rest[:carry], rest[carry:]
+        send, sum_ref = rest
+    else:
+        (send,) = rest
+    rows = keep.shape[0] // 2
+    send[0:rows, :] = (keep[rows:, :].astype(F32) + got[rows : 2 * rows, :].astype(F32)).astype(BF16)
+    if carry:
+        values = jnp.concatenate([ref[...] for ref in mine], 1) + read_carried(got, 2 * rows)
+        sum_ref[...] = values
+        write_carried(values, send, rows)
+
+
+def total_kernel(carry, keep, got, late, *rest):
+    if carry:
+        mine, out_ref, sum_ref = rest
+    else:
+        (out_ref,) = rest
+    rows = keep.shape[0] // 2
+    total = keep[0:rows, :].astype(F32) + got[0:rows, :].astype(F32) + late[0:rows, :].astype(F32)
+    out_ref[0:rows, :] = total.astype(BF16)
+    if carry:
+        values = mine[...] + read_carried(late, rows)
+        sum_ref[...] = values
+        write_carried(values, out_ref, rows)
 
 
 def stack_kernel(*refs):
@@ -356,7 +424,7 @@
     def hold(self, value):
         return after(value, self.latest)
 
-    def call(self, kernel, name, ins, outs, scratch, flops, *args, spec=IN_VMEM, aliases=None):
+    def call(self, kernel, name, ins, outs, scratch, flops, *args, specs=None, aliases=None):
         single = not isinstance(outs, list)
         size = sum(a.size * a.dtype.itemsize for a in args if a.size < 2000000)
         size += sum(math.prod(o.shape) * o.dtype.itemsize for o in ([outs] if single else outs))
@@ -367,15 +435,15 @@
         result = pl.pallas_call(
             kernel,
             in_specs=[ANY_HBM if i else IN_VMEM for i in ins],
-            out_specs=spec if single else [IN_VMEM] * len(outs),
+            out_specs=specs or (IN_VMEM if single else [IN_VMEM] * len(outs)),
             out_shape=outs,
             scratch_shapes=scratch,
             input_output_aliases=aliases or {},
             compiler_params=pltpu.CompilerParams(vmem_limit_bytes=24 * 1024 * 1024),
-            cost_estimate=pl.CostEstimate(flops=int(flops) * self.weight, bytes_accessed=int(size) * self.weight, transcendentals=0),
+            cost_estimate=pl.CostEstimate(flops=int(flops * self.weight), bytes_accessed=int(size * self.weight), transcendentals=0),
             name=name,
         )(*args)
-        self.latest = result if single else result[0]
+        self.latest = result if single else result[-1]
         return result
 
 
@@ -397,6 +465,8 @@
     top = layers - 1
     fast = lax.axis_size("dp") == 4 and lax.axis_size("replica") == 2
     counts = [1] * layers
+    carrier = 1 if fast else None
+    weight = {}
     tile, triple = (rows, half), (rows, taps * half)
     flops = 2 * rows * half * half * taps
     sequence = Sequence()
@@ -406,23 +476,41 @@
     alpha_parts = [None] * layers
     kept, got, late, summed, crossed = {}, {}, {}, {}, {}
 
-    def forward_own(layer):
-        owns[layer] = sequence.call(
-            functools.partial(forward_own_kernel, layer), "forward_own", [0, 0], struct(tile, F32),
-            [pltpu.VMEM(triple, BF16)], flops, mine[layer], weight,
-        )
-
-    def forward_partner(layer):
+    loaded = (2, taps * half, half)
+    sems = DMA((2 * taps,))
+
+    def forward_own(layer, load=None):
+        outs, args, ins = struct(tile, F32), [mine[layer], weight[layer]], [0, 0]
+        scratch = [pltpu.VMEM(triple, BF16)]
+        if load is not None:
+            outs, args, ins = [outs, struct(loaded, BF16)], args + [conv_weights], ins + [1]
+            scratch.append(sems)
+        result = sequence.call(
+            functools.partial(forward_own_kernel, layer, load), "forward_own", ins, outs, scratch, flops, *args
+        )
+        if load is None:
+            owns[layer] = result
+        else:
+            owns[layer], weight[load] = result
+
+    def forward_partner(layer, load=None):
         last = layer == top
+        ins, args = [0] * 5, [partners[layer], weight[layer], owns[layer], streams[layer], live]
+        outs = [struct(tile, BF16)] if last else [struct(tile, F32), struct(tile, BF16)]
+        scratch = [pltpu.VMEM(triple, BF16)]
+        if not last:
+            ins, args = ins + [0], args + [alphas]
+        if load is not None:
+            ins, args, outs = ins + [1], args + [conv_weights], outs + [struct(loaded, BF16)]
+            scratch.append(sems)
         result = sequence.call(
-            functools.partial(forward_partner_kernel, layer, last), "forward_partner",
-            [0, 0, 0, 0, 0] + ([] if last else [0]),
-            struct(tile, BF16) if last else [struct(tile, F32), struct(tile, BF16)],
-            [pltpu.VMEM(triple, BF16)], flops,
-            partners[layer], weight, owns[layer], streams[layer], live, *([] if last else [alphas]),
-        )
+            functools.partial(forward_partner_kernel, layer, last, load), "forward_partner", ins, outs, scratch,
+            flops, *args,
+        )
+        if load is not None:
+            weight[load] = result[-1]
         if last:
-            return result
+            return result[0]
         streams.append(result[0])
         mine.append(result[1])
         partners[layer + 1] = across_chan(result[1])
@@ -430,14 +518,13 @@
     def back_partner(layer):
         shifted[layer], part = sequence.call(
             functools.partial(back_partner_kernel, layer), "back_partner", [0, 0],
-            [struct(triple, BF16), struct(tile, BF16)], [], flops, rounded[layer + 1], weight,
+            [struct(triple, BF16), struct(tile, BF16)], [], flops, rounded[layer + 1], weight[layer],
         )
         arrived[layer] = across_chan(part)
 
     def back_own(layer):
         back_owns[layer] = sequence.call(
-            functools.partial(back_own_kernel, layer), "back_own", [0, 0], struct(tile, F32),
-            [], flops, shifted[layer], weight,
+            back_own_kernel, "back_own", [0, 0], struct(tile, F32), [], flops, shifted[layer], weight[layer]
         )
 
     def send_gradient(layer):
@@ -499,40 +586,62 @@
             summed[layer, 0] = lax.psum(part, "replica")
             crossed[layer, 0] = jnp.zeros_like(part)
             return
-        pieces = counts[layer]
-        piece = struct((channels // 4 // pieces, taps * half), BF16)
+        pieces, depth = counts[layer], channels // 4 // counts[layer]
+        carried = alpha_parts if layer == carrier else []
+        outs = [struct((depth, taps * half), BF16)] * (2 * pieces)
+        if carried:
+            outs[0] = struct((depth + CARRIED, taps * half), BF16)
+        args = [own_turned[layer], shifted[layer], across[layer][0], across_other[layer], far_shifted[layer], *carried]
         out = sequence.call(
-            functools.partial(paired_weight_kernel, pieces, across[layer][1]), "paired_weight", [0] * 5,
-            [piece] * (2 * pieces), [pltpu.VMEM((half, rows), BF16)], 2 * flops,
-            own_turned[layer], shifted[layer], across[layer][0], across_other[layer], far_shifted[layer],
+            functools.partial(paired_weight_kernel, pieces, across[layer][1], len(carried)), "paired_weight",
+            [0] * len(args), outs, [pltpu.VMEM((half, rows), BF16)], 2 * flops, *args,
         )
         for part in range(pieces):
             got[layer, part] = swap(out[part], "dp", lambda i: i ^ 1)
             kept[layer, part] = out[pieces + part]
+
+    carry_sum = [None]
 
     def fold(layer, part=0):
         if not fast:
             return
         keep, came = kept[layer, part], got[layer, part]
-        send = sequence.call(
-            fold_kernel, "fold", [0] * 2, struct((keep.shape[0] // 2, keep.shape[1]), BF16), [], keep.size, keep, came
-        )
-        late[layer, part] = swap(send, "dp", lambda i: i ^ 3)
+        depth, carried = keep.shape[0] // 2, alpha_parts if layer == carrier else []
+        outs = [struct((depth + CARRIED * bool(carried), taps * half), BF16)]
+        if carried:
+            outs.append(struct((1, taps * half), F32))
+        result = sequence.call(
+            functools.partial(fold_kernel, len(carried)), "fold", [0] * (2 + len(carried)), outs, [], keep.size,
+            keep, came, *carried,
+        )
+        if carried:
+            carry_sum[0] = result[1]
+        late[layer, part] = swap(result[0], "dp", lambda i: i ^ 3)
 
     def total(layer, part=0):
         if not fast:
             return
         keep, came, last = kept[layer, part], got[layer, part], late[layer, part]
-        summed[layer, part] = sequence.call(
-            total_kernel, "total", [0] * 3, struct(last.shape, BF16), [], 2 * flops, keep, came, last
-        )
-        crossed[layer, part] = across_replica(summed[layer, part])
-
-    stream, snaked, grad, live, alphas, weight = sequence.call(
+        outs, args = [struct(last.shape, BF16)], [keep, came, last]
+        if layer == carrier:
+            outs.append(struct((1, taps * half), F32))
+            args.append(carry_sum[0])
+        result = sequence.call(
+            functools.partial(total_kernel, layer == carrier), "total", [0] * len(args), outs, [], 2 * flops, *args
+        )
+        if layer == carrier:
+            carry_sum[0] = result[1]
+        summed[layer, part] = result[0]
+
+    def cross(layer, part=0):
+        if fast:
+            crossed[layer, part] = across_replica(sequence.hold(summed[layer, part]))
+
+    stream, snaked, grad, live, alphas, weight[0] = sequence.call(
         prep_kernel, "prep", [1] * 7,
         [struct(tile, F32), struct(tile, BF16), struct(tile, BF16), struct((rows, 128), F32),
-         struct(snake_alpha.shape, F32), struct((layers, 2, taps * half, half), BF16)],
-        [pltpu.SMEM(seg_lengths.shape, jnp.int32)] * 3 + [pltpu.VMEM(tile, BF16)] * 2 + [DMA((6,)), DMA((2 * layers * taps,))],
+         struct(snake_alpha.shape, F32), struct(loaded, BF16)],
+        [pltpu.SMEM(seg_lengths.shape, jnp.int32)] * 3 + [pltpu.VMEM(tile, BF16)] * 2 + [DMA((6,)), sems],
         40 * rows * half,
         seg_lengths, seg_owner, seg_start, activations, cotangent, snake_alpha, conv_weights,
     )
@@ -544,15 +653,22 @@
 
     def finish(chosen, before=None):
         pairs = [] if before is None else [before]
+        carry = carrier in chosen
+        if carry:
+            pairs.append(carry_sum[0])
         for layer in chosen:
             for part in range(counts[layer]):
                 pairs += [summed[layer, part], crossed[layer, part]]
+        out = struct((layers, taps, depth, half), F32)
         return sequence.call(
-            functools.partial(finish_kernel, fast, before is not None, tuple((layer, counts[layer]) for layer in chosen)),
+            functools.partial(
+                finish_kernel, fast, before is not None, carry, tuple((layer, counts[layer]) for layer in chosen)
+            ),
             "finish", [2] * (before is not None) + [0] * (len(pairs) - (before is not None)),
-            struct((layers, taps, depth, half), F32),
+            [out, struct((layers, half), F32)] if carry else [out],
             [pltpu.VMEM((len(chosen), taps, depth, half), F32), DMA((len(chosen),))],
-            layers * taps * depth * half, *pairs, spec=ANY_HBM, aliases={0: 0} if before is not None else None,
+            layers * taps * depth * half, *pairs, specs=[ANY_HBM] + [IN_VMEM] * carry,
+            aliases={0: 0} if before is not None else None,
         )
 
     rounds = [("replica", 1 << bit) for bit in range(8) if lax.axis_size("replica") >> (bit + 1)]
@@ -574,13 +690,13 @@
         arrivals.append((value, swap(value, axis, lambda place: place ^ apart)))
 
     send_gradient(2)
+    forward_own(0, load=2)
+    forward_partner(0, load=1)
     back_partner(2)
-    forward_own(0)
-    forward_partner(0)
-    back_own(2)
     forward_own(1)
     forward_partner(1)
     turn(2)
+    back_own(2)
     grad = combine(2, grad)
     send_gradient(1)
     far_rows(2)
@@ -591,32 +707,40 @@
     back_own(1)
     combine(1, grad)
     back_partner(0)
+    back_own(0)
     weights(2)
+    sequence.weight = 10
+    combine(0, None)
     own_rows(1)
-    back_own(0)
     own_rows(0)
-    combine(0, None)
     forward_own(2)
     residual_out = forward_partner(2)
     far_rows(1)
+    fold(2)
     share(1, 0)
     send_gradient(0)
-    fold(2)
+    sequence.weight = 10
+    total(2)
     weights(1)
-    total(2)
+    cross(2)
+    sequence.weight = 0.01
+    far_rows(0)
+    weights(0)
+    sequence.weight = 10
     fold(1)
-    far_rows(0)
-    alpha_round()
-    weights(0)
+    fold(0)
     total(1)
-    alpha_round()
-    fold(0)
-    weight_grads = finish((2, 1))
-    alpha_grads = alpha_round()
+    cross(1)
     total(0)
-    while alpha_grads is None:
+    cross(0)
+    if fast:
+        weight_grads, alpha_grads = finish((2, 1))
+        (weight_grads,) = finish((0,), weight_grads)
+    else:
         alpha_grads = alpha_round()
-    weight_grads = finish((0,), weight_grads)
+        while alpha_grads is None:
+            alpha_grads = alpha_round()
+        (weight_grads,) = finish((2, 1, 0))
     return (residual_out, weight_grads, alpha_grads)
 
 

time: 96.2 us -> 97.4 us (1.012)
  waiting for transfers between devices: 34.9 us -> 36.6 us
    ppermute x25 -> x22, waiting for transfers between devices: 34.9 us -> 36.6 us  [swap(): lax.ppermute(x, axis, [(i, other(i)) for i in range(lax.axis_size(axis))])]
    ppermute x25 -> x22, starting transfers between devices: 29.4 us -> 28.6 us  [swap(): lax.ppermute(x, axis, [(i, other(i)) for i in range(lax.axis_size(axis))])]
    pallas_call x39 -> x35, Pallas kernels: 30.7 us -> 31 us  [call(): pl.pallas_call(kernel, in_specs=[ANY_HBM if i else IN_VMEM for i in ins],...]
  transfers between devices with their start and end apart: 25 -> 22, of which waited for: 9 -> 12; matrix products, arithmetic and copies ran while one was open for 0% -> 0% of each run, Pallas kernels for 27% -> 28%
where the time goes in v6:
time: 97.4 us; the launch traced here: 97.2 us
  waiting for transfers between devices  36.6 us (38%)
  Pallas kernels  31 us (32%)
  starting transfers between devices  28.6 us (29%)
  between operations  1.07 us (1%)
    ppermute x22, waiting for transfers between devices, swap(): lax.ppermute(x, axis, [(i, other(i)) for i in range(lax.axis_size(axis))])  36.6 us
    pallas_call x35, Pallas kernels, call(): pl.pallas_call(kernel, in_specs=[ANY_HBM if i else IN_VMEM for i in ins],...  31 us
    ppermute x22, starting transfers between devices, swap(): lax.ppermute(x, axis, [(i, other(i)) for i in range(lax.axis_size(axis))])  28.6 us
  transfers between devices with their start and end apart: 22, of which 12 were waited for; matrix products, arithmetic and copies ran while one was open for 0% of the time, Pallas kernels for 28%

profile of v6, /device:TPU:0, one launch (start us, length us, event | category | flops | bytes accessed | tf_op | source)
XLA Modules:
  0.0 97.2 jit_solution(16610385859104333645)
XLA Ops:
  0.6 2.5 %prep.1 = (f32[512,384]{1,0:T(8,128)S(1)}, bf16[512,384]{1,0:T(8,128)(2,1)S(1)}, bf16[512,384]{1,0:T(8,128)(2,1)S(1)}, f32[512,128]{1,0:T(8,128)S(1)}, f32[3,384...) custom-call(s32[16]{0:T(128)} %len_hbm.1, s32[16]{0:T(128)} %own_hbm.1, s32[16]{0:T(128)} %start_hbm.1, ...), custom_call_target="tpu_custom_call" | custom-call | flops 78643200 | bytes 44003200 | tf_op jit(solution)/shard_map/prep/pallas_call | solution.py:435
  3.2 3.0 %collective-permute-start.4 = (bf16[512,384]{1,0:T(8,128)(2,1)S(1)}, bf16[512,384]{1,0:T(8,128)(2,1)S(1)}, u32[]{:S(2)}, u32[]{:S(2)}) collective-permute-start(bf16[512,384]{1,0:T(8,128)(2,1)S(1)} %get-tuple-element.102.grad_ref.rest_0_), channel_id=1, source_target_pairs={{0,2},{2,0},{1,3},{3,1},{4,6},{6,4},{5,7},{7,5},{8,10},{10,8},{9,1... | collective-permute-start | bytes 1179656 | tf_op jit(solution)/shard_map/ppermute | solution.py:451
  6.2 1.6 %forward_own.3 = (f32[512,384]{1,0:T(8,128)S(1)}, bf16[2,1152,384]{2,1,0:T(8,128)(2,1)S(1)}) custom-call(bf16[512,384]{1,0:T(8,128)(2,1)S(1)} %get-tuple-element.119.snake_ref.refs_1_.own_ref, bf16[2,1152,384]{2,1,0:T(8,128)(2,1)S(1)} %get-tuple-element.80.weight_ref, bf16[3,3,768,384]{3,2,1,0:T(8,128)(2,1)} %rest_1_.1), custom_call_target="tpu_custom_call" | custom-call | flops 4529848320 | bytes 47185920 | tf_op jit(solution)/shard_map/forward_own/pallas_call | solution.py:435
  7.9 2.3 %forward_partner.3 = (f32[512,384]{1,0:T(8,128)S(1)}, bf16[512,384]{1,0:T(8,128)(2,1)S(1)}, bf16[2,1152,384]{2,1,0:T(8,128)(2,1)S(1)}) custom-call(bf16[512,384]{1,0:T(8,128)(2,1)S(1)} %collective-permute-done.snake_ref.partner_ref, bf16[2,1152,384]{2,1,0:T(8,128)(2,1)S(1)} %get-tuple-element.80.weight_ref, f32[512,384]{1,0:T(8,128)S(1)} %get-tuple-element.84.own_ref, ...), custom_call_target="tpu_custom_call" | custom-call | flops 4529848320 | bytes 69514240 | tf_op jit(solution)/shard_map/forward_partner/pallas_call | solution.py:435
  10.7 0.9 back_partner.3
  12.6 1.8 %forward_partner.4 = (f32[512,384]{1,0:T(8,128)S(1)}, bf16[512,384]{1,0:T(8,128)(2,1)S(1)}) custom-call(bf16[512,384]{1,0:T(8,128)(2,1)S(1)} %collective-permute-done.1.snake_ref.partner_ref, bf16[2,1152,384]{2,1,0:T(8,128)(2,1)S(1)} %get-tuple-element.90.weight_ref, f32[512,384]{1,0:T(8,128)S(1)} %forward_own.4.own_ref, ...), custom_call_target="tpu_custom_call" | custom-call | flops 4529848320 | bytes 51819520 | tf_op jit(solution)/shard_map/forward_partner/pallas_call | solution.py:435
  16.1 1.6 %combine.3 = (f32[1,384]{1,0:T(1,128)S(1)}, f32[512,384]{1,0:T(8,128)S(1)}, bf16[512,384]{1,0:T(8,128)(2,1)S(1)}) custom-call(f32[512,384]{1,0:T(8,128)S(1)} %back_own.3.own_ref, bf16[512,384]{1,0:T(8,128)(2,1)S(1)} %collective-permute-done.3.partner_ref, f32[512,384]{1,0:T(8,128)S(1)} %get-tuple-element.100.stream_ref.old_ref, ...), custom_call_target="tpu_custom_call" | custom-call | flops 117964800 | bytes 38072320 | tf_op jit(solution)/shard_map/combine/pallas_call | solution.py:435
  17.7 2.0 %collective-permute-start.9 = (bf16[512,384]{1,0:T(8,128)(2,1)S(1)}, bf16[512,384]{1,0:T(8,128)(2,1)S(1)}, u32[]{:S(2)}, u32[]{:S(2)}) collective-permute-start(bf16[512,384]{1,0:T(8,128)(2,1)S(1)} %get-tuple-element.122.grad_ref), channel_id=1, source_target_pairs={{0,2},{2,0},{1,3},{3,1},{4,6},{6,4},{5,7},{7,5},{8,10},{10,8},{9,1... | collective-permute-start | bytes 1179656 | tf_op jit(solution)/shard_map/ppermute | solution.py:451
  23.3 1.7 %combine.4 = (f32[1,384]{1,0:T(1,128)S(1)}, bf16[512,384]{1,0:T(8,128)(2,1)S(1)}) custom-call(f32[512,384]{1,0:T(8,128)S(1)} %back_own.4.own_ref, bf16[512,384]{1,0:T(8,128)(2,1)S(1)} %collective-permute-done.5.partner_ref, f32[512,384]{1,0:T(8,128)S(1)} %get-tuple-element.95.old_ref.stream_ref, f32[3,384]{1,0:T(4,128)S(1)} %get-tuple-element.87.rest_0_.alphas_ref, ...), custom_call_target="tpu_custom_call" | custom-call | flops 117964800 | bytes 34140160 | tf_op jit(solution)/shard_map/combine/pallas_call | solution.py:435
  25.0 0.9 back_partner.5
  27.1 1.4 %paired_weight.3 = (bf16[192,1152]{1,0:T(8,128)(2,1)S(1)}, bf16[192,1152]{1,0:T(8,128)(2,1)S(1)}) custom-call(bf16[384,512]{1,0:T(8,128)(2,1)S(1)} %own_rows.3.own_ref, bf16[512,1152]{1,0:T(8,128)(2,1)S(1)} %get-tuple-element.99.shifted_ref, bf16[192,512]{1,0:T(8,128)(2,1)S(1)} %collective-permute-done.6.across_ref, ...), custom_call_target="tpu_custom_call" | custom-call | flops 9059696640 | bytes 40304640 | tf_op jit(solution)/shard_map/paired_weight/pallas_call | solution.py:435
  28.5 2.1 %collective-permute-start.10 = (bf16[192,1152]{1,0:T(8,128)(2,1)S(1)}, bf16[192,1152]{1,0:T(8,128)(2,1)S(1)}, u32[]{:S(2)}, u32[]{:S(2)}) collective-permute-start(bf16[192,1152]{1,0:T(8,128)(2,1)S(1)} %get-tuple-element.125), channel_id=1, source_target_pairs={{0,4},{4,0},{8,12},{12,8},{1,5},{5,1},{9,13},{13,9},{2,6},{6,2},{1... | collective-permute-start | bytes 1327112 | tf_op jit(solution)/shard_map/ppermute | solution.py:451
  30.6 1.4 %combine.5.rest_0_ = f32[1,384]{1,0:T(1,128)S(1)} custom-call(f32[512,384]{1,0:T(8,128)S(1)} %back_own.5.own_ref, bf16[512,384]{1,0:T(8,128)(2,1)S(1)} %collective-permute-done.8.partner_ref, f32[512,384]{1,0:T(8,128)S(1)} %get-tuple-element.85.old_ref.stream_ref, f32[3,384]{1,0:T(4,128)S(1)} %get-tuple-element.87.rest_0_.alphas_ref), custom_call_target="tpu_custom_call" | custom-call | flops 117964800 | bytes 19722240 | tf_op jit(solution)/shard_map/combine/pallas_call | solution.py:435
  33.4 1.6 %forward_partner.5 = bf16[512,384]{1,0:T(8,128)(2,1)} custom-call(bf16[512,384]{1,0:T(8,128)(2,1)S(1)} %collective-permute-done.2.partner_ref.snake_ref, bf16[2,1152,384]{2,1,0:T(8,128)(2,1)S(1)} %get-tuple-element.82.weight_ref, f32[512,384]{1,0:T(8,128)S(1)} %forward_own.5.own_ref, f32[512,384]{1,0:T(8,128)S(1)} %get-tuple-element.100.stream_ref.old_ref, ...), custom_call_target="tpu_custom_call" | custom-call | flops 4529848320 | bytes 43909120 | tf_op jit(solution)/shard_map/forward_partner/pallas_call | solution.py:435
  35.2 6.1 %collective-permute-done.10.got = bf16[192,1152]{1,0:T(8,128)(2,1)S(1)} collective-permute-done((bf16[192,1152]{1,0:T(8,128)(2,1)S(1)}, bf16[192,1152]{1,0:T(8,128)(2,1)S(1)}, u32[]{:S(2)}, u32[]{:S(2)}) %collective-permute-start.10) | collective-permute-done | bytes 442400 | tf_op jit(solution)/shard_map/ppermute | solution.py:451
  41.3 3.8 %collective-permute-start.11 = (bf16[96,1152]{1,0:T(8,128)(2,1)S(1)}, bf16[96,1152]{1,0:T(8,128)(2,1)S(1)}, u32[]{:S(2)}, u32[]{:S(2)}) collective-permute-start(bf16[96,1152]{1,0:T(8,128)(2,1)S(1)} %fold.3), channel_id=1, source_target_pairs={{0,12},{4,8},{8,4},{12,0},{1,13},{5,9},{9,5},{13,1},{2,14},{6,10},... | collective-permute-start | bytes 663560 | tf_op jit(solution)/shard_map/ppermute | solution.py:451
  45.2 1.5 %collective-permute-start.14 = (bf16[512,384]{1,0:T(8,128)(2,1)S(1)}, bf16[512,384]{1,0:T(8,128)(2,1)S(1)}, u32[]{:S(2)}, u32[]{:S(2)}) collective-permute-start(bf16[512,384]{1,0:T(8,128)(2,1)S(1)} %get-tuple-element.132.grad_ref), channel_id=1, source_target_pairs={{0,2},{2,0},{1,3},{3,1},{4,6},{6,4},{5,7},{7,5},{8,10},{10,8},{9,1... | collective-permute-start | bytes 1179656 | tf_op jit(solution)/shard_map/ppermute | solution.py:451
  46.7 3.8 %collective-permute-done.11.late = bf16[96,1152]{1,0:T(8,128)(2,1)S(1)} collective-permute-done((bf16[96,1152]{1,0:T(8,128)(2,1)S(1)}, bf16[96,1152]{1,0:T(8,128)(2,1)S(1)}, u32[]{:S(2)}, u32[]{:S(2)}) %collective-permute-start.11) | collective-permute-done | bytes 221216 | tf_op jit(solution)/shard_map/ppermute | solution.py:451
  50.5 1.4 %paired_weight.4 = (bf16[208,1152]{1,0:T(8,128)(2,1)S(1)}, bf16[192,1152]{1,0:T(8,128)(2,1)S(1)}) custom-call(bf16[384,512]{1,0:T(8,128)(2,1)S(1)} %own_rows.4.own_ref, bf16[512,1152]{1,0:T(8,128)(2,1)S(1)} %get-tuple-element.107.shifted_ref, bf16[384,512]{1,0:T(8,128)(2,1)S(1)} %collective-permute-done.12.across_ref, ...), custom_call_target="tpu_custom_call" | custom-call | flops 9059696640 | bytes 44651520 | tf_op jit(solution)/shard_map/paired_weight/pallas_call | solution.py:435
  51.9 4.4 %collective-permute-start.15 = (bf16[208,1152]{1,0:T(8,128)(2,1)S(1)}, bf16[208,1152]{1,0:T(8,128)(2,1)S(1)}, u32[]{:S(2)}, u32[]{:S(2)}) collective-permute-start(bf16[208,1152]{1,0:T(8,128)(2,1)S(1)} %get-tuple-element.137), channel_id=1, source_target_pairs={{0,4},{4,0},{8,12},{12,8},{1,5},{5,1},{9,13},{13,9},{2,6},{6,2},{1... | collective-permute-start | bytes 1437704 | tf_op jit(solution)/shard_map/ppermute | solution.py:451
  56.9 1.4 %paired_weight.5 = (bf16[192,1152]{1,0:T(8,128)(2,1)S(1)}, bf16[192,1152]{1,0:T(8,128)(2,1)S(1)}) custom-call(bf16[384,512]{1,0:T(8,128)(2,1)S(1)} %own_rows.5.own_ref, bf16[512,1152]{1,0:T(8,128)(2,1)S(1)} %get-tuple-element.112.shifted_ref, bf16[384,512]{1,0:T(8,128)(2,1)S(1)} %collective-permute-done.12.across_ref, ...), custom_call_target="tpu_custom_call" | custom-call | flops 9059696 | bytes 44236 | tf_op jit(solution)/shard_map/paired_weight/pallas_call | solution.py:435
  58.4 9.8 %collective-permute-done.15.got = bf16[208,1152]{1,0:T(8,128)(2,1)S(1)} collective-permute-done((bf16[208,1152]{1,0:T(8,128)(2,1)S(1)}, bf16[208,1152]{1,0:T(8,128)(2,1)S(1)}, u32[]{:S(2)}, u32[]{:S(2)}) %collective-permute-start.15) | collective-permute-done | bytes 479264 | tf_op jit(solution)/shard_map/ppermute | solution.py:451
  68.3 2.5 %collective-permute-start.17 = (bf16[112,1152]{1,0:T(8,128)(2,1)S(1)}, bf16[112,1152]{1,0:T(8,128)(2,1)S(1)}, u32[]{:S(2)}, u32[]{:S(2)}) collective-permute-start(bf16[112,1152]{1,0:T(8,128)(2,1)S(1)} %get-tuple-element.142), channel_id=1, source_target_pairs={{0,12},{4,8},{8,4},{12,0},{1,13},{5,9},{9,5},{13,1},{2,14},{6,10},... | collective-permute-start | bytes 774152 | tf_op jit(solution)/shard_map/ppermute | solution.py:451
  70.8 1.5 %collective-permute-start.19 = (bf16[96,1152]{1,0:T(8,128)(2,1)S(1)}, bf16[96,1152]{1,0:T(8,128)(2,1)S(1)}, u32[]{:S(2)}, u32[]{:S(2)}) collective-permute-start(bf16[96,1152]{1,0:T(8,128)(2,1)S(1)} %total.3.refs_1_), channel_id=1, source_target_pairs={{0,2},{2,0},{1,3},{3,1},{4,6},{6,4},{5,7},{7,5},{8,10},{10,8},{9,1... | collective-permute-start | bytes 663560 | tf_op jit(solution)/shard_map/ppermute | solution.py:451
  72.3 4.9 %collective-permute-done.16.got = bf16[192,1152]{1,0:T(8,128)(2,1)S(1)} collective-permute-done((bf16[192,1152]{1,0:T(8,128)(2,1)S(1)}, bf16[192,1152]{1,0:T(8,128)(2,1)S(1)}, u32[]{:S(2)}, u32[]{:S(2)}) %collective-permute-start.16) | collective-permute-done | bytes 442400 | tf_op jit(solution)/shard_map/ppermute | solution.py:451
  77.3 2.6 %collective-permute-start.18 = (bf16[96,1152]{1,0:T(8,128)(2,1)S(1)}, bf16[96,1152]{1,0:T(8,128)(2,1)S(1)}, u32[]{:S(2)}, u32[]{:S(2)}) collective-permute-start(bf16[96,1152]{1,0:T(8,128)(2,1)S(1)} %fold.5), channel_id=1, source_target_pairs={{0,12},{4,8},{8,4},{12,0},{1,13},{5,9},{9,5},{13,1},{2,14},{6,10},... | collective-permute-start | bytes 663560 | tf_op jit(solution)/shard_map/ppermute | solution.py:451
  79.8 5.9 %collective-permute-done.17.late = bf16[112,1152]{1,0:T(8,128)(2,1)S(1)} collective-permute-done((bf16[112,1152]{1,0:T(8,128)(2,1)S(1)}, bf16[112,1152]{1,0:T(8,128)(2,1)S(1)}, u32[]{:S(2)}, u32[]{:S(2)}) %collective-permute-start.17) | collective-permute-done | bytes 258080 | tf_op jit(solution)/shard_map/ppermute | solution.py:451
  85.9 1.6 %collective-permute-start.20 = (bf16[112,1152]{1,0:T(8,128)(2,1)S(1)}, bf16[112,1152]{1,0:T(8,128)(2,1)S(1)}, u32[]{:S(2)}, u32[]{:S(2)}) collective-permute-start(bf16[112,1152]{1,0:T(8,128)(2,1)S(1)} %get-tuple-element.147.refs_3_), channel_id=1, source_target_pairs={{0,2},{2,0},{1,3},{3,1},{4,6},{6,4},{5,7},{7,5},{8,10},{10,8},{9,1... | collective-permute-start | bytes 774152 | tf_op jit(solution)/shard_map/ppermute | solution.py:451
  88.2 1.6 %collective-permute-start.21 = (bf16[96,1152]{1,0:T(8,128)(2,1)S(1)}, bf16[96,1152]{1,0:T(8,128)(2,1)S(1)}, u32[]{:S(2)}, u32[]{:S(2)}) collective-permute-start(bf16[96,1152]{1,0:T(8,128)(2,1)S(1)} %total.5.refs_1_), channel_id=1, source_target_pairs={{0,2},{2,0},{1,3},{3,1},{4,6},{6,4},{5,7},{7,5},{8,10},{10,8},{9,1... | collective-permute-start | bytes 663560 | tf_op jit(solution)/shard_map/ppermute | solution.py:451
  89.8 3.9 %collective-permute-done.20.refs_4_ = bf16[112,1152]{1,0:T(8,128)(2,1)S(1)} collective-permute-done((bf16[112,1152]{1,0:T(8,128)(2,1)S(1)}, bf16[112,1152]{1,0:T(8,128)(2,1)S(1)}, u32[]{:S(2)}, u32[]{:S(2)}) %collective-permute-start.20) | collective-permute-done | bytes 258080 | tf_op jit(solution)/shard_map/ppermute | solution.py:451
  93.7 1.9 %finish.2 = (f32[3,3,192,384]{3,2,1,0:T(8,128)}, f32[3,384]{1,0:T(4,128)}) custom-call(f32[1,1152]{1,0:T(1,128)S(1)} %get-tuple-element.145.refs_0_, bf16[96,1152]{1,0:T(8,128)(2,1)S(1)} %total.3.refs_1_, bf16[96,1152]{1,0:T(8,128)(2,1)S(1)} %collective-permute-done.19.refs_2_, bf16[112,1152]{1,0:T(8,128)(2,1)S(1)} %get-tuple-element.147.refs_3_, ...), custom_call_target="tpu_custom_call" | custom-call | flops 6635520 | bytes 36218880 | tf_op jit(solution)/shard_map/finish/pallas_call | solution.py:435
  96.0 1.0 %finish.3 = f32[3,3,192,384]{3,2,1,0:T(8,128)} custom-call(f32[3,3,192,384]{3,2,1,0:T(8,128)} %get-tuple-element.148.refs_0_, bf16[96,1152]{1,0:T(8,128)(2,1)S(1)} %total.5.refs_1_, bf16[96,1152]{1,0:T(8,128)(2,1)S(1)} %collective-permute-done.21.refs_2_), custom_call_target="tpu_custom_call", output_to_operand_aliasing={{}: (0, {})} | custom-call | flops 6635520 | bytes 57507840 | tf_op jit(solution)/shard_map/finish/pallas_call | solution.py:435
  (47 shorter events, 11.8 us)
Async XLA Ops:
  3.2 14.5 %collective-permute-start.4 = (bf16[512,384]{1,0:T(8,128)(2,1)S(1)}, bf16[512,384]{1,0:T(8,128)(2,1)S(1)}, u32[]{:S(2)}, u32[]{:S(2)}) collective-permute-start(bf16[512,384]{1,0:T(8,128)(2,1)S(1)} %get-tuple-element.102.grad_ref.rest_0_), channel_id=1, source_target_pairs={{0,2},{2,0},{1,3},{3,1},{4,6},{6,4},{5,7},{7,5},{8,10},{10,8},{9,1... | collective-permute-start | bytes 1179656 | tf_op jit(solution)/shard_map/ppermute | solution.py:451
  6.2 1.7 %collective-permute-start = (bf16[512,384]{1,0:T(8,128)(2,1)S(1)}, bf16[512,384]{1,0:T(8,128)(2,1)S(1)}, u32[]{:S(2)}, u32[]{:S(2)}) collective-permute-start(bf16[512,384]{1,0:T(8,128)(2,1)S(1)} %get-tuple-element.119.snake_ref.refs_1_.own_ref), channel_id=1, source_target_pairs={{0,1},{1,0},{2,3},{3,2},{4,5},{5,4},{6,7},{7,6},{8,9},{9,8},{10,11... | collective-permute-start | bytes 1179656 | tf_op jit(solution)/shard_map/ppermute | solution.py:451
  10.2 2.4 %collective-permute-start.1 = (bf16[512,384]{1,0:T(8,128)(2,1)S(1)}, bf16[512,384]{1,0:T(8,128)(2,1)S(1)}, u32[]{:S(2)}, u32[]{:S(2)}) collective-permute-start(bf16[512,384]{1,0:T(8,128)(2,1)S(1)} %get-tuple-element.118.snake_ref.refs_0_.own_ref), channel_id=1, source_target_pairs={{0,1},{1,0},{2,3},{3,2},{4,5},{5,4},{6,7},{7,6},{8,9},{9,8},{10,11... | collective-permute-start | bytes 1179656 | tf_op jit(solution)/shard_map/ppermute | solution.py:451
  11.6 4.4 %collective-permute-start.3 = (bf16[512,384]{1,0:T(8,128)(2,1)S(1)}, bf16[512,384]{1,0:T(8,128)(2,1)S(1)}, u32[]{:S(2)}, u32[]{:S(2)}) collective-permute-start(bf16[512,384]{1,0:T(8,128)(2,1)S(1)} %get-tuple-element.92), channel_id=1, source_target_pairs={{0,1},{1,0},{2,3},{3,2},{4,5},{5,4},{6,7},{7,6},{8,9},{9,8},{10,11... | collective-permute-start | bytes 1179656 | tf_op jit(solution)/shard_map/ppermute | solution.py:451
  14.3 5.6 %collective-permute-start.2 = (bf16[512,384]{1,0:T(8,128)(2,1)S(1)}, bf16[512,384]{1,0:T(8,128)(2,1)S(1)}, u32[]{:S(2)}, u32[]{:S(2)}) collective-permute-start(bf16[512,384]{1,0:T(8,128)(2,1)S(1)} %get-tuple-element.120.refs_0_.own_ref.snake_ref), channel_id=1, source_target_pairs={{0,1},{1,0},{2,3},{3,2},{4,5},{5,4},{6,7},{7,6},{8,9},{9,8},{10,11... | collective-permute-start | bytes 1179656 | tf_op jit(solution)/shard_map/ppermute | solution.py:451
  15.0 7.8 %collective-permute-start.6 = (bf16[192,512]{1,0:T(8,128)(2,1)S(1)}, bf16[192,512]{1,0:T(8,128)(2,1)S(1)}, u32[]{:S(2)}, u32[]{:S(2)}) collective-permute-start(bf16[192,512]{1,0:T(8,128)(2,1)S(1)} %turn.2), channel_id=1, source_target_pairs={{0,2},{2,0},{1,3},{3,1},{4,6},{6,4},{5,7},{7,5},{8,10},{10,8},{9,1... | collective-permute-start | bytes 589832 | tf_op jit(solution)/shard_map/ppermute | solution.py:451
  17.7 17.3 %collective-permute-start.9 = (bf16[512,384]{1,0:T(8,128)(2,1)S(1)}, bf16[512,384]{1,0:T(8,128)(2,1)S(1)}, u32[]{:S(2)}, u32[]{:S(2)}) collective-permute-start(bf16[512,384]{1,0:T(8,128)(2,1)S(1)} %get-tuple-element.122.grad_ref), channel_id=1, source_target_pairs={{0,2},{2,0},{1,3},{3,1},{4,6},{6,4},{5,7},{7,5},{8,10},{10,8},{9,1... | collective-permute-start | bytes 1179656 | tf_op jit(solution)/shard_map/ppermute | solution.py:451
  20.5 24.7 %collective-permute-start.12 = (bf16[384,512]{1,0:T(8,128)(2,1)S(1)}, bf16[384,512]{1,0:T(8,128)(2,1)S(1)}, u32[]{:S(2)}, u32[]{:S(2)}) collective-permute-start(bf16[384,512]{1,0:T(8,128)(2,1)S(1)} %turn.3), channel_id=1, source_target_pairs={{0,2},{2,0},{1,3},{3,1},{4,6},{6,4},{5,7},{7,5},{8,10},{10,8},{9,1... | collective-permute-start | bytes 1179656 | tf_op jit(solution)/shard_map/ppermute | solution.py:451
  21.5 1.8 %collective-permute-start.5 = (bf16[512,384]{1,0:T(8,128)(2,1)S(1)}, bf16[512,384]{1,0:T(8,128)(2,1)S(1)}, u32[]{:S(2)}, u32[]{:S(2)}) collective-permute-start(bf16[512,384]{1,0:T(8,128)(2,1)S(1)} %get-tuple-element.108), channel_id=1, source_target_pairs={{0,1},{1,0},{2,3},{3,2},{4,5},{5,4},{6,7},{7,6},{8,9},{9,8},{10,11... | collective-permute-start | bytes 1179656 | tf_op jit(solution)/shard_map/ppermute | solution.py:451
  22.9 4.2 %collective-permute-start.7 = (bf16[192,512]{1,0:T(8,128)(2,1)S(1)}, bf16[192,512]{1,0:T(8,128)(2,1)S(1)}, u32[]{:S(2)}, u32[]{:S(2)}) collective-permute-start(bf16[192,512]{1,0:T(8,128)(2,1)S(1)} %collective-permute-done.6.across_ref), channel_id=1, source_target_pairs={{0,1},{1,0},{2,3},{3,2},{4,5},{5,4},{6,7},{7,6},{8,9},{9,8},{10,11... | collective-permute-start | bytes 589832 | tf_op jit(solution)/shard_map/ppermute | solution.py:451
  26.9 3.7 %collective-permute-start.8 = (bf16[512,384]{1,0:T(8,128)(2,1)S(1)}, bf16[512,384]{1,0:T(8,128)(2,1)S(1)}, u32[]{:S(2)}, u32[]{:S(2)}) collective-permute-start(bf16[512,384]{1,0:T(8,128)(2,1)S(1)} %get-tuple-element.117), channel_id=1, source_target_pairs={{0,1},{1,0},{2,3},{3,2},{4,5},{5,4},{6,7},{7,6},{8,9},{9,8},{10,11... | collective-permute-start | bytes 1179656 | tf_op jit(solution)/shard_map/ppermute | solution.py:451
  28.5 12.8 %collective-permute-start.10 = (bf16[192,1152]{1,0:T(8,128)(2,1)S(1)}, bf16[192,1152]{1,0:T(8,128)(2,1)S(1)}, u32[]{:S(2)}, u32[]{:S(2)}) collective-permute-start(bf16[192,1152]{1,0:T(8,128)(2,1)S(1)} %get-tuple-element.125), channel_id=1, source_target_pairs={{0,4},{4,0},{8,12},{12,8},{1,5},{5,1},{9,13},{13,9},{2,6},{6,2},{1... | collective-permute-start | bytes 1327112 | tf_op jit(solution)/shard_map/ppermute | solution.py:451
  41.3 9.1 %collective-permute-start.11 = (bf16[96,1152]{1,0:T(8,128)(2,1)S(1)}, bf16[96,1152]{1,0:T(8,128)(2,1)S(1)}, u32[]{:S(2)}, u32[]{:S(2)}) collective-permute-start(bf16[96,1152]{1,0:T(8,128)(2,1)S(1)} %fold.3), channel_id=1, source_target_pairs={{0,12},{4,8},{8,4},{12,0},{1,13},{5,9},{9,5},{13,1},{2,14},{6,10},... | collective-permute-start | bytes 663560 | tf_op jit(solution)/shard_map/ppermute | solution.py:451
  45.2 5.4 %collective-permute-start.13 = (bf16[384,512]{1,0:T(8,128)(2,1)S(1)}, bf16[384,512]{1,0:T(8,128)(2,1)S(1)}, u32[]{:S(2)}, u32[]{:S(2)}) collective-permute-start(bf16[384,512]{1,0:T(8,128)(2,1)S(1)} %collective-permute-done.12.across_ref), channel_id=1, source_target_pairs={{0,1},{1,0},{2,3},{3,2},{4,5},{5,4},{6,7},{7,6},{8,9},{9,8},{10,11... | collective-permute-start | bytes 1179656 | tf_op jit(solution)/shard_map/ppermute | solution.py:451
  45.2 11.5 %collective-permute-start.14 = (bf16[512,384]{1,0:T(8,128)(2,1)S(1)}, bf16[512,384]{1,0:T(8,128)(2,1)S(1)}, u32[]{:S(2)}, u32[]{:S(2)}) collective-permute-start(bf16[512,384]{1,0:T(8,128)(2,1)S(1)} %get-tuple-element.132.grad_ref), channel_id=1, source_target_pairs={{0,2},{2,0},{1,3},{3,1},{4,6},{6,4},{5,7},{7,5},{8,10},{10,8},{9,1... | collective-permute-start | bytes 1179656 | tf_op jit(solution)/shard_map/ppermute | solution.py:451
  51.9 16.3 %collective-permute-start.15 = (bf16[208,1152]{1,0:T(8,128)(2,1)S(1)}, bf16[208,1152]{1,0:T(8,128)(2,1)S(1)}, u32[]{:S(2)}, u32[]{:S(2)}) collective-permute-start(bf16[208,1152]{1,0:T(8,128)(2,1)S(1)} %get-tuple-element.137), channel_id=1, source_target_pairs={{0,4},{4,0},{8,12},{12,8},{1,5},{5,1},{9,13},{13,9},{2,6},{6,2},{1... | collective-permute-start | bytes 1437704 | tf_op jit(solution)/shard_map/ppermute | solution.py:451
  58.3 18.9 %collective-permute-start.16 = (bf16[192,1152]{1,0:T(8,128)(2,1)S(1)}, bf16[192,1152]{1,0:T(8,128)(2,1)S(1)}, u32[]{:S(2)}, u32[]{:S(2)}) collective-permute-start(bf16[192,1152]{1,0:T(8,128)(2,1)S(1)} %get-tuple-element.140), channel_id=1, source_target_pairs={{0,4},{4,0},{8,12},{12,8},{1,5},{5,1},{9,13},{13,9},{2,6},{6,2},{1... | collective-permute-start | bytes 1327112 | tf_op jit(solution)/shard_map/ppermute | solution.py:451
  68.3 17.5 %collective-permute-start.17 = (bf16[112,1152]{1,0:T(8,128)(2,1)S(1)}, bf16[112,1152]{1,0:T(8,128)(2,1)S(1)}, u32[]{:S(2)}, u32[]{:S(2)}) collective-permute-start(bf16[112,1152]{1,0:T(8,128)(2,1)S(1)} %get-tuple-element.142), channel_id=1, source_target_pairs={{0,12},{4,8},{8,4},{12,0},{1,13},{5,9},{9,5},{13,1},{2,14},{6,10},... | collective-permute-start | bytes 774152 | tf_op jit(solution)/shard_map/ppermute | solution.py:451
  70.8 19.0 %collective-permute-start.19 = (bf16[96,1152]{1,0:T(8,128)(2,1)S(1)}, bf16[96,1152]{1,0:T(8,128)(2,1)S(1)}, u32[]{:S(2)}, u32[]{:S(2)}) collective-permute-start(bf16[96,1152]{1,0:T(8,128)(2,1)S(1)} %total.3.refs_1_), channel_id=1, source_target_pairs={{0,2},{2,0},{1,3},{3,1},{4,6},{6,4},{5,7},{7,5},{8,10},{10,8},{9,1... | collective-permute-start | bytes 663560 | tf_op jit(solution)/shard_map/ppermute | solution.py:451
  77.3 10.9 %collective-permute-start.18 = (bf16[96,1152]{1,0:T(8,128)(2,1)S(1)}, bf16[96,1152]{1,0:T(8,128)(2,1)S(1)}, u32[]{:S(2)}, u32[]{:S(2)}) collective-permute-start(bf16[96,1152]{1,0:T(8,128)(2,1)S(1)} %fold.5), channel_id=1, source_target_pairs={{0,12},{4,8},{8,4},{12,0},{1,13},{5,9},{9,5},{13,1},{2,14},{6,10},... | collective-permute-start | bytes 663560 | tf_op jit(solution)/shard_map/ppermute | solution.py:451
  85.9 7.8 %collective-permute-start.20 = (bf16[112,1152]{1,0:T(8,128)(2,1)S(1)}, bf16[112,1152]{1,0:T(8,128)(2,1)S(1)}, u32[]{:S(2)}, u32[]{:S(2)}) collective-permute-start(bf16[112,1152]{1,0:T(8,128)(2,1)S(1)} %get-tuple-element.147.refs_3_), channel_id=1, source_target_pairs={{0,2},{2,0},{1,3},{3,1},{4,6},{6,4},{5,7},{7,5},{8,10},{10,8},{9,1... | collective-permute-start | bytes 774152 | tf_op jit(solution)/shard_map/ppermute | solution.py:451
  88.2 7.8 %collective-permute-start.21 = (bf16[96,1152]{1,0:T(8,128)(2,1)S(1)}, bf16[96,1152]{1,0:T(8,128)(2,1)S(1)}, u32[]{:S(2)}, u32[]{:S(2)}) collective-permute-start(bf16[96,1152]{1,0:T(8,128)(2,1)S(1)} %total.5.refs_1_), channel_id=1, source_target_pairs={{0,2},{2,0},{1,3},{3,1},{4,6},{6,4},{5,7},{7,5},{8,10},{10,8},{9,1... | collective-permute-start | bytes 663560 | tf_op jit(solution)/shard_map/ppermute | solution.py:451

commit v7 on v6

--- a/solution.py
+++ b/solution.py
@@ -689,8 +689,8 @@
         axis, apart = rounds.pop(0)
         arrivals.append((value, swap(value, axis, lambda place: place ^ apart)))
 
+    forward_own(0, load=2)
     send_gradient(2)
-    forward_own(0, load=2)
     forward_partner(0, load=1)
     back_partner(2)
     forward_own(1)
@@ -701,7 +701,7 @@
     send_gradient(1)
     far_rows(2)
     own_rows(2)
-    turn(1, 0)
+    turn(1)
     back_partner(1)
     share(2)
     back_own(1)
@@ -712,20 +712,22 @@
     sequence.weight = 10
     combine(0, None)
     own_rows(1)
+    turn(0)
+    far_rows(1)
     own_rows(0)
+    share(1)
     forward_own(2)
     residual_out = forward_partner(2)
-    far_rows(1)
+    sequence.weight = 10
+    weights(1)
+    send_gradient(0)
+    share(0)
     fold(2)
-    share(1, 0)
-    send_gradient(0)
-    sequence.weight = 10
+    far_rows(0)
+    sequence.weight = 0.01
+    weights(0)
     total(2)
-    weights(1)
     cross(2)
-    sequence.weight = 0.01
-    far_rows(0)
-    weights(0)
     sequence.weight = 10
     fold(1)
     fold(0)

time: 97.4 us -> 97.9 us (level)
  the two profiles are of different devices: /device:TPU:0 before, /device:TPU:14 now
where the time goes in v7:
time: 97.9 us; the launch traced here: 97.7 us
  waiting for transfers between devices  48.5 us (50%)
  Pallas kernels  30.9 us (32%)
  starting transfers between devices  17.1 us (17%)
  between operations  1.12 us (1%)
    ppermute x24, waiting for transfers between devices, swap(): lax.ppermute(x, axis, [(i, other(i)) for i in range(lax.axis_size(axis))])  48.5 us
    pallas_call x36, Pallas kernels, call(): pl.pallas_call(kernel, in_specs=[ANY_HBM if i else IN_VMEM for i in ins],...  30.9 us
    ppermute x24, starting transfers between devices, swap(): lax.ppermute(x, axis, [(i, other(i)) for i in range(lax.axis_size(axis))])  17.1 us
  transfers between devices with their start and end apart: 24, of which 10 were waited for; matrix products, arithmetic and copies ran while one was open for 0% of the time, Pallas kernels for 28%

profile of v7, /device:TPU:14, one launch (start us, length us, event | category | flops | bytes accessed | tf_op | source)
XLA Modules:
  0.0 97.7 jit_solution(13678147645538602317)
XLA Ops:
  0.6 2.5 %prep.1 = (f32[512,384]{1,0:T(8,128)S(1)}, bf16[512,384]{1,0:T(8,128)(2,1)S(1)}, bf16[512,384]{1,0:T(8,128)(2,1)S(1)}, f32[512,128]{1,0:T(8,128)S(1)}, f32[3,384...) custom-call(s32[16]{0:T(128)} %len_hbm.1, s32[16]{0:T(128)} %own_hbm.1, s32[16]{0:T(128)} %start_hbm.1, ...), custom_call_target="tpu_custom_call" | custom-call | flops 78643200 | bytes 44003200 | tf_op jit(solution)/shard_map/prep/pallas_call | solution.py:435
  3.2 1.6 %forward_own.3 = (f32[512,384]{1,0:T(8,128)S(1)}, bf16[2,1152,384]{2,1,0:T(8,128)(2,1)S(1)}) custom-call(bf16[512,384]{1,0:T(8,128)(2,1)S(1)} %get-tuple-element.124.snake_ref.refs_0_.own_ref, bf16[2,1152,384]{2,1,0:T(8,128)(2,1)S(1)} %get-tuple-element.82.weight_ref, bf16[3,3,768,384]{3,2,1,0:T(8,128)(2,1)} %rest_1_.1), custom_call_target="tpu_custom_call" | custom-call | flops 4529848320 | bytes 47185920 | tf_op jit(solution)/shard_map/forward_own/pallas_call | solution.py:435
  5.5 2.3 %forward_partner.3 = (f32[512,384]{1,0:T(8,128)S(1)}, bf16[512,384]{1,0:T(8,128)(2,1)S(1)}, bf16[2,1152,384]{2,1,0:T(8,128)(2,1)S(1)}) custom-call(bf16[512,384]{1,0:T(8,128)(2,1)S(1)} %collective-permute-done.snake_ref.partner_ref, bf16[2,1152,384]{2,1,0:T(8,128)(2,1)S(1)} %get-tuple-element.82.weight_ref, f32[512,384]{1,0:T(8,128)S(1)} %get-tuple-element.86.own_ref, ...), custom_call_target="tpu_custom_call" | custom-call | flops 4529848320 | bytes 69514240 | tf_op jit(solution)/shard_map/forward_partner/pallas_call | solution.py:435
  8.1 0.9 back_partner.3
  10.2 1.7 %forward_partner.4 = (f32[512,384]{1,0:T(8,128)S(1)}, bf16[512,384]{1,0:T(8,128)(2,1)S(1)}) custom-call(bf16[512,384]{1,0:T(8,128)(2,1)S(1)} %collective-permute-done.1.snake_ref.partner_ref, bf16[2,1152,384]{2,1,0:T(8,128)(2,1)S(1)} %get-tuple-element.92.weight_ref, f32[512,384]{1,0:T(8,128)S(1)} %forward_own.4.own_ref, ...), custom_call_target="tpu_custom_call" | custom-call | flops 4529848320 | bytes 51819520 | tf_op jit(solution)/shard_map/forward_partner/pallas_call | solution.py:435
  12.3 1.6 %collective-permute-start.7 = (bf16[192,512]{1,0:T(8,128)(2,1)S(1)}, bf16[192,512]{1,0:T(8,128)(2,1)S(1)}, u32[]{:S(2)}, u32[]{:S(2)}) collective-permute-start(bf16[192,512]{1,0:T(8,128)(2,1)S(1)} %turn.3), channel_id=1, source_target_pairs={{0,2},{2,0},{1,3},{3,1},{4,6},{6,4},{5,7},{7,5},{8,10},{10,8},{9,1... | collective-permute-start | bytes 589832 | tf_op jit(solution)/shard_map/ppermute | solution.py:451
  14.8 1.6 %combine.3 = (f32[1,384]{1,0:T(1,128)S(1)}, f32[512,384]{1,0:T(8,128)S(1)}, bf16[512,384]{1,0:T(8,128)(2,1)S(1)}) custom-call(f32[512,384]{1,0:T(8,128)S(1)} %back_own.3.own_ref, bf16[512,384]{1,0:T(8,128)(2,1)S(1)} %collective-permute-done.3.partner_ref, f32[512,384]{1,0:T(8,128)S(1)} %get-tuple-element.102.stream_ref.old_ref, ...), custom_call_target="tpu_custom_call" | custom-call | flops 117964800 | bytes 38072320 | tf_op jit(solution)/shard_map/combine/pallas_call | solution.py:435
  17.8 1.8 %collective-permute-start.10 = (bf16[192,512]{1,0:T(8,128)(2,1)S(1)}, bf16[192,512]{1,0:T(8,128)(2,1)S(1)}, u32[]{:S(2)}, u32[]{:S(2)}) collective-permute-start(bf16[192,512]{1,0:T(8,128)(2,1)S(1)} %turn.4), channel_id=1, source_target_pairs={{0,2},{2,0},{1,3},{3,1},{4,6},{6,4},{5,7},{7,5},{8,10},{10,8},{9,1... | collective-permute-start | bytes 589832 | tf_op jit(solution)/shard_map/ppermute | solution.py:451
  19.6 0.9 back_partner.4
  20.6 0.9 back_own.4.own_ref
  22.3 1.7 %combine.4 = (f32[1,384]{1,0:T(1,128)S(1)}, bf16[512,384]{1,0:T(8,128)(2,1)S(1)}) custom-call(f32[512,384]{1,0:T(8,128)S(1)} %back_own.4.own_ref, bf16[512,384]{1,0:T(8,128)(2,1)S(1)} %collective-permute-done.6.partner_ref, f32[512,384]{1,0:T(8,128)S(1)} %get-tuple-element.97.old_ref.stream_ref, f32[3,384]{1,0:T(4,128)S(1)} %get-tuple-element.89.rest_0_.alphas_ref, ...), custom_call_target="tpu_custom_call" | custom-call | flops 117964800 | bytes 34140160 | tf_op jit(solution)/shard_map/combine/pallas_call | solution.py:435
  24.0 0.9 back_partner.5
  24.9 0.9 back_own.5.own_ref
  26.1 1.4 %paired_weight.3 = (bf16[192,1152]{1,0:T(8,128)(2,1)S(1)}, bf16[192,1152]{1,0:T(8,128)(2,1)S(1)}) custom-call(bf16[384,512]{1,0:T(8,128)(2,1)S(1)} %own_rows.3.own_ref, bf16[512,1152]{1,0:T(8,128)(2,1)S(1)} %get-tuple-element.101.shifted_ref, bf16[192,512]{1,0:T(8,128)(2,1)S(1)} %collective-permute-done.7.across_ref, ...), custom_call_target="tpu_custom_call" | custom-call | flops 9059696640 | bytes 40304640 | tf_op jit(solution)/shard_map/paired_weight/pallas_call | solution.py:435
  28.0 1.4 %combine.5.rest_0_ = f32[1,384]{1,0:T(1,128)S(1)} custom-call(f32[512,384]{1,0:T(8,128)S(1)} %back_own.5.own_ref, bf16[512,384]{1,0:T(8,128)(2,1)S(1)} %collective-permute-done.9.partner_ref, f32[512,384]{1,0:T(8,128)S(1)} %get-tuple-element.87.old_ref.stream_ref, f32[3,384]{1,0:T(4,128)S(1)} %get-tuple-element.89.rest_0_.alphas_ref), custom_call_target="tpu_custom_call" | custom-call | flops 117964800 | bytes 19722240 | tf_op jit(solution)/shard_map/combine/pallas_call | solution.py:435
  30.4 2.9 %collective-permute-done.10.across_ref = bf16[192,512]{1,0:T(8,128)(2,1)S(1)} collective-permute-done((bf16[192,512]{1,0:T(8,128)(2,1)S(1)}, bf16[192,512]{1,0:T(8,128)(2,1)S(1)}, u32[]{:S(2)}, u32[]{:S(2)}) %collective-permute-start.10) | collective-permute-done | bytes 196640 | tf_op jit(solution)/shard_map/ppermute | solution.py:451
  34.1 1.6 %forward_partner.5 = bf16[512,384]{1,0:T(8,128)(2,1)} custom-call(bf16[512,384]{1,0:T(8,128)(2,1)S(1)} %collective-permute-done.2.partner_ref.snake_ref, bf16[2,1152,384]{2,1,0:T(8,128)(2,1)S(1)} %get-tuple-element.84.weight_ref, f32[512,384]{1,0:T(8,128)S(1)} %forward_own.5.own_ref, f32[512,384]{1,0:T(8,128)S(1)} %get-tuple-element.102.stream_ref.old_ref, ...), custom_call_target="tpu_custom_call" | custom-call | flops 4529848320 | bytes 43909120 | tf_op jit(solution)/shard_map/forward_partner/pallas_call | solution.py:435
  35.7 1.4 %paired_weight.4 = (bf16[208,1152]{1,0:T(8,128)(2,1)S(1)}, bf16[192,1152]{1,0:T(8,128)(2,1)S(1)}) custom-call(bf16[384,512]{1,0:T(8,128)(2,1)S(1)} %own_rows.4.own_ref, bf16[512,1152]{1,0:T(8,128)(2,1)S(1)} %get-tuple-element.110.shifted_ref, bf16[192,512]{1,0:T(8,128)(2,1)S(1)} %collective-permute-done.10.across_ref, ...), custom_call_target="tpu_custom_call" | custom-call | flops 9059696640 | bytes 40719360 | tf_op jit(solution)/shard_map/paired_weight/pallas_call | solution.py:435
  37.7 1.5 %collective-permute-start.14 = (bf16[192,512]{1,0:T(8,128)(2,1)S(1)}, bf16[192,512]{1,0:T(8,128)(2,1)S(1)}, u32[]{:S(2)}, u32[]{:S(2)}) collective-permute-start(bf16[192,512]{1,0:T(8,128)(2,1)S(1)} %turn.5), channel_id=1, source_target_pairs={{0,2},{2,0},{1,3},{3,1},{4,6},{6,4},{5,7},{7,5},{8,10},{10,8},{9,1... | collective-permute-start | bytes 589832 | tf_op jit(solution)/shard_map/ppermute | solution.py:451
  39.6 13.3 %collective-permute-done.14.across_ref = bf16[192,512]{1,0:T(8,128)(2,1)S(1)} collective-permute-done((bf16[192,512]{1,0:T(8,128)(2,1)S(1)}, bf16[192,512]{1,0:T(8,128)(2,1)S(1)}, u32[]{:S(2)}, u32[]{:S(2)}) %collective-permute-start.14) | collective-permute-done | bytes 196640 | tf_op jit(solution)/shard_map/ppermute | solution.py:451
  53.0 1.6 %collective-permute-start.16 = (bf16[96,1152]{1,0:T(8,128)(2,1)S(1)}, bf16[96,1152]{1,0:T(8,128)(2,1)S(1)}, u32[]{:S(2)}, u32[]{:S(2)}) collective-permute-start(bf16[96,1152]{1,0:T(8,128)(2,1)S(1)} %fold.3), channel_id=1, source_target_pairs={{0,12},{4,8},{8,4},{12,0},{1,13},{5,9},{9,5},{13,1},{2,14},{6,10},... | collective-permute-start | bytes 663560 | tf_op jit(solution)/shard_map/ppermute | solution.py:451
  54.8 1.4 %paired_weight.5 = (bf16[192,1152]{1,0:T(8,128)(2,1)S(1)}, bf16[192,1152]{1,0:T(8,128)(2,1)S(1)}) custom-call(bf16[384,512]{1,0:T(8,128)(2,1)S(1)} %own_rows.5.own_ref, bf16[512,1152]{1,0:T(8,128)(2,1)S(1)} %get-tuple-element.115.shifted_ref, bf16[192,512]{1,0:T(8,128)(2,1)S(1)} %collective-permute-done.14.across_ref, ...), custom_call_target="tpu_custom_call" | custom-call | flops 9059696 | bytes 40304 | tf_op jit(solution)/shard_map/paired_weight/pallas_call | solution.py:435
  56.2 2.5 %collective-permute-start.18 = (bf16[192,1152]{1,0:T(8,128)(2,1)S(1)}, bf16[192,1152]{1,0:T(8,128)(2,1)S(1)}, u32[]{:S(2)}, u32[]{:S(2)}) collective-permute-start(bf16[192,1152]{1,0:T(8,128)(2,1)S(1)} %get-tuple-element.144), channel_id=1, source_target_pairs={{0,4},{4,0},{8,12},{12,8},{1,5},{5,1},{9,13},{13,9},{2,6},{6,2},{1... | collective-permute-start | bytes 1327112 | tf_op jit(solution)/shard_map/ppermute | solution.py:451
  58.8 6.8 %collective-permute-done.16.late = bf16[96,1152]{1,0:T(8,128)(2,1)S(1)} collective-permute-done((bf16[96,1152]{1,0:T(8,128)(2,1)S(1)}, bf16[96,1152]{1,0:T(8,128)(2,1)S(1)}, u32[]{:S(2)}, u32[]{:S(2)}) %collective-permute-start.16) | collective-permute-done | bytes 221216 | tf_op jit(solution)/shard_map/ppermute | solution.py:451
  65.8 1.6 %collective-permute-start.19 = (bf16[112,1152]{1,0:T(8,128)(2,1)S(1)}, bf16[112,1152]{1,0:T(8,128)(2,1)S(1)}, u32[]{:S(2)}, u32[]{:S(2)}) collective-permute-start(bf16[112,1152]{1,0:T(8,128)(2,1)S(1)} %get-tuple-element.146), channel_id=1, source_target_pairs={{0,12},{4,8},{8,4},{12,0},{1,13},{5,9},{9,5},{13,1},{2,14},{6,10},... | collective-permute-start | bytes 774152 | tf_op jit(solution)/shard_map/ppermute | solution.py:451
  68.0 4.9 %collective-permute-done.18.got = bf16[192,1152]{1,0:T(8,128)(2,1)S(1)} collective-permute-done((bf16[192,1152]{1,0:T(8,128)(2,1)S(1)}, bf16[192,1152]{1,0:T(8,128)(2,1)S(1)}, u32[]{:S(2)}, u32[]{:S(2)}) %collective-permute-start.18) | collective-permute-done | bytes 442400 | tf_op jit(solution)/shard_map/ppermute | solution.py:451
  73.3 12.0 %collective-permute-done.19.late = bf16[112,1152]{1,0:T(8,128)(2,1)S(1)} collective-permute-done((bf16[112,1152]{1,0:T(8,128)(2,1)S(1)}, bf16[112,1152]{1,0:T(8,128)(2,1)S(1)}, u32[]{:S(2)}, u32[]{:S(2)}) %collective-permute-start.19) | collective-permute-done | bytes 258080 | tf_op jit(solution)/shard_map/ppermute | solution.py:451
  86.0 2.7 %collective-permute-done.20.late = bf16[96,1152]{1,0:T(8,128)(2,1)S(1)} collective-permute-done((bf16[96,1152]{1,0:T(8,128)(2,1)S(1)}, bf16[96,1152]{1,0:T(8,128)(2,1)S(1)}, u32[]{:S(2)}, u32[]{:S(2)}) %collective-permute-start.20) | collective-permute-done | bytes 221216 | tf_op jit(solution)/shard_map/ppermute | solution.py:451
  89.4 3.8 %collective-permute-done.22.refs_4_ = bf16[112,1152]{1,0:T(8,128)(2,1)S(1)} collective-permute-done((bf16[112,1152]{1,0:T(8,128)(2,1)S(1)}, bf16[112,1152]{1,0:T(8,128)(2,1)S(1)}, u32[]{:S(2)}, u32[]{:S(2)}) %collective-permute-start.22) | collective-permute-done | bytes 258080 | tf_op jit(solution)/shard_map/ppermute | solution.py:451
  93.2 1.9 %finish.2 = (f32[3,3,192,384]{3,2,1,0:T(8,128)}, f32[3,384]{1,0:T(4,128)}) custom-call(f32[1,1152]{1,0:T(1,128)S(1)} %get-tuple-element.149.refs_0_, bf16[96,1152]{1,0:T(8,128)(2,1)S(1)} %total.3.refs_1_, bf16[96,1152]{1,0:T(8,128)(2,1)S(1)} %collective-permute-done.21.refs_2_, bf16[112,1152]{1,0:T(8,128)(2,1)S(1)} %get-tuple-element.151.refs_3_, ...), custom_call_target="tpu_custom_call" | custom-call | flops 6635520 | bytes 36218880 | tf_op jit(solution)/shard_map/finish/pallas_call | solution.py:435
  95.1 1.4 %collective-permute-done.23.refs_2_ = bf16[96,1152]{1,0:T(8,128)(2,1)S(1)} collective-permute-done((bf16[96,1152]{1,0:T(8,128)(2,1)S(1)}, bf16[96,1152]{1,0:T(8,128)(2,1)S(1)}, u32[]{:S(2)}, u32[]{:S(2)}) %collective-permute-start.23) | collective-permute-done | bytes 221216 | tf_op jit(solution)/shard_map/ppermute | solution.py:451
  96.5 1.0 %finish.3 = f32[3,3,192,384]{3,2,1,0:T(8,128)} custom-call(f32[3,3,192,384]{3,2,1,0:T(8,128)} %get-tuple-element.152.refs_0_, bf16[96,1152]{1,0:T(8,128)(2,1)S(1)} %total.5.refs_1_, bf16[96,1152]{1,0:T(8,128)(2,1)S(1)} %collective-permute-done.23.refs_2_), custom_call_target="tpu_custom_call", output_to_operand_aliasing={{}: (0, {})} | custom-call | flops 6635520 | bytes 57507840 | tf_op jit(solution)/shard_map/finish/pallas_call | solution.py:435
  (52 shorter events, 12.1 us)
Async XLA Ops:
  3.2 2.3 %collective-permute-start = (bf16[512,384]{1,0:T(8,128)(2,1)S(1)}, bf16[512,384]{1,0:T(8,128)(2,1)S(1)}, u32[]{:S(2)}, u32[]{:S(2)}) collective-permute-start(bf16[512,384]{1,0:T(8,128)(2,1)S(1)} %get-tuple-element.124.snake_ref.refs_0_.own_ref), channel_id=1, source_target_pairs={{0,1},{1,0},{2,3},{3,2},{4,5},{5,4},{6,7},{7,6},{8,9},{9,8},{10,11... | collective-permute-start | bytes 1179656 | tf_op jit(solution)/shard_map/ppermute | solution.py:451
  4.9 12.0 %collective-permute-start.5 = (bf16[512,384]{1,0:T(8,128)(2,1)S(1)}, bf16[512,384]{1,0:T(8,128)(2,1)S(1)}, u32[]{:S(2)}, u32[]{:S(2)}) collective-permute-start(bf16[512,384]{1,0:T(8,128)(2,1)S(1)} %get-tuple-element.105.grad_ref.rest_0_), channel_id=1, source_target_pairs={{0,2},{2,0},{1,3},{3,1},{4,6},{6,4},{5,7},{7,5},{8,10},{10,8},{9,1... | collective-permute-start | bytes 1179656 | tf_op jit(solution)/shard_map/ppermute | solution.py:451
  7.8 2.4 %collective-permute-start.1 = (bf16[512,384]{1,0:T(8,128)(2,1)S(1)}, bf16[512,384]{1,0:T(8,128)(2,1)S(1)}, u32[]{:S(2)}, u32[]{:S(2)}) collective-permute-start(bf16[512,384]{1,0:T(8,128)(2,1)S(1)} %get-tuple-element.121.snake_ref.refs_0_.own_ref), channel_id=1, source_target_pairs={{0,1},{1,0},{2,3},{3,2},{4,5},{5,4},{6,7},{7,6},{8,9},{9,8},{10,11... | collective-permute-start | bytes 1179656 | tf_op jit(solution)/shard_map/ppermute | solution.py:451
  9.0 5.8 %collective-permute-start.3 = (bf16[512,384]{1,0:T(8,128)(2,1)S(1)}, bf16[512,384]{1,0:T(8,128)(2,1)S(1)}, u32[]{:S(2)}, u32[]{:S(2)}) collective-permute-start(bf16[512,384]{1,0:T(8,128)(2,1)S(1)} %get-tuple-element.94), channel_id=1, source_target_pairs={{0,1},{1,0},{2,3},{3,2},{4,5},{5,4},{6,7},{7,6},{8,9},{9,8},{10,11... | collective-permute-start | bytes 1179656 | tf_op jit(solution)/shard_map/ppermute | solution.py:451
  11.9 5.4 %collective-permute-start.2 = (bf16[512,384]{1,0:T(8,128)(2,1)S(1)}, bf16[512,384]{1,0:T(8,128)(2,1)S(1)}, u32[]{:S(2)}, u32[]{:S(2)}) collective-permute-start(bf16[512,384]{1,0:T(8,128)(2,1)S(1)} %get-tuple-element.125.refs_0_.own_ref.snake_ref), channel_id=1, source_target_pairs={{0,1},{1,0},{2,3},{3,2},{4,5},{5,4},{6,7},{7,6},{8,9},{9,8},{10,11... | collective-permute-start | bytes 1179656 | tf_op jit(solution)/shard_map/ppermute | solution.py:451
  12.3 9.2 %collective-permute-start.7 = (bf16[192,512]{1,0:T(8,128)(2,1)S(1)}, bf16[192,512]{1,0:T(8,128)(2,1)S(1)}, u32[]{:S(2)}, u32[]{:S(2)}) collective-permute-start(bf16[192,512]{1,0:T(8,128)(2,1)S(1)} %turn.3), channel_id=1, source_target_pairs={{0,2},{2,0},{1,3},{3,1},{4,6},{6,4},{5,7},{7,5},{8,10},{10,8},{9,1... | collective-permute-start | bytes 589832 | tf_op jit(solution)/shard_map/ppermute | solution.py:451
  16.9 13.0 %collective-permute-start.4 = (bf16[512,384]{1,0:T(8,128)(2,1)S(1)}, bf16[512,384]{1,0:T(8,128)(2,1)S(1)}, u32[]{:S(2)}, u32[]{:S(2)}) collective-permute-start(bf16[512,384]{1,0:T(8,128)(2,1)S(1)} %get-tuple-element.109.grad_ref), channel_id=1, source_target_pairs={{0,2},{2,0},{1,3},{3,1},{4,6},{6,4},{5,7},{7,5},{8,10},{10,8},{9,1... | collective-permute-start | bytes 1179656 | tf_op jit(solution)/shard_map/ppermute | solution.py:451
  17.8 15.5 %collective-permute-start.10 = (bf16[192,512]{1,0:T(8,128)(2,1)S(1)}, bf16[192,512]{1,0:T(8,128)(2,1)S(1)}, u32[]{:S(2)}, u32[]{:S(2)}) collective-permute-start(bf16[192,512]{1,0:T(8,128)(2,1)S(1)} %turn.4), channel_id=1, source_target_pairs={{0,2},{2,0},{1,3},{3,1},{4,6},{6,4},{5,7},{7,5},{8,10},{10,8},{9,1... | collective-permute-start | bytes 589832 | tf_op jit(solution)/shard_map/ppermute | solution.py:451
  20.5 1.8 %collective-permute-start.6 = (bf16[512,384]{1,0:T(8,128)(2,1)S(1)}, bf16[512,384]{1,0:T(8,128)(2,1)S(1)}, u32[]{:S(2)}, u32[]{:S(2)}) collective-permute-start(bf16[512,384]{1,0:T(8,128)(2,1)S(1)} %get-tuple-element.111), channel_id=1, source_target_pairs={{0,1},{1,0},{2,3},{3,2},{4,5},{5,4},{6,7},{7,6},{8,9},{9,8},{10,11... | collective-permute-start | bytes 1179656 | tf_op jit(solution)/shard_map/ppermute | solution.py:451
  21.5 4.5 %collective-permute-start.8 = (bf16[192,512]{1,0:T(8,128)(2,1)S(1)}, bf16[192,512]{1,0:T(8,128)(2,1)S(1)}, u32[]{:S(2)}, u32[]{:S(2)}) collective-permute-start(bf16[192,512]{1,0:T(8,128)(2,1)S(1)} %collective-permute-done.7.across_ref), channel_id=1, source_target_pairs={{0,1},{1,0},{2,3},{3,2},{4,5},{5,4},{6,7},{7,6},{8,9},{9,8},{10,11... | collective-permute-start | bytes 589832 | tf_op jit(solution)/shard_map/ppermute | solution.py:451
  25.8 2.1 %collective-permute-start.9 = (bf16[512,384]{1,0:T(8,128)(2,1)S(1)}, bf16[512,384]{1,0:T(8,128)(2,1)S(1)}, u32[]{:S(2)}, u32[]{:S(2)}) collective-permute-start(bf16[512,384]{1,0:T(8,128)(2,1)S(1)} %get-tuple-element.120), channel_id=1, source_target_pairs={{0,1},{1,0},{2,3},{3,2},{4,5},{5,4},{6,7},{7,6},{8,9},{9,8},{10,11... | collective-permute-start | bytes 1179656 | tf_op jit(solution)/shard_map/ppermute | solution.py:451
  27.4 25.5 %collective-permute-start.13 = (bf16[192,1152]{1,0:T(8,128)(2,1)S(1)}, bf16[192,1152]{1,0:T(8,128)(2,1)S(1)}, u32[]{:S(2)}, u32[]{:S(2)}) collective-permute-start(bf16[192,1152]{1,0:T(8,128)(2,1)S(1)} %get-tuple-element.134), channel_id=1, source_target_pairs={{0,4},{4,0},{8,12},{12,8},{1,5},{5,1},{9,13},{13,9},{2,6},{6,2},{1... | collective-permute-start | bytes 1327112 | tf_op jit(solution)/shard_map/ppermute | solution.py:451
  33.3 2.4 %collective-permute-start.11 = (bf16[192,512]{1,0:T(8,128)(2,1)S(1)}, bf16[192,512]{1,0:T(8,128)(2,1)S(1)}, u32[]{:S(2)}, u32[]{:S(2)}) collective-permute-start(bf16[192,512]{1,0:T(8,128)(2,1)S(1)} %collective-permute-done.10.across_ref), channel_id=1, source_target_pairs={{0,1},{1,0},{2,3},{3,2},{4,5},{5,4},{6,7},{7,6},{8,9},{9,8},{10,11... | collective-permute-start | bytes 589832 | tf_op jit(solution)/shard_map/ppermute | solution.py:451
  37.1 17.5 %collective-permute-start.12 = (bf16[512,384]{1,0:T(8,128)(2,1)S(1)}, bf16[512,384]{1,0:T(8,128)(2,1)S(1)}, u32[]{:S(2)}, u32[]{:S(2)}) collective-permute-start(bf16[512,384]{1,0:T(8,128)(2,1)S(1)} %get-tuple-element.132.grad_ref), channel_id=1, source_target_pairs={{0,2},{2,0},{1,3},{3,1},{4,6},{6,4},{5,7},{7,5},{8,10},{10,8},{9,1... | collective-permute-start | bytes 1179656 | tf_op jit(solution)/shard_map/ppermute | solution.py:451
  37.7 15.2 %collective-permute-start.14 = (bf16[192,512]{1,0:T(8,128)(2,1)S(1)}, bf16[192,512]{1,0:T(8,128)(2,1)S(1)}, u32[]{:S(2)}, u32[]{:S(2)}) collective-permute-start(bf16[192,512]{1,0:T(8,128)(2,1)S(1)} %turn.5), channel_id=1, source_target_pairs={{0,2},{2,0},{1,3},{3,1},{4,6},{6,4},{5,7},{7,5},{8,10},{10,8},{9,1... | collective-permute-start | bytes 589832 | tf_op jit(solution)/shard_map/ppermute | solution.py:451
  39.2 26.5 %collective-permute-start.17 = (bf16[208,1152]{1,0:T(8,128)(2,1)S(1)}, bf16[208,1152]{1,0:T(8,128)(2,1)S(1)}, u32[]{:S(2)}, u32[]{:S(2)}) collective-permute-start(bf16[208,1152]{1,0:T(8,128)(2,1)S(1)} %get-tuple-element.141), channel_id=1, source_target_pairs={{0,4},{4,0},{8,12},{12,8},{1,5},{5,1},{9,13},{13,9},{2,6},{6,2},{1... | collective-permute-start | bytes 1437704 | tf_op jit(solution)/shard_map/ppermute | solution.py:451
  52.9 1.9 %collective-permute-start.15 = (bf16[192,512]{1,0:T(8,128)(2,1)S(1)}, bf16[192,512]{1,0:T(8,128)(2,1)S(1)}, u32[]{:S(2)}, u32[]{:S(2)}) collective-permute-start(bf16[192,512]{1,0:T(8,128)(2,1)S(1)} %collective-permute-done.14.across_ref), channel_id=1, source_target_pairs={{0,1},{1,0},{2,3},{3,2},{4,5},{5,4},{6,7},{7,6},{8,9},{9,8},{10,11... | collective-permute-start | bytes 589832 | tf_op jit(solution)/shard_map/ppermute | solution.py:451
  53.0 12.6 %collective-permute-start.16 = (bf16[96,1152]{1,0:T(8,128)(2,1)S(1)}, bf16[96,1152]{1,0:T(8,128)(2,1)S(1)}, u32[]{:S(2)}, u32[]{:S(2)}) collective-permute-start(bf16[96,1152]{1,0:T(8,128)(2,1)S(1)} %fold.3), channel_id=1, source_target_pairs={{0,12},{4,8},{8,4},{12,0},{1,13},{5,9},{9,5},{13,1},{2,14},{6,10},... | collective-permute-start | bytes 663560 | tf_op jit(solution)/shard_map/ppermute | solution.py:451
  56.2 16.6 %collective-permute-start.18 = (bf16[192,1152]{1,0:T(8,128)(2,1)S(1)}, bf16[192,1152]{1,0:T(8,128)(2,1)S(1)}, u32[]{:S(2)}, u32[]{:S(2)}) collective-permute-start(bf16[192,1152]{1,0:T(8,128)(2,1)S(1)} %get-tuple-element.144), channel_id=1, source_target_pairs={{0,4},{4,0},{8,12},{12,8},{1,5},{5,1},{9,13},{13,9},{2,6},{6,2},{1... | collective-permute-start | bytes 1327112 | tf_op jit(solution)/shard_map/ppermute | solution.py:451
  65.8 19.5 %collective-permute-start.19 = (bf16[112,1152]{1,0:T(8,128)(2,1)S(1)}, bf16[112,1152]{1,0:T(8,128)(2,1)S(1)}, u32[]{:S(2)}, u32[]{:S(2)}) collective-permute-start(bf16[112,1152]{1,0:T(8,128)(2,1)S(1)} %get-tuple-element.146), channel_id=1, source_target_pairs={{0,12},{4,8},{8,4},{12,0},{1,13},{5,9},{9,5},{13,1},{2,14},{6,10},... | collective-permute-start | bytes 774152 | tf_op jit(solution)/shard_map/ppermute | solution.py:451
  67.4 22.0 %collective-permute-start.21 = (bf16[96,1152]{1,0:T(8,128)(2,1)S(1)}, bf16[96,1152]{1,0:T(8,128)(2,1)S(1)}, u32[]{:S(2)}, u32[]{:S(2)}) collective-permute-start(bf16[96,1152]{1,0:T(8,128)(2,1)S(1)} %total.3.refs_1_), channel_id=1, source_target_pairs={{0,2},{2,0},{1,3},{3,1},{4,6},{6,4},{5,7},{7,5},{8,10},{10,8},{9,1... | collective-permute-start | bytes 663560 | tf_op jit(solution)/shard_map/ppermute | solution.py:451
  72.9 15.8 %collective-permute-start.20 = (bf16[96,1152]{1,0:T(8,128)(2,1)S(1)}, bf16[96,1152]{1,0:T(8,128)(2,1)S(1)}, u32[]{:S(2)}, u32[]{:S(2)}) collective-permute-start(bf16[96,1152]{1,0:T(8,128)(2,1)S(1)} %fold.5), channel_id=1, source_target_pairs={{0,12},{4,8},{8,4},{12,0},{1,13},{5,9},{9,5},{13,1},{2,14},{6,10},... | collective-permute-start | bytes 663560 | tf_op jit(solution)/shard_map/ppermute | solution.py:451
  85.4 7.8 %collective-permute-start.22 = (bf16[112,1152]{1,0:T(8,128)(2,1)S(1)}, bf16[112,1152]{1,0:T(8,128)(2,1)S(1)}, u32[]{:S(2)}, u32[]{:S(2)}) collective-permute-start(bf16[112,1152]{1,0:T(8,128)(2,1)S(1)} %get-tuple-element.151.refs_3_), channel_id=1, source_target_pairs={{0,2},{2,0},{1,3},{3,1},{4,6},{6,4},{5,7},{7,5},{8,10},{10,8},{9,1... | collective-permute-start | bytes 774152 | tf_op jit(solution)/shard_map/ppermute | solution.py:451
  88.8 7.7 %collective-permute-start.23 = (bf16[96,1152]{1,0:T(8,128)(2,1)S(1)}, bf16[96,1152]{1,0:T(8,128)(2,1)S(1)}, u32[]{:S(2)}, u32[]{:S(2)}) collective-permute-start(bf16[96,1152]{1,0:T(8,128)(2,1)S(1)} %total.5.refs_1_), channel_id=1, source_target_pairs={{0,2},{2,0},{1,3},{3,1},{4,6},{6,4},{5,7},{7,5},{8,10},{10,8},{9,1... | collective-permute-start | bytes 663560 | tf_op jit(solution)/shard_map/ppermute | solution.py:451

commit v8 on v6

--- a/solution.py
+++ b/solution.py
@@ -250,7 +250,7 @@
 
 def block_place(pieces, slice_index, part):
     apart = jnp.bitwise_xor(slice_index, lax.axis_index("dp"))
-    order = (2 * pieces, 0, 1, 2 * pieces + 1)
+    order = (2 * pieces, 0, 2 * pieces + 1, 1)
     return 2 * part + jnp.where(
         apart == 0, order[0], jnp.where(apart == 1, order[1], jnp.where(apart == 2, order[2], order[3]))
     )
@@ -616,7 +616,7 @@
         )
         if carried:
             carry_sum[0] = result[1]
-        late[layer, part] = swap(result[0], "dp", lambda i: i ^ 3)
+        late[layer, part] = swap(result[0], "dp", lambda i: i ^ 2)
 
     def total(layer, part=0):
         if not fast:
@@ -689,8 +689,8 @@
         axis, apart = rounds.pop(0)
         arrivals.append((value, swap(value, axis, lambda place: place ^ apart)))
 
+    forward_own(0, load=2)
     send_gradient(2)
-    forward_own(0, load=2)
     forward_partner(0, load=1)
     back_partner(2)
     forward_own(1)
@@ -714,18 +714,18 @@
     own_rows(1)
     own_rows(0)
     forward_own(2)
-    residual_out = forward_partner(2)
     far_rows(1)
-    fold(2)
     share(1, 0)
     send_gradient(0)
-    sequence.weight = 10
-    total(2)
+    sequence.weight = 0.01
+    residual_out = forward_partner(2)
+    fold(2)
     weights(1)
-    cross(2)
     sequence.weight = 0.01
     far_rows(0)
     weights(0)
+    total(2)
+    cross(2)
     sequence.weight = 10
     fold(1)
     fold(0)

time: 97.4 us -> 96.7 us (level)
  starting transfers between devices: 28.6 us -> 23.2 us
  waiting for transfers between devices: 36.6 us -> 41.4 us
    ppermute x22, starting transfers between devices: 28.6 us -> 23.2 us  [swap(): lax.ppermute(x, axis, [(i, other(i)) for i in range(lax.axis_size(axis))])]
    ppermute x22, waiting for transfers between devices: 36.6 us -> 41.4 us  [swap(): lax.ppermute(x, axis, [(i, other(i)) for i in range(lax.axis_size(axis))])]
  transfers between devices with their start and end apart: 22 -> 22, of which waited for: 12 -> 9; matrix products, arithmetic and copies ran while one was open for 0% -> 0% of each run, Pallas kernels for 28% -> 28%
where the time goes in v8:
time: 96.7 us; the launch traced here: 96.5 us
  waiting for transfers between devices  41.4 us (43%)
  Pallas kernels  30.9 us (32%)
  starting transfers between devices  23.2 us (24%)
  between operations  1.1 us (1%)
    ppermute x22, waiting for transfers between devices, swap(): lax.ppermute(x, axis, [(i, other(i)) for i in range(lax.axis_size(axis))])  41.4 us
    pallas_call x35, Pallas kernels, call(): pl.pallas_call(kernel, in_specs=[ANY_HBM if i else IN_VMEM for i in ins],...  30.9 us
    ppermute x22, starting transfers between devices, swap(): lax.ppermute(x, axis, [(i, other(i)) for i in range(lax.axis_size(axis))])  23.2 us
  transfers between devices with their start and end apart: 22, of which 9 were waited for; matrix products, arithmetic and copies ran while one was open for 0% of the time, Pallas kernels for 28%

profile of v8, /device:TPU:0, one launch (start us, length us, event | category | flops | bytes accessed | tf_op | source)
XLA Modules:
  0.0 96.5 jit_solution(7422469008793679499)
XLA Ops:
  0.6 2.5 %prep.1 = (f32[512,384]{1,0:T(8,128)S(1)}, bf16[512,384]{1,0:T(8,128)(2,1)S(1)}, bf16[512,384]{1,0:T(8,128)(2,1)S(1)}, f32[512,128]{1,0:T(8,128)S(1)}, f32[3,384...) custom-call(s32[16]{0:T(128)} %len_hbm.1, s32[16]{0:T(128)} %own_hbm.1, s32[16]{0:T(128)} %start_hbm.1, ...), custom_call_target="tpu_custom_call" | custom-call | flops 78643200 | bytes 44003200 | tf_op jit(solution)/shard_map/prep/pallas_call | solution.py:435
  3.7 1.6 %forward_own.3 = (f32[512,384]{1,0:T(8,128)S(1)}, bf16[2,1152,384]{2,1,0:T(8,128)(2,1)S(1)}) custom-call(bf16[512,384]{1,0:T(8,128)(2,1)S(1)} %get-tuple-element.120.snake_ref.refs_1_.own_ref, bf16[2,1152,384]{2,1,0:T(8,128)(2,1)S(1)} %get-tuple-element.80.weight_ref, bf16[3,3,768,384]{3,2,1,0:T(8,128)(2,1)} %rest_1_.1), custom_call_target="tpu_custom_call" | custom-call | flops 4529848320 | bytes 47185920 | tf_op jit(solution)/shard_map/forward_own/pallas_call | solution.py:435
  5.3 2.6 %collective-permute-start.5 = (bf16[512,384]{1,0:T(8,128)(2,1)S(1)}, bf16[512,384]{1,0:T(8,128)(2,1)S(1)}, u32[]{:S(2)}, u32[]{:S(2)}) collective-permute-start(bf16[512,384]{1,0:T(8,128)(2,1)S(1)} %get-tuple-element.103.grad_ref.rest_0_), channel_id=1, source_target_pairs={{0,2},{2,0},{1,3},{3,1},{4,6},{6,4},{5,7},{7,5},{8,10},{10,8},{9,1... | collective-permute-start | bytes 1179656 | tf_op jit(solution)/shard_map/ppermute | solution.py:451
  7.9 2.3 %forward_partner.3 = (f32[512,384]{1,0:T(8,128)S(1)}, bf16[512,384]{1,0:T(8,128)(2,1)S(1)}, bf16[2,1152,384]{2,1,0:T(8,128)(2,1)S(1)}) custom-call(bf16[512,384]{1,0:T(8,128)(2,1)S(1)} %collective-permute-done.snake_ref.partner_ref, bf16[2,1152,384]{2,1,0:T(8,128)(2,1)S(1)} %get-tuple-element.80.weight_ref, f32[512,384]{1,0:T(8,128)S(1)} %get-tuple-element.84.own_ref, ...), custom_call_target="tpu_custom_call" | custom-call | flops 4529848320 | bytes 69514240 | tf_op jit(solution)/shard_map/forward_partner/pallas_call | solution.py:435
  10.5 0.9 back_partner.3
  12.6 1.7 %forward_partner.4 = (f32[512,384]{1,0:T(8,128)S(1)}, bf16[512,384]{1,0:T(8,128)(2,1)S(1)}) custom-call(bf16[512,384]{1,0:T(8,128)(2,1)S(1)} %collective-permute-done.1.snake_ref.partner_ref, bf16[2,1152,384]{2,1,0:T(8,128)(2,1)S(1)} %get-tuple-element.90.weight_ref, f32[512,384]{1,0:T(8,128)S(1)} %forward_own.4.own_ref, ...), custom_call_target="tpu_custom_call" | custom-call | flops 4529848320 | bytes 51819520 | tf_op jit(solution)/shard_map/forward_partner/pallas_call | solution.py:435
  16.0 1.6 %combine.3 = (f32[1,384]{1,0:T(1,128)S(1)}, f32[512,384]{1,0:T(8,128)S(1)}, bf16[512,384]{1,0:T(8,128)(2,1)S(1)}) custom-call(f32[512,384]{1,0:T(8,128)S(1)} %back_own.3.own_ref, bf16[512,384]{1,0:T(8,128)(2,1)S(1)} %collective-permute-done.3.partner_ref, f32[512,384]{1,0:T(8,128)S(1)} %get-tuple-element.100.stream_ref.old_ref, ...), custom_call_target="tpu_custom_call" | custom-call | flops 117964800 | bytes 38072320 | tf_op jit(solution)/shard_map/combine/pallas_call | solution.py:435
  17.7 2.1 %collective-permute-start.4 = (bf16[512,384]{1,0:T(8,128)(2,1)S(1)}, bf16[512,384]{1,0:T(8,128)(2,1)S(1)}, u32[]{:S(2)}, u32[]{:S(2)}) collective-permute-start(bf16[512,384]{1,0:T(8,128)(2,1)S(1)} %get-tuple-element.107.grad_ref), channel_id=1, source_target_pairs={{0,2},{2,0},{1,3},{3,1},{4,6},{6,4},{5,7},{7,5},{8,10},{10,8},{9,1... | collective-permute-start | bytes 1179656 | tf_op jit(solution)/shard_map/ppermute | solution.py:451
  20.7 0.9 back_partner.4
  23.4 1.7 %combine.4 = (f32[1,384]{1,0:T(1,128)S(1)}, bf16[512,384]{1,0:T(8,128)(2,1)S(1)}) custom-call(f32[512,384]{1,0:T(8,128)S(1)} %back_own.4.own_ref, bf16[512,384]{1,0:T(8,128)(2,1)S(1)} %collective-permute-done.6.partner_ref, f32[512,384]{1,0:T(8,128)S(1)} %get-tuple-element.95.old_ref.stream_ref, f32[3,384]{1,0:T(4,128)S(1)} %get-tuple-element.87.rest_0_.alphas_ref, ...), custom_call_target="tpu_custom_call" | custom-call | flops 117964800 | bytes 34140160 | tf_op jit(solution)/shard_map/combine/pallas_call | solution.py:435
  26.0 0.9 back_own.5.own_ref
  27.1 1.4 %paired_weight.3 = (bf16[192,1152]{1,0:T(8,128)(2,1)S(1)}, bf16[192,1152]{1,0:T(8,128)(2,1)S(1)}) custom-call(bf16[384,512]{1,0:T(8,128)(2,1)S(1)} %own_rows.3.own_ref, bf16[512,1152]{1,0:T(8,128)(2,1)S(1)} %get-tuple-element.99.shifted_ref, bf16[192,512]{1,0:T(8,128)(2,1)S(1)} %collective-permute-done.7.across_ref, ...), custom_call_target="tpu_custom_call" | custom-call | flops 9059696640 | bytes 40304640 | tf_op jit(solution)/shard_map/paired_weight/pallas_call | solution.py:435
  28.5 1.9 %collective-permute-start.10 = (bf16[192,1152]{1,0:T(8,128)(2,1)S(1)}, bf16[192,1152]{1,0:T(8,128)(2,1)S(1)}, u32[]{:S(2)}, u32[]{:S(2)}) collective-permute-start(bf16[192,1152]{1,0:T(8,128)(2,1)S(1)} %get-tuple-element.125), channel_id=1, source_target_pairs={{0,4},{4,0},{8,12},{12,8},{1,5},{5,1},{9,13},{13,9},{2,6},{6,2},{1... | collective-permute-start | bytes 1327112 | tf_op jit(solution)/shard_map/ppermute | solution.py:451
  30.4 1.4 %combine.5.rest_0_ = f32[1,384]{1,0:T(1,128)S(1)} custom-call(f32[512,384]{1,0:T(8,128)S(1)} %back_own.5.own_ref, bf16[512,384]{1,0:T(8,128)(2,1)S(1)} %collective-permute-done.9.partner_ref, f32[512,384]{1,0:T(8,128)S(1)} %get-tuple-element.85.old_ref.stream_ref, f32[3,384]{1,0:T(4,128)S(1)} %get-tuple-element.87.rest_0_.alphas_ref), custom_call_target="tpu_custom_call" | custom-call | flops 117964800 | bytes 19722240 | tf_op jit(solution)/shard_map/combine/pallas_call | solution.py:435
  33.4 5.3 %collective-permute-done.11.across_ref = bf16[384,512]{1,0:T(8,128)(2,1)S(1)} collective-permute-done((bf16[384,512]{1,0:T(8,128)(2,1)S(1)}, bf16[384,512]{1,0:T(8,128)(2,1)S(1)}, u32[]{:S(2)}, u32[]{:S(2)}) %collective-permute-start.11) | collective-permute-done | bytes 393248 | tf_op jit(solution)/shard_map/ppermute | solution.py:451
  38.8 1.7 %collective-permute-start.13 = (bf16[512,384]{1,0:T(8,128)(2,1)S(1)}, bf16[512,384]{1,0:T(8,128)(2,1)S(1)}, u32[]{:S(2)}, u32[]{:S(2)}) collective-permute-start(bf16[512,384]{1,0:T(8,128)(2,1)S(1)} %get-tuple-element.131.grad_ref), channel_id=1, source_target_pairs={{0,2},{2,0},{1,3},{3,1},{4,6},{6,4},{5,7},{7,5},{8,10},{10,8},{9,1... | collective-permute-start | bytes 1179656 | tf_op jit(solution)/shard_map/ppermute | solution.py:451
  40.5 1.6 %forward_partner.5 = bf16[512,384]{1,0:T(8,128)(2,1)} custom-call(bf16[512,384]{1,0:T(8,128)(2,1)S(1)} %collective-permute-done.2.partner_ref.snake_ref, bf16[2,1152,384]{2,1,0:T(8,128)(2,1)S(1)} %get-tuple-element.82.weight_ref, f32[512,384]{1,0:T(8,128)S(1)} %forward_own.5.own_ref, f32[512,384]{1,0:T(8,128)S(1)} %get-tuple-element.100.stream_ref.old_ref, ...), custom_call_target="tpu_custom_call" | custom-call | flops 4529848 | bytes 43909 | tf_op jit(solution)/shard_map/forward_partner/pallas_call | solution.py:435
  42.1 1.4 %paired_weight.4 = (bf16[208,1152]{1,0:T(8,128)(2,1)S(1)}, bf16[192,1152]{1,0:T(8,128)(2,1)S(1)}) custom-call(bf16[384,512]{1,0:T(8,128)(2,1)S(1)} %own_rows.4.own_ref, bf16[512,1152]{1,0:T(8,128)(2,1)S(1)} %get-tuple-element.108.shifted_ref, bf16[384,512]{1,0:T(8,128)(2,1)S(1)} %collective-permute-done.11.across_ref, ...), custom_call_target="tpu_custom_call" | custom-call | flops 9059696 | bytes 44651 | tf_op jit(solution)/shard_map/paired_weight/pallas_call | solution.py:435
  43.5 1.6 %collective-permute-start.15 = (bf16[208,1152]{1,0:T(8,128)(2,1)S(1)}, bf16[208,1152]{1,0:T(8,128)(2,1)S(1)}, u32[]{:S(2)}, u32[]{:S(2)}) collective-permute-start(bf16[208,1152]{1,0:T(8,128)(2,1)S(1)} %get-tuple-element.137), channel_id=1, source_target_pairs={{0,4},{4,0},{8,12},{12,8},{1,5},{5,1},{9,13},{13,9},{2,6},{6,2},{1... | collective-permute-start | bytes 1437704 | tf_op jit(solution)/shard_map/ppermute | solution.py:451
  45.1 2.6 %collective-permute-start.14 = (bf16[96,1152]{1,0:T(8,128)(2,1)S(1)}, bf16[96,1152]{1,0:T(8,128)(2,1)S(1)}, u32[]{:S(2)}, u32[]{:S(2)}) collective-permute-start(bf16[96,1152]{1,0:T(8,128)(2,1)S(1)} %fold.3), channel_id=1, source_target_pairs={{0,8},{4,12},{8,0},{12,4},{1,9},{5,13},{9,1},{13,5},{2,10},{6,14},... | collective-permute-start | bytes 663560 | tf_op jit(solution)/shard_map/ppermute | solution.py:451
  47.7 2.5 %collective-permute-done.13.grad_ref = bf16[512,384]{1,0:T(8,128)(2,1)S(1)} collective-permute-done((bf16[512,384]{1,0:T(8,128)(2,1)S(1)}, bf16[512,384]{1,0:T(8,128)(2,1)S(1)}, u32[]{:S(2)}, u32[]{:S(2)}) %collective-permute-start.13) | collective-permute-done | bytes 393248 | tf_op jit(solution)/shard_map/ppermute | solution.py:451
  50.5 1.4 %paired_weight.5 = (bf16[192,1152]{1,0:T(8,128)(2,1)S(1)}, bf16[192,1152]{1,0:T(8,128)(2,1)S(1)}) custom-call(bf16[384,512]{1,0:T(8,128)(2,1)S(1)} %own_rows.5.own_ref, bf16[512,1152]{1,0:T(8,128)(2,1)S(1)} %get-tuple-element.113.shifted_ref, bf16[384,512]{1,0:T(8,128)(2,1)S(1)} %collective-permute-done.11.across_ref, ...), custom_call_target="tpu_custom_call" | custom-call | flops 9059696 | bytes 44236 | tf_op jit(solution)/shard_map/paired_weight/pallas_call | solution.py:435
  51.9 1.9 %collective-permute-start.16 = (bf16[192,1152]{1,0:T(8,128)(2,1)S(1)}, bf16[192,1152]{1,0:T(8,128)(2,1)S(1)}, u32[]{:S(2)}, u32[]{:S(2)}) collective-permute-start(bf16[192,1152]{1,0:T(8,128)(2,1)S(1)} %get-tuple-element.140), channel_id=1, source_target_pairs={{0,4},{4,0},{8,12},{12,8},{1,5},{5,1},{9,13},{13,9},{2,6},{6,2},{1... | collective-permute-start | bytes 1327112 | tf_op jit(solution)/shard_map/ppermute | solution.py:451
  53.8 7.4 %collective-permute-done.14.late = bf16[96,1152]{1,0:T(8,128)(2,1)S(1)} collective-permute-done((bf16[96,1152]{1,0:T(8,128)(2,1)S(1)}, bf16[96,1152]{1,0:T(8,128)(2,1)S(1)}, u32[]{:S(2)}, u32[]{:S(2)}) %collective-permute-start.14) | collective-permute-done | bytes 221216 | tf_op jit(solution)/shard_map/ppermute | solution.py:451
  62.2 2.6 %collective-permute-start.17 = (bf16[112,1152]{1,0:T(8,128)(2,1)S(1)}, bf16[112,1152]{1,0:T(8,128)(2,1)S(1)}, u32[]{:S(2)}, u32[]{:S(2)}) collective-permute-start(bf16[112,1152]{1,0:T(8,128)(2,1)S(1)} %get-tuple-element.142), channel_id=1, source_target_pairs={{0,8},{4,12},{8,0},{12,4},{1,9},{5,13},{9,1},{13,5},{2,10},{6,14},... | collective-permute-start | bytes 774152 | tf_op jit(solution)/shard_map/ppermute | solution.py:451
  64.8 1.0 %collective-permute-start.19 = (bf16[96,1152]{1,0:T(8,128)(2,1)S(1)}, bf16[96,1152]{1,0:T(8,128)(2,1)S(1)}, u32[]{:S(2)}, u32[]{:S(2)}) collective-permute-start(bf16[96,1152]{1,0:T(8,128)(2,1)S(1)} %total.3.refs_1_), channel_id=1, source_target_pairs={{0,2},{2,0},{1,3},{3,1},{4,6},{6,4},{5,7},{7,5},{8,10},{10,8},{9,1... | collective-permute-start | bytes 663560 | tf_op jit(solution)/shard_map/ppermute | solution.py:451
  65.9 10.6 %collective-permute-done.16.got = bf16[192,1152]{1,0:T(8,128)(2,1)S(1)} collective-permute-done((bf16[192,1152]{1,0:T(8,128)(2,1)S(1)}, bf16[192,1152]{1,0:T(8,128)(2,1)S(1)}, u32[]{:S(2)}, u32[]{:S(2)}) %collective-permute-start.16) | collective-permute-done | bytes 442400 | tf_op jit(solution)/shard_map/ppermute | solution.py:451
  76.5 1.7 %collective-permute-start.18 = (bf16[96,1152]{1,0:T(8,128)(2,1)S(1)}, bf16[96,1152]{1,0:T(8,128)(2,1)S(1)}, u32[]{:S(2)}, u32[]{:S(2)}) collective-permute-start(bf16[96,1152]{1,0:T(8,128)(2,1)S(1)} %fold.5), channel_id=1, source_target_pairs={{0,8},{4,12},{8,0},{12,4},{1,9},{5,13},{9,1},{13,5},{2,10},{6,14},... | collective-permute-start | bytes 663560 | tf_op jit(solution)/shard_map/ppermute | solution.py:451
  78.9 10.0 %collective-permute-done.18.late = bf16[96,1152]{1,0:T(8,128)(2,1)S(1)} collective-permute-done((bf16[96,1152]{1,0:T(8,128)(2,1)S(1)}, bf16[96,1152]{1,0:T(8,128)(2,1)S(1)}, u32[]{:S(2)}, u32[]{:S(2)}) %collective-permute-start.18) | collective-permute-done | bytes 221216 | tf_op jit(solution)/shard_map/ppermute | solution.py:451
  89.1 1.9 %finish.2 = (f32[3,3,192,384]{3,2,1,0:T(8,128)}, f32[3,384]{1,0:T(4,128)}) custom-call(f32[1,1152]{1,0:T(1,128)S(1)} %get-tuple-element.145.refs_0_, bf16[96,1152]{1,0:T(8,128)(2,1)S(1)} %total.3.refs_1_, bf16[96,1152]{1,0:T(8,128)(2,1)S(1)} %collective-permute-done.19.refs_2_, bf16[112,1152]{1,0:T(8,128)(2,1)S(1)} %get-tuple-element.147.refs_3_, ...), custom_call_target="tpu_custom_call" | custom-call | flops 6635520 | bytes 36218880 | tf_op jit(solution)/shard_map/finish/pallas_call | solution.py:435
  91.0 4.4 %collective-permute-done.21.refs_2_ = bf16[96,1152]{1,0:T(8,128)(2,1)S(1)} collective-permute-done((bf16[96,1152]{1,0:T(8,128)(2,1)S(1)}, bf16[96,1152]{1,0:T(8,128)(2,1)S(1)}, u32[]{:S(2)}, u32[]{:S(2)}) %collective-permute-start.21) | collective-permute-done | bytes 221216 | tf_op jit(solution)/shard_map/ppermute | solution.py:451
  95.4 1.0 %finish.3 = f32[3,3,192,384]{3,2,1,0:T(8,128)} custom-call(f32[3,3,192,384]{3,2,1,0:T(8,128)} %get-tuple-element.148.refs_0_, bf16[96,1152]{1,0:T(8,128)(2,1)S(1)} %total.5.refs_1_, bf16[96,1152]{1,0:T(8,128)(2,1)S(1)} %collective-permute-done.21.refs_2_), custom_call_target="tpu_custom_call", output_to_operand_aliasing={{}: (0, {})} | custom-call | flops 6635520 | bytes 57507840 | tf_op jit(solution)/shard_map/finish/pallas_call | solution.py:435
  (47 shorter events, 11.2 us)
Async XLA Ops:
  3.2 4.7 %collective-permute-start = (bf16[512,384]{1,0:T(8,128)(2,1)S(1)}, bf16[512,384]{1,0:T(8,128)(2,1)S(1)}, u32[]{:S(2)}, u32[]{:S(2)}) collective-permute-start(bf16[512,384]{1,0:T(8,128)(2,1)S(1)} %get-tuple-element.120.snake_ref.refs_1_.own_ref), channel_id=1, source_target_pairs={{0,1},{1,0},{2,3},{3,2},{4,5},{5,4},{6,7},{7,6},{8,9},{9,8},{10,11... | collective-permute-start | bytes 1179656 | tf_op jit(solution)/shard_map/ppermute | solution.py:451
  5.3 12.3 %collective-permute-start.5 = (bf16[512,384]{1,0:T(8,128)(2,1)S(1)}, bf16[512,384]{1,0:T(8,128)(2,1)S(1)}, u32[]{:S(2)}, u32[]{:S(2)}) collective-permute-start(bf16[512,384]{1,0:T(8,128)(2,1)S(1)} %get-tuple-element.103.grad_ref.rest_0_), channel_id=1, source_target_pairs={{0,2},{2,0},{1,3},{3,1},{4,6},{6,4},{5,7},{7,5},{8,10},{10,8},{9,1... | collective-permute-start | bytes 1179656 | tf_op jit(solution)/shard_map/ppermute | solution.py:451
  10.2 2.4 %collective-permute-start.1 = (bf16[512,384]{1,0:T(8,128)(2,1)S(1)}, bf16[512,384]{1,0:T(8,128)(2,1)S(1)}, u32[]{:S(2)}, u32[]{:S(2)}) collective-permute-start(bf16[512,384]{1,0:T(8,128)(2,1)S(1)} %get-tuple-element.119.snake_ref.refs_0_.own_ref), channel_id=1, source_target_pairs={{0,1},{1,0},{2,3},{3,2},{4,5},{5,4},{6,7},{7,6},{8,9},{9,8},{10,11... | collective-permute-start | bytes 1179656 | tf_op jit(solution)/shard_map/ppermute | solution.py:451
  11.4 4.6 %collective-permute-start.3 = (bf16[512,384]{1,0:T(8,128)(2,1)S(1)}, bf16[512,384]{1,0:T(8,128)(2,1)S(1)}, u32[]{:S(2)}, u32[]{:S(2)}) collective-permute-start(bf16[512,384]{1,0:T(8,128)(2,1)S(1)} %get-tuple-element.92), channel_id=1, source_target_pairs={{0,1},{1,0},{2,3},{3,2},{4,5},{5,4},{6,7},{7,6},{8,9},{9,8},{10,11... | collective-permute-start | bytes 1179656 | tf_op jit(solution)/shard_map/ppermute | solution.py:451
  14.3 5.7 %collective-permute-start.2 = (bf16[512,384]{1,0:T(8,128)(2,1)S(1)}, bf16[512,384]{1,0:T(8,128)(2,1)S(1)}, u32[]{:S(2)}, u32[]{:S(2)}) collective-permute-start(bf16[512,384]{1,0:T(8,128)(2,1)S(1)} %get-tuple-element.121.refs_0_.own_ref.snake_ref), channel_id=1, source_target_pairs={{0,1},{1,0},{2,3},{3,2},{4,5},{5,4},{6,7},{7,6},{8,9},{9,8},{10,11... | collective-permute-start | bytes 1179656 | tf_op jit(solution)/shard_map/ppermute | solution.py:451
  14.7 7.8 %collective-permute-start.7 = (bf16[192,512]{1,0:T(8,128)(2,1)S(1)}, bf16[192,512]{1,0:T(8,128)(2,1)S(1)}, u32[]{:S(2)}, u32[]{:S(2)}) collective-permute-start(bf16[192,512]{1,0:T(8,128)(2,1)S(1)} %turn.2), channel_id=1, source_target_pairs={{0,2},{2,0},{1,3},{3,1},{4,6},{6,4},{5,7},{7,5},{8,10},{10,8},{9,1... | collective-permute-start | bytes 589832 | tf_op jit(solution)/shard_map/ppermute | solution.py:451
  17.7 15.6 %collective-permute-start.4 = (bf16[512,384]{1,0:T(8,128)(2,1)S(1)}, bf16[512,384]{1,0:T(8,128)(2,1)S(1)}, u32[]{:S(2)}, u32[]{:S(2)}) collective-permute-start(bf16[512,384]{1,0:T(8,128)(2,1)S(1)} %get-tuple-element.107.grad_ref), channel_id=1, source_target_pairs={{0,2},{2,0},{1,3},{3,1},{4,6},{6,4},{5,7},{7,5},{8,10},{10,8},{9,1... | collective-permute-start | bytes 1179656 | tf_op jit(solution)/shard_map/ppermute | solution.py:451
  20.6 18.2 %collective-permute-start.11 = (bf16[384,512]{1,0:T(8,128)(2,1)S(1)}, bf16[384,512]{1,0:T(8,128)(2,1)S(1)}, u32[]{:S(2)}, u32[]{:S(2)}) collective-permute-start(bf16[384,512]{1,0:T(8,128)(2,1)S(1)} %turn.3), channel_id=1, source_target_pairs={{0,2},{2,0},{1,3},{3,1},{4,6},{6,4},{5,7},{7,5},{8,10},{10,8},{9,1... | collective-permute-start | bytes 1179656 | tf_op jit(solution)/shard_map/ppermute | solution.py:451
  21.6 1.8 %collective-permute-start.6 = (bf16[512,384]{1,0:T(8,128)(2,1)S(1)}, bf16[512,384]{1,0:T(8,128)(2,1)S(1)}, u32[]{:S(2)}, u32[]{:S(2)}) collective-permute-start(bf16[512,384]{1,0:T(8,128)(2,1)S(1)} %get-tuple-element.109), channel_id=1, source_target_pairs={{0,1},{1,0},{2,3},{3,2},{4,5},{5,4},{6,7},{7,6},{8,9},{9,8},{10,11... | collective-permute-start | bytes 1179656 | tf_op jit(solution)/shard_map/ppermute | solution.py:451
  22.6 4.5 %collective-permute-start.8 = (bf16[192,512]{1,0:T(8,128)(2,1)S(1)}, bf16[192,512]{1,0:T(8,128)(2,1)S(1)}, u32[]{:S(2)}, u32[]{:S(2)}) collective-permute-start(bf16[192,512]{1,0:T(8,128)(2,1)S(1)} %collective-permute-done.7.across_ref), channel_id=1, source_target_pairs={{0,1},{1,0},{2,3},{3,2},{4,5},{5,4},{6,7},{7,6},{8,9},{9,8},{10,11... | collective-permute-start | bytes 589832 | tf_op jit(solution)/shard_map/ppermute | solution.py:451
  26.9 3.5 %collective-permute-start.9 = (bf16[512,384]{1,0:T(8,128)(2,1)S(1)}, bf16[512,384]{1,0:T(8,128)(2,1)S(1)}, u32[]{:S(2)}, u32[]{:S(2)}) collective-permute-start(bf16[512,384]{1,0:T(8,128)(2,1)S(1)} %get-tuple-element.118), channel_id=1, source_target_pairs={{0,1},{1,0},{2,3},{3,2},{4,5},{5,4},{6,7},{7,6},{8,9},{9,8},{10,11... | collective-permute-start | bytes 1179656 | tf_op jit(solution)/shard_map/ppermute | solution.py:451
  28.5 13.6 %collective-permute-start.10 = (bf16[192,1152]{1,0:T(8,128)(2,1)S(1)}, bf16[192,1152]{1,0:T(8,128)(2,1)S(1)}, u32[]{:S(2)}, u32[]{:S(2)}) collective-permute-start(bf16[192,1152]{1,0:T(8,128)(2,1)S(1)} %get-tuple-element.125), channel_id=1, source_target_pairs={{0,4},{4,0},{8,12},{12,8},{1,5},{5,1},{9,13},{13,9},{2,6},{6,2},{1... | collective-permute-start | bytes 1327112 | tf_op jit(solution)/shard_map/ppermute | solution.py:451
  38.8 3.3 %collective-permute-start.12 = (bf16[384,512]{1,0:T(8,128)(2,1)S(1)}, bf16[384,512]{1,0:T(8,128)(2,1)S(1)}, u32[]{:S(2)}, u32[]{:S(2)}) collective-permute-start(bf16[384,512]{1,0:T(8,128)(2,1)S(1)} %collective-permute-done.11.across_ref), channel_id=1, source_target_pairs={{0,1},{1,0},{2,3},{3,2},{4,5},{5,4},{6,7},{7,6},{8,9},{9,8},{10,11... | collective-permute-start | bytes 1179656 | tf_op jit(solution)/shard_map/ppermute | solution.py:451
  38.8 11.5 %collective-permute-start.13 = (bf16[512,384]{1,0:T(8,128)(2,1)S(1)}, bf16[512,384]{1,0:T(8,128)(2,1)S(1)}, u32[]{:S(2)}, u32[]{:S(2)}) collective-permute-start(bf16[512,384]{1,0:T(8,128)(2,1)S(1)} %get-tuple-element.131.grad_ref), channel_id=1, source_target_pairs={{0,2},{2,0},{1,3},{3,1},{4,6},{6,4},{5,7},{7,5},{8,10},{10,8},{9,1... | collective-permute-start | bytes 1179656 | tf_op jit(solution)/shard_map/ppermute | solution.py:451
  43.5 18.6 %collective-permute-start.15 = (bf16[208,1152]{1,0:T(8,128)(2,1)S(1)}, bf16[208,1152]{1,0:T(8,128)(2,1)S(1)}, u32[]{:S(2)}, u32[]{:S(2)}) collective-permute-start(bf16[208,1152]{1,0:T(8,128)(2,1)S(1)} %get-tuple-element.137), channel_id=1, source_target_pairs={{0,4},{4,0},{8,12},{12,8},{1,5},{5,1},{9,13},{13,9},{2,6},{6,2},{1... | collective-permute-start | bytes 1437704 | tf_op jit(solution)/shard_map/ppermute | solution.py:451
  45.1 16.1 %collective-permute-start.14 = (bf16[96,1152]{1,0:T(8,128)(2,1)S(1)}, bf16[96,1152]{1,0:T(8,128)(2,1)S(1)}, u32[]{:S(2)}, u32[]{:S(2)}) collective-permute-start(bf16[96,1152]{1,0:T(8,128)(2,1)S(1)} %fold.3), channel_id=1, source_target_pairs={{0,8},{4,12},{8,0},{12,4},{1,9},{5,13},{9,1},{13,5},{2,10},{6,14},... | collective-permute-start | bytes 663560 | tf_op jit(solution)/shard_map/ppermute | solution.py:451
  51.9 24.5 %collective-permute-start.16 = (bf16[192,1152]{1,0:T(8,128)(2,1)S(1)}, bf16[192,1152]{1,0:T(8,128)(2,1)S(1)}, u32[]{:S(2)}, u32[]{:S(2)}) collective-permute-start(bf16[192,1152]{1,0:T(8,128)(2,1)S(1)} %get-tuple-element.140), channel_id=1, source_target_pairs={{0,4},{4,0},{8,12},{12,8},{1,5},{5,1},{9,13},{13,9},{2,6},{6,2},{1... | collective-permute-start | bytes 1327112 | tf_op jit(solution)/shard_map/ppermute | solution.py:451
  62.2 16.0 %collective-permute-start.17 = (bf16[112,1152]{1,0:T(8,128)(2,1)S(1)}, bf16[112,1152]{1,0:T(8,128)(2,1)S(1)}, u32[]{:S(2)}, u32[]{:S(2)}) collective-permute-start(bf16[112,1152]{1,0:T(8,128)(2,1)S(1)} %get-tuple-element.142), channel_id=1, source_target_pairs={{0,8},{4,12},{8,0},{12,4},{1,9},{5,13},{9,1},{13,5},{2,10},{6,14},... | collective-permute-start | bytes 774152 | tf_op jit(solution)/shard_map/ppermute | solution.py:451
  64.8 24.3 %collective-permute-start.19 = (bf16[96,1152]{1,0:T(8,128)(2,1)S(1)}, bf16[96,1152]{1,0:T(8,128)(2,1)S(1)}, u32[]{:S(2)}, u32[]{:S(2)}) collective-permute-start(bf16[96,1152]{1,0:T(8,128)(2,1)S(1)} %total.3.refs_1_), channel_id=1, source_target_pairs={{0,2},{2,0},{1,3},{3,1},{4,6},{6,4},{5,7},{7,5},{8,10},{10,8},{9,1... | collective-permute-start | bytes 663560 | tf_op jit(solution)/shard_map/ppermute | solution.py:451
  76.5 12.4 %collective-permute-start.18 = (bf16[96,1152]{1,0:T(8,128)(2,1)S(1)}, bf16[96,1152]{1,0:T(8,128)(2,1)S(1)}, u32[]{:S(2)}, u32[]{:S(2)}) collective-permute-start(bf16[96,1152]{1,0:T(8,128)(2,1)S(1)} %fold.5), channel_id=1, source_target_pairs={{0,8},{4,12},{8,0},{12,4},{1,9},{5,13},{9,1},{13,5},{2,10},{6,14},... | collective-permute-start | bytes 663560 | tf_op jit(solution)/shard_map/ppermute | solution.py:451
  78.3 10.7 %collective-permute-start.20 = (bf16[112,1152]{1,0:T(8,128)(2,1)S(1)}, bf16[112,1152]{1,0:T(8,128)(2,1)S(1)}, u32[]{:S(2)}, u32[]{:S(2)}) collective-permute-start(bf16[112,1152]{1,0:T(8,128)(2,1)S(1)} %get-tuple-element.147.refs_3_), channel_id=1, source_target_pairs={{0,2},{2,0},{1,3},{3,1},{4,6},{6,4},{5,7},{7,5},{8,10},{10,8},{9,1... | collective-permute-start | bytes 774152 | tf_op jit(solution)/shard_map/ppermute | solution.py:451
  89.0 6.4 %collective-permute-start.21 = (bf16[96,1152]{1,0:T(8,128)(2,1)S(1)}, bf16[96,1152]{1,0:T(8,128)(2,1)S(1)}, u32[]{:S(2)}, u32[]{:S(2)}) collective-permute-start(bf16[96,1152]{1,0:T(8,128)(2,1)S(1)} %total.5.refs_1_), channel_id=1, source_target_pairs={{0,2},{2,0},{1,3},{3,1},{4,6},{6,4},{5,7},{7,5},{8,10},{10,8},{9,1... | collective-permute-start | bytes 663560 | tf_op jit(solution)/shard_map/ppermute | solution.py:451

commit v9 on v7

--- a/solution.py
+++ b/solution.py
@@ -250,7 +250,7 @@
 
 def block_place(pieces, slice_index, part):
     apart = jnp.bitwise_xor(slice_index, lax.axis_index("dp"))
-    order = (2 * pieces, 0, 1, 2 * pieces + 1)
+    order = (2 * pieces, 0, 2 * pieces + 1, 1)
     return 2 * part + jnp.where(
         apart == 0, order[0], jnp.where(apart == 1, order[1], jnp.where(apart == 2, order[2], order[3]))
     )
@@ -616,7 +616,7 @@
         )
         if carried:
             carry_sum[0] = result[1]
-        late[layer, part] = swap(result[0], "dp", lambda i: i ^ 3)
+        late[layer, part] = swap(result[0], "dp", lambda i: i ^ 2)
 
     def total(layer, part=0):
         if not fast:
@@ -706,30 +706,30 @@
     share(2)
     back_own(1)
     combine(1, grad)
+    weights(2)
     back_partner(0)
     back_own(0)
-    weights(2)
     sequence.weight = 10
     combine(0, None)
     own_rows(1)
-    turn(0)
     far_rows(1)
     own_rows(0)
     share(1)
     forward_own(2)
     residual_out = forward_partner(2)
-    sequence.weight = 10
+    sequence.weight = 0.01
     weights(1)
+    turn(0)
     send_gradient(0)
+    fold(2)
     share(0)
-    fold(2)
     far_rows(0)
     sequence.weight = 0.01
     weights(0)
+    sequence.weight = 10
+    fold(1)
     total(2)
     cross(2)
-    sequence.weight = 10
-    fold(1)
     fold(0)
     total(1)
     cross(1)

time: 97.9 us -> 97.6 us (level)
  the two profiles are of different devices: /device:TPU:14 before, /device:TPU:0 now
where the time goes in v9:
time: 97.6 us; the launch traced here: 97.4 us
  waiting for transfers between devices  41.7 us (43%)
  Pallas kernels  30.9 us (32%)
  starting transfers between devices  23.7 us (24%)
  between operations  1.1 us (1%)
    ppermute x24, waiting for transfers between devices, swap(): lax.ppermute(x, axis, [(i, other(i)) for i in range(lax.axis_size(axis))])  41.7 us
    pallas_call x36, Pallas kernels, call(): pl.pallas_call(kernel, in_specs=[ANY_HBM if i else IN_VMEM for i in ins],...  30.9 us
    ppermute x24, starting transfers between devices, swap(): lax.ppermute(x, axis, [(i, other(i)) for i in range(lax.axis_size(axis))])  23.7 us
  transfers between devices with their start and end apart: 24, of which 9 were waited for; matrix products, arithmetic and copies ran while one was open for 0% of the time, Pallas kernels for 28%

profile of v9, /device:TPU:0, one launch (start us, length us, event | category | flops | bytes accessed | tf_op | source)
XLA Modules:
  0.0 97.4 jit_solution(6265049844201521327)
XLA Ops:
  0.6 2.5 %prep.1 = (f32[512,384]{1,0:T(8,128)S(1)}, bf16[512,384]{1,0:T(8,128)(2,1)S(1)}, bf16[512,384]{1,0:T(8,128)(2,1)S(1)}, f32[512,128]{1,0:T(8,128)S(1)}, f32[3,384...) custom-call(s32[16]{0:T(128)} %len_hbm.1, s32[16]{0:T(128)} %own_hbm.1, s32[16]{0:T(128)} %start_hbm.1, ...), custom_call_target="tpu_custom_call" | custom-call | flops 78643200 | bytes 44003200 | tf_op jit(solution)/shard_map/prep/pallas_call | solution.py:435
  3.7 1.6 %forward_own.3 = (f32[512,384]{1,0:T(8,128)S(1)}, bf16[2,1152,384]{2,1,0:T(8,128)(2,1)S(1)}) custom-call(bf16[512,384]{1,0:T(8,128)(2,1)S(1)} %get-tuple-element.129.snake_ref.own_ref.refs_0_, bf16[2,1152,384]{2,1,0:T(8,128)(2,1)S(1)} %get-tuple-element.81.weight_ref, bf16[3,3,768,384]{3,2,1,0:T(8,128)(2,1)} %rest_1_.1), custom_call_target="tpu_custom_call" | custom-call | flops 4529848320 | bytes 47185920 | tf_op jit(solution)/shard_map/forward_own/pallas_call | solution.py:435
  5.3 2.6 %collective-permute-start.5 = (bf16[512,384]{1,0:T(8,128)(2,1)S(1)}, bf16[512,384]{1,0:T(8,128)(2,1)S(1)}, u32[]{:S(2)}, u32[]{:S(2)}) collective-permute-start(bf16[512,384]{1,0:T(8,128)(2,1)S(1)} %get-tuple-element.104.grad_ref.rest_0_), channel_id=1, source_target_pairs={{0,2},{2,0},{1,3},{3,1},{4,6},{6,4},{5,7},{7,5},{8,10},{10,8},{9,1... | collective-permute-start | bytes 1179656 | tf_op jit(solution)/shard_map/ppermute | solution.py:451
  7.9 2.3 %forward_partner.3 = (f32[512,384]{1,0:T(8,128)S(1)}, bf16[512,384]{1,0:T(8,128)(2,1)S(1)}, bf16[2,1152,384]{2,1,0:T(8,128)(2,1)S(1)}) custom-call(bf16[512,384]{1,0:T(8,128)(2,1)S(1)} %collective-permute-done.snake_ref.partner_ref, bf16[2,1152,384]{2,1,0:T(8,128)(2,1)S(1)} %get-tuple-element.81.weight_ref, f32[512,384]{1,0:T(8,128)S(1)} %get-tuple-element.85.own_ref, ...), custom_call_target="tpu_custom_call" | custom-call | flops 4529848320 | bytes 69514240 | tf_op jit(solution)/shard_map/forward_partner/pallas_call | solution.py:435
  12.6 1.7 %forward_partner.4 = (f32[512,384]{1,0:T(8,128)S(1)}, bf16[512,384]{1,0:T(8,128)(2,1)S(1)}) custom-call(bf16[512,384]{1,0:T(8,128)(2,1)S(1)} %collective-permute-done.1.snake_ref.partner_ref, bf16[2,1152,384]{2,1,0:T(8,128)(2,1)S(1)} %get-tuple-element.91.weight_ref, f32[512,384]{1,0:T(8,128)S(1)} %forward_own.4.own_ref, ...), custom_call_target="tpu_custom_call" | custom-call | flops 4529848320 | bytes 51819520 | tf_op jit(solution)/shard_map/forward_partner/pallas_call | solution.py:435
  16.0 1.6 %combine.3 = (f32[1,384]{1,0:T(1,128)S(1)}, f32[512,384]{1,0:T(8,128)S(1)}, bf16[512,384]{1,0:T(8,128)(2,1)S(1)}) custom-call(f32[512,384]{1,0:T(8,128)S(1)} %back_own.3.own_ref, bf16[512,384]{1,0:T(8,128)(2,1)S(1)} %collective-permute-done.3.partner_ref, f32[512,384]{1,0:T(8,128)S(1)} %get-tuple-element.101.stream_ref.old_ref, ...), custom_call_target="tpu_custom_call" | custom-call | flops 117964800 | bytes 38072320 | tf_op jit(solution)/shard_map/combine/pallas_call | solution.py:435
  17.7 2.2 %collective-permute-start.4 = (bf16[512,384]{1,0:T(8,128)(2,1)S(1)}, bf16[512,384]{1,0:T(8,128)(2,1)S(1)}, u32[]{:S(2)}, u32[]{:S(2)}) collective-permute-start(bf16[512,384]{1,0:T(8,128)(2,1)S(1)} %get-tuple-element.108.grad_ref), channel_id=1, source_target_pairs={{0,2},{2,0},{1,3},{3,1},{4,6},{6,4},{5,7},{7,5},{8,10},{10,8},{9,1... | collective-permute-start | bytes 1179656 | tf_op jit(solution)/shard_map/ppermute | solution.py:451
  20.6 0.9 back_partner.4
  21.6 0.9 collective-permute-done.7.across_ref
  23.4 1.7 %combine.4 = (f32[1,384]{1,0:T(1,128)S(1)}, bf16[512,384]{1,0:T(8,128)(2,1)S(1)}) custom-call(f32[512,384]{1,0:T(8,128)S(1)} %back_own.4.own_ref, bf16[512,384]{1,0:T(8,128)(2,1)S(1)} %collective-permute-done.6.partner_ref, f32[512,384]{1,0:T(8,128)S(1)} %get-tuple-element.96.old_ref.stream_ref, f32[3,384]{1,0:T(4,128)S(1)} %get-tuple-element.88.rest_0_.alphas_ref, ...), custom_call_target="tpu_custom_call" | custom-call | flops 117964800 | bytes 34140160 | tf_op jit(solution)/shard_map/combine/pallas_call | solution.py:435
  25.2 1.4 %paired_weight.3 = (bf16[192,1152]{1,0:T(8,128)(2,1)S(1)}, bf16[192,1152]{1,0:T(8,128)(2,1)S(1)}) custom-call(bf16[384,512]{1,0:T(8,128)(2,1)S(1)} %own_rows.3.own_ref, bf16[512,1152]{1,0:T(8,128)(2,1)S(1)} %get-tuple-element.100.shifted_ref, bf16[192,512]{1,0:T(8,128)(2,1)S(1)} %collective-permute-done.7.across_ref, ...), custom_call_target="tpu_custom_call" | custom-call | flops 9059696640 | bytes 40304640 | tf_op jit(solution)/shard_map/paired_weight/pallas_call | solution.py:435
  26.6 1.7 %collective-permute-start.13 = (bf16[192,1152]{1,0:T(8,128)(2,1)S(1)}, bf16[192,1152]{1,0:T(8,128)(2,1)S(1)}, u32[]{:S(2)}, u32[]{:S(2)}) collective-permute-start(bf16[192,1152]{1,0:T(8,128)(2,1)S(1)} %get-tuple-element.132), channel_id=1, source_target_pairs={{0,4},{4,0},{8,12},{12,8},{1,5},{5,1},{9,13},{13,9},{2,6},{6,2},{1... | collective-permute-start | bytes 1327112 | tf_op jit(solution)/shard_map/ppermute | solution.py:451
  28.3 0.9 back_partner.5
  31.0 1.4 %combine.5.rest_0_ = f32[1,384]{1,0:T(1,128)S(1)} custom-call(f32[512,384]{1,0:T(8,128)S(1)} %back_own.5.own_ref, bf16[512,384]{1,0:T(8,128)(2,1)S(1)} %collective-permute-done.9.partner_ref, f32[512,384]{1,0:T(8,128)S(1)} %get-tuple-element.86.old_ref.stream_ref, f32[3,384]{1,0:T(4,128)S(1)} %get-tuple-element.88.rest_0_.alphas_ref), custom_call_target="tpu_custom_call" | custom-call | flops 117964800 | bytes 19722240 | tf_op jit(solution)/shard_map/combine/pallas_call | solution.py:435
  33.2 1.3 %collective-permute-done.10.across_ref = bf16[192,512]{1,0:T(8,128)(2,1)S(1)} collective-permute-done((bf16[192,512]{1,0:T(8,128)(2,1)S(1)}, bf16[192,512]{1,0:T(8,128)(2,1)S(1)}, u32[]{:S(2)}, u32[]{:S(2)}) %collective-permute-start.10) | collective-permute-done | bytes 196640 | tf_op jit(solution)/shard_map/ppermute | solution.py:451
  35.3 1.6 %forward_partner.5 = bf16[512,384]{1,0:T(8,128)(2,1)} custom-call(bf16[512,384]{1,0:T(8,128)(2,1)S(1)} %collective-permute-done.2.partner_ref.snake_ref, bf16[2,1152,384]{2,1,0:T(8,128)(2,1)S(1)} %get-tuple-element.83.weight_ref, f32[512,384]{1,0:T(8,128)S(1)} %forward_own.5.own_ref, f32[512,384]{1,0:T(8,128)S(1)} %get-tuple-element.101.stream_ref.old_ref, ...), custom_call_target="tpu_custom_call" | custom-call | flops 4529848320 | bytes 43909120 | tf_op jit(solution)/shard_map/forward_partner/pallas_call | solution.py:435
  36.9 1.4 %paired_weight.4 = (bf16[208,1152]{1,0:T(8,128)(2,1)S(1)}, bf16[192,1152]{1,0:T(8,128)(2,1)S(1)}) custom-call(bf16[384,512]{1,0:T(8,128)(2,1)S(1)} %own_rows.4.own_ref, bf16[512,1152]{1,0:T(8,128)(2,1)S(1)} %get-tuple-element.109.shifted_ref, bf16[192,512]{1,0:T(8,128)(2,1)S(1)} %collective-permute-done.10.across_ref, ...), custom_call_target="tpu_custom_call" | custom-call | flops 9059696 | bytes 40719 | tf_op jit(solution)/shard_map/paired_weight/pallas_call | solution.py:435
  38.3 1.9 %collective-permute-start.16 = (bf16[208,1152]{1,0:T(8,128)(2,1)S(1)}, bf16[208,1152]{1,0:T(8,128)(2,1)S(1)}, u32[]{:S(2)}, u32[]{:S(2)}) collective-permute-start(bf16[208,1152]{1,0:T(8,128)(2,1)S(1)} %get-tuple-element.138), channel_id=1, source_target_pairs={{0,4},{4,0},{8,12},{12,8},{1,5},{5,1},{9,13},{13,9},{2,6},{6,2},{1... | collective-permute-start | bytes 1437704 | tf_op jit(solution)/shard_map/ppermute | solution.py:451
  40.3 1.6 %collective-permute-start.12 = (bf16[512,384]{1,0:T(8,128)(2,1)S(1)}, bf16[512,384]{1,0:T(8,128)(2,1)S(1)}, u32[]{:S(2)}, u32[]{:S(2)}) collective-permute-start(bf16[512,384]{1,0:T(8,128)(2,1)S(1)} %get-tuple-element.130.grad_ref), channel_id=1, source_target_pairs={{0,2},{2,0},{1,3},{3,1},{4,6},{6,4},{5,7},{7,5},{8,10},{10,8},{9,1... | collective-permute-start | bytes 1179656 | tf_op jit(solution)/shard_map/ppermute | solution.py:451
  42.5 2.7 %collective-permute-start.17 = (bf16[96,1152]{1,0:T(8,128)(2,1)S(1)}, bf16[96,1152]{1,0:T(8,128)(2,1)S(1)}, u32[]{:S(2)}, u32[]{:S(2)}) collective-permute-start(bf16[96,1152]{1,0:T(8,128)(2,1)S(1)} %fold.3), channel_id=1, source_target_pairs={{0,8},{4,12},{8,0},{12,4},{1,9},{5,13},{9,1},{13,5},{2,10},{6,14},... | collective-permute-start | bytes 663560 | tf_op jit(solution)/shard_map/ppermute | solution.py:451
  45.1 10.7 %collective-permute-done.14.across_ref = bf16[192,512]{1,0:T(8,128)(2,1)S(1)} collective-permute-done((bf16[192,512]{1,0:T(8,128)(2,1)S(1)}, bf16[192,512]{1,0:T(8,128)(2,1)S(1)}, u32[]{:S(2)}, u32[]{:S(2)}) %collective-permute-start.14) | collective-permute-done | bytes 196640 | tf_op jit(solution)/shard_map/ppermute | solution.py:451
  56.1 1.2 %collective-permute-done.15.across_other_ref = bf16[192,512]{1,0:T(8,128)(2,1)S(1)} collective-permute-done((bf16[192,512]{1,0:T(8,128)(2,1)S(1)}, bf16[192,512]{1,0:T(8,128)(2,1)S(1)}, u32[]{:S(2)}, u32[]{:S(2)}) %collective-permute-start.15) | collective-permute-done | bytes 196640 | tf_op jit(solution)/shard_map/ppermute | solution.py:451
  57.3 1.4 %paired_weight.5 = (bf16[192,1152]{1,0:T(8,128)(2,1)S(1)}, bf16[192,1152]{1,0:T(8,128)(2,1)S(1)}) custom-call(bf16[384,512]{1,0:T(8,128)(2,1)S(1)} %own_rows.5.own_ref, bf16[512,1152]{1,0:T(8,128)(2,1)S(1)} %get-tuple-element.117.shifted_ref, bf16[192,512]{1,0:T(8,128)(2,1)S(1)} %collective-permute-done.14.across_ref, ...), custom_call_target="tpu_custom_call" | custom-call | flops 9059696 | bytes 40304 | tf_op jit(solution)/shard_map/paired_weight/pallas_call | solution.py:435
  59.1 2.8 %collective-permute-start.19 = (bf16[112,1152]{1,0:T(8,128)(2,1)S(1)}, bf16[112,1152]{1,0:T(8,128)(2,1)S(1)}, u32[]{:S(2)}, u32[]{:S(2)}) collective-permute-start(bf16[112,1152]{1,0:T(8,128)(2,1)S(1)} %get-tuple-element.144), channel_id=1, source_target_pairs={{0,8},{4,12},{8,0},{12,4},{1,9},{5,13},{9,1},{13,5},{2,10},{6,14},... | collective-permute-start | bytes 774152 | tf_op jit(solution)/shard_map/ppermute | solution.py:451
  62.0 1.6 %collective-permute-start.21 = (bf16[96,1152]{1,0:T(8,128)(2,1)S(1)}, bf16[96,1152]{1,0:T(8,128)(2,1)S(1)}, u32[]{:S(2)}, u32[]{:S(2)}) collective-permute-start(bf16[96,1152]{1,0:T(8,128)(2,1)S(1)} %total.3.refs_1_), channel_id=1, source_target_pairs={{0,2},{2,0},{1,3},{3,1},{4,6},{6,4},{5,7},{7,5},{8,10},{10,8},{9,1... | collective-permute-start | bytes 663560 | tf_op jit(solution)/shard_map/ppermute | solution.py:451
  63.6 12.9 %collective-permute-done.18.got = bf16[192,1152]{1,0:T(8,128)(2,1)S(1)} collective-permute-done((bf16[192,1152]{1,0:T(8,128)(2,1)S(1)}, bf16[192,1152]{1,0:T(8,128)(2,1)S(1)}, u32[]{:S(2)}, u32[]{:S(2)}) %collective-permute-start.18) | collective-permute-done | bytes 442400 | tf_op jit(solution)/shard_map/ppermute | solution.py:451
  77.3 1.6 %collective-permute-start.22 = (bf16[112,1152]{1,0:T(8,128)(2,1)S(1)}, bf16[112,1152]{1,0:T(8,128)(2,1)S(1)}, u32[]{:S(2)}, u32[]{:S(2)}) collective-permute-start(bf16[112,1152]{1,0:T(8,128)(2,1)S(1)} %get-tuple-element.149.refs_3_), channel_id=1, source_target_pairs={{0,2},{2,0},{1,3},{3,1},{4,6},{6,4},{5,7},{7,5},{8,10},{10,8},{9,1... | collective-permute-start | bytes 774152 | tf_op jit(solution)/shard_map/ppermute | solution.py:451
  78.9 9.9 %collective-permute-done.20.late = bf16[96,1152]{1,0:T(8,128)(2,1)S(1)} collective-permute-done((bf16[96,1152]{1,0:T(8,128)(2,1)S(1)}, bf16[96,1152]{1,0:T(8,128)(2,1)S(1)}, u32[]{:S(2)}, u32[]{:S(2)}) %collective-permute-start.20) | collective-permute-done | bytes 221216 | tf_op jit(solution)/shard_map/ppermute | solution.py:451
  88.8 1.6 %collective-permute-start.23 = (bf16[96,1152]{1,0:T(8,128)(2,1)S(1)}, bf16[96,1152]{1,0:T(8,128)(2,1)S(1)}, u32[]{:S(2)}, u32[]{:S(2)}) collective-permute-start(bf16[96,1152]{1,0:T(8,128)(2,1)S(1)} %total.5.refs_1_), channel_id=1, source_target_pairs={{0,2},{2,0},{1,3},{3,1},{4,6},{6,4},{5,7},{7,5},{8,10},{10,8},{9,1... | collective-permute-start | bytes 663560 | tf_op jit(solution)/shard_map/ppermute | solution.py:451
  90.4 1.9 %finish.2 = (f32[3,3,192,384]{3,2,1,0:T(8,128)}, f32[3,384]{1,0:T(4,128)}) custom-call(f32[1,1152]{1,0:T(1,128)S(1)} %get-tuple-element.147.refs_0_, bf16[96,1152]{1,0:T(8,128)(2,1)S(1)} %total.3.refs_1_, bf16[96,1152]{1,0:T(8,128)(2,1)S(1)} %collective-permute-done.21.refs_2_, bf16[112,1152]{1,0:T(8,128)(2,1)S(1)} %get-tuple-element.149.refs_3_, ...), custom_call_target="tpu_custom_call" | custom-call | flops 6635520 | bytes 36218880 | tf_op jit(solution)/shard_map/finish/pallas_call | solution.py:435
  92.3 4.0 %collective-permute-done.23.refs_2_ = bf16[96,1152]{1,0:T(8,128)(2,1)S(1)} collective-permute-done((bf16[96,1152]{1,0:T(8,128)(2,1)S(1)}, bf16[96,1152]{1,0:T(8,128)(2,1)S(1)}, u32[]{:S(2)}, u32[]{:S(2)}) %collective-permute-start.23) | collective-permute-done | bytes 221216 | tf_op jit(solution)/shard_map/ppermute | solution.py:451
  96.2 1.0 %finish.3 = f32[3,3,192,384]{3,2,1,0:T(8,128)} custom-call(f32[3,3,192,384]{3,2,1,0:T(8,128)} %get-tuple-element.150.refs_0_, bf16[96,1152]{1,0:T(8,128)(2,1)S(1)} %total.5.refs_1_, bf16[96,1152]{1,0:T(8,128)(2,1)S(1)} %collective-permute-done.23.refs_2_), custom_call_target="tpu_custom_call", output_to_operand_aliasing={{}: (0, {})} | custom-call | flops 6635520 | bytes 57507840 | tf_op jit(solution)/shard_map/finish/pallas_call | solution.py:435
  (52 shorter events, 12.1 us)
Async XLA Ops:
  3.2 4.7 %collective-permute-start = (bf16[512,384]{1,0:T(8,128)(2,1)S(1)}, bf16[512,384]{1,0:T(8,128)(2,1)S(1)}, u32[]{:S(2)}, u32[]{:S(2)}) collective-permute-start(bf16[512,384]{1,0:T(8,128)(2,1)S(1)} %get-tuple-element.129.snake_ref.own_ref.refs_0_), channel_id=1, source_target_pairs={{0,1},{1,0},{2,3},{3,2},{4,5},{5,4},{6,7},{7,6},{8,9},{9,8},{10,11... | collective-permute-start | bytes 1179656 | tf_op jit(solution)/shard_map/ppermute | solution.py:451
  5.3 12.3 %collective-permute-start.5 = (bf16[512,384]{1,0:T(8,128)(2,1)S(1)}, bf16[512,384]{1,0:T(8,128)(2,1)S(1)}, u32[]{:S(2)}, u32[]{:S(2)}) collective-permute-start(bf16[512,384]{1,0:T(8,128)(2,1)S(1)} %get-tuple-element.104.grad_ref.rest_0_), channel_id=1, source_target_pairs={{0,2},{2,0},{1,3},{3,1},{4,6},{6,4},{5,7},{7,5},{8,10},{10,8},{9,1... | collective-permute-start | bytes 1179656 | tf_op jit(solution)/shard_map/ppermute | solution.py:451
  10.2 2.4 %collective-permute-start.1 = (bf16[512,384]{1,0:T(8,128)(2,1)S(1)}, bf16[512,384]{1,0:T(8,128)(2,1)S(1)}, u32[]{:S(2)}, u32[]{:S(2)}) collective-permute-start(bf16[512,384]{1,0:T(8,128)(2,1)S(1)} %get-tuple-element.119.snake_ref.refs_0_.own_ref), channel_id=1, source_target_pairs={{0,1},{1,0},{2,3},{3,2},{4,5},{5,4},{6,7},{7,6},{8,9},{9,8},{10,11... | collective-permute-start | bytes 1179656 | tf_op jit(solution)/shard_map/ppermute | solution.py:451
  11.4 4.6 %collective-permute-start.3 = (bf16[512,384]{1,0:T(8,128)(2,1)S(1)}, bf16[512,384]{1,0:T(8,128)(2,1)S(1)}, u32[]{:S(2)}, u32[]{:S(2)}) collective-permute-start(bf16[512,384]{1,0:T(8,128)(2,1)S(1)} %get-tuple-element.93), channel_id=1, source_target_pairs={{0,1},{1,0},{2,3},{3,2},{4,5},{5,4},{6,7},{7,6},{8,9},{9,8},{10,11... | collective-permute-start | bytes 1179656 | tf_op jit(solution)/shard_map/ppermute | solution.py:451
  14.3 5.8 %collective-permute-start.2 = (bf16[512,384]{1,0:T(8,128)(2,1)S(1)}, bf16[512,384]{1,0:T(8,128)(2,1)S(1)}, u32[]{:S(2)}, u32[]{:S(2)}) collective-permute-start(bf16[512,384]{1,0:T(8,128)(2,1)S(1)} %get-tuple-element.122.refs_0_.own_ref.snake_ref), channel_id=1, source_target_pairs={{0,1},{1,0},{2,3},{3,2},{4,5},{5,4},{6,7},{7,6},{8,9},{9,8},{10,11... | collective-permute-start | bytes 1179656 | tf_op jit(solution)/shard_map/ppermute | solution.py:451
  14.7 7.8 %collective-permute-start.7 = (bf16[192,512]{1,0:T(8,128)(2,1)S(1)}, bf16[192,512]{1,0:T(8,128)(2,1)S(1)}, u32[]{:S(2)}, u32[]{:S(2)}) collective-permute-start(bf16[192,512]{1,0:T(8,128)(2,1)S(1)} %turn.3), channel_id=1, source_target_pairs={{0,2},{2,0},{1,3},{3,1},{4,6},{6,4},{5,7},{7,5},{8,10},{10,8},{9,1... | collective-permute-start | bytes 589832 | tf_op jit(solution)/shard_map/ppermute | solution.py:451
  17.7 15.0 %collective-permute-start.4 = (bf16[512,384]{1,0:T(8,128)(2,1)S(1)}, bf16[512,384]{1,0:T(8,128)(2,1)S(1)}, u32[]{:S(2)}, u32[]{:S(2)}) collective-permute-start(bf16[512,384]{1,0:T(8,128)(2,1)S(1)} %get-tuple-element.108.grad_ref), channel_id=1, source_target_pairs={{0,2},{2,0},{1,3},{3,1},{4,6},{6,4},{5,7},{7,5},{8,10},{10,8},{9,1... | collective-permute-start | bytes 1179656 | tf_op jit(solution)/shard_map/ppermute | solution.py:451
  20.5 14.0 %collective-permute-start.10 = (bf16[192,512]{1,0:T(8,128)(2,1)S(1)}, bf16[192,512]{1,0:T(8,128)(2,1)S(1)}, u32[]{:S(2)}, u32[]{:S(2)}) collective-permute-start(bf16[192,512]{1,0:T(8,128)(2,1)S(1)} %turn.4), channel_id=1, source_target_pairs={{0,2},{2,0},{1,3},{3,1},{4,6},{6,4},{5,7},{7,5},{8,10},{10,8},{9,1... | collective-permute-start | bytes 589832 | tf_op jit(solution)/shard_map/ppermute | solution.py:451
  21.5 1.9 %collective-permute-start.6 = (bf16[512,384]{1,0:T(8,128)(2,1)S(1)}, bf16[512,384]{1,0:T(8,128)(2,1)S(1)}, u32[]{:S(2)}, u32[]{:S(2)}) collective-permute-start(bf16[512,384]{1,0:T(8,128)(2,1)S(1)} %get-tuple-element.110), channel_id=1, source_target_pairs={{0,1},{1,0},{2,3},{3,2},{4,5},{5,4},{6,7},{7,6},{8,9},{9,8},{10,11... | collective-permute-start | bytes 1179656 | tf_op jit(solution)/shard_map/ppermute | solution.py:451
  22.5 2.6 %collective-permute-start.8 = (bf16[192,512]{1,0:T(8,128)(2,1)S(1)}, bf16[192,512]{1,0:T(8,128)(2,1)S(1)}, u32[]{:S(2)}, u32[]{:S(2)}) collective-permute-start(bf16[192,512]{1,0:T(8,128)(2,1)S(1)} %collective-permute-done.7.across_ref), channel_id=1, source_target_pairs={{0,1},{1,0},{2,3},{3,2},{4,5},{5,4},{6,7},{7,6},{8,9},{9,8},{10,11... | collective-permute-start | bytes 589832 | tf_op jit(solution)/shard_map/ppermute | solution.py:451
  26.6 15.9 %collective-permute-start.13 = (bf16[192,1152]{1,0:T(8,128)(2,1)S(1)}, bf16[192,1152]{1,0:T(8,128)(2,1)S(1)}, u32[]{:S(2)}, u32[]{:S(2)}) collective-permute-start(bf16[192,1152]{1,0:T(8,128)(2,1)S(1)} %get-tuple-element.132), channel_id=1, source_target_pairs={{0,4},{4,0},{8,12},{12,8},{1,5},{5,1},{9,13},{13,9},{2,6},{6,2},{1... | collective-permute-start | bytes 1327112 | tf_op jit(solution)/shard_map/ppermute | solution.py:451
  29.2 1.8 %collective-permute-start.9 = (bf16[512,384]{1,0:T(8,128)(2,1)S(1)}, bf16[512,384]{1,0:T(8,128)(2,1)S(1)}, u32[]{:S(2)}, u32[]{:S(2)}) collective-permute-start(bf16[512,384]{1,0:T(8,128)(2,1)S(1)} %get-tuple-element.118), channel_id=1, source_target_pairs={{0,1},{1,0},{2,3},{3,2},{4,5},{5,4},{6,7},{7,6},{8,9},{9,8},{10,11... | collective-permute-start | bytes 1179656 | tf_op jit(solution)/shard_map/ppermute | solution.py:451
  34.5 2.4 %collective-permute-start.11 = (bf16[192,512]{1,0:T(8,128)(2,1)S(1)}, bf16[192,512]{1,0:T(8,128)(2,1)S(1)}, u32[]{:S(2)}, u32[]{:S(2)}) collective-permute-start(bf16[192,512]{1,0:T(8,128)(2,1)S(1)} %collective-permute-done.10.across_ref), channel_id=1, source_target_pairs={{0,1},{1,0},{2,3},{3,2},{4,5},{5,4},{6,7},{7,6},{8,9},{9,8},{10,11... | collective-permute-start | bytes 589832 | tf_op jit(solution)/shard_map/ppermute | solution.py:451
  38.3 20.7 %collective-permute-start.16 = (bf16[208,1152]{1,0:T(8,128)(2,1)S(1)}, bf16[208,1152]{1,0:T(8,128)(2,1)S(1)}, u32[]{:S(2)}, u32[]{:S(2)}) collective-permute-start(bf16[208,1152]{1,0:T(8,128)(2,1)S(1)} %get-tuple-element.138), channel_id=1, source_target_pairs={{0,4},{4,0},{8,12},{12,8},{1,5},{5,1},{9,13},{13,9},{2,6},{6,2},{1... | collective-permute-start | bytes 1437704 | tf_op jit(solution)/shard_map/ppermute | solution.py:451
  40.3 15.5 %collective-permute-start.12 = (bf16[512,384]{1,0:T(8,128)(2,1)S(1)}, bf16[512,384]{1,0:T(8,128)(2,1)S(1)}, u32[]{:S(2)}, u32[]{:S(2)}) collective-permute-start(bf16[512,384]{1,0:T(8,128)(2,1)S(1)} %get-tuple-element.130.grad_ref), channel_id=1, source_target_pairs={{0,2},{2,0},{1,3},{3,1},{4,6},{6,4},{5,7},{7,5},{8,10},{10,8},{9,1... | collective-permute-start | bytes 1179656 | tf_op jit(solution)/shard_map/ppermute | solution.py:451
  41.9 14.0 %collective-permute-start.14 = (bf16[192,512]{1,0:T(8,128)(2,1)S(1)}, bf16[192,512]{1,0:T(8,128)(2,1)S(1)}, u32[]{:S(2)}, u32[]{:S(2)}) collective-permute-start(bf16[192,512]{1,0:T(8,128)(2,1)S(1)} %turn.5), channel_id=1, source_target_pairs={{0,2},{2,0},{1,3},{3,1},{4,6},{6,4},{5,7},{7,5},{8,10},{10,8},{9,1... | collective-permute-start | bytes 589832 | tf_op jit(solution)/shard_map/ppermute | solution.py:451
  42.5 19.5 %collective-permute-start.17 = (bf16[96,1152]{1,0:T(8,128)(2,1)S(1)}, bf16[96,1152]{1,0:T(8,128)(2,1)S(1)}, u32[]{:S(2)}, u32[]{:S(2)}) collective-permute-start(bf16[96,1152]{1,0:T(8,128)(2,1)S(1)} %fold.3), channel_id=1, source_target_pairs={{0,8},{4,12},{8,0},{12,4},{1,9},{5,13},{9,1},{13,5},{2,10},{6,14},... | collective-permute-start | bytes 663560 | tf_op jit(solution)/shard_map/ppermute | solution.py:451
  55.9 1.4 %collective-permute-start.15 = (bf16[192,512]{1,0:T(8,128)(2,1)S(1)}, bf16[192,512]{1,0:T(8,128)(2,1)S(1)}, u32[]{:S(2)}, u32[]{:S(2)}) collective-permute-start(bf16[192,512]{1,0:T(8,128)(2,1)S(1)} %collective-permute-done.14.across_ref), channel_id=1, source_target_pairs={{0,1},{1,0},{2,3},{3,2},{4,5},{5,4},{6,7},{7,6},{8,9},{9,8},{10,11... | collective-permute-start | bytes 589832 | tf_op jit(solution)/shard_map/ppermute | solution.py:451
  58.7 17.8 %collective-permute-start.18 = (bf16[192,1152]{1,0:T(8,128)(2,1)S(1)}, bf16[192,1152]{1,0:T(8,128)(2,1)S(1)}, u32[]{:S(2)}, u32[]{:S(2)}) collective-permute-start(bf16[192,1152]{1,0:T(8,128)(2,1)S(1)} %get-tuple-element.142), channel_id=1, source_target_pairs={{0,4},{4,0},{8,12},{12,8},{1,5},{5,1},{9,13},{13,9},{2,6},{6,2},{1... | collective-permute-start | bytes 1327112 | tf_op jit(solution)/shard_map/ppermute | solution.py:451
  59.1 18.0 %collective-permute-start.19 = (bf16[112,1152]{1,0:T(8,128)(2,1)S(1)}, bf16[112,1152]{1,0:T(8,128)(2,1)S(1)}, u32[]{:S(2)}, u32[]{:S(2)}) collective-permute-start(bf16[112,1152]{1,0:T(8,128)(2,1)S(1)} %get-tuple-element.144), channel_id=1, source_target_pairs={{0,8},{4,12},{8,0},{12,4},{1,9},{5,13},{9,1},{13,5},{2,10},{6,14},... | collective-permute-start | bytes 774152 | tf_op jit(solution)/shard_map/ppermute | solution.py:451
  62.0 28.4 %collective-permute-start.21 = (bf16[96,1152]{1,0:T(8,128)(2,1)S(1)}, bf16[96,1152]{1,0:T(8,128)(2,1)S(1)}, u32[]{:S(2)}, u32[]{:S(2)}) collective-permute-start(bf16[96,1152]{1,0:T(8,128)(2,1)S(1)} %total.3.refs_1_), channel_id=1, source_target_pairs={{0,2},{2,0},{1,3},{3,1},{4,6},{6,4},{5,7},{7,5},{8,10},{10,8},{9,1... | collective-permute-start | bytes 663560 | tf_op jit(solution)/shard_map/ppermute | solution.py:451
  76.6 12.2 %collective-permute-start.20 = (bf16[96,1152]{1,0:T(8,128)(2,1)S(1)}, bf16[96,1152]{1,0:T(8,128)(2,1)S(1)}, u32[]{:S(2)}, u32[]{:S(2)}) collective-permute-start(bf16[96,1152]{1,0:T(8,128)(2,1)S(1)} %fold.5), channel_id=1, source_target_pairs={{0,8},{4,12},{8,0},{12,4},{1,9},{5,13},{9,1},{13,5},{2,10},{6,14},... | collective-permute-start | bytes 663560 | tf_op jit(solution)/shard_map/ppermute | solution.py:451
  77.3 13.1 %collective-permute-start.22 = (bf16[112,1152]{1,0:T(8,128)(2,1)S(1)}, bf16[112,1152]{1,0:T(8,128)(2,1)S(1)}, u32[]{:S(2)}, u32[]{:S(2)}) collective-permute-start(bf16[112,1152]{1,0:T(8,128)(2,1)S(1)} %get-tuple-element.149.refs_3_), channel_id=1, source_target_pairs={{0,2},{2,0},{1,3},{3,1},{4,6},{6,4},{5,7},{7,5},{8,10},{10,8},{9,1... | collective-permute-start | bytes 774152 | tf_op jit(solution)/shard_map/ppermute | solution.py:451
  88.8 7.4 %collective-permute-start.23 = (bf16[96,1152]{1,0:T(8,128)(2,1)S(1)}, bf16[96,1152]{1,0:T(8,128)(2,1)S(1)}, u32[]{:S(2)}, u32[]{:S(2)}) collective-permute-start(bf16[96,1152]{1,0:T(8,128)(2,1)S(1)} %total.5.refs_1_), channel_id=1, source_target_pairs={{0,2},{2,0},{1,3},{3,1},{4,6},{6,4},{5,7},{7,5},{8,10},{10,8},{9,1... | collective-permute-start | bytes 663560 | tf_op jit(solution)/shard_map/ppermute | solution.py:451

commit v10 on v9

--- a/solution.py
+++ b/solution.py
@@ -350,7 +350,7 @@
     for index, (layer, pieces) in enumerate(counts):
         for part in range(pieces):
             mine_ref, other_ref = refs.pop(0), refs.pop(0)
-            size = rows_of
+            size = rows_of // pieces
             if carry and other_ref.shape[0] > size:
                 alpha = alpha_mine[...] + read_carried(other_ref, size)
                 for place in range(3):
@@ -464,7 +464,7 @@
     layers, taps, channels, _ = conv_weights.shape
     top = layers - 1
     fast = lax.axis_size("dp") == 4 and lax.axis_size("replica") == 2
-    counts = [1] * layers
+    counts = [2, 1, 1] if fast else [1, 1, 1]
     carrier = 1 if fast else None
     weight = {}
     tile, triple = (rows, half), (rows, taps * half)
@@ -575,6 +575,11 @@
                 functools.partial(far_kernel, layer), "far_rows", [0], struct(triple, BF16), [],
                 10 * rows * half, far[layer],
             )
+
+    def launch(layer, part):
+        if fast:
+            send, kept[layer, part] = kept[layer, part]
+            got[layer, part] = swap(sequence.hold(send) if part else send, "dp", lambda i: i ^ 1)
 
     def weights(layer):
         if not fast:
@@ -597,8 +602,8 @@
             [0] * len(args), outs, [pltpu.VMEM((half, rows), BF16)], 2 * flops, *args,
         )
         for part in range(pieces):
-            got[layer, part] = swap(out[part], "dp", lambda i: i ^ 1)
-            kept[layer, part] = out[pieces + part]
+            kept[layer, part] = (out[part], out[pieces + part])
+        launch(layer, 0)
 
     carry_sum = [None]
 
@@ -701,7 +706,7 @@
     send_gradient(1)
     far_rows(2)
     own_rows(2)
-    turn(1)
+    turn(1, 0)
     back_partner(1)
     share(2)
     back_own(1)
@@ -714,29 +719,31 @@
     own_rows(1)
     far_rows(1)
     own_rows(0)
-    share(1)
+    share(1, 0)
+    send_gradient(0)
     forward_own(2)
     residual_out = forward_partner(2)
     sequence.weight = 0.01
     weights(1)
-    turn(0)
-    send_gradient(0)
     fold(2)
-    share(0)
     far_rows(0)
     sequence.weight = 0.01
     weights(0)
     sequence.weight = 10
     fold(1)
     total(2)
-    cross(2)
-    fold(0)
+    fold(0, 0)
+    launch(0, 1)
     total(1)
     cross(1)
-    total(0)
-    cross(0)
+    cross(2)
+    fold(0, 1)
+    total(0, 0)
+    cross(0, 0)
     if fast:
         weight_grads, alpha_grads = finish((2, 1))
+        total(0, 1)
+        cross(0, 1)
         (weight_grads,) = finish((0,), weight_grads)
     else:
         alpha_grads = alpha_round()

time: 97.6 us -> 104 us (1.066)
  starting transfers between devices: 23.7 us -> 28.4 us
  waiting for transfers between devices: 41.7 us -> 43.1 us
    ppermute x24 -> x25, starting transfers between devices: 23.7 us -> 28.4 us  [swap(): lax.ppermute(x, axis, [(i, other(i)) for i in range(lax.axis_size(axis))])]
    ppermute x24 -> x25, waiting for transfers between devices: 41.7 us -> 43.1 us  [swap(): lax.ppermute(x, axis, [(i, other(i)) for i in range(lax.axis_size(axis))])]
    pallas_call x36 -> x37, Pallas kernels: 30.9 us -> 30.7 us  [call(): pl.pallas_call(kernel, in_specs=[ANY_HBM if i else IN_VMEM for i in ins],...]
  transfers between devices with their start and end apart: 24 -> 25, of which waited for: 9 -> 13; matrix products, arithmetic and copies ran while one was open for 0% -> 0% of each run, Pallas kernels for 28% -> 26%
where the time goes in v10:
time: 104 us; the launch traced here: 103 us
  waiting for transfers between devices  43.1 us (41%)
  Pallas kernels  30.7 us (30%)
  starting transfers between devices  28.4 us (27%)
  between operations  1.12 us (1%)
    ppermute x25, waiting for transfers between devices, swap(): lax.ppermute(x, axis, [(i, other(i)) for i in range(lax.axis_size(axis))])  43.1 us
    pallas_call x37, Pallas kernels, call(): pl.pallas_call(kernel, in_specs=[ANY_HBM if i else IN_VMEM for i in ins],...  30.7 us
    ppermute x25, starting transfers between devices, swap(): lax.ppermute(x, axis, [(i, other(i)) for i in range(lax.axis_size(axis))])  28.4 us
  transfers between devices with their start and end apart: 25, of which 13 were waited for; matrix products, arithmetic and copies ran while one was open for 0% of the time, Pallas kernels for 26%

profile of v10, /device:TPU:0, one launch (start us, length us, event | category | flops | bytes accessed | tf_op | source)
XLA Modules:
  0.0 103.3 jit_solution(13608908184214278300)
XLA Ops:
  0.6 2.5 %prep.1 = (f32[512,384]{1,0:T(8,128)S(1)}, bf16[512,384]{1,0:T(8,128)(2,1)S(1)}, bf16[512,384]{1,0:T(8,128)(2,1)S(1)}, f32[512,128]{1,0:T(8,128)S(1)}, f32[3,384...) custom-call(s32[16]{0:T(128)} %len_hbm.1, s32[16]{0:T(128)} %own_hbm.1, s32[16]{0:T(128)} %start_hbm.1, ...), custom_call_target="tpu_custom_call" | custom-call | flops 78643200 | bytes 44003200 | tf_op jit(solution)/shard_map/prep/pallas_call | solution.py:435
  3.7 1.6 %forward_own.3 = (f32[512,384]{1,0:T(8,128)S(1)}, bf16[2,1152,384]{2,1,0:T(8,128)(2,1)S(1)}) custom-call(bf16[512,384]{1,0:T(8,128)(2,1)S(1)} %get-tuple-element.125.snake_ref.refs_1_.own_ref, bf16[2,1152,384]{2,1,0:T(8,128)(2,1)S(1)} %get-tuple-element.85.weight_ref, bf16[3,3,768,384]{3,2,1,0:T(8,128)(2,1)} %rest_1_.1), custom_call_target="tpu_custom_call" | custom-call | flops 4529848320 | bytes 47185920 | tf_op jit(solution)/shard_map/forward_own/pallas_call | solution.py:435
  5.3 2.6 %collective-permute-start.5 = (bf16[512,384]{1,0:T(8,128)(2,1)S(1)}, bf16[512,384]{1,0:T(8,128)(2,1)S(1)}, u32[]{:S(2)}, u32[]{:S(2)}) collective-permute-start(bf16[512,384]{1,0:T(8,128)(2,1)S(1)} %get-tuple-element.108.grad_ref.rest_0_), channel_id=1, source_target_pairs={{0,2},{2,0},{1,3},{3,1},{4,6},{6,4},{5,7},{7,5},{8,10},{10,8},{9,1... | collective-permute-start | bytes 1179656 | tf_op jit(solution)/shard_map/ppermute | solution.py:451
  7.9 2.3 %forward_partner.3 = (f32[512,384]{1,0:T(8,128)S(1)}, bf16[512,384]{1,0:T(8,128)(2,1)S(1)}, bf16[2,1152,384]{2,1,0:T(8,128)(2,1)S(1)}) custom-call(bf16[512,384]{1,0:T(8,128)(2,1)S(1)} %collective-permute-done.snake_ref.partner_ref, bf16[2,1152,384]{2,1,0:T(8,128)(2,1)S(1)} %get-tuple-element.85.weight_ref, f32[512,384]{1,0:T(8,128)S(1)} %get-tuple-element.89.own_ref, ...), custom_call_target="tpu_custom_call" | custom-call | flops 4529848320 | bytes 69514240 | tf_op jit(solution)/shard_map/forward_partner/pallas_call | solution.py:435
  12.5 1.7 %forward_partner.4 = (f32[512,384]{1,0:T(8,128)S(1)}, bf16[512,384]{1,0:T(8,128)(2,1)S(1)}) custom-call(bf16[512,384]{1,0:T(8,128)(2,1)S(1)} %collective-permute-done.1.snake_ref.partner_ref, bf16[2,1152,384]{2,1,0:T(8,128)(2,1)S(1)} %get-tuple-element.95.weight_ref, f32[512,384]{1,0:T(8,128)S(1)} %forward_own.4.own_ref, ...), custom_call_target="tpu_custom_call" | custom-call | flops 4529848320 | bytes 51819520 | tf_op jit(solution)/shard_map/forward_partner/pallas_call | solution.py:435
  16.0 1.6 %combine.3 = (f32[1,384]{1,0:T(1,128)S(1)}, f32[512,384]{1,0:T(8,128)S(1)}, bf16[512,384]{1,0:T(8,128)(2,1)S(1)}) custom-call(f32[512,384]{1,0:T(8,128)S(1)} %back_own.3.own_ref, bf16[512,384]{1,0:T(8,128)(2,1)S(1)} %collective-permute-done.3.partner_ref, f32[512,384]{1,0:T(8,128)S(1)} %get-tuple-element.105.stream_ref.old_ref, ...), custom_call_target="tpu_custom_call" | custom-call | flops 117964800 | bytes 38072320 | tf_op jit(solution)/shard_map/combine/pallas_call | solution.py:435
  17.6 2.1 %collective-permute-start.4 = (bf16[512,384]{1,0:T(8,128)(2,1)S(1)}, bf16[512,384]{1,0:T(8,128)(2,1)S(1)}, u32[]{:S(2)}, u32[]{:S(2)}) collective-permute-start(bf16[512,384]{1,0:T(8,128)(2,1)S(1)} %get-tuple-element.112.grad_ref), channel_id=1, source_target_pairs={{0,2},{2,0},{1,3},{3,1},{4,6},{6,4},{5,7},{7,5},{8,10},{10,8},{9,1... | collective-permute-start | bytes 1179656 | tf_op jit(solution)/shard_map/ppermute | solution.py:451
  23.4 1.7 %combine.4 = (f32[1,384]{1,0:T(1,128)S(1)}, bf16[512,384]{1,0:T(8,128)(2,1)S(1)}) custom-call(f32[512,384]{1,0:T(8,128)S(1)} %back_own.4.own_ref, bf16[512,384]{1,0:T(8,128)(2,1)S(1)} %collective-permute-done.6.partner_ref, f32[512,384]{1,0:T(8,128)S(1)} %get-tuple-element.100.old_ref.stream_ref, f32[3,384]{1,0:T(4,128)S(1)} %get-tuple-element.92.rest_0_.alphas_ref, ...), custom_call_target="tpu_custom_call" | custom-call | flops 117964800 | bytes 34140160 | tf_op jit(solution)/shard_map/combine/pallas_call | solution.py:435
  26.5 1.9 %collective-permute-start.13 = (bf16[192,1152]{1,0:T(8,128)(2,1)S(1)}, bf16[192,1152]{1,0:T(8,128)(2,1)S(1)}, u32[]{:S(2)}, u32[]{:S(2)}) collective-permute-start(bf16[192,1152]{1,0:T(8,128)(2,1)S(1)} %get-tuple-element.135), channel_id=1, source_target_pairs={{0,4},{4,0},{8,12},{12,8},{1,5},{5,1},{9,13},{13,9},{2,6},{6,2},{1... | collective-permute-start | bytes 1327112 | tf_op jit(solution)/shard_map/ppermute | solution.py:451
  31.1 1.4 %combine.5.rest_0_ = f32[1,384]{1,0:T(1,128)S(1)} custom-call(f32[512,384]{1,0:T(8,128)S(1)} %back_own.5.own_ref, bf16[512,384]{1,0:T(8,128)(2,1)S(1)} %collective-permute-done.9.partner_ref, f32[512,384]{1,0:T(8,128)S(1)} %get-tuple-element.90.old_ref.stream_ref, f32[3,384]{1,0:T(4,128)S(1)} %get-tuple-element.92.rest_0_.alphas_ref), custom_call_target="tpu_custom_call" | custom-call | flops 117964800 | bytes 19722240 | tf_op jit(solution)/shard_map/combine/pallas_call | solution.py:435
  33.3 5.4 %collective-permute-done.10.across_ref = bf16[384,512]{1,0:T(8,128)(2,1)S(1)} collective-permute-done((bf16[384,512]{1,0:T(8,128)(2,1)S(1)}, bf16[384,512]{1,0:T(8,128)(2,1)S(1)}, u32[]{:S(2)}, u32[]{:S(2)}) %collective-permute-start.10) | collective-permute-done | bytes 393248 | tf_op jit(solution)/shard_map/ppermute | solution.py:451
  39.6 1.5 %forward_partner.5 = bf16[512,384]{1,0:T(8,128)(2,1)} custom-call(bf16[512,384]{1,0:T(8,128)(2,1)S(1)} %collective-permute-done.2.partner_ref.snake_ref, bf16[2,1152,384]{2,1,0:T(8,128)(2,1)S(1)} %get-tuple-element.87.weight_ref, f32[512,384]{1,0:T(8,128)S(1)} %forward_own.5.own_ref, f32[512,384]{1,0:T(8,128)S(1)} %get-tuple-element.105.stream_ref.old_ref, ...), custom_call_target="tpu_custom_call" | custom-call | flops 4529848320 | bytes 43909120 | tf_op jit(solution)/shard_map/forward_partner/pallas_call | solution.py:435
  41.3 1.4 %paired_weight.4 = (bf16[208,1152]{1,0:T(8,128)(2,1)S(1)}, bf16[192,1152]{1,0:T(8,128)(2,1)S(1)}) custom-call(bf16[384,512]{1,0:T(8,128)(2,1)S(1)} %own_rows.4.own_ref, bf16[512,1152]{1,0:T(8,128)(2,1)S(1)} %get-tuple-element.113.shifted_ref, bf16[384,512]{1,0:T(8,128)(2,1)S(1)} %collective-permute-done.10.across_ref, ...), custom_call_target="tpu_custom_call" | custom-call | flops 9059696 | bytes 44651 | tf_op jit(solution)/shard_map/paired_weight/pallas_call | solution.py:435
  42.7 1.9 %collective-permute-start.14 = (bf16[208,1152]{1,0:T(8,128)(2,1)S(1)}, bf16[208,1152]{1,0:T(8,128)(2,1)S(1)}, u32[]{:S(2)}, u32[]{:S(2)}) collective-permute-start(bf16[208,1152]{1,0:T(8,128)(2,1)S(1)} %get-tuple-element.141), channel_id=1, source_target_pairs={{0,4},{4,0},{8,12},{12,8},{1,5},{5,1},{9,13},{13,9},{2,6},{6,2},{1... | collective-permute-start | bytes 1437704 | tf_op jit(solution)/shard_map/ppermute | solution.py:451
  44.6 1.5 %collective-permute-start.12 = (bf16[512,384]{1,0:T(8,128)(2,1)S(1)}, bf16[512,384]{1,0:T(8,128)(2,1)S(1)}, u32[]{:S(2)}, u32[]{:S(2)}) collective-permute-start(bf16[512,384]{1,0:T(8,128)(2,1)S(1)} %get-tuple-element.133.grad_ref), channel_id=1, source_target_pairs={{0,2},{2,0},{1,3},{3,1},{4,6},{6,4},{5,7},{7,5},{8,10},{10,8},{9,1... | collective-permute-start | bytes 1179656 | tf_op jit(solution)/shard_map/ppermute | solution.py:451
  46.1 2.7 %collective-permute-start.15 = (bf16[96,1152]{1,0:T(8,128)(2,1)S(1)}, bf16[96,1152]{1,0:T(8,128)(2,1)S(1)}, u32[]{:S(2)}, u32[]{:S(2)}) collective-permute-start(bf16[96,1152]{1,0:T(8,128)(2,1)S(1)} %fold.4), channel_id=1, source_target_pairs={{0,8},{4,12},{8,0},{12,4},{1,9},{5,13},{9,1},{13,5},{2,10},{6,14},... | collective-permute-start | bytes 663560 | tf_op jit(solution)/shard_map/ppermute | solution.py:451
  48.8 6.9 %collective-permute-done.12.grad_ref = bf16[512,384]{1,0:T(8,128)(2,1)S(1)} collective-permute-done((bf16[512,384]{1,0:T(8,128)(2,1)S(1)}, bf16[512,384]{1,0:T(8,128)(2,1)S(1)}, u32[]{:S(2)}, u32[]{:S(2)}) %collective-permute-start.12) | collective-permute-done | bytes 393248 | tf_op jit(solution)/shard_map/ppermute | solution.py:451
  55.9 1.4 %paired_weight.5 = (bf16[96,1152]{1,0:T(8,128)(2,1)S(1)}, bf16[96,1152]{1,0:T(8,128)(2,1)S(1)}, bf16[96,1152]{1,0:T(8,128)(2,1)S(1)}, bf16[96,1152]{1,0:T(8,128)(2,1)S(1)}) custom-call(bf16[384,512]{1,0:T(8,128)(2,1)S(1)} %own_rows.5.own_ref, bf16[512,1152]{1,0:T(8,128)(2,1)S(1)} %get-tuple-element.121.shifted_ref, ...), custom_call_target="tpu_custom_call" | custom-call | flops 9059696 | bytes 44236 | tf_op jit(solution)/shard_map/paired_weight/pallas_call | solution.py:435
  57.7 3.6 %collective-permute-done.14.got = bf16[208,1152]{1,0:T(8,128)(2,1)S(1)} collective-permute-done((bf16[208,1152]{1,0:T(8,128)(2,1)S(1)}, bf16[208,1152]{1,0:T(8,128)(2,1)S(1)}, u32[]{:S(2)}, u32[]{:S(2)}) %collective-permute-start.14) | collective-permute-done | bytes 479264 | tf_op jit(solution)/shard_map/ppermute | solution.py:451
  61.4 2.0 %collective-permute-start.17 = (bf16[112,1152]{1,0:T(8,128)(2,1)S(1)}, bf16[112,1152]{1,0:T(8,128)(2,1)S(1)}, u32[]{:S(2)}, u32[]{:S(2)}) collective-permute-start(bf16[112,1152]{1,0:T(8,128)(2,1)S(1)} %get-tuple-element.147), channel_id=1, source_target_pairs={{0,8},{4,12},{8,0},{12,4},{1,9},{5,13},{9,1},{13,5},{2,10},{6,14},... | collective-permute-start | bytes 774152 | tf_op jit(solution)/shard_map/ppermute | solution.py:451
  63.5 5.8 %collective-permute-done.16.got = bf16[96,1152]{1,0:T(8,128)(2,1)S(1)} collective-permute-done((bf16[96,1152]{1,0:T(8,128)(2,1)S(1)}, bf16[96,1152]{1,0:T(8,128)(2,1)S(1)}, u32[]{:S(2)}, u32[]{:S(2)}) %collective-permute-start.16) | collective-permute-done | bytes 221216 | tf_op jit(solution)/shard_map/ppermute | solution.py:451
  69.3 2.0 %collective-permute-start.18 = (bf16[96,1152]{1,0:T(8,128)(2,1)S(1)}, bf16[96,1152]{1,0:T(8,128)(2,1)S(1)}, u32[]{:S(2)}, u32[]{:S(2)}) collective-permute-start(bf16[96,1152]{1,0:T(8,128)(2,1)S(1)} %get-tuple-element.151), channel_id=1, source_target_pairs={{0,4},{4,0},{8,12},{12,8},{1,5},{5,1},{9,13},{13,9},{2,6},{6,2},{1... | collective-permute-start | bytes 663560 | tf_op jit(solution)/shard_map/ppermute | solution.py:451
  71.4 7.4 %collective-permute-done.17.late = bf16[112,1152]{1,0:T(8,128)(2,1)S(1)} collective-permute-done((bf16[112,1152]{1,0:T(8,128)(2,1)S(1)}, bf16[112,1152]{1,0:T(8,128)(2,1)S(1)}, u32[]{:S(2)}, u32[]{:S(2)}) %collective-permute-start.17) | collective-permute-done | bytes 258080 | tf_op jit(solution)/shard_map/ppermute | solution.py:451
  78.9 1.6 %collective-permute-done.18.got = bf16[96,1152]{1,0:T(8,128)(2,1)S(1)} collective-permute-done((bf16[96,1152]{1,0:T(8,128)(2,1)S(1)}, bf16[96,1152]{1,0:T(8,128)(2,1)S(1)}, u32[]{:S(2)}, u32[]{:S(2)}) %collective-permute-start.18) | collective-permute-done | bytes 221216 | tf_op jit(solution)/shard_map/ppermute | solution.py:451
  80.6 2.7 %collective-permute-start.22 = (bf16[48,1152]{1,0:T(8,128)(2,1)S(1)}, bf16[48,1152]{1,0:T(8,128)(2,1)S(1)}, u32[]{:S(2)}, u32[]{:S(2)}) collective-permute-start(bf16[48,1152]{1,0:T(8,128)(2,1)S(1)} %fold.7), channel_id=1, source_target_pairs={{0,8},{4,12},{8,0},{12,4},{1,9},{5,13},{9,1},{13,5},{2,10},{6,14},... | collective-permute-start | bytes 331784 | tf_op jit(solution)/shard_map/ppermute | solution.py:451
  83.3 2.7 %collective-permute-start.20 = (bf16[96,1152]{1,0:T(8,128)(2,1)S(1)}, bf16[96,1152]{1,0:T(8,128)(2,1)S(1)}, u32[]{:S(2)}, u32[]{:S(2)}) collective-permute-start(bf16[96,1152]{1,0:T(8,128)(2,1)S(1)} %total.4.refs_1_), channel_id=1, source_target_pairs={{0,2},{2,0},{1,3},{3,1},{4,6},{6,4},{5,7},{7,5},{8,10},{10,8},{9,1... | collective-permute-start | bytes 663560 | tf_op jit(solution)/shard_map/ppermute | solution.py:451
  86.1 2.1 %collective-permute-start.23 = (bf16[48,1152]{1,0:T(8,128)(2,1)S(1)}, bf16[48,1152]{1,0:T(8,128)(2,1)S(1)}, u32[]{:S(2)}, u32[]{:S(2)}) collective-permute-start(bf16[48,1152]{1,0:T(8,128)(2,1)S(1)} %total.6.refs_1_), channel_id=1, source_target_pairs={{0,2},{2,0},{1,3},{3,1},{4,6},{6,4},{5,7},{7,5},{8,10},{10,8},{9,1... | collective-permute-start | bytes 331784 | tf_op jit(solution)/shard_map/ppermute | solution.py:451
  88.1 3.5 %collective-permute-done.20.refs_2_ = bf16[96,1152]{1,0:T(8,128)(2,1)S(1)} collective-permute-done((bf16[96,1152]{1,0:T(8,128)(2,1)S(1)}, bf16[96,1152]{1,0:T(8,128)(2,1)S(1)}, u32[]{:S(2)}, u32[]{:S(2)}) %collective-permute-start.20) | collective-permute-done | bytes 221216 | tf_op jit(solution)/shard_map/ppermute | solution.py:451
  91.6 3.8 %collective-permute-done.21.refs_4_ = bf16[112,1152]{1,0:T(8,128)(2,1)S(1)} collective-permute-done((bf16[112,1152]{1,0:T(8,128)(2,1)S(1)}, bf16[112,1152]{1,0:T(8,128)(2,1)S(1)}, u32[]{:S(2)}, u32[]{:S(2)}) %collective-permute-start.21) | collective-permute-done | bytes 258080 | tf_op jit(solution)/shard_map/ppermute | solution.py:451
  95.4 1.9 %finish.2 = (f32[3,3,192,384]{3,2,1,0:T(8,128)}, f32[3,384]{1,0:T(4,128)}) custom-call(f32[1,1152]{1,0:T(1,128)S(1)} %get-tuple-element.153.refs_0_, bf16[96,1152]{1,0:T(8,128)(2,1)S(1)} %total.4.refs_1_, bf16[96,1152]{1,0:T(8,128)(2,1)S(1)} %collective-permute-done.20.refs_2_, bf16[112,1152]{1,0:T(8,128)(2,1)S(1)} %get-tuple-element.155.refs_3_, ...), custom_call_target="tpu_custom_call" | custom-call | flops 6635520 | bytes 36218880 | tf_op jit(solution)/shard_map/finish/pallas_call | solution.py:435
  97.4 1.7 %collective-permute-start.24 = (bf16[48,1152]{1,0:T(8,128)(2,1)S(1)}, bf16[48,1152]{1,0:T(8,128)(2,1)S(1)}, u32[]{:S(2)}, u32[]{:S(2)}) collective-permute-start(bf16[48,1152]{1,0:T(8,128)(2,1)S(1)} %total.7.refs_3_), channel_id=1, source_target_pairs={{0,2},{2,0},{1,3},{3,1},{4,6},{6,4},{5,7},{7,5},{8,10},{10,8},{9,1... | collective-permute-start | bytes 331784 | tf_op jit(solution)/shard_map/ppermute | solution.py:451
  99.0 3.1 %collective-permute-done.24.refs_4_ = bf16[48,1152]{1,0:T(8,128)(2,1)S(1)} collective-permute-done((bf16[48,1152]{1,0:T(8,128)(2,1)S(1)}, bf16[48,1152]{1,0:T(8,128)(2,1)S(1)}, u32[]{:S(2)}, u32[]{:S(2)}) %collective-permute-start.24) | collective-permute-done | bytes 110624 | tf_op jit(solution)/shard_map/ppermute | solution.py:451
  (55 shorter events, 16.3 us)
Async XLA Ops:
  3.2 4.7 %collective-permute-start = (bf16[512,384]{1,0:T(8,128)(2,1)S(1)}, bf16[512,384]{1,0:T(8,128)(2,1)S(1)}, u32[]{:S(2)}, u32[]{:S(2)}) collective-permute-start(bf16[512,384]{1,0:T(8,128)(2,1)S(1)} %get-tuple-element.125.snake_ref.refs_1_.own_ref), channel_id=1, source_target_pairs={{0,1},{1,0},{2,3},{3,2},{4,5},{5,4},{6,7},{7,6},{8,9},{9,8},{10,11... | collective-permute-start | bytes 1179656 | tf_op jit(solution)/shard_map/ppermute | solution.py:451
  5.3 12.3 %collective-permute-start.5 = (bf16[512,384]{1,0:T(8,128)(2,1)S(1)}, bf16[512,384]{1,0:T(8,128)(2,1)S(1)}, u32[]{:S(2)}, u32[]{:S(2)}) collective-permute-start(bf16[512,384]{1,0:T(8,128)(2,1)S(1)} %get-tuple-element.108.grad_ref.rest_0_), channel_id=1, source_target_pairs={{0,2},{2,0},{1,3},{3,1},{4,6},{6,4},{5,7},{7,5},{8,10},{10,8},{9,1... | collective-permute-start | bytes 1179656 | tf_op jit(solution)/shard_map/ppermute | solution.py:451
  10.2 2.3 %collective-permute-start.1 = (bf16[512,384]{1,0:T(8,128)(2,1)S(1)}, bf16[512,384]{1,0:T(8,128)(2,1)S(1)}, u32[]{:S(2)}, u32[]{:S(2)}) collective-permute-start(bf16[512,384]{1,0:T(8,128)(2,1)S(1)} %get-tuple-element.123.snake_ref.refs_0_.own_ref), channel_id=1, source_target_pairs={{0,1},{1,0},{2,3},{3,2},{4,5},{5,4},{6,7},{7,6},{8,9},{9,8},{10,11... | collective-permute-start | bytes 1179656 | tf_op jit(solution)/shard_map/ppermute | solution.py:451
  11.3 4.6 %collective-permute-start.3 = (bf16[512,384]{1,0:T(8,128)(2,1)S(1)}, bf16[512,384]{1,0:T(8,128)(2,1)S(1)}, u32[]{:S(2)}, u32[]{:S(2)}) collective-permute-start(bf16[512,384]{1,0:T(8,128)(2,1)S(1)} %get-tuple-element.97), channel_id=1, source_target_pairs={{0,1},{1,0},{2,3},{3,2},{4,5},{5,4},{6,7},{7,6},{8,9},{9,8},{10,11... | collective-permute-start | bytes 1179656 | tf_op jit(solution)/shard_map/ppermute | solution.py:451
  14.2 5.8 %collective-permute-start.2 = (bf16[512,384]{1,0:T(8,128)(2,1)S(1)}, bf16[512,384]{1,0:T(8,128)(2,1)S(1)}, u32[]{:S(2)}, u32[]{:S(2)}) collective-permute-start(bf16[512,384]{1,0:T(8,128)(2,1)S(1)} %get-tuple-element.126.refs_0_.own_ref.snake_ref), channel_id=1, source_target_pairs={{0,1},{1,0},{2,3},{3,2},{4,5},{5,4},{6,7},{7,6},{8,9},{9,8},{10,11... | collective-permute-start | bytes 1179656 | tf_op jit(solution)/shard_map/ppermute | solution.py:451
  14.7 7.8 %collective-permute-start.7 = (bf16[192,512]{1,0:T(8,128)(2,1)S(1)}, bf16[192,512]{1,0:T(8,128)(2,1)S(1)}, u32[]{:S(2)}, u32[]{:S(2)}) collective-permute-start(bf16[192,512]{1,0:T(8,128)(2,1)S(1)} %turn.2), channel_id=1, source_target_pairs={{0,2},{2,0},{1,3},{3,1},{4,6},{6,4},{5,7},{7,5},{8,10},{10,8},{9,1... | collective-permute-start | bytes 589832 | tf_op jit(solution)/shard_map/ppermute | solution.py:451
  17.6 15.1 %collective-permute-start.4 = (bf16[512,384]{1,0:T(8,128)(2,1)S(1)}, bf16[512,384]{1,0:T(8,128)(2,1)S(1)}, u32[]{:S(2)}, u32[]{:S(2)}) collective-permute-start(bf16[512,384]{1,0:T(8,128)(2,1)S(1)} %get-tuple-element.112.grad_ref), channel_id=1, source_target_pairs={{0,2},{2,0},{1,3},{3,1},{4,6},{6,4},{5,7},{7,5},{8,10},{10,8},{9,1... | collective-permute-start | bytes 1179656 | tf_op jit(solution)/shard_map/ppermute | solution.py:451
  20.6 18.1 %collective-permute-start.10 = (bf16[384,512]{1,0:T(8,128)(2,1)S(1)}, bf16[384,512]{1,0:T(8,128)(2,1)S(1)}, u32[]{:S(2)}, u32[]{:S(2)}) collective-permute-start(bf16[384,512]{1,0:T(8,128)(2,1)S(1)} %turn.3), channel_id=1, source_target_pairs={{0,2},{2,0},{1,3},{3,1},{4,6},{6,4},{5,7},{7,5},{8,10},{10,8},{9,1... | collective-permute-start | bytes 1179656 | tf_op jit(solution)/shard_map/ppermute | solution.py:451
  21.6 1.8 %collective-permute-start.6 = (bf16[512,384]{1,0:T(8,128)(2,1)S(1)}, bf16[512,384]{1,0:T(8,128)(2,1)S(1)}, u32[]{:S(2)}, u32[]{:S(2)}) collective-permute-start(bf16[512,384]{1,0:T(8,128)(2,1)S(1)} %get-tuple-element.114), channel_id=1, source_target_pairs={{0,1},{1,0},{2,3},{3,2},{4,5},{5,4},{6,7},{7,6},{8,9},{9,8},{10,11... | collective-permute-start | bytes 1179656 | tf_op jit(solution)/shard_map/ppermute | solution.py:451
  22.5 2.6 %collective-permute-start.8 = (bf16[192,512]{1,0:T(8,128)(2,1)S(1)}, bf16[192,512]{1,0:T(8,128)(2,1)S(1)}, u32[]{:S(2)}, u32[]{:S(2)}) collective-permute-start(bf16[192,512]{1,0:T(8,128)(2,1)S(1)} %collective-permute-done.7.across_ref), channel_id=1, source_target_pairs={{0,1},{1,0},{2,3},{3,2},{4,5},{5,4},{6,7},{7,6},{8,9},{9,8},{10,11... | collective-permute-start | bytes 589832 | tf_op jit(solution)/shard_map/ppermute | solution.py:451
  26.5 19.6 %collective-permute-start.13 = (bf16[192,1152]{1,0:T(8,128)(2,1)S(1)}, bf16[192,1152]{1,0:T(8,128)(2,1)S(1)}, u32[]{:S(2)}, u32[]{:S(2)}) collective-permute-start(bf16[192,1152]{1,0:T(8,128)(2,1)S(1)} %get-tuple-element.135), channel_id=1, source_target_pairs={{0,4},{4,0},{8,12},{12,8},{1,5},{5,1},{9,13},{13,9},{2,6},{6,2},{1... | collective-permute-start | bytes 1327112 | tf_op jit(solution)/shard_map/ppermute | solution.py:451
  29.3 1.8 %collective-permute-start.9 = (bf16[512,384]{1,0:T(8,128)(2,1)S(1)}, bf16[512,384]{1,0:T(8,128)(2,1)S(1)}, u32[]{:S(2)}, u32[]{:S(2)}) collective-permute-start(bf16[512,384]{1,0:T(8,128)(2,1)S(1)} %get-tuple-element.122), channel_id=1, source_target_pairs={{0,1},{1,0},{2,3},{3,2},{4,5},{5,4},{6,7},{7,6},{8,9},{9,8},{10,11... | collective-permute-start | bytes 1179656 | tf_op jit(solution)/shard_map/ppermute | solution.py:451
  39.5 1.8 %collective-permute-start.11 = (bf16[384,512]{1,0:T(8,128)(2,1)S(1)}, bf16[384,512]{1,0:T(8,128)(2,1)S(1)}, u32[]{:S(2)}, u32[]{:S(2)}) collective-permute-start(bf16[384,512]{1,0:T(8,128)(2,1)S(1)} %collective-permute-done.10.across_ref), channel_id=1, source_target_pairs={{0,1},{1,0},{2,3},{3,2},{4,5},{5,4},{6,7},{7,6},{8,9},{9,8},{10,11... | collective-permute-start | bytes 1179656 | tf_op jit(solution)/shard_map/ppermute | solution.py:451
  42.7 18.6 %collective-permute-start.14 = (bf16[208,1152]{1,0:T(8,128)(2,1)S(1)}, bf16[208,1152]{1,0:T(8,128)(2,1)S(1)}, u32[]{:S(2)}, u32[]{:S(2)}) collective-permute-start(bf16[208,1152]{1,0:T(8,128)(2,1)S(1)} %get-tuple-element.141), channel_id=1, source_target_pairs={{0,4},{4,0},{8,12},{12,8},{1,5},{5,1},{9,13},{13,9},{2,6},{6,2},{1... | collective-permute-start | bytes 1437704 | tf_op jit(solution)/shard_map/ppermute | solution.py:451
  44.6 11.1 %collective-permute-start.12 = (bf16[512,384]{1,0:T(8,128)(2,1)S(1)}, bf16[512,384]{1,0:T(8,128)(2,1)S(1)}, u32[]{:S(2)}, u32[]{:S(2)}) collective-permute-start(bf16[512,384]{1,0:T(8,128)(2,1)S(1)} %get-tuple-element.133.grad_ref), channel_id=1, source_target_pairs={{0,2},{2,0},{1,3},{3,1},{4,6},{6,4},{5,7},{7,5},{8,10},{10,8},{9,1... | collective-permute-start | bytes 1179656 | tf_op jit(solution)/shard_map/ppermute | solution.py:451
  46.1 17.2 %collective-permute-start.15 = (bf16[96,1152]{1,0:T(8,128)(2,1)S(1)}, bf16[96,1152]{1,0:T(8,128)(2,1)S(1)}, u32[]{:S(2)}, u32[]{:S(2)}) collective-permute-start(bf16[96,1152]{1,0:T(8,128)(2,1)S(1)} %fold.4), channel_id=1, source_target_pairs={{0,8},{4,12},{8,0},{12,4},{1,9},{5,13},{9,1},{13,5},{2,10},{6,14},... | collective-permute-start | bytes 663560 | tf_op jit(solution)/shard_map/ppermute | solution.py:451
  57.3 12.0 %collective-permute-start.16 = (bf16[96,1152]{1,0:T(8,128)(2,1)S(1)}, bf16[96,1152]{1,0:T(8,128)(2,1)S(1)}, u32[]{:S(2)}, u32[]{:S(2)}) collective-permute-start(bf16[96,1152]{1,0:T(8,128)(2,1)S(1)} %get-tuple-element.145), channel_id=1, source_target_pairs={{0,4},{4,0},{8,12},{12,8},{1,5},{5,1},{9,13},{13,9},{2,6},{6,2},{1... | collective-permute-start | bytes 663560 | tf_op jit(solution)/shard_map/ppermute | solution.py:451
  61.4 17.5 %collective-permute-start.17 = (bf16[112,1152]{1,0:T(8,128)(2,1)S(1)}, bf16[112,1152]{1,0:T(8,128)(2,1)S(1)}, u32[]{:S(2)}, u32[]{:S(2)}) collective-permute-start(bf16[112,1152]{1,0:T(8,128)(2,1)S(1)} %get-tuple-element.147), channel_id=1, source_target_pairs={{0,8},{4,12},{8,0},{12,4},{1,9},{5,13},{9,1},{13,5},{2,10},{6,14},... | collective-permute-start | bytes 774152 | tf_op jit(solution)/shard_map/ppermute | solution.py:451
  69.3 16.7 %collective-permute-start.19 = (bf16[48,1152]{1,0:T(8,128)(2,1)S(1)}, bf16[48,1152]{1,0:T(8,128)(2,1)S(1)}, u32[]{:S(2)}, u32[]{:S(2)}) collective-permute-start(bf16[48,1152]{1,0:T(8,128)(2,1)S(1)} %fold.6), channel_id=1, source_target_pairs={{0,8},{4,12},{8,0},{12,4},{1,9},{5,13},{9,1},{13,5},{2,10},{6,14},... | collective-permute-start | bytes 331784 | tf_op jit(solution)/shard_map/ppermute | solution.py:451
  69.3 11.2 %collective-permute-start.18 = (bf16[96,1152]{1,0:T(8,128)(2,1)S(1)}, bf16[96,1152]{1,0:T(8,128)(2,1)S(1)}, u32[]{:S(2)}, u32[]{:S(2)}) collective-permute-start(bf16[96,1152]{1,0:T(8,128)(2,1)S(1)} %get-tuple-element.151), channel_id=1, source_target_pairs={{0,4},{4,0},{8,12},{12,8},{1,5},{5,1},{9,13},{13,9},{2,6},{6,2},{1... | collective-permute-start | bytes 663560 | tf_op jit(solution)/shard_map/ppermute | solution.py:451
  80.6 16.7 %collective-permute-start.22 = (bf16[48,1152]{1,0:T(8,128)(2,1)S(1)}, bf16[48,1152]{1,0:T(8,128)(2,1)S(1)}, u32[]{:S(2)}, u32[]{:S(2)}) collective-permute-start(bf16[48,1152]{1,0:T(8,128)(2,1)S(1)} %fold.7), channel_id=1, source_target_pairs={{0,8},{4,12},{8,0},{12,4},{1,9},{5,13},{9,1},{13,5},{2,10},{6,14},... | collective-permute-start | bytes 331784 | tf_op jit(solution)/shard_map/ppermute | solution.py:451
  83.3 8.3 %collective-permute-start.20 = (bf16[96,1152]{1,0:T(8,128)(2,1)S(1)}, bf16[96,1152]{1,0:T(8,128)(2,1)S(1)}, u32[]{:S(2)}, u32[]{:S(2)}) collective-permute-start(bf16[96,1152]{1,0:T(8,128)(2,1)S(1)} %total.4.refs_1_), channel_id=1, source_target_pairs={{0,2},{2,0},{1,3},{3,1},{4,6},{6,4},{5,7},{7,5},{8,10},{10,8},{9,1... | collective-permute-start | bytes 663560 | tf_op jit(solution)/shard_map/ppermute | solution.py:451
  86.0 9.5 %collective-permute-start.21 = (bf16[112,1152]{1,0:T(8,128)(2,1)S(1)}, bf16[112,1152]{1,0:T(8,128)(2,1)S(1)}, u32[]{:S(2)}, u32[]{:S(2)}) collective-permute-start(bf16[112,1152]{1,0:T(8,128)(2,1)S(1)} %get-tuple-element.155.refs_3_), channel_id=1, source_target_pairs={{0,2},{2,0},{1,3},{3,1},{4,6},{6,4},{5,7},{7,5},{8,10},{10,8},{9,1... | collective-permute-start | bytes 774152 | tf_op jit(solution)/shard_map/ppermute | solution.py:451
  86.1 13.0 %collective-permute-start.23 = (bf16[48,1152]{1,0:T(8,128)(2,1)S(1)}, bf16[48,1152]{1,0:T(8,128)(2,1)S(1)}, u32[]{:S(2)}, u32[]{:S(2)}) collective-permute-start(bf16[48,1152]{1,0:T(8,128)(2,1)S(1)} %total.6.refs_1_), channel_id=1, source_target_pairs={{0,2},{2,0},{1,3},{3,1},{4,6},{6,4},{5,7},{7,5},{8,10},{10,8},{9,1... | collective-permute-start | bytes 331784 | tf_op jit(solution)/shard_map/ppermute | solution.py:451
  97.4 4.8 %collective-permute-start.24 = (bf16[48,1152]{1,0:T(8,128)(2,1)S(1)}, bf16[48,1152]{1,0:T(8,128)(2,1)S(1)}, u32[]{:S(2)}, u32[]{:S(2)}) collective-permute-start(bf16[48,1152]{1,0:T(8,128)(2,1)S(1)} %total.7.refs_3_), channel_id=1, source_target_pairs={{0,2},{2,0},{1,3},{3,1},{4,6},{6,4},{5,7},{7,5},{8,10},{10,8},{9,1... | collective-permute-start | bytes 331784 | tf_op jit(solution)/shard_map/ppermute | solution.py:451

commit v11 on v9

--- a/solution.py
+++ b/solution.py
@@ -280,6 +280,15 @@
     return [turned_ref[pl.ds(local * 2 * size + begin, size), :] for local in range(2)]
 
 
+def turn_whole_kernel(own_ref, partner_ref, out_ref, turned_ref):
+    size = own_ref.shape[1] // 4
+    chan = lax.axis_index("chan")
+    for ref, side in ((own_ref, chan), (partner_ref, 1 - chan)):
+        turned_ref[...] = ref[...].T
+        for local, piece in enumerate(pick_parts(turned_ref, 1 - lax.axis_index("replica"), size)):
+            out_ref[pl.ds(pl.multiple_of((2 * side + local) * size, size), size), :] = piece
+
+
 def turn_kernel(*refs):
     snakes, out_ref, turned_ref = refs[:-2], refs[-2], refs[-1]
     size = snakes[0].shape[1] // 4
@@ -325,7 +334,10 @@
     outs, turned_ref = rest[:-1], rest[-1]
     half = own_ref.shape[0]
     chan = lax.axis_index("chan")
-    for ref, side in ((across_ref, chan), (across_other_ref, 1 - chan)):
+    whole = across_ref.shape[0] == half
+    sources = ((across_ref, 0, 0), (across_ref, 1, half // 2)) if whole else (
+        (across_ref, chan, 0), (across_other_ref, 1 - chan, 0))
+    for ref, side, low in sources:
         place_rows(pieces, ref[low : low + half // 2, :], side, turned_ref, slice(None))
     for tap in range(3):
         span = slice(tap * half, (tap + 1) * half)
@@ -554,6 +566,14 @@
             for index, layer in enumerate(chosen):
                 across[layer] = (moved_rows, index * half // 2)
 
+    def turn_whole(layer):
+        if fast:
+            across_other[layer] = across_replica(sequence.call(
+                turn_whole_kernel, "turn_whole", [0, 0], struct((half, rows), BF16),
+                [pltpu.VMEM((half, rows), BF16)], 10 * rows * half, mine[layer], partners[layer],
+            ))
+            across[layer] = (across_other[layer], 0)
+
     def share(*chosen):
         if fast:
             shared = across_chan(sequence.hold(across[chosen[0]][0]))
@@ -715,18 +735,17 @@
     far_rows(1)
     own_rows(0)
     share(1)
+    turn_whole(0)
+    send_gradient(0)
     forward_own(2)
     residual_out = forward_partner(2)
     sequence.weight = 0.01
     weights(1)
-    turn(0)
-    send_gradient(0)
     fold(2)
-    share(0)
     far_rows(0)
     sequence.weight = 0.01
     weights(0)
-    sequence.weight = 10
+    sequence.weight = 3
     fold(1)
     total(2)
     cross(2)

time: 97.6 us -> 93.4 us (0.957)
  waiting for transfers between devices: 41.7 us -> 39.3 us
  starting transfers between devices: 23.7 us -> 21.7 us
    ppermute x24 -> x23, waiting for transfers between devices: 41.7 us -> 39.3 us  [swap(): lax.ppermute(x, axis, [(i, other(i)) for i in range(lax.axis_size(axis))])]
    ppermute x24 -> x23, starting transfers between devices: 23.7 us -> 21.7 us  [swap(): lax.ppermute(x, axis, [(i, other(i)) for i in range(lax.axis_size(axis))])]
  transfers between devices with their start and end apart: 24 -> 23, of which waited for: 9 -> 7; matrix products, arithmetic and copies ran while one was open for 0% -> 0% of each run, Pallas kernels for 28% -> 30%
where the time goes in v11:
time: 93.4 us; the launch traced here: 93.2 us
  waiting for transfers between devices  39.3 us (42%)
  Pallas kernels  31.1 us (33%)
  starting transfers between devices  21.7 us (23%)
  between operations  1.1 us (1%)
    ppermute x23, waiting for transfers between devices, swap(): lax.ppermute(x, axis, [(i, other(i)) for i in range(lax.axis_size(axis))])  39.3 us
    pallas_call x36, Pallas kernels, call(): pl.pallas_call(kernel, in_specs=[ANY_HBM if i else IN_VMEM for i in ins],...  31.1 us
    ppermute x23, starting transfers between devices, swap(): lax.ppermute(x, axis, [(i, other(i)) for i in range(lax.axis_size(axis))])  21.7 us
  transfers between devices with their start and end apart: 23, of which 7 were waited for; matrix products, arithmetic and copies ran while one was open for 0% of the time, Pallas kernels for 30%

profile of v11, /device:TPU:0, one launch (start us, length us, event | category | flops | bytes accessed | tf_op | source)
XLA Modules:
  0.0 93.2 jit_solution(2159457835148161021)
XLA Ops:
  0.6 2.5 %prep.1 = (f32[512,384]{1,0:T(8,128)S(1)}, bf16[512,384]{1,0:T(8,128)(2,1)S(1)}, bf16[512,384]{1,0:T(8,128)(2,1)S(1)}, f32[512,128]{1,0:T(8,128)S(1)}, f32[3,384...) custom-call(s32[16]{0:T(128)} %len_hbm.1, s32[16]{0:T(128)} %own_hbm.1, s32[16]{0:T(128)} %start_hbm.1, ...), custom_call_target="tpu_custom_call" | custom-call | flops 78643200 | bytes 44003200 | tf_op jit(solution)/shard_map/prep/pallas_call | solution.py:447
  3.7 1.6 %forward_own.3 = (f32[512,384]{1,0:T(8,128)S(1)}, bf16[2,1152,384]{2,1,0:T(8,128)(2,1)S(1)}) custom-call(bf16[512,384]{1,0:T(8,128)(2,1)S(1)} %get-tuple-element.121.snake_ref.own_ref, bf16[2,1152,384]{2,1,0:T(8,128)(2,1)S(1)} %get-tuple-element.80.weight_ref, bf16[3,3,768,384]{3,2,1,0:T(8,128)(2,1)} %rest_1_.1), custom_call_target="tpu_custom_call" | custom-call | flops 4529848320 | bytes 47185920 | tf_op jit(solution)/shard_map/forward_own/pallas_call | solution.py:447
  5.3 2.6 %collective-permute-start.5 = (bf16[512,384]{1,0:T(8,128)(2,1)S(1)}, bf16[512,384]{1,0:T(8,128)(2,1)S(1)}, u32[]{:S(2)}, u32[]{:S(2)}) collective-permute-start(bf16[512,384]{1,0:T(8,128)(2,1)S(1)} %get-tuple-element.103.grad_ref.rest_0_), channel_id=1, source_target_pairs={{0,2},{2,0},{1,3},{3,1},{4,6},{6,4},{5,7},{7,5},{8,10},{10,8},{9,1... | collective-permute-start | bytes 1179656 | tf_op jit(solution)/shard_map/ppermute | solution.py:463
  7.9 2.3 %forward_partner.3 = (f32[512,384]{1,0:T(8,128)S(1)}, bf16[512,384]{1,0:T(8,128)(2,1)S(1)}, bf16[2,1152,384]{2,1,0:T(8,128)(2,1)S(1)}) custom-call(bf16[512,384]{1,0:T(8,128)(2,1)S(1)} %collective-permute-done.snake_ref.partner_ref, bf16[2,1152,384]{2,1,0:T(8,128)(2,1)S(1)} %get-tuple-element.80.weight_ref, f32[512,384]{1,0:T(8,128)S(1)} %get-tuple-element.84.own_ref, ...), custom_call_target="tpu_custom_call" | custom-call | flops 4529848320 | bytes 69514240 | tf_op jit(solution)/shard_map/forward_partner/pallas_call | solution.py:447
  10.5 0.9 back_partner.3
  12.6 1.7 %forward_partner.4 = (f32[512,384]{1,0:T(8,128)S(1)}, bf16[512,384]{1,0:T(8,128)(2,1)S(1)}) custom-call(bf16[512,384]{1,0:T(8,128)(2,1)S(1)} %collective-permute-done.1.snake_ref.partner_ref, bf16[2,1152,384]{2,1,0:T(8,128)(2,1)S(1)} %get-tuple-element.90.weight_ref, f32[512,384]{1,0:T(8,128)S(1)} %forward_own.4.own_ref, ...), custom_call_target="tpu_custom_call" | custom-call | flops 4529848320 | bytes 51819520 | tf_op jit(solution)/shard_map/forward_partner/pallas_call | solution.py:447
  16.0 1.6 %combine.3 = (f32[1,384]{1,0:T(1,128)S(1)}, f32[512,384]{1,0:T(8,128)S(1)}, bf16[512,384]{1,0:T(8,128)(2,1)S(1)}) custom-call(f32[512,384]{1,0:T(8,128)S(1)} %back_own.3.own_ref, bf16[512,384]{1,0:T(8,128)(2,1)S(1)} %collective-permute-done.3.partner_ref, f32[512,384]{1,0:T(8,128)S(1)} %get-tuple-element.100.stream_ref.old_ref, ...), custom_call_target="tpu_custom_call" | custom-call | flops 117964800 | bytes 38072320 | tf_op jit(solution)/shard_map/combine/pallas_call | solution.py:447
  17.7 2.1 %collective-permute-start.4 = (bf16[512,384]{1,0:T(8,128)(2,1)S(1)}, bf16[512,384]{1,0:T(8,128)(2,1)S(1)}, u32[]{:S(2)}, u32[]{:S(2)}) collective-permute-start(bf16[512,384]{1,0:T(8,128)(2,1)S(1)} %get-tuple-element.107.grad_ref), channel_id=1, source_target_pairs={{0,2},{2,0},{1,3},{3,1},{4,6},{6,4},{5,7},{7,5},{8,10},{10,8},{9,1... | collective-permute-start | bytes 1179656 | tf_op jit(solution)/shard_map/ppermute | solution.py:463
  20.6 0.9 back_partner.4
  21.6 1.0 %collective-permute-done.7.across_ref = bf16[192,512]{1,0:T(8,128)(2,1)S(1)} collective-permute-done((bf16[192,512]{1,0:T(8,128)(2,1)S(1)}, bf16[192,512]{1,0:T(8,128)(2,1)S(1)}, u32[]{:S(2)}, u32[]{:S(2)}) %collective-permute-start.7) | collective-permute-done | bytes 196640 | tf_op jit(solution)/shard_map/ppermute | solution.py:463
  22.6 0.9 back_own.4.own_ref
  23.5 1.7 %combine.4 = (f32[1,384]{1,0:T(1,128)S(1)}, bf16[512,384]{1,0:T(8,128)(2,1)S(1)}) custom-call(f32[512,384]{1,0:T(8,128)S(1)} %back_own.4.own_ref, bf16[512,384]{1,0:T(8,128)(2,1)S(1)} %collective-permute-done.6.partner_ref, f32[512,384]{1,0:T(8,128)S(1)} %get-tuple-element.95.old_ref.stream_ref, f32[3,384]{1,0:T(4,128)S(1)} %get-tuple-element.87.rest_0_.alphas_ref, ...), custom_call_target="tpu_custom_call" | custom-call | flops 117964800 | bytes 34140160 | tf_op jit(solution)/shard_map/combine/pallas_call | solution.py:447
  25.2 1.4 %paired_weight.3 = (bf16[192,1152]{1,0:T(8,128)(2,1)S(1)}, bf16[192,1152]{1,0:T(8,128)(2,1)S(1)}) custom-call(bf16[384,512]{1,0:T(8,128)(2,1)S(1)} %own_rows.3.own_ref, bf16[512,1152]{1,0:T(8,128)(2,1)S(1)} %get-tuple-element.99.shifted_ref, bf16[192,512]{1,0:T(8,128)(2,1)S(1)} %collective-permute-done.7.across_ref, ...), custom_call_target="tpu_custom_call" | custom-call | flops 9059696640 | bytes 40304640 | tf_op jit(solution)/shard_map/paired_weight/pallas_call | solution.py:447
  26.6 1.7 %collective-permute-start.13 = (bf16[192,1152]{1,0:T(8,128)(2,1)S(1)}, bf16[192,1152]{1,0:T(8,128)(2,1)S(1)}, u32[]{:S(2)}, u32[]{:S(2)}) collective-permute-start(bf16[192,1152]{1,0:T(8,128)(2,1)S(1)} %get-tuple-element.131), channel_id=1, source_target_pairs={{0,4},{4,0},{8,12},{12,8},{1,5},{5,1},{9,13},{13,9},{2,6},{6,2},{1... | collective-permute-start | bytes 1327112 | tf_op jit(solution)/shard_map/ppermute | solution.py:463
  28.3 0.9 back_partner.5
  31.0 1.4 %combine.5.rest_0_ = f32[1,384]{1,0:T(1,128)S(1)} custom-call(f32[512,384]{1,0:T(8,128)S(1)} %back_own.5.own_ref, bf16[512,384]{1,0:T(8,128)(2,1)S(1)} %collective-permute-done.9.partner_ref, f32[512,384]{1,0:T(8,128)S(1)} %get-tuple-element.85.old_ref.stream_ref, f32[3,384]{1,0:T(4,128)S(1)} %get-tuple-element.87.rest_0_.alphas_ref), custom_call_target="tpu_custom_call" | custom-call | flops 117964800 | bytes 19722240 | tf_op jit(solution)/shard_map/combine/pallas_call | solution.py:447
  33.5 1.9 %collective-permute-start.14 = (bf16[384,512]{1,0:T(8,128)(2,1)S(1)}, bf16[384,512]{1,0:T(8,128)(2,1)S(1)}, u32[]{:S(2)}, u32[]{:S(2)}) collective-permute-start(bf16[384,512]{1,0:T(8,128)(2,1)S(1)} %turn_whole.1), channel_id=1, source_target_pairs={{0,2},{2,0},{1,3},{3,1},{4,6},{6,4},{5,7},{7,5},{8,10},{10,8},{9,1... | collective-permute-start | bytes 1179656 | tf_op jit(solution)/shard_map/ppermute | solution.py:463
  36.2 1.0 %collective-permute-start.12 = (bf16[512,384]{1,0:T(8,128)(2,1)S(1)}, bf16[512,384]{1,0:T(8,128)(2,1)S(1)}, u32[]{:S(2)}, u32[]{:S(2)}) collective-permute-start(bf16[512,384]{1,0:T(8,128)(2,1)S(1)} %get-tuple-element.129.grad_ref), channel_id=1, source_target_pairs={{0,2},{2,0},{1,3},{3,1},{4,6},{6,4},{5,7},{7,5},{8,10},{10,8},{9,1... | collective-permute-start | bytes 1179656 | tf_op jit(solution)/shard_map/ppermute | solution.py:463
  37.1 1.6 %forward_partner.5 = bf16[512,384]{1,0:T(8,128)(2,1)} custom-call(bf16[512,384]{1,0:T(8,128)(2,1)S(1)} %collective-permute-done.2.partner_ref.snake_ref, bf16[2,1152,384]{2,1,0:T(8,128)(2,1)S(1)} %get-tuple-element.82.weight_ref, f32[512,384]{1,0:T(8,128)S(1)} %forward_own.5.own_ref, f32[512,384]{1,0:T(8,128)S(1)} %get-tuple-element.100.stream_ref.old_ref, ...), custom_call_target="tpu_custom_call" | custom-call | flops 4529848320 | bytes 43909120 | tf_op jit(solution)/shard_map/forward_partner/pallas_call | solution.py:447
  38.7 1.4 %paired_weight.4 = (bf16[208,1152]{1,0:T(8,128)(2,1)S(1)}, bf16[192,1152]{1,0:T(8,128)(2,1)S(1)}) custom-call(bf16[384,512]{1,0:T(8,128)(2,1)S(1)} %own_rows.4.own_ref, bf16[512,1152]{1,0:T(8,128)(2,1)S(1)} %get-tuple-element.108.shifted_ref, bf16[192,512]{1,0:T(8,128)(2,1)S(1)} %collective-permute-done.10.across_ref, ...), custom_call_target="tpu_custom_call" | custom-call | flops 9059696 | bytes 40719 | tf_op jit(solution)/shard_map/paired_weight/pallas_call | solution.py:447
  40.1 1.6 %collective-permute-start.15 = (bf16[208,1152]{1,0:T(8,128)(2,1)S(1)}, bf16[208,1152]{1,0:T(8,128)(2,1)S(1)}, u32[]{:S(2)}, u32[]{:S(2)}) collective-permute-start(bf16[208,1152]{1,0:T(8,128)(2,1)S(1)} %get-tuple-element.136), channel_id=1, source_target_pairs={{0,4},{4,0},{8,12},{12,8},{1,5},{5,1},{9,13},{13,9},{2,6},{6,2},{1... | collective-permute-start | bytes 1437704 | tf_op jit(solution)/shard_map/ppermute | solution.py:463
  41.8 2.7 %collective-permute-start.16 = (bf16[96,1152]{1,0:T(8,128)(2,1)S(1)}, bf16[96,1152]{1,0:T(8,128)(2,1)S(1)}, u32[]{:S(2)}, u32[]{:S(2)}) collective-permute-start(bf16[96,1152]{1,0:T(8,128)(2,1)S(1)} %fold.3), channel_id=1, source_target_pairs={{0,8},{4,12},{8,0},{12,4},{1,9},{5,13},{9,1},{13,5},{2,10},{6,14},... | collective-permute-start | bytes 663560 | tf_op jit(solution)/shard_map/ppermute | solution.py:463
  44.5 8.7 %collective-permute-done.12.grad_ref = bf16[512,384]{1,0:T(8,128)(2,1)S(1)} collective-permute-done((bf16[512,384]{1,0:T(8,128)(2,1)S(1)}, bf16[512,384]{1,0:T(8,128)(2,1)S(1)}, u32[]{:S(2)}, u32[]{:S(2)}) %collective-permute-start.12) | collective-permute-done | bytes 393248 | tf_op jit(solution)/shard_map/ppermute | solution.py:463
  53.5 1.4 %paired_weight.5 = (bf16[192,1152]{1,0:T(8,128)(2,1)S(1)}, bf16[192,1152]{1,0:T(8,128)(2,1)S(1)}) custom-call(bf16[384,512]{1,0:T(8,128)(2,1)S(1)} %own_rows.5.own_ref, bf16[512,1152]{1,0:T(8,128)(2,1)S(1)} %get-tuple-element.116.shifted_ref, bf16[384,512]{1,0:T(8,128)(2,1)S(1)} %collective-permute-done.14.across_ref.across_other_ref, ...), custom_call_target="tpu_custom_call" | custom-call | flops 9059696 | bytes 44236 | tf_op jit(solution)/shard_map/paired_weight/pallas_call | solution.py:447
  55.3 3.4 %collective-permute-done.15.got = bf16[208,1152]{1,0:T(8,128)(2,1)S(1)} collective-permute-done((bf16[208,1152]{1,0:T(8,128)(2,1)S(1)}, bf16[208,1152]{1,0:T(8,128)(2,1)S(1)}, u32[]{:S(2)}, u32[]{:S(2)}) %collective-permute-start.15) | collective-permute-done | bytes 479264 | tf_op jit(solution)/shard_map/ppermute | solution.py:463
  58.8 1.8 %collective-permute-start.18 = (bf16[112,1152]{1,0:T(8,128)(2,1)S(1)}, bf16[112,1152]{1,0:T(8,128)(2,1)S(1)}, u32[]{:S(2)}, u32[]{:S(2)}) collective-permute-start(bf16[112,1152]{1,0:T(8,128)(2,1)S(1)} %get-tuple-element.142), channel_id=1, source_target_pairs={{0,8},{4,12},{8,0},{12,4},{1,9},{5,13},{9,1},{13,5},{2,10},{6,14},... | collective-permute-start | bytes 774152 | tf_op jit(solution)/shard_map/ppermute | solution.py:463
  61.2 11.8 %collective-permute-done.17.got = bf16[192,1152]{1,0:T(8,128)(2,1)S(1)} collective-permute-done((bf16[192,1152]{1,0:T(8,128)(2,1)S(1)}, bf16[192,1152]{1,0:T(8,128)(2,1)S(1)}, u32[]{:S(2)}, u32[]{:S(2)}) %collective-permute-start.17) | collective-permute-done | bytes 442400 | tf_op jit(solution)/shard_map/ppermute | solution.py:463
  73.1 1.7 %collective-permute-start.19 = (bf16[96,1152]{1,0:T(8,128)(2,1)S(1)}, bf16[96,1152]{1,0:T(8,128)(2,1)S(1)}, u32[]{:S(2)}, u32[]{:S(2)}) collective-permute-start(bf16[96,1152]{1,0:T(8,128)(2,1)S(1)} %fold.5), channel_id=1, source_target_pairs={{0,8},{4,12},{8,0},{12,4},{1,9},{5,13},{9,1},{13,5},{2,10},{6,14},... | collective-permute-start | bytes 663560 | tf_op jit(solution)/shard_map/ppermute | solution.py:463
  75.6 10.0 %collective-permute-done.19.late = bf16[96,1152]{1,0:T(8,128)(2,1)S(1)} collective-permute-done((bf16[96,1152]{1,0:T(8,128)(2,1)S(1)}, bf16[96,1152]{1,0:T(8,128)(2,1)S(1)}, u32[]{:S(2)}, u32[]{:S(2)}) %collective-permute-start.19) | collective-permute-done | bytes 221216 | tf_op jit(solution)/shard_map/ppermute | solution.py:463
  86.4 1.9 %finish.2 = (f32[3,3,192,384]{3,2,1,0:T(8,128)}, f32[3,384]{1,0:T(4,128)}) custom-call(f32[1,1152]{1,0:T(1,128)S(1)} %get-tuple-element.145.refs_0_, bf16[96,1152]{1,0:T(8,128)(2,1)S(1)} %total.3.refs_1_, bf16[96,1152]{1,0:T(8,128)(2,1)S(1)} %collective-permute-done.20.refs_2_, bf16[112,1152]{1,0:T(8,128)(2,1)S(1)} %get-tuple-element.147.refs_3_, ...), custom_call_target="tpu_custom_call" | custom-call | flops 1990656 | bytes 10865664 | tf_op jit(solution)/shard_map/finish/pallas_call | solution.py:447
  88.3 3.7 %collective-permute-done.22.refs_2_ = bf16[96,1152]{1,0:T(8,128)(2,1)S(1)} collective-permute-done((bf16[96,1152]{1,0:T(8,128)(2,1)S(1)}, bf16[96,1152]{1,0:T(8,128)(2,1)S(1)}, u32[]{:S(2)}, u32[]{:S(2)}) %collective-permute-start.22) | collective-permute-done | bytes 221216 | tf_op jit(solution)/shard_map/ppermute | solution.py:463
  92.0 1.0 %finish.3 = f32[3,3,192,384]{3,2,1,0:T(8,128)} custom-call(f32[3,3,192,384]{3,2,1,0:T(8,128)} %get-tuple-element.148.refs_0_, bf16[96,1152]{1,0:T(8,128)(2,1)S(1)} %total.5.refs_1_, bf16[96,1152]{1,0:T(8,128)(2,1)S(1)} %collective-permute-done.22.refs_2_), custom_call_target="tpu_custom_call", output_to_operand_aliasing={{}: (0, {})} | custom-call | flops 1990656 | bytes 17252352 | tf_op jit(solution)/shard_map/finish/pallas_call | solution.py:447
  (50 shorter events, 11.4 us)
Async XLA Ops:
  3.2 4.7 %collective-permute-start = (bf16[512,384]{1,0:T(8,128)(2,1)S(1)}, bf16[512,384]{1,0:T(8,128)(2,1)S(1)}, u32[]{:S(2)}, u32[]{:S(2)}) collective-permute-start(bf16[512,384]{1,0:T(8,128)(2,1)S(1)} %get-tuple-element.121.snake_ref.own_ref), channel_id=1, source_target_pairs={{0,1},{1,0},{2,3},{3,2},{4,5},{5,4},{6,7},{7,6},{8,9},{9,8},{10,11... | collective-permute-start | bytes 1179656 | tf_op jit(solution)/shard_map/ppermute | solution.py:463
  5.3 12.3 %collective-permute-start.5 = (bf16[512,384]{1,0:T(8,128)(2,1)S(1)}, bf16[512,384]{1,0:T(8,128)(2,1)S(1)}, u32[]{:S(2)}, u32[]{:S(2)}) collective-permute-start(bf16[512,384]{1,0:T(8,128)(2,1)S(1)} %get-tuple-element.103.grad_ref.rest_0_), channel_id=1, source_target_pairs={{0,2},{2,0},{1,3},{3,1},{4,6},{6,4},{5,7},{7,5},{8,10},{10,8},{9,1... | collective-permute-start | bytes 1179656 | tf_op jit(solution)/shard_map/ppermute | solution.py:463
  10.2 2.4 %collective-permute-start.1 = (bf16[512,384]{1,0:T(8,128)(2,1)S(1)}, bf16[512,384]{1,0:T(8,128)(2,1)S(1)}, u32[]{:S(2)}, u32[]{:S(2)}) collective-permute-start(bf16[512,384]{1,0:T(8,128)(2,1)S(1)} %get-tuple-element.118.snake_ref.refs_0_.own_ref), channel_id=1, source_target_pairs={{0,1},{1,0},{2,3},{3,2},{4,5},{5,4},{6,7},{7,6},{8,9},{9,8},{10,11... | collective-permute-start | bytes 1179656 | tf_op jit(solution)/shard_map/ppermute | solution.py:463
  11.4 4.6 %collective-permute-start.3 = (bf16[512,384]{1,0:T(8,128)(2,1)S(1)}, bf16[512,384]{1,0:T(8,128)(2,1)S(1)}, u32[]{:S(2)}, u32[]{:S(2)}) collective-permute-start(bf16[512,384]{1,0:T(8,128)(2,1)S(1)} %get-tuple-element.92), channel_id=1, source_target_pairs={{0,1},{1,0},{2,3},{3,2},{4,5},{5,4},{6,7},{7,6},{8,9},{9,8},{10,11... | collective-permute-start | bytes 1179656 | tf_op jit(solution)/shard_map/ppermute | solution.py:463
  14.3 5.7 %collective-permute-start.2 = (bf16[512,384]{1,0:T(8,128)(2,1)S(1)}, bf16[512,384]{1,0:T(8,128)(2,1)S(1)}, u32[]{:S(2)}, u32[]{:S(2)}) collective-permute-start(bf16[512,384]{1,0:T(8,128)(2,1)S(1)} %get-tuple-element.122.refs_0_.own_ref.snake_ref), channel_id=1, source_target_pairs={{0,1},{1,0},{2,3},{3,2},{4,5},{5,4},{6,7},{7,6},{8,9},{9,8},{10,11... | collective-permute-start | bytes 1179656 | tf_op jit(solution)/shard_map/ppermute | solution.py:463
  14.8 7.8 %collective-permute-start.7 = (bf16[192,512]{1,0:T(8,128)(2,1)S(1)}, bf16[192,512]{1,0:T(8,128)(2,1)S(1)}, u32[]{:S(2)}, u32[]{:S(2)}) collective-permute-start(bf16[192,512]{1,0:T(8,128)(2,1)S(1)} %turn.2), channel_id=1, source_target_pairs={{0,2},{2,0},{1,3},{3,1},{4,6},{6,4},{5,7},{7,5},{8,10},{10,8},{9,1... | collective-permute-start | bytes 589832 | tf_op jit(solution)/shard_map/ppermute | solution.py:463
  17.7 15.0 %collective-permute-start.4 = (bf16[512,384]{1,0:T(8,128)(2,1)S(1)}, bf16[512,384]{1,0:T(8,128)(2,1)S(1)}, u32[]{:S(2)}, u32[]{:S(2)}) collective-permute-start(bf16[512,384]{1,0:T(8,128)(2,1)S(1)} %get-tuple-element.107.grad_ref), channel_id=1, source_target_pairs={{0,2},{2,0},{1,3},{3,1},{4,6},{6,4},{5,7},{7,5},{8,10},{10,8},{9,1... | collective-permute-start | bytes 1179656 | tf_op jit(solution)/shard_map/ppermute | solution.py:463
  20.5 14.9 %collective-permute-start.10 = (bf16[192,512]{1,0:T(8,128)(2,1)S(1)}, bf16[192,512]{1,0:T(8,128)(2,1)S(1)}, u32[]{:S(2)}, u32[]{:S(2)}) collective-permute-start(bf16[192,512]{1,0:T(8,128)(2,1)S(1)} %turn.3), channel_id=1, source_target_pairs={{0,2},{2,0},{1,3},{3,1},{4,6},{6,4},{5,7},{7,5},{8,10},{10,8},{9,1... | collective-permute-start | bytes 589832 | tf_op jit(solution)/shard_map/ppermute | solution.py:463
  21.5 2.0 %collective-permute-start.6 = (bf16[512,384]{1,0:T(8,128)(2,1)S(1)}, bf16[512,384]{1,0:T(8,128)(2,1)S(1)}, u32[]{:S(2)}, u32[]{:S(2)}) collective-permute-start(bf16[512,384]{1,0:T(8,128)(2,1)S(1)} %get-tuple-element.109), channel_id=1, source_target_pairs={{0,1},{1,0},{2,3},{3,2},{4,5},{5,4},{6,7},{7,6},{8,9},{9,8},{10,11... | collective-permute-start | bytes 1179656 | tf_op jit(solution)/shard_map/ppermute | solution.py:463
  22.6 2.6 %collective-permute-start.8 = (bf16[192,512]{1,0:T(8,128)(2,1)S(1)}, bf16[192,512]{1,0:T(8,128)(2,1)S(1)}, u32[]{:S(2)}, u32[]{:S(2)}) collective-permute-start(bf16[192,512]{1,0:T(8,128)(2,1)S(1)} %collective-permute-done.7.across_ref), channel_id=1, source_target_pairs={{0,1},{1,0},{2,3},{3,2},{4,5},{5,4},{6,7},{7,6},{8,9},{9,8},{10,11... | collective-permute-start | bytes 589832 | tf_op jit(solution)/shard_map/ppermute | solution.py:463
  26.6 15.1 %collective-permute-start.13 = (bf16[192,1152]{1,0:T(8,128)(2,1)S(1)}, bf16[192,1152]{1,0:T(8,128)(2,1)S(1)}, u32[]{:S(2)}, u32[]{:S(2)}) collective-permute-start(bf16[192,1152]{1,0:T(8,128)(2,1)S(1)} %get-tuple-element.131), channel_id=1, source_target_pairs={{0,4},{4,0},{8,12},{12,8},{1,5},{5,1},{9,13},{13,9},{2,6},{6,2},{1... | collective-permute-start | bytes 1327112 | tf_op jit(solution)/shard_map/ppermute | solution.py:463
  29.2 1.8 %collective-permute-start.9 = (bf16[512,384]{1,0:T(8,128)(2,1)S(1)}, bf16[512,384]{1,0:T(8,128)(2,1)S(1)}, u32[]{:S(2)}, u32[]{:S(2)}) collective-permute-start(bf16[512,384]{1,0:T(8,128)(2,1)S(1)} %get-tuple-element.117), channel_id=1, source_target_pairs={{0,1},{1,0},{2,3},{3,2},{4,5},{5,4},{6,7},{7,6},{8,9},{9,8},{10,11... | collective-permute-start | bytes 1179656 | tf_op jit(solution)/shard_map/ppermute | solution.py:463
  33.5 19.9 %collective-permute-start.14 = (bf16[384,512]{1,0:T(8,128)(2,1)S(1)}, bf16[384,512]{1,0:T(8,128)(2,1)S(1)}, u32[]{:S(2)}, u32[]{:S(2)}) collective-permute-start(bf16[384,512]{1,0:T(8,128)(2,1)S(1)} %turn_whole.1), channel_id=1, source_target_pairs={{0,2},{2,0},{1,3},{3,1},{4,6},{6,4},{5,7},{7,5},{8,10},{10,8},{9,1... | collective-permute-start | bytes 1179656 | tf_op jit(solution)/shard_map/ppermute | solution.py:463
  35.4 3.4 %collective-permute-start.11 = (bf16[192,512]{1,0:T(8,128)(2,1)S(1)}, bf16[192,512]{1,0:T(8,128)(2,1)S(1)}, u32[]{:S(2)}, u32[]{:S(2)}) collective-permute-start(bf16[192,512]{1,0:T(8,128)(2,1)S(1)} %collective-permute-done.10.across_ref), channel_id=1, source_target_pairs={{0,1},{1,0},{2,3},{3,2},{4,5},{5,4},{6,7},{7,6},{8,9},{9,8},{10,11... | collective-permute-start | bytes 589832 | tf_op jit(solution)/shard_map/ppermute | solution.py:463
  36.2 17.0 %collective-permute-start.12 = (bf16[512,384]{1,0:T(8,128)(2,1)S(1)}, bf16[512,384]{1,0:T(8,128)(2,1)S(1)}, u32[]{:S(2)}, u32[]{:S(2)}) collective-permute-start(bf16[512,384]{1,0:T(8,128)(2,1)S(1)} %get-tuple-element.129.grad_ref), channel_id=1, source_target_pairs={{0,2},{2,0},{1,3},{3,1},{4,6},{6,4},{5,7},{7,5},{8,10},{10,8},{9,1... | collective-permute-start | bytes 1179656 | tf_op jit(solution)/shard_map/ppermute | solution.py:463
  40.1 18.6 %collective-permute-start.15 = (bf16[208,1152]{1,0:T(8,128)(2,1)S(1)}, bf16[208,1152]{1,0:T(8,128)(2,1)S(1)}, u32[]{:S(2)}, u32[]{:S(2)}) collective-permute-start(bf16[208,1152]{1,0:T(8,128)(2,1)S(1)} %get-tuple-element.136), channel_id=1, source_target_pairs={{0,4},{4,0},{8,12},{12,8},{1,5},{5,1},{9,13},{13,9},{2,6},{6,2},{1... | collective-permute-start | bytes 1437704 | tf_op jit(solution)/shard_map/ppermute | solution.py:463
  41.8 18.7 %collective-permute-start.16 = (bf16[96,1152]{1,0:T(8,128)(2,1)S(1)}, bf16[96,1152]{1,0:T(8,128)(2,1)S(1)}, u32[]{:S(2)}, u32[]{:S(2)}) collective-permute-start(bf16[96,1152]{1,0:T(8,128)(2,1)S(1)} %fold.3), channel_id=1, source_target_pairs={{0,8},{4,12},{8,0},{12,4},{1,9},{5,13},{9,1},{13,5},{2,10},{6,14},... | collective-permute-start | bytes 663560 | tf_op jit(solution)/shard_map/ppermute | solution.py:463
  54.8 18.2 %collective-permute-start.17 = (bf16[192,1152]{1,0:T(8,128)(2,1)S(1)}, bf16[192,1152]{1,0:T(8,128)(2,1)S(1)}, u32[]{:S(2)}, u32[]{:S(2)}) collective-permute-start(bf16[192,1152]{1,0:T(8,128)(2,1)S(1)} %get-tuple-element.140), channel_id=1, source_target_pairs={{0,4},{4,0},{8,12},{12,8},{1,5},{5,1},{9,13},{13,9},{2,6},{6,2},{1... | collective-permute-start | bytes 1327112 | tf_op jit(solution)/shard_map/ppermute | solution.py:463
  58.8 16.0 %collective-permute-start.18 = (bf16[112,1152]{1,0:T(8,128)(2,1)S(1)}, bf16[112,1152]{1,0:T(8,128)(2,1)S(1)}, u32[]{:S(2)}, u32[]{:S(2)}) collective-permute-start(bf16[112,1152]{1,0:T(8,128)(2,1)S(1)} %get-tuple-element.142), channel_id=1, source_target_pairs={{0,8},{4,12},{8,0},{12,4},{1,9},{5,13},{9,1},{13,5},{2,10},{6,14},... | collective-permute-start | bytes 774152 | tf_op jit(solution)/shard_map/ppermute | solution.py:463
  60.6 25.8 %collective-permute-start.20 = (bf16[96,1152]{1,0:T(8,128)(2,1)S(1)}, bf16[96,1152]{1,0:T(8,128)(2,1)S(1)}, u32[]{:S(2)}, u32[]{:S(2)}) collective-permute-start(bf16[96,1152]{1,0:T(8,128)(2,1)S(1)} %total.3.refs_1_), channel_id=1, source_target_pairs={{0,2},{2,0},{1,3},{3,1},{4,6},{6,4},{5,7},{7,5},{8,10},{10,8},{9,1... | collective-permute-start | bytes 663560 | tf_op jit(solution)/shard_map/ppermute | solution.py:463
  73.1 12.5 %collective-permute-start.19 = (bf16[96,1152]{1,0:T(8,128)(2,1)S(1)}, bf16[96,1152]{1,0:T(8,128)(2,1)S(1)}, u32[]{:S(2)}, u32[]{:S(2)}) collective-permute-start(bf16[96,1152]{1,0:T(8,128)(2,1)S(1)} %fold.5), channel_id=1, source_target_pairs={{0,8},{4,12},{8,0},{12,4},{1,9},{5,13},{9,1},{13,5},{2,10},{6,14},... | collective-permute-start | bytes 663560 | tf_op jit(solution)/shard_map/ppermute | solution.py:463
  75.0 11.4 %collective-permute-start.21 = (bf16[112,1152]{1,0:T(8,128)(2,1)S(1)}, bf16[112,1152]{1,0:T(8,128)(2,1)S(1)}, u32[]{:S(2)}, u32[]{:S(2)}) collective-permute-start(bf16[112,1152]{1,0:T(8,128)(2,1)S(1)} %get-tuple-element.147.refs_3_), channel_id=1, source_target_pairs={{0,2},{2,0},{1,3},{3,1},{4,6},{6,4},{5,7},{7,5},{8,10},{10,8},{9,1... | collective-permute-start | bytes 774152 | tf_op jit(solution)/shard_map/ppermute | solution.py:463
  85.6 6.4 %collective-permute-start.22 = (bf16[96,1152]{1,0:T(8,128)(2,1)S(1)}, bf16[96,1152]{1,0:T(8,128)(2,1)S(1)}, u32[]{:S(2)}, u32[]{:S(2)}) collective-permute-start(bf16[96,1152]{1,0:T(8,128)(2,1)S(1)} %total.5.refs_1_), channel_id=1, source_target_pairs={{0,2},{2,0},{1,3},{3,1},{4,6},{6,4},{5,7},{7,5},{8,10},{10,8},{9,1... | collective-permute-start | bytes 663560 | tf_op jit(solution)/shard_map/ppermute | solution.py:463

commit v12 on v11

--- a/solution.py
+++ b/solution.py
@@ -709,8 +709,8 @@
         axis, apart = rounds.pop(0)
         arrivals.append((value, swap(value, axis, lambda place: place ^ apart)))
 
+    send_gradient(2)
     forward_own(0, load=2)
-    send_gradient(2)
     forward_partner(0, load=1)
     back_partner(2)
     forward_own(1)

time: 93.4 us -> 92.7 us (level)
  transfers between devices with their start and end apart: 23 -> 23, of which waited for: 7 -> 8; matrix products, arithmetic and copies ran while one was open for 0% -> 0% of each run, Pallas kernels for 30% -> 30%
where the time goes in v12:
time: 92.7 us; the launch traced here: 92.5 us
  waiting for transfers between devices  38.6 us (42%)
  Pallas kernels  31.1 us (34%)
  starting transfers between devices  21.8 us (24%)
  between operations  1.1 us (1%)
    ppermute x23, waiting for transfers between devices, swap(): lax.ppermute(x, axis, [(i, other(i)) for i in range(lax.axis_size(axis))])  38.6 us
    pallas_call x36, Pallas kernels, call(): pl.pallas_call(kernel, in_specs=[ANY_HBM if i else IN_VMEM for i in ins],...  31.1 us
    ppermute x23, starting transfers between devices, swap(): lax.ppermute(x, axis, [(i, other(i)) for i in range(lax.axis_size(axis))])  21.8 us
  transfers between devices with their start and end apart: 23, of which 8 were waited for; matrix products, arithmetic and copies ran while one was open for 0% of the time, Pallas kernels for 30%

profile of v12, /device:TPU:0, one launch (start us, length us, event | category | flops | bytes accessed | tf_op | source)
XLA Modules:
  0.0 92.5 jit_solution(3468624261272589212)
XLA Ops:
  0.6 2.5 %prep.1 = (f32[512,384]{1,0:T(8,128)S(1)}, bf16[512,384]{1,0:T(8,128)(2,1)S(1)}, bf16[512,384]{1,0:T(8,128)(2,1)S(1)}, f32[512,128]{1,0:T(8,128)S(1)}, f32[3,384...) custom-call(s32[16]{0:T(128)} %len_hbm.1, s32[16]{0:T(128)} %own_hbm.1, s32[16]{0:T(128)} %start_hbm.1, ...), custom_call_target="tpu_custom_call" | custom-call | flops 78643200 | bytes 44003200 | tf_op jit(solution)/shard_map/prep/pallas_call | solution.py:447
  3.2 3.0 %collective-permute-start.5 = (bf16[512,384]{1,0:T(8,128)(2,1)S(1)}, bf16[512,384]{1,0:T(8,128)(2,1)S(1)}, u32[]{:S(2)}, u32[]{:S(2)}) collective-permute-start(bf16[512,384]{1,0:T(8,128)(2,1)S(1)} %get-tuple-element.103.grad_ref.rest_0_), channel_id=1, source_target_pairs={{0,2},{2,0},{1,3},{3,1},{4,6},{6,4},{5,7},{7,5},{8,10},{10,8},{9,1... | collective-permute-start | bytes 1179656 | tf_op jit(solution)/shard_map/ppermute | solution.py:463
  6.2 1.6 %forward_own.3 = (f32[512,384]{1,0:T(8,128)S(1)}, bf16[2,1152,384]{2,1,0:T(8,128)(2,1)S(1)}) custom-call(bf16[512,384]{1,0:T(8,128)(2,1)S(1)} %get-tuple-element.121.snake_ref.own_ref, bf16[2,1152,384]{2,1,0:T(8,128)(2,1)S(1)} %get-tuple-element.80.weight_ref, bf16[3,3,768,384]{3,2,1,0:T(8,128)(2,1)} %rest_1_.1), custom_call_target="tpu_custom_call" | custom-call | flops 4529848320 | bytes 47185920 | tf_op jit(solution)/shard_map/forward_own/pallas_call | solution.py:447
  7.9 2.3 %forward_partner.3 = (f32[512,384]{1,0:T(8,128)S(1)}, bf16[512,384]{1,0:T(8,128)(2,1)S(1)}, bf16[2,1152,384]{2,1,0:T(8,128)(2,1)S(1)}) custom-call(bf16[512,384]{1,0:T(8,128)(2,1)S(1)} %collective-permute-done.snake_ref.partner_ref, bf16[2,1152,384]{2,1,0:T(8,128)(2,1)S(1)} %get-tuple-element.80.weight_ref, f32[512,384]{1,0:T(8,128)S(1)} %get-tuple-element.84.own_ref, ...), custom_call_target="tpu_custom_call" | custom-call | flops 4529848320 | bytes 69514240 | tf_op jit(solution)/shard_map/forward_partner/pallas_call | solution.py:447
  10.7 0.9 back_partner.3
  12.6 1.7 %forward_partner.4 = (f32[512,384]{1,0:T(8,128)S(1)}, bf16[512,384]{1,0:T(8,128)(2,1)S(1)}) custom-call(bf16[512,384]{1,0:T(8,128)(2,1)S(1)} %collective-permute-done.1.snake_ref.partner_ref, bf16[2,1152,384]{2,1,0:T(8,128)(2,1)S(1)} %get-tuple-element.90.weight_ref, f32[512,384]{1,0:T(8,128)S(1)} %forward_own.4.own_ref, ...), custom_call_target="tpu_custom_call" | custom-call | flops 4529848320 | bytes 51819520 | tf_op jit(solution)/shard_map/forward_partner/pallas_call | solution.py:447
  16.0 1.6 %combine.3 = (f32[1,384]{1,0:T(1,128)S(1)}, f32[512,384]{1,0:T(8,128)S(1)}, bf16[512,384]{1,0:T(8,128)(2,1)S(1)}) custom-call(f32[512,384]{1,0:T(8,128)S(1)} %back_own.3.own_ref, bf16[512,384]{1,0:T(8,128)(2,1)S(1)} %collective-permute-done.3.partner_ref, f32[512,384]{1,0:T(8,128)S(1)} %get-tuple-element.100.stream_ref.old_ref, ...), custom_call_target="tpu_custom_call" | custom-call | flops 117964800 | bytes 38072320 | tf_op jit(solution)/shard_map/combine/pallas_call | solution.py:447
  17.6 2.0 %collective-permute-start.4 = (bf16[512,384]{1,0:T(8,128)(2,1)S(1)}, bf16[512,384]{1,0:T(8,128)(2,1)S(1)}, u32[]{:S(2)}, u32[]{:S(2)}) collective-permute-start(bf16[512,384]{1,0:T(8,128)(2,1)S(1)} %get-tuple-element.107.grad_ref), channel_id=1, source_target_pairs={{0,2},{2,0},{1,3},{3,1},{4,6},{6,4},{5,7},{7,5},{8,10},{10,8},{9,1... | collective-permute-start | bytes 1179656 | tf_op jit(solution)/shard_map/ppermute | solution.py:463
  21.5 1.4 %collective-permute-done.7.across_ref = bf16[192,512]{1,0:T(8,128)(2,1)S(1)} collective-permute-done((bf16[192,512]{1,0:T(8,128)(2,1)S(1)}, bf16[192,512]{1,0:T(8,128)(2,1)S(1)}, u32[]{:S(2)}, u32[]{:S(2)}) %collective-permute-start.7) | collective-permute-done | bytes 196640 | tf_op jit(solution)/shard_map/ppermute | solution.py:463
  23.7 1.7 %combine.4 = (f32[1,384]{1,0:T(1,128)S(1)}, bf16[512,384]{1,0:T(8,128)(2,1)S(1)}) custom-call(f32[512,384]{1,0:T(8,128)S(1)} %back_own.4.own_ref, bf16[512,384]{1,0:T(8,128)(2,1)S(1)} %collective-permute-done.6.partner_ref, f32[512,384]{1,0:T(8,128)S(1)} %get-tuple-element.95.old_ref.stream_ref, f32[3,384]{1,0:T(4,128)S(1)} %get-tuple-element.87.rest_0_.alphas_ref, ...), custom_call_target="tpu_custom_call" | custom-call | flops 117964800 | bytes 34140160 | tf_op jit(solution)/shard_map/combine/pallas_call | solution.py:447
  25.5 1.4 %paired_weight.3 = (bf16[192,1152]{1,0:T(8,128)(2,1)S(1)}, bf16[192,1152]{1,0:T(8,128)(2,1)S(1)}) custom-call(bf16[384,512]{1,0:T(8,128)(2,1)S(1)} %own_rows.3.own_ref, bf16[512,1152]{1,0:T(8,128)(2,1)S(1)} %get-tuple-element.99.shifted_ref, bf16[192,512]{1,0:T(8,128)(2,1)S(1)} %collective-permute-done.7.across_ref, ...), custom_call_target="tpu_custom_call" | custom-call | flops 9059696640 | bytes 40304640 | tf_op jit(solution)/shard_map/paired_weight/pallas_call | solution.py:447
  26.9 1.6 %collective-permute-start.13 = (bf16[192,1152]{1,0:T(8,128)(2,1)S(1)}, bf16[192,1152]{1,0:T(8,128)(2,1)S(1)}, u32[]{:S(2)}, u32[]{:S(2)}) collective-permute-start(bf16[192,1152]{1,0:T(8,128)(2,1)S(1)} %get-tuple-element.131), channel_id=1, source_target_pairs={{0,4},{4,0},{8,12},{12,8},{1,5},{5,1},{9,13},{13,9},{2,6},{6,2},{1... | collective-permute-start | bytes 1327112 | tf_op jit(solution)/shard_map/ppermute | solution.py:463
  28.5 0.9 back_partner.5
  31.2 1.4 %combine.5.rest_0_ = f32[1,384]{1,0:T(1,128)S(1)} custom-call(f32[512,384]{1,0:T(8,128)S(1)} %back_own.5.own_ref, bf16[512,384]{1,0:T(8,128)(2,1)S(1)} %collective-permute-done.9.partner_ref, f32[512,384]{1,0:T(8,128)S(1)} %get-tuple-element.85.old_ref.stream_ref, f32[3,384]{1,0:T(4,128)S(1)} %get-tuple-element.87.rest_0_.alphas_ref), custom_call_target="tpu_custom_call" | custom-call | flops 117964800 | bytes 19722240 | tf_op jit(solution)/shard_map/combine/pallas_call | solution.py:447
  33.7 1.5 %collective-permute-start.14 = (bf16[384,512]{1,0:T(8,128)(2,1)S(1)}, bf16[384,512]{1,0:T(8,128)(2,1)S(1)}, u32[]{:S(2)}, u32[]{:S(2)}) collective-permute-start(bf16[384,512]{1,0:T(8,128)(2,1)S(1)} %turn_whole.1), channel_id=1, source_target_pairs={{0,2},{2,0},{1,3},{3,1},{4,6},{6,4},{5,7},{7,5},{8,10},{10,8},{9,1... | collective-permute-start | bytes 1179656 | tf_op jit(solution)/shard_map/ppermute | solution.py:463
  36.7 1.6 %forward_partner.5 = bf16[512,384]{1,0:T(8,128)(2,1)} custom-call(bf16[512,384]{1,0:T(8,128)(2,1)S(1)} %collective-permute-done.2.partner_ref.snake_ref, bf16[2,1152,384]{2,1,0:T(8,128)(2,1)S(1)} %get-tuple-element.82.weight_ref, f32[512,384]{1,0:T(8,128)S(1)} %forward_own.5.own_ref, f32[512,384]{1,0:T(8,128)S(1)} %get-tuple-element.100.stream_ref.old_ref, ...), custom_call_target="tpu_custom_call" | custom-call | flops 4529848320 | bytes 43909120 | tf_op jit(solution)/shard_map/forward_partner/pallas_call | solution.py:447
  38.3 1.4 %paired_weight.4 = (bf16[208,1152]{1,0:T(8,128)(2,1)S(1)}, bf16[192,1152]{1,0:T(8,128)(2,1)S(1)}) custom-call(bf16[384,512]{1,0:T(8,128)(2,1)S(1)} %own_rows.4.own_ref, bf16[512,1152]{1,0:T(8,128)(2,1)S(1)} %get-tuple-element.108.shifted_ref, bf16[192,512]{1,0:T(8,128)(2,1)S(1)} %collective-permute-done.10.across_ref, ...), custom_call_target="tpu_custom_call" | custom-call | flops 9059696 | bytes 40719 | tf_op jit(solution)/shard_map/paired_weight/pallas_call | solution.py:447
  39.7 0.9 collective-permute-start.15
  40.7 2.7 %collective-permute-start.16 = (bf16[96,1152]{1,0:T(8,128)(2,1)S(1)}, bf16[96,1152]{1,0:T(8,128)(2,1)S(1)}, u32[]{:S(2)}, u32[]{:S(2)}) collective-permute-start(bf16[96,1152]{1,0:T(8,128)(2,1)S(1)} %fold.3), channel_id=1, source_target_pairs={{0,8},{4,12},{8,0},{12,4},{1,9},{5,13},{9,1},{13,5},{2,10},{6,14},... | collective-permute-start | bytes 663560 | tf_op jit(solution)/shard_map/ppermute | solution.py:463
  43.3 10.1 %collective-permute-done.12.grad_ref = bf16[512,384]{1,0:T(8,128)(2,1)S(1)} collective-permute-done((bf16[512,384]{1,0:T(8,128)(2,1)S(1)}, bf16[512,384]{1,0:T(8,128)(2,1)S(1)}, u32[]{:S(2)}, u32[]{:S(2)}) %collective-permute-start.12) | collective-permute-done | bytes 393248 | tf_op jit(solution)/shard_map/ppermute | solution.py:463
  53.7 1.4 %paired_weight.5 = (bf16[192,1152]{1,0:T(8,128)(2,1)S(1)}, bf16[192,1152]{1,0:T(8,128)(2,1)S(1)}) custom-call(bf16[384,512]{1,0:T(8,128)(2,1)S(1)} %own_rows.5.own_ref, bf16[512,1152]{1,0:T(8,128)(2,1)S(1)} %get-tuple-element.116.shifted_ref, bf16[384,512]{1,0:T(8,128)(2,1)S(1)} %collective-permute-done.14.across_ref.across_other_ref, ...), custom_call_target="tpu_custom_call" | custom-call | flops 9059696 | bytes 44236 | tf_op jit(solution)/shard_map/paired_weight/pallas_call | solution.py:447
  55.6 2.3 %collective-permute-done.15.got = bf16[208,1152]{1,0:T(8,128)(2,1)S(1)} collective-permute-done((bf16[208,1152]{1,0:T(8,128)(2,1)S(1)}, bf16[208,1152]{1,0:T(8,128)(2,1)S(1)}, u32[]{:S(2)}, u32[]{:S(2)}) %collective-permute-start.15) | collective-permute-done | bytes 479264 | tf_op jit(solution)/shard_map/ppermute | solution.py:463
  58.0 1.4 %collective-permute-start.18 = (bf16[112,1152]{1,0:T(8,128)(2,1)S(1)}, bf16[112,1152]{1,0:T(8,128)(2,1)S(1)}, u32[]{:S(2)}, u32[]{:S(2)}) collective-permute-start(bf16[112,1152]{1,0:T(8,128)(2,1)S(1)} %get-tuple-element.142), channel_id=1, source_target_pairs={{0,8},{4,12},{8,0},{12,4},{1,9},{5,13},{9,1},{13,5},{2,10},{6,14},... | collective-permute-start | bytes 774152 | tf_op jit(solution)/shard_map/ppermute | solution.py:463
  59.5 1.5 %collective-permute-start.20 = (bf16[96,1152]{1,0:T(8,128)(2,1)S(1)}, bf16[96,1152]{1,0:T(8,128)(2,1)S(1)}, u32[]{:S(2)}, u32[]{:S(2)}) collective-permute-start(bf16[96,1152]{1,0:T(8,128)(2,1)S(1)} %total.3.refs_1_), channel_id=1, source_target_pairs={{0,2},{2,0},{1,3},{3,1},{4,6},{6,4},{5,7},{7,5},{8,10},{10,8},{9,1... | collective-permute-start | bytes 663560 | tf_op jit(solution)/shard_map/ppermute | solution.py:463
  61.0 11.6 %collective-permute-done.17.got = bf16[192,1152]{1,0:T(8,128)(2,1)S(1)} collective-permute-done((bf16[192,1152]{1,0:T(8,128)(2,1)S(1)}, bf16[192,1152]{1,0:T(8,128)(2,1)S(1)}, u32[]{:S(2)}, u32[]{:S(2)}) %collective-permute-start.17) | collective-permute-done | bytes 442400 | tf_op jit(solution)/shard_map/ppermute | solution.py:463
  72.7 1.0 %collective-permute-start.19 = (bf16[96,1152]{1,0:T(8,128)(2,1)S(1)}, bf16[96,1152]{1,0:T(8,128)(2,1)S(1)}, u32[]{:S(2)}, u32[]{:S(2)}) collective-permute-start(bf16[96,1152]{1,0:T(8,128)(2,1)S(1)} %fold.5), channel_id=1, source_target_pairs={{0,8},{4,12},{8,0},{12,4},{1,9},{5,13},{9,1},{13,5},{2,10},{6,14},... | collective-permute-start | bytes 663560 | tf_op jit(solution)/shard_map/ppermute | solution.py:463
  73.8 1.5 %collective-permute-start.21 = (bf16[112,1152]{1,0:T(8,128)(2,1)S(1)}, bf16[112,1152]{1,0:T(8,128)(2,1)S(1)}, u32[]{:S(2)}, u32[]{:S(2)}) collective-permute-start(bf16[112,1152]{1,0:T(8,128)(2,1)S(1)} %get-tuple-element.147.refs_3_), channel_id=1, source_target_pairs={{0,2},{2,0},{1,3},{3,1},{4,6},{6,4},{5,7},{7,5},{8,10},{10,8},{9,1... | collective-permute-start | bytes 774152 | tf_op jit(solution)/shard_map/ppermute | solution.py:463
  75.4 9.2 %collective-permute-done.19.late = bf16[96,1152]{1,0:T(8,128)(2,1)S(1)} collective-permute-done((bf16[96,1152]{1,0:T(8,128)(2,1)S(1)}, bf16[96,1152]{1,0:T(8,128)(2,1)S(1)}, u32[]{:S(2)}, u32[]{:S(2)}) %collective-permute-start.19) | collective-permute-done | bytes 221216 | tf_op jit(solution)/shard_map/ppermute | solution.py:463
  84.7 1.6 %collective-permute-start.22 = (bf16[96,1152]{1,0:T(8,128)(2,1)S(1)}, bf16[96,1152]{1,0:T(8,128)(2,1)S(1)}, u32[]{:S(2)}, u32[]{:S(2)}) collective-permute-start(bf16[96,1152]{1,0:T(8,128)(2,1)S(1)} %total.5.refs_1_), channel_id=1, source_target_pairs={{0,2},{2,0},{1,3},{3,1},{4,6},{6,4},{5,7},{7,5},{8,10},{10,8},{9,1... | collective-permute-start | bytes 663560 | tf_op jit(solution)/shard_map/ppermute | solution.py:463
  86.2 1.9 %finish.2 = (f32[3,3,192,384]{3,2,1,0:T(8,128)}, f32[3,384]{1,0:T(4,128)}) custom-call(f32[1,1152]{1,0:T(1,128)S(1)} %get-tuple-element.145.refs_0_, bf16[96,1152]{1,0:T(8,128)(2,1)S(1)} %total.3.refs_1_, bf16[96,1152]{1,0:T(8,128)(2,1)S(1)} %collective-permute-done.20.refs_2_, bf16[112,1152]{1,0:T(8,128)(2,1)S(1)} %get-tuple-element.147.refs_3_, ...), custom_call_target="tpu_custom_call" | custom-call | flops 1990656 | bytes 10865664 | tf_op jit(solution)/shard_map/finish/pallas_call | solution.py:447
  88.1 3.2 %collective-permute-done.22.refs_2_ = bf16[96,1152]{1,0:T(8,128)(2,1)S(1)} collective-permute-done((bf16[96,1152]{1,0:T(8,128)(2,1)S(1)}, bf16[96,1152]{1,0:T(8,128)(2,1)S(1)}, u32[]{:S(2)}, u32[]{:S(2)}) %collective-permute-start.22) | collective-permute-done | bytes 221216 | tf_op jit(solution)/shard_map/ppermute | solution.py:463
  91.4 1.0 %finish.3 = f32[3,3,192,384]{3,2,1,0:T(8,128)} custom-call(f32[3,3,192,384]{3,2,1,0:T(8,128)} %get-tuple-element.148.refs_0_, bf16[96,1152]{1,0:T(8,128)(2,1)S(1)} %total.5.refs_1_, bf16[96,1152]{1,0:T(8,128)(2,1)S(1)} %collective-permute-done.22.refs_2_), custom_call_target="tpu_custom_call", output_to_operand_aliasing={{}: (0, {})} | custom-call | flops 1990656 | bytes 17252352 | tf_op jit(solution)/shard_map/finish/pallas_call | solution.py:447
  (50 shorter events, 11.5 us)
Async XLA Ops:
  3.2 14.5 %collective-permute-start.5 = (bf16[512,384]{1,0:T(8,128)(2,1)S(1)}, bf16[512,384]{1,0:T(8,128)(2,1)S(1)}, u32[]{:S(2)}, u32[]{:S(2)}) collective-permute-start(bf16[512,384]{1,0:T(8,128)(2,1)S(1)} %get-tuple-element.103.grad_ref.rest_0_), channel_id=1, source_target_pairs={{0,2},{2,0},{1,3},{3,1},{4,6},{6,4},{5,7},{7,5},{8,10},{10,8},{9,1... | collective-permute-start | bytes 1179656 | tf_op jit(solution)/shard_map/ppermute | solution.py:463
  6.2 1.7 %collective-permute-start = (bf16[512,384]{1,0:T(8,128)(2,1)S(1)}, bf16[512,384]{1,0:T(8,128)(2,1)S(1)}, u32[]{:S(2)}, u32[]{:S(2)}) collective-permute-start(bf16[512,384]{1,0:T(8,128)(2,1)S(1)} %get-tuple-element.121.snake_ref.own_ref), channel_id=1, source_target_pairs={{0,1},{1,0},{2,3},{3,2},{4,5},{5,4},{6,7},{7,6},{8,9},{9,8},{10,11... | collective-permute-start | bytes 1179656 | tf_op jit(solution)/shard_map/ppermute | solution.py:463
  10.2 2.4 %collective-permute-start.1 = (bf16[512,384]{1,0:T(8,128)(2,1)S(1)}, bf16[512,384]{1,0:T(8,128)(2,1)S(1)}, u32[]{:S(2)}, u32[]{:S(2)}) collective-permute-start(bf16[512,384]{1,0:T(8,128)(2,1)S(1)} %get-tuple-element.118.snake_ref.refs_0_.own_ref), channel_id=1, source_target_pairs={{0,1},{1,0},{2,3},{3,2},{4,5},{5,4},{6,7},{7,6},{8,9},{9,8},{10,11... | collective-permute-start | bytes 1179656 | tf_op jit(solution)/shard_map/ppermute | solution.py:463
  11.6 4.4 %collective-permute-start.3 = (bf16[512,384]{1,0:T(8,128)(2,1)S(1)}, bf16[512,384]{1,0:T(8,128)(2,1)S(1)}, u32[]{:S(2)}, u32[]{:S(2)}) collective-permute-start(bf16[512,384]{1,0:T(8,128)(2,1)S(1)} %get-tuple-element.92), channel_id=1, source_target_pairs={{0,1},{1,0},{2,3},{3,2},{4,5},{5,4},{6,7},{7,6},{8,9},{9,8},{10,11... | collective-permute-start | bytes 1179656 | tf_op jit(solution)/shard_map/ppermute | solution.py:463
  14.3 5.6 %collective-permute-start.2 = (bf16[512,384]{1,0:T(8,128)(2,1)S(1)}, bf16[512,384]{1,0:T(8,128)(2,1)S(1)}, u32[]{:S(2)}, u32[]{:S(2)}) collective-permute-start(bf16[512,384]{1,0:T(8,128)(2,1)S(1)} %get-tuple-element.122.refs_0_.own_ref.snake_ref), channel_id=1, source_target_pairs={{0,1},{1,0},{2,3},{3,2},{4,5},{5,4},{6,7},{7,6},{8,9},{9,8},{10,11... | collective-permute-start | bytes 1179656 | tf_op jit(solution)/shard_map/ppermute | solution.py:463
  15.0 7.8 %collective-permute-start.7 = (bf16[192,512]{1,0:T(8,128)(2,1)S(1)}, bf16[192,512]{1,0:T(8,128)(2,1)S(1)}, u32[]{:S(2)}, u32[]{:S(2)}) collective-permute-start(bf16[192,512]{1,0:T(8,128)(2,1)S(1)} %turn.2), channel_id=1, source_target_pairs={{0,2},{2,0},{1,3},{3,1},{4,6},{6,4},{5,7},{7,5},{8,10},{10,8},{9,1... | collective-permute-start | bytes 589832 | tf_op jit(solution)/shard_map/ppermute | solution.py:463
  17.6 15.3 %collective-permute-start.4 = (bf16[512,384]{1,0:T(8,128)(2,1)S(1)}, bf16[512,384]{1,0:T(8,128)(2,1)S(1)}, u32[]{:S(2)}, u32[]{:S(2)}) collective-permute-start(bf16[512,384]{1,0:T(8,128)(2,1)S(1)} %get-tuple-element.107.grad_ref), channel_id=1, source_target_pairs={{0,2},{2,0},{1,3},{3,1},{4,6},{6,4},{5,7},{7,5},{8,10},{10,8},{9,1... | collective-permute-start | bytes 1179656 | tf_op jit(solution)/shard_map/ppermute | solution.py:463
  20.3 14.9 %collective-permute-start.10 = (bf16[192,512]{1,0:T(8,128)(2,1)S(1)}, bf16[192,512]{1,0:T(8,128)(2,1)S(1)}, u32[]{:S(2)}, u32[]{:S(2)}) collective-permute-start(bf16[192,512]{1,0:T(8,128)(2,1)S(1)} %turn.3), channel_id=1, source_target_pairs={{0,2},{2,0},{1,3},{3,1},{4,6},{6,4},{5,7},{7,5},{8,10},{10,8},{9,1... | collective-permute-start | bytes 589832 | tf_op jit(solution)/shard_map/ppermute | solution.py:463
  21.4 2.3 %collective-permute-start.6 = (bf16[512,384]{1,0:T(8,128)(2,1)S(1)}, bf16[512,384]{1,0:T(8,128)(2,1)S(1)}, u32[]{:S(2)}, u32[]{:S(2)}) collective-permute-start(bf16[512,384]{1,0:T(8,128)(2,1)S(1)} %get-tuple-element.109), channel_id=1, source_target_pairs={{0,1},{1,0},{2,3},{3,2},{4,5},{5,4},{6,7},{7,6},{8,9},{9,8},{10,11... | collective-permute-start | bytes 1179656 | tf_op jit(solution)/shard_map/ppermute | solution.py:463
  22.8 2.6 %collective-permute-start.8 = (bf16[192,512]{1,0:T(8,128)(2,1)S(1)}, bf16[192,512]{1,0:T(8,128)(2,1)S(1)}, u32[]{:S(2)}, u32[]{:S(2)}) collective-permute-start(bf16[192,512]{1,0:T(8,128)(2,1)S(1)} %collective-permute-done.7.across_ref), channel_id=1, source_target_pairs={{0,1},{1,0},{2,3},{3,2},{4,5},{5,4},{6,7},{7,6},{8,9},{9,8},{10,11... | collective-permute-start | bytes 589832 | tf_op jit(solution)/shard_map/ppermute | solution.py:463
  26.9 13.7 %collective-permute-start.13 = (bf16[192,1152]{1,0:T(8,128)(2,1)S(1)}, bf16[192,1152]{1,0:T(8,128)(2,1)S(1)}, u32[]{:S(2)}, u32[]{:S(2)}) collective-permute-start(bf16[192,1152]{1,0:T(8,128)(2,1)S(1)} %get-tuple-element.131), channel_id=1, source_target_pairs={{0,4},{4,0},{8,12},{12,8},{1,5},{5,1},{9,13},{13,9},{2,6},{6,2},{1... | collective-permute-start | bytes 1327112 | tf_op jit(solution)/shard_map/ppermute | solution.py:463
  29.4 1.8 %collective-permute-start.9 = (bf16[512,384]{1,0:T(8,128)(2,1)S(1)}, bf16[512,384]{1,0:T(8,128)(2,1)S(1)}, u32[]{:S(2)}, u32[]{:S(2)}) collective-permute-start(bf16[512,384]{1,0:T(8,128)(2,1)S(1)} %get-tuple-element.117), channel_id=1, source_target_pairs={{0,1},{1,0},{2,3},{3,2},{4,5},{5,4},{6,7},{7,6},{8,9},{9,8},{10,11... | collective-permute-start | bytes 1179656 | tf_op jit(solution)/shard_map/ppermute | solution.py:463
  33.7 20.0 %collective-permute-start.14 = (bf16[384,512]{1,0:T(8,128)(2,1)S(1)}, bf16[384,512]{1,0:T(8,128)(2,1)S(1)}, u32[]{:S(2)}, u32[]{:S(2)}) collective-permute-start(bf16[384,512]{1,0:T(8,128)(2,1)S(1)} %turn_whole.1), channel_id=1, source_target_pairs={{0,2},{2,0},{1,3},{3,1},{4,6},{6,4},{5,7},{7,5},{8,10},{10,8},{9,1... | collective-permute-start | bytes 1179656 | tf_op jit(solution)/shard_map/ppermute | solution.py:463
  35.2 3.1 %collective-permute-start.11 = (bf16[192,512]{1,0:T(8,128)(2,1)S(1)}, bf16[192,512]{1,0:T(8,128)(2,1)S(1)}, u32[]{:S(2)}, u32[]{:S(2)}) collective-permute-start(bf16[192,512]{1,0:T(8,128)(2,1)S(1)} %collective-permute-done.10.across_ref), channel_id=1, source_target_pairs={{0,1},{1,0},{2,3},{3,2},{4,5},{5,4},{6,7},{7,6},{8,9},{9,8},{10,11... | collective-permute-start | bytes 589832 | tf_op jit(solution)/shard_map/ppermute | solution.py:463
  36.0 17.5 %collective-permute-start.12 = (bf16[512,384]{1,0:T(8,128)(2,1)S(1)}, bf16[512,384]{1,0:T(8,128)(2,1)S(1)}, u32[]{:S(2)}, u32[]{:S(2)}) collective-permute-start(bf16[512,384]{1,0:T(8,128)(2,1)S(1)} %get-tuple-element.129.grad_ref), channel_id=1, source_target_pairs={{0,2},{2,0},{1,3},{3,1},{4,6},{6,4},{5,7},{7,5},{8,10},{10,8},{9,1... | collective-permute-start | bytes 1179656 | tf_op jit(solution)/shard_map/ppermute | solution.py:463
  39.7 18.2 %collective-permute-start.15 = (bf16[208,1152]{1,0:T(8,128)(2,1)S(1)}, bf16[208,1152]{1,0:T(8,128)(2,1)S(1)}, u32[]{:S(2)}, u32[]{:S(2)}) collective-permute-start(bf16[208,1152]{1,0:T(8,128)(2,1)S(1)} %get-tuple-element.136), channel_id=1, source_target_pairs={{0,4},{4,0},{8,12},{12,8},{1,5},{5,1},{9,13},{13,9},{2,6},{6,2},{1... | collective-permute-start | bytes 1437704 | tf_op jit(solution)/shard_map/ppermute | solution.py:463
  40.7 18.7 %collective-permute-start.16 = (bf16[96,1152]{1,0:T(8,128)(2,1)S(1)}, bf16[96,1152]{1,0:T(8,128)(2,1)S(1)}, u32[]{:S(2)}, u32[]{:S(2)}) collective-permute-start(bf16[96,1152]{1,0:T(8,128)(2,1)S(1)} %fold.3), channel_id=1, source_target_pairs={{0,8},{4,12},{8,0},{12,4},{1,9},{5,13},{9,1},{13,5},{2,10},{6,14},... | collective-permute-start | bytes 663560 | tf_op jit(solution)/shard_map/ppermute | solution.py:463
  55.1 17.5 %collective-permute-start.17 = (bf16[192,1152]{1,0:T(8,128)(2,1)S(1)}, bf16[192,1152]{1,0:T(8,128)(2,1)S(1)}, u32[]{:S(2)}, u32[]{:S(2)}) collective-permute-start(bf16[192,1152]{1,0:T(8,128)(2,1)S(1)} %get-tuple-element.140), channel_id=1, source_target_pairs={{0,4},{4,0},{8,12},{12,8},{1,5},{5,1},{9,13},{13,9},{2,6},{6,2},{1... | collective-permute-start | bytes 1327112 | tf_op jit(solution)/shard_map/ppermute | solution.py:463
  58.0 15.7 %collective-permute-start.18 = (bf16[112,1152]{1,0:T(8,128)(2,1)S(1)}, bf16[112,1152]{1,0:T(8,128)(2,1)S(1)}, u32[]{:S(2)}, u32[]{:S(2)}) collective-permute-start(bf16[112,1152]{1,0:T(8,128)(2,1)S(1)} %get-tuple-element.142), channel_id=1, source_target_pairs={{0,8},{4,12},{8,0},{12,4},{1,9},{5,13},{9,1},{13,5},{2,10},{6,14},... | collective-permute-start | bytes 774152 | tf_op jit(solution)/shard_map/ppermute | solution.py:463
  59.5 26.7 %collective-permute-start.20 = (bf16[96,1152]{1,0:T(8,128)(2,1)S(1)}, bf16[96,1152]{1,0:T(8,128)(2,1)S(1)}, u32[]{:S(2)}, u32[]{:S(2)}) collective-permute-start(bf16[96,1152]{1,0:T(8,128)(2,1)S(1)} %total.3.refs_1_), channel_id=1, source_target_pairs={{0,2},{2,0},{1,3},{3,1},{4,6},{6,4},{5,7},{7,5},{8,10},{10,8},{9,1... | collective-permute-start | bytes 663560 | tf_op jit(solution)/shard_map/ppermute | solution.py:463
  72.7 11.9 %collective-permute-start.19 = (bf16[96,1152]{1,0:T(8,128)(2,1)S(1)}, bf16[96,1152]{1,0:T(8,128)(2,1)S(1)}, u32[]{:S(2)}, u32[]{:S(2)}) collective-permute-start(bf16[96,1152]{1,0:T(8,128)(2,1)S(1)} %fold.5), channel_id=1, source_target_pairs={{0,8},{4,12},{8,0},{12,4},{1,9},{5,13},{9,1},{13,5},{2,10},{6,14},... | collective-permute-start | bytes 663560 | tf_op jit(solution)/shard_map/ppermute | solution.py:463
  73.8 12.4 %collective-permute-start.21 = (bf16[112,1152]{1,0:T(8,128)(2,1)S(1)}, bf16[112,1152]{1,0:T(8,128)(2,1)S(1)}, u32[]{:S(2)}, u32[]{:S(2)}) collective-permute-start(bf16[112,1152]{1,0:T(8,128)(2,1)S(1)} %get-tuple-element.147.refs_3_), channel_id=1, source_target_pairs={{0,2},{2,0},{1,3},{3,1},{4,6},{6,4},{5,7},{7,5},{8,10},{10,8},{9,1... | collective-permute-start | bytes 774152 | tf_op jit(solution)/shard_map/ppermute | solution.py:463
  84.7 6.7 %collective-permute-start.22 = (bf16[96,1152]{1,0:T(8,128)(2,1)S(1)}, bf16[96,1152]{1,0:T(8,128)(2,1)S(1)}, u32[]{:S(2)}, u32[]{:S(2)}) collective-permute-start(bf16[96,1152]{1,0:T(8,128)(2,1)S(1)} %total.5.refs_1_), channel_id=1, source_target_pairs={{0,2},{2,0},{1,3},{3,1},{4,6},{6,4},{5,7},{7,5},{8,10},{10,8},{9,1... | collective-permute-start | bytes 663560 | tf_op jit(solution)/shard_map/ppermute | solution.py:463

commit v13 on v12

--- a/solution.py
+++ b/solution.py
@@ -738,10 +738,10 @@
     turn_whole(0)
     send_gradient(0)
     forward_own(2)
-    residual_out = forward_partner(2)
     sequence.weight = 0.01
     weights(1)
     fold(2)
+    residual_out = forward_partner(2)
     far_rows(0)
     sequence.weight = 0.01
     weights(0)

time: 92.7 us -> 92.5 us (level)
  transfers between devices with their start and end apart: 23 -> 23, of which waited for: 8 -> 9; matrix products, arithmetic and copies ran while one was open for 0% -> 0% of each run, Pallas kernels for 30% -> 30%
where the time goes in v13:
time: 92.5 us; the launch traced here: 92.3 us
  waiting for transfers between devices  38.5 us (42%)
  Pallas kernels  31.1 us (34%)
  starting transfers between devices  21.6 us (23%)
  between operations  1.1 us (1%)
    ppermute x23, waiting for transfers between devices, swap(): lax.ppermute(x, axis, [(i, other(i)) for i in range(lax.axis_size(axis))])  38.5 us
    pallas_call x36, Pallas kernels, call(): pl.pallas_call(kernel, in_specs=[ANY_HBM if i else IN_VMEM for i in ins],...  31.1 us
    ppermute x23, starting transfers between devices, swap(): lax.ppermute(x, axis, [(i, other(i)) for i in range(lax.axis_size(axis))])  21.6 us
  transfers between devices with their start and end apart: 23, of which 9 were waited for; matrix products, arithmetic and copies ran while one was open for 0% of the time, Pallas kernels for 30%

profile of v13, /device:TPU:0, one launch (start us, length us, event | category | flops | bytes accessed | tf_op | source)
XLA Modules:
  0.0 92.3 jit_solution(7662690217745182057)
XLA Ops:
  0.6 2.5 %prep.1 = (f32[512,384]{1,0:T(8,128)S(1)}, bf16[512,384]{1,0:T(8,128)(2,1)S(1)}, bf16[512,384]{1,0:T(8,128)(2,1)S(1)}, f32[512,128]{1,0:T(8,128)S(1)}, f32[3,384...) custom-call(s32[16]{0:T(128)} %len_hbm.1, s32[16]{0:T(128)} %own_hbm.1, s32[16]{0:T(128)} %start_hbm.1, ...), custom_call_target="tpu_custom_call" | custom-call | flops 78643200 | bytes 44003200 | tf_op jit(solution)/shard_map/prep/pallas_call | solution.py:447
  3.2 3.0 %collective-permute-start.3 = (bf16[512,384]{1,0:T(8,128)(2,1)S(1)}, bf16[512,384]{1,0:T(8,128)(2,1)S(1)}, u32[]{:S(2)}, u32[]{:S(2)}) collective-permute-start(bf16[512,384]{1,0:T(8,128)(2,1)S(1)} %get-tuple-element.97.grad_ref.rest_0_), channel_id=1, source_target_pairs={{0,2},{2,0},{1,3},{3,1},{4,6},{6,4},{5,7},{7,5},{8,10},{10,8},{9,1... | collective-permute-start | bytes 1179656 | tf_op jit(solution)/shard_map/ppermute | solution.py:463
  6.2 1.6 %forward_own.3 = (f32[512,384]{1,0:T(8,128)S(1)}, bf16[2,1152,384]{2,1,0:T(8,128)(2,1)S(1)}) custom-call(bf16[512,384]{1,0:T(8,128)(2,1)S(1)} %get-tuple-element.121.snake_ref.own_ref, bf16[2,1152,384]{2,1,0:T(8,128)(2,1)S(1)} %get-tuple-element.80.weight_ref, bf16[3,3,768,384]{3,2,1,0:T(8,128)(2,1)} %rest_1_.1), custom_call_target="tpu_custom_call" | custom-call | flops 4529848320 | bytes 47185920 | tf_op jit(solution)/shard_map/forward_own/pallas_call | solution.py:447
  7.9 2.3 %forward_partner.3 = (f32[512,384]{1,0:T(8,128)S(1)}, bf16[512,384]{1,0:T(8,128)(2,1)S(1)}, bf16[2,1152,384]{2,1,0:T(8,128)(2,1)S(1)}) custom-call(bf16[512,384]{1,0:T(8,128)(2,1)S(1)} %collective-permute-done.snake_ref.partner_ref, bf16[2,1152,384]{2,1,0:T(8,128)(2,1)S(1)} %get-tuple-element.80.weight_ref, f32[512,384]{1,0:T(8,128)S(1)} %get-tuple-element.84.own_ref, ...), custom_call_target="tpu_custom_call" | custom-call | flops 4529848320 | bytes 69514240 | tf_op jit(solution)/shard_map/forward_partner/pallas_call | solution.py:447
  10.7 0.9 back_partner.3
  12.6 1.7 %forward_partner.4 = (f32[512,384]{1,0:T(8,128)S(1)}, bf16[512,384]{1,0:T(8,128)(2,1)S(1)}) custom-call(bf16[512,384]{1,0:T(8,128)(2,1)S(1)} %collective-permute-done.1.snake_ref.partner_ref, bf16[2,1152,384]{2,1,0:T(8,128)(2,1)S(1)} %get-tuple-element.90.weight_ref, f32[512,384]{1,0:T(8,128)S(1)} %forward_own.4.own_ref, ...), custom_call_target="tpu_custom_call" | custom-call | flops 4529848320 | bytes 51819520 | tf_op jit(solution)/shard_map/forward_partner/pallas_call | solution.py:447
  16.0 1.6 %combine.3 = (f32[1,384]{1,0:T(1,128)S(1)}, f32[512,384]{1,0:T(8,128)S(1)}, bf16[512,384]{1,0:T(8,128)(2,1)S(1)}) custom-call(f32[512,384]{1,0:T(8,128)S(1)} %back_own.3.own_ref, bf16[512,384]{1,0:T(8,128)(2,1)S(1)} %collective-permute-done.4.partner_ref, f32[512,384]{1,0:T(8,128)S(1)} %get-tuple-element.101.stream_ref.old_ref, ...), custom_call_target="tpu_custom_call" | custom-call | flops 117964800 | bytes 38072320 | tf_op jit(solution)/shard_map/combine/pallas_call | solution.py:447
  17.6 2.0 %collective-permute-start.9 = (bf16[512,384]{1,0:T(8,128)(2,1)S(1)}, bf16[512,384]{1,0:T(8,128)(2,1)S(1)}, u32[]{:S(2)}, u32[]{:S(2)}) collective-permute-start(bf16[512,384]{1,0:T(8,128)(2,1)S(1)} %get-tuple-element.118.grad_ref), channel_id=1, source_target_pairs={{0,2},{2,0},{1,3},{3,1},{4,6},{6,4},{5,7},{7,5},{8,10},{10,8},{9,1... | collective-permute-start | bytes 1179656 | tf_op jit(solution)/shard_map/ppermute | solution.py:463
  20.5 0.9 back_partner.4
  21.4 1.4 %collective-permute-done.6.across_ref = bf16[192,512]{1,0:T(8,128)(2,1)S(1)} collective-permute-done((bf16[192,512]{1,0:T(8,128)(2,1)S(1)}, bf16[192,512]{1,0:T(8,128)(2,1)S(1)}, u32[]{:S(2)}, u32[]{:S(2)}) %collective-permute-start.6) | collective-permute-done | bytes 196640 | tf_op jit(solution)/shard_map/ppermute | solution.py:463
  22.8 0.9 back_own.4.own_ref
  23.7 1.7 %combine.4 = (f32[1,384]{1,0:T(1,128)S(1)}, bf16[512,384]{1,0:T(8,128)(2,1)S(1)}) custom-call(f32[512,384]{1,0:T(8,128)S(1)} %back_own.4.own_ref, bf16[512,384]{1,0:T(8,128)(2,1)S(1)} %collective-permute-done.5.partner_ref, f32[512,384]{1,0:T(8,128)S(1)} %get-tuple-element.95.old_ref.stream_ref, f32[3,384]{1,0:T(4,128)S(1)} %get-tuple-element.87.rest_0_.alphas_ref, ...), custom_call_target="tpu_custom_call" | custom-call | flops 117964800 | bytes 34140160 | tf_op jit(solution)/shard_map/combine/pallas_call | solution.py:447
  25.4 1.4 %paired_weight.3 = (bf16[192,1152]{1,0:T(8,128)(2,1)S(1)}, bf16[192,1152]{1,0:T(8,128)(2,1)S(1)}) custom-call(bf16[384,512]{1,0:T(8,128)(2,1)S(1)} %own_rows.3.own_ref, bf16[512,1152]{1,0:T(8,128)(2,1)S(1)} %get-tuple-element.100.shifted_ref, bf16[192,512]{1,0:T(8,128)(2,1)S(1)} %collective-permute-done.6.across_ref, ...), custom_call_target="tpu_custom_call" | custom-call | flops 9059696640 | bytes 40304640 | tf_op jit(solution)/shard_map/paired_weight/pallas_call | solution.py:447
  26.8 1.6 %collective-permute-start.12 = (bf16[192,1152]{1,0:T(8,128)(2,1)S(1)}, bf16[192,1152]{1,0:T(8,128)(2,1)S(1)}, u32[]{:S(2)}, u32[]{:S(2)}) collective-permute-start(bf16[192,1152]{1,0:T(8,128)(2,1)S(1)} %get-tuple-element.129), channel_id=1, source_target_pairs={{0,4},{4,0},{8,12},{12,8},{1,5},{5,1},{9,13},{13,9},{2,6},{6,2},{1... | collective-permute-start | bytes 1327112 | tf_op jit(solution)/shard_map/ppermute | solution.py:463
  28.5 0.9 back_partner.5
  31.2 1.4 %combine.5.rest_0_ = f32[1,384]{1,0:T(1,128)S(1)} custom-call(f32[512,384]{1,0:T(8,128)S(1)} %back_own.5.own_ref, bf16[512,384]{1,0:T(8,128)(2,1)S(1)} %collective-permute-done.8.partner_ref, f32[512,384]{1,0:T(8,128)S(1)} %get-tuple-element.85.old_ref.stream_ref, f32[3,384]{1,0:T(4,128)S(1)} %get-tuple-element.87.rest_0_.alphas_ref), custom_call_target="tpu_custom_call" | custom-call | flops 117964800 | bytes 19722240 | tf_op jit(solution)/shard_map/combine/pallas_call | solution.py:447
  33.7 1.5 %collective-permute-start.14 = (bf16[384,512]{1,0:T(8,128)(2,1)S(1)}, bf16[384,512]{1,0:T(8,128)(2,1)S(1)}, u32[]{:S(2)}, u32[]{:S(2)}) collective-permute-start(bf16[384,512]{1,0:T(8,128)(2,1)S(1)} %turn_whole.1), channel_id=1, source_target_pairs={{0,2},{2,0},{1,3},{3,1},{4,6},{6,4},{5,7},{7,5},{8,10},{10,8},{9,1... | collective-permute-start | bytes 1179656 | tf_op jit(solution)/shard_map/ppermute | solution.py:463
  36.6 1.4 %paired_weight.4 = (bf16[208,1152]{1,0:T(8,128)(2,1)S(1)}, bf16[192,1152]{1,0:T(8,128)(2,1)S(1)}) custom-call(bf16[384,512]{1,0:T(8,128)(2,1)S(1)} %own_rows.4.own_ref, bf16[512,1152]{1,0:T(8,128)(2,1)S(1)} %get-tuple-element.107.shifted_ref, bf16[192,512]{1,0:T(8,128)(2,1)S(1)} %collective-permute-done.10.across_ref, ...), custom_call_target="tpu_custom_call" | custom-call | flops 9059696 | bytes 40719 | tf_op jit(solution)/shard_map/paired_weight/pallas_call | solution.py:447
  38.0 1.1 %collective-permute-start.15 = (bf16[208,1152]{1,0:T(8,128)(2,1)S(1)}, bf16[208,1152]{1,0:T(8,128)(2,1)S(1)}, u32[]{:S(2)}, u32[]{:S(2)}) collective-permute-start(bf16[208,1152]{1,0:T(8,128)(2,1)S(1)} %get-tuple-element.136), channel_id=1, source_target_pairs={{0,4},{4,0},{8,12},{12,8},{1,5},{5,1},{9,13},{13,9},{2,6},{6,2},{1... | collective-permute-start | bytes 1437704 | tf_op jit(solution)/shard_map/ppermute | solution.py:463
  39.5 2.6 %collective-permute-start.16 = (bf16[96,1152]{1,0:T(8,128)(2,1)S(1)}, bf16[96,1152]{1,0:T(8,128)(2,1)S(1)}, u32[]{:S(2)}, u32[]{:S(2)}) collective-permute-start(bf16[96,1152]{1,0:T(8,128)(2,1)S(1)} %fold.3), channel_id=1, source_target_pairs={{0,8},{4,12},{8,0},{12,4},{1,9},{5,13},{9,1},{13,5},{2,10},{6,14},... | collective-permute-start | bytes 663560 | tf_op jit(solution)/shard_map/ppermute | solution.py:463
  42.2 1.6 %forward_partner.5 = bf16[512,384]{1,0:T(8,128)(2,1)} custom-call(bf16[512,384]{1,0:T(8,128)(2,1)S(1)} %collective-permute-done.2.partner_ref.snake_ref, bf16[2,1152,384]{2,1,0:T(8,128)(2,1)S(1)} %get-tuple-element.82.weight_ref, f32[512,384]{1,0:T(8,128)S(1)} %forward_own.5.own_ref, f32[512,384]{1,0:T(8,128)S(1)} %get-tuple-element.101.stream_ref.old_ref, ...), custom_call_target="tpu_custom_call" | custom-call | flops 4529848 | bytes 43909 | tf_op jit(solution)/shard_map/forward_partner/pallas_call | solution.py:447
  43.8 9.6 %collective-permute-done.13.grad_ref = bf16[512,384]{1,0:T(8,128)(2,1)S(1)} collective-permute-done((bf16[512,384]{1,0:T(8,128)(2,1)S(1)}, bf16[512,384]{1,0:T(8,128)(2,1)S(1)}, u32[]{:S(2)}, u32[]{:S(2)}) %collective-permute-start.13) | collective-permute-done | bytes 393248 | tf_op jit(solution)/shard_map/ppermute | solution.py:463
  53.6 1.4 %paired_weight.5 = (bf16[192,1152]{1,0:T(8,128)(2,1)S(1)}, bf16[192,1152]{1,0:T(8,128)(2,1)S(1)}) custom-call(bf16[384,512]{1,0:T(8,128)(2,1)S(1)} %own_rows.5.own_ref, bf16[512,1152]{1,0:T(8,128)(2,1)S(1)} %get-tuple-element.115.shifted_ref, bf16[384,512]{1,0:T(8,128)(2,1)S(1)} %collective-permute-done.14.across_ref.across_other_ref, ...), custom_call_target="tpu_custom_call" | custom-call | flops 9059696 | bytes 44236 | tf_op jit(solution)/shard_map/paired_weight/pallas_call | solution.py:447
  56.0 2.3 %collective-permute-start.18 = (bf16[112,1152]{1,0:T(8,128)(2,1)S(1)}, bf16[112,1152]{1,0:T(8,128)(2,1)S(1)}, u32[]{:S(2)}, u32[]{:S(2)}) collective-permute-start(bf16[112,1152]{1,0:T(8,128)(2,1)S(1)} %get-tuple-element.142), channel_id=1, source_target_pairs={{0,8},{4,12},{8,0},{12,4},{1,9},{5,13},{9,1},{13,5},{2,10},{6,14},... | collective-permute-start | bytes 774152 | tf_op jit(solution)/shard_map/ppermute | solution.py:463
  58.4 1.4 %collective-permute-start.20 = (bf16[96,1152]{1,0:T(8,128)(2,1)S(1)}, bf16[96,1152]{1,0:T(8,128)(2,1)S(1)}, u32[]{:S(2)}, u32[]{:S(2)}) collective-permute-start(bf16[96,1152]{1,0:T(8,128)(2,1)S(1)} %total.3.refs_1_), channel_id=1, source_target_pairs={{0,2},{2,0},{1,3},{3,1},{4,6},{6,4},{5,7},{7,5},{8,10},{10,8},{9,1... | collective-permute-start | bytes 663560 | tf_op jit(solution)/shard_map/ppermute | solution.py:463
  59.8 12.3 %collective-permute-done.17.got = bf16[192,1152]{1,0:T(8,128)(2,1)S(1)} collective-permute-done((bf16[192,1152]{1,0:T(8,128)(2,1)S(1)}, bf16[192,1152]{1,0:T(8,128)(2,1)S(1)}, u32[]{:S(2)}, u32[]{:S(2)}) %collective-permute-start.17) | collective-permute-done | bytes 442400 | tf_op jit(solution)/shard_map/ppermute | solution.py:463
  72.9 1.3 %collective-permute-start.21 = (bf16[112,1152]{1,0:T(8,128)(2,1)S(1)}, bf16[112,1152]{1,0:T(8,128)(2,1)S(1)}, u32[]{:S(2)}, u32[]{:S(2)}) collective-permute-start(bf16[112,1152]{1,0:T(8,128)(2,1)S(1)} %get-tuple-element.147.refs_3_), channel_id=1, source_target_pairs={{0,2},{2,0},{1,3},{3,1},{4,6},{6,4},{5,7},{7,5},{8,10},{10,8},{9,1... | collective-permute-start | bytes 774152 | tf_op jit(solution)/shard_map/ppermute | solution.py:463
  74.2 9.4 %collective-permute-done.19.late = bf16[96,1152]{1,0:T(8,128)(2,1)S(1)} collective-permute-done((bf16[96,1152]{1,0:T(8,128)(2,1)S(1)}, bf16[96,1152]{1,0:T(8,128)(2,1)S(1)}, u32[]{:S(2)}, u32[]{:S(2)}) %collective-permute-start.19) | collective-permute-done | bytes 221216 | tf_op jit(solution)/shard_map/ppermute | solution.py:463
  83.7 1.3 %collective-permute-start.22 = (bf16[96,1152]{1,0:T(8,128)(2,1)S(1)}, bf16[96,1152]{1,0:T(8,128)(2,1)S(1)}, u32[]{:S(2)}, u32[]{:S(2)}) collective-permute-start(bf16[96,1152]{1,0:T(8,128)(2,1)S(1)} %total.5.refs_1_), channel_id=1, source_target_pairs={{0,2},{2,0},{1,3},{3,1},{4,6},{6,4},{5,7},{7,5},{8,10},{10,8},{9,1... | collective-permute-start | bytes 663560 | tf_op jit(solution)/shard_map/ppermute | solution.py:463
  85.0 1.9 %finish.2 = (f32[3,3,192,384]{3,2,1,0:T(8,128)}, f32[3,384]{1,0:T(4,128)}) custom-call(f32[1,1152]{1,0:T(1,128)S(1)} %get-tuple-element.145.refs_0_, bf16[96,1152]{1,0:T(8,128)(2,1)S(1)} %total.3.refs_1_, bf16[96,1152]{1,0:T(8,128)(2,1)S(1)} %collective-permute-done.20.refs_2_, bf16[112,1152]{1,0:T(8,128)(2,1)S(1)} %get-tuple-element.147.refs_3_, ...), custom_call_target="tpu_custom_call" | custom-call | flops 1990656 | bytes 10865664 | tf_op jit(solution)/shard_map/finish/pallas_call | solution.py:447
  86.9 4.2 %collective-permute-done.22.refs_2_ = bf16[96,1152]{1,0:T(8,128)(2,1)S(1)} collective-permute-done((bf16[96,1152]{1,0:T(8,128)(2,1)S(1)}, bf16[96,1152]{1,0:T(8,128)(2,1)S(1)}, u32[]{:S(2)}, u32[]{:S(2)}) %collective-permute-start.22) | collective-permute-done | bytes 221216 | tf_op jit(solution)/shard_map/ppermute | solution.py:463
  91.1 1.0 %finish.3 = f32[3,3,192,384]{3,2,1,0:T(8,128)} custom-call(f32[3,3,192,384]{3,2,1,0:T(8,128)} %get-tuple-element.148.refs_0_, bf16[96,1152]{1,0:T(8,128)(2,1)S(1)} %total.5.refs_1_, bf16[96,1152]{1,0:T(8,128)(2,1)S(1)} %collective-permute-done.22.refs_2_), custom_call_target="tpu_custom_call", output_to_operand_aliasing={{}: (0, {})} | custom-call | flops 1990656 | bytes 17252352 | tf_op jit(solution)/shard_map/finish/pallas_call | solution.py:447
  (50 shorter events, 11.0 us)
Async XLA Ops:
  3.2 14.4 %collective-permute-start.3 = (bf16[512,384]{1,0:T(8,128)(2,1)S(1)}, bf16[512,384]{1,0:T(8,128)(2,1)S(1)}, u32[]{:S(2)}, u32[]{:S(2)}) collective-permute-start(bf16[512,384]{1,0:T(8,128)(2,1)S(1)} %get-tuple-element.97.grad_ref.rest_0_), channel_id=1, source_target_pairs={{0,2},{2,0},{1,3},{3,1},{4,6},{6,4},{5,7},{7,5},{8,10},{10,8},{9,1... | collective-permute-start | bytes 1179656 | tf_op jit(solution)/shard_map/ppermute | solution.py:463
  6.2 1.7 %collective-permute-start = (bf16[512,384]{1,0:T(8,128)(2,1)S(1)}, bf16[512,384]{1,0:T(8,128)(2,1)S(1)}, u32[]{:S(2)}, u32[]{:S(2)}) collective-permute-start(bf16[512,384]{1,0:T(8,128)(2,1)S(1)} %get-tuple-element.121.snake_ref.own_ref), channel_id=1, source_target_pairs={{0,1},{1,0},{2,3},{3,2},{4,5},{5,4},{6,7},{7,6},{8,9},{9,8},{10,11... | collective-permute-start | bytes 1179656 | tf_op jit(solution)/shard_map/ppermute | solution.py:463
  10.2 2.4 %collective-permute-start.1 = (bf16[512,384]{1,0:T(8,128)(2,1)S(1)}, bf16[512,384]{1,0:T(8,128)(2,1)S(1)}, u32[]{:S(2)}, u32[]{:S(2)}) collective-permute-start(bf16[512,384]{1,0:T(8,128)(2,1)S(1)} %get-tuple-element.117.snake_ref.refs_0_.own_ref), channel_id=1, source_target_pairs={{0,1},{1,0},{2,3},{3,2},{4,5},{5,4},{6,7},{7,6},{8,9},{9,8},{10,11... | collective-permute-start | bytes 1179656 | tf_op jit(solution)/shard_map/ppermute | solution.py:463
  11.6 4.4 %collective-permute-start.4 = (bf16[512,384]{1,0:T(8,128)(2,1)S(1)}, bf16[512,384]{1,0:T(8,128)(2,1)S(1)}, u32[]{:S(2)}, u32[]{:S(2)}) collective-permute-start(bf16[512,384]{1,0:T(8,128)(2,1)S(1)} %get-tuple-element.92), channel_id=1, source_target_pairs={{0,1},{1,0},{2,3},{3,2},{4,5},{5,4},{6,7},{7,6},{8,9},{9,8},{10,11... | collective-permute-start | bytes 1179656 | tf_op jit(solution)/shard_map/ppermute | solution.py:463
  14.3 5.6 %collective-permute-start.2 = (bf16[512,384]{1,0:T(8,128)(2,1)S(1)}, bf16[512,384]{1,0:T(8,128)(2,1)S(1)}, u32[]{:S(2)}, u32[]{:S(2)}) collective-permute-start(bf16[512,384]{1,0:T(8,128)(2,1)S(1)} %get-tuple-element.122.refs_0_.own_ref.snake_ref), channel_id=1, source_target_pairs={{0,1},{1,0},{2,3},{3,2},{4,5},{5,4},{6,7},{7,6},{8,9},{9,8},{10,11... | collective-permute-start | bytes 1179656 | tf_op jit(solution)/shard_map/ppermute | solution.py:463
  15.0 7.8 %collective-permute-start.6 = (bf16[192,512]{1,0:T(8,128)(2,1)S(1)}, bf16[192,512]{1,0:T(8,128)(2,1)S(1)}, u32[]{:S(2)}, u32[]{:S(2)}) collective-permute-start(bf16[192,512]{1,0:T(8,128)(2,1)S(1)} %turn.2), channel_id=1, source_target_pairs={{0,2},{2,0},{1,3},{3,1},{4,6},{6,4},{5,7},{7,5},{8,10},{10,8},{9,1... | collective-permute-start | bytes 589832 | tf_op jit(solution)/shard_map/ppermute | solution.py:463
  17.6 15.3 %collective-permute-start.9 = (bf16[512,384]{1,0:T(8,128)(2,1)S(1)}, bf16[512,384]{1,0:T(8,128)(2,1)S(1)}, u32[]{:S(2)}, u32[]{:S(2)}) collective-permute-start(bf16[512,384]{1,0:T(8,128)(2,1)S(1)} %get-tuple-element.118.grad_ref), channel_id=1, source_target_pairs={{0,2},{2,0},{1,3},{3,1},{4,6},{6,4},{5,7},{7,5},{8,10},{10,8},{9,1... | collective-permute-start | bytes 1179656 | tf_op jit(solution)/shard_map/ppermute | solution.py:463
  20.3 14.8 %collective-permute-start.10 = (bf16[192,512]{1,0:T(8,128)(2,1)S(1)}, bf16[192,512]{1,0:T(8,128)(2,1)S(1)}, u32[]{:S(2)}, u32[]{:S(2)}) collective-permute-start(bf16[192,512]{1,0:T(8,128)(2,1)S(1)} %turn.3), channel_id=1, source_target_pairs={{0,2},{2,0},{1,3},{3,1},{4,6},{6,4},{5,7},{7,5},{8,10},{10,8},{9,1... | collective-permute-start | bytes 589832 | tf_op jit(solution)/shard_map/ppermute | solution.py:463
  21.4 2.3 %collective-permute-start.5 = (bf16[512,384]{1,0:T(8,128)(2,1)S(1)}, bf16[512,384]{1,0:T(8,128)(2,1)S(1)}, u32[]{:S(2)}, u32[]{:S(2)}) collective-permute-start(bf16[512,384]{1,0:T(8,128)(2,1)S(1)} %get-tuple-element.108), channel_id=1, source_target_pairs={{0,1},{1,0},{2,3},{3,2},{4,5},{5,4},{6,7},{7,6},{8,9},{9,8},{10,11... | collective-permute-start | bytes 1179656 | tf_op jit(solution)/shard_map/ppermute | solution.py:463
  22.8 2.6 %collective-permute-start.7 = (bf16[192,512]{1,0:T(8,128)(2,1)S(1)}, bf16[192,512]{1,0:T(8,128)(2,1)S(1)}, u32[]{:S(2)}, u32[]{:S(2)}) collective-permute-start(bf16[192,512]{1,0:T(8,128)(2,1)S(1)} %collective-permute-done.6.across_ref), channel_id=1, source_target_pairs={{0,1},{1,0},{2,3},{3,2},{4,5},{5,4},{6,7},{7,6},{8,9},{9,8},{10,11... | collective-permute-start | bytes 589832 | tf_op jit(solution)/shard_map/ppermute | solution.py:463
  26.8 12.6 %collective-permute-start.12 = (bf16[192,1152]{1,0:T(8,128)(2,1)S(1)}, bf16[192,1152]{1,0:T(8,128)(2,1)S(1)}, u32[]{:S(2)}, u32[]{:S(2)}) collective-permute-start(bf16[192,1152]{1,0:T(8,128)(2,1)S(1)} %get-tuple-element.129), channel_id=1, source_target_pairs={{0,4},{4,0},{8,12},{12,8},{1,5},{5,1},{9,13},{13,9},{2,6},{6,2},{1... | collective-permute-start | bytes 1327112 | tf_op jit(solution)/shard_map/ppermute | solution.py:463
  29.4 1.8 %collective-permute-start.8 = (bf16[512,384]{1,0:T(8,128)(2,1)S(1)}, bf16[512,384]{1,0:T(8,128)(2,1)S(1)}, u32[]{:S(2)}, u32[]{:S(2)}) collective-permute-start(bf16[512,384]{1,0:T(8,128)(2,1)S(1)} %get-tuple-element.116), channel_id=1, source_target_pairs={{0,1},{1,0},{2,3},{3,2},{4,5},{5,4},{6,7},{7,6},{8,9},{9,8},{10,11... | collective-permute-start | bytes 1179656 | tf_op jit(solution)/shard_map/ppermute | solution.py:463
  33.7 20.0 %collective-permute-start.14 = (bf16[384,512]{1,0:T(8,128)(2,1)S(1)}, bf16[384,512]{1,0:T(8,128)(2,1)S(1)}, u32[]{:S(2)}, u32[]{:S(2)}) collective-permute-start(bf16[384,512]{1,0:T(8,128)(2,1)S(1)} %turn_whole.1), channel_id=1, source_target_pairs={{0,2},{2,0},{1,3},{3,1},{4,6},{6,4},{5,7},{7,5},{8,10},{10,8},{9,1... | collective-permute-start | bytes 1179656 | tf_op jit(solution)/shard_map/ppermute | solution.py:463
  35.1 1.4 %collective-permute-start.11 = (bf16[192,512]{1,0:T(8,128)(2,1)S(1)}, bf16[192,512]{1,0:T(8,128)(2,1)S(1)}, u32[]{:S(2)}, u32[]{:S(2)}) collective-permute-start(bf16[192,512]{1,0:T(8,128)(2,1)S(1)} %collective-permute-done.10.across_ref), channel_id=1, source_target_pairs={{0,1},{1,0},{2,3},{3,2},{4,5},{5,4},{6,7},{7,6},{8,9},{9,8},{10,11... | collective-permute-start | bytes 589832 | tf_op jit(solution)/shard_map/ppermute | solution.py:463
  35.1 18.3 %collective-permute-start.13 = (bf16[512,384]{1,0:T(8,128)(2,1)S(1)}, bf16[512,384]{1,0:T(8,128)(2,1)S(1)}, u32[]{:S(2)}, u32[]{:S(2)}) collective-permute-start(bf16[512,384]{1,0:T(8,128)(2,1)S(1)} %get-tuple-element.131.grad_ref), channel_id=1, source_target_pairs={{0,2},{2,0},{1,3},{3,1},{4,6},{6,4},{5,7},{7,5},{8,10},{10,8},{9,1... | collective-permute-start | bytes 1179656 | tf_op jit(solution)/shard_map/ppermute | solution.py:463
  38.0 17.9 %collective-permute-start.15 = (bf16[208,1152]{1,0:T(8,128)(2,1)S(1)}, bf16[208,1152]{1,0:T(8,128)(2,1)S(1)}, u32[]{:S(2)}, u32[]{:S(2)}) collective-permute-start(bf16[208,1152]{1,0:T(8,128)(2,1)S(1)} %get-tuple-element.136), channel_id=1, source_target_pairs={{0,4},{4,0},{8,12},{12,8},{1,5},{5,1},{9,13},{13,9},{2,6},{6,2},{1... | collective-permute-start | bytes 1437704 | tf_op jit(solution)/shard_map/ppermute | solution.py:463
  39.5 18.8 %collective-permute-start.16 = (bf16[96,1152]{1,0:T(8,128)(2,1)S(1)}, bf16[96,1152]{1,0:T(8,128)(2,1)S(1)}, u32[]{:S(2)}, u32[]{:S(2)}) collective-permute-start(bf16[96,1152]{1,0:T(8,128)(2,1)S(1)} %fold.3), channel_id=1, source_target_pairs={{0,8},{4,12},{8,0},{12,4},{1,9},{5,13},{9,1},{13,5},{2,10},{6,14},... | collective-permute-start | bytes 663560 | tf_op jit(solution)/shard_map/ppermute | solution.py:463
  55.0 17.1 %collective-permute-start.17 = (bf16[192,1152]{1,0:T(8,128)(2,1)S(1)}, bf16[192,1152]{1,0:T(8,128)(2,1)S(1)}, u32[]{:S(2)}, u32[]{:S(2)}) collective-permute-start(bf16[192,1152]{1,0:T(8,128)(2,1)S(1)} %get-tuple-element.140), channel_id=1, source_target_pairs={{0,4},{4,0},{8,12},{12,8},{1,5},{5,1},{9,13},{13,9},{2,6},{6,2},{1... | collective-permute-start | bytes 1327112 | tf_op jit(solution)/shard_map/ppermute | solution.py:463
  56.0 16.8 %collective-permute-start.18 = (bf16[112,1152]{1,0:T(8,128)(2,1)S(1)}, bf16[112,1152]{1,0:T(8,128)(2,1)S(1)}, u32[]{:S(2)}, u32[]{:S(2)}) collective-permute-start(bf16[112,1152]{1,0:T(8,128)(2,1)S(1)} %get-tuple-element.142), channel_id=1, source_target_pairs={{0,8},{4,12},{8,0},{12,4},{1,9},{5,13},{9,1},{13,5},{2,10},{6,14},... | collective-permute-start | bytes 774152 | tf_op jit(solution)/shard_map/ppermute | solution.py:463
  58.4 26.6 %collective-permute-start.20 = (bf16[96,1152]{1,0:T(8,128)(2,1)S(1)}, bf16[96,1152]{1,0:T(8,128)(2,1)S(1)}, u32[]{:S(2)}, u32[]{:S(2)}) collective-permute-start(bf16[96,1152]{1,0:T(8,128)(2,1)S(1)} %total.3.refs_1_), channel_id=1, source_target_pairs={{0,2},{2,0},{1,3},{3,1},{4,6},{6,4},{5,7},{7,5},{8,10},{10,8},{9,1... | collective-permute-start | bytes 663560 | tf_op jit(solution)/shard_map/ppermute | solution.py:463
  72.2 11.5 %collective-permute-start.19 = (bf16[96,1152]{1,0:T(8,128)(2,1)S(1)}, bf16[96,1152]{1,0:T(8,128)(2,1)S(1)}, u32[]{:S(2)}, u32[]{:S(2)}) collective-permute-start(bf16[96,1152]{1,0:T(8,128)(2,1)S(1)} %fold.5), channel_id=1, source_target_pairs={{0,8},{4,12},{8,0},{12,4},{1,9},{5,13},{9,1},{13,5},{2,10},{6,14},... | collective-permute-start | bytes 663560 | tf_op jit(solution)/shard_map/ppermute | solution.py:463
  72.9 12.1 %collective-permute-start.21 = (bf16[112,1152]{1,0:T(8,128)(2,1)S(1)}, bf16[112,1152]{1,0:T(8,128)(2,1)S(1)}, u32[]{:S(2)}, u32[]{:S(2)}) collective-permute-start(bf16[112,1152]{1,0:T(8,128)(2,1)S(1)} %get-tuple-element.147.refs_3_), channel_id=1, source_target_pairs={{0,2},{2,0},{1,3},{3,1},{4,6},{6,4},{5,7},{7,5},{8,10},{10,8},{9,1... | collective-permute-start | bytes 774152 | tf_op jit(solution)/shard_map/ppermute | solution.py:463
  83.7 7.4 %collective-permute-start.22 = (bf16[96,1152]{1,0:T(8,128)(2,1)S(1)}, bf16[96,1152]{1,0:T(8,128)(2,1)S(1)}, u32[]{:S(2)}, u32[]{:S(2)}) collective-permute-start(bf16[96,1152]{1,0:T(8,128)(2,1)S(1)} %total.5.refs_1_), channel_id=1, source_target_pairs={{0,2},{2,0},{1,3},{3,1},{4,6},{6,4},{5,7},{7,5},{8,10},{10,8},{9,1... | collective-permute-start | bytes 663560 | tf_op jit(solution)/shard_map/ppermute | solution.py:463
